TPU v7x, 256 devices: a whole 4x4x8 slice. The times are simulated.
256 devices in a mesh: seq: 64 (over x, z, core), tp: 4 (over y).
Axes of the slice: x: 4, y: 4, z: 8, core: 2. Of those that a mesh axis runs over, the one named last changes fastest.
Arguments:
- hidden: bfloat16 [32768, 4608], P('seq', 'tp'), may hold values from -60 to 60, as said below
- norm_gain: float32 [4608], replicated, may hold values from 0.1 to 1.9
- w_query: bfloat16 [4608, 2048], P(None, 'tp'), may hold values from -0.25 to 0.25
- w_key: bfloat16 [4608, 1024], P(None, 'tp'), may hold values from -0.09375 to 0.09375
- w_value: bfloat16 [4608, 1024], P(None, 'tp'), may hold values from -0.09375 to 0.09375
- segment_ids: int32 [32768], P('seq'), may hold values from 0 to 15, as said below
- page_table: int32 [64, 4], P('seq'), may hold values from 0 to 3, each once within a row
Outputs:
- attended: bfloat16 [32768, 2048], P('seq', 'tp')
- kv_cache: bfloat16 [256, 128, 2, 1024], P(('seq', 'tp'))
Inputs may be any that keep to these rules, and one draw needn't show every extreme that they name: hidden is finite. `segment_ids`: never falling along the stream and rising by one at each document start; every number from 0 to 15 appears; no document is longer than 4096 tokens. `page_table`: each row holds every number from 0 to 3 once.
All inputs are finite; a program needn't handle non-finite values.
Results may differ from a plain program's by a relative error of at most 0.012.
The roundings to bfloat16 on the way count: a program that leaves them out, or rounds other values in their place, can miss the bound.
Values may be sent and summed in bfloat16 or wider, within the bound.
No kernel may reach another device: no remote copies, remote signals or barrier semaphores. Data moves between devices by JAX's collectives and lax.ppermute only.
A program may use at most 128 MiB of HBM per device.

v0:
```python
import functools

import jax
import jax.numpy as jnp
import numpy as np
from jax import lax
from jax.experimental import pallas as pl
from jax.experimental.pallas import tpu as pltpu
from jax.sharding import PartitionSpec as P

HD = 128
WIN = 4096
PAGE = 128

logit_cap = 50.0
query_scale = 144.0 ** (-0.5)
norm_eps = 1e-06
log2e = 1.4426950408889634

VMEM = pltpu.VMEM
SMEM = pltpu.SMEM


def whole(space=VMEM):
    return pl.BlockSpec(memory_space=space)


def shifted(block, axis, distance):
    devices = range(lax.axis_size(axis))
    route = [(i - distance, i) for i in devices if i - distance in devices]
    return lax.ppermute(block, axis, route)


def turned(block, axis, distance):
    count = lax.axis_size(axis)
    return lax.ppermute(block, axis, [(i, (i + distance) % count) for i in range(count)])


def swapped(block):
    return lax.ppermute(block, "seq", [(i, i ^ 1) for i in range(lax.axis_size("seq"))])


def rope(x, cos, sin):
    return x * cos + pltpu.roll(x, HD // 2, 1) * sin


def kv_kernel(layout, shards, table, *refs):
    segments, first_page, carried, count = layout
    pieces = refs[: len(segments)]
    gain, wk, wv, cos, sin = refs[len(segments) : len(segments) + 5]
    outs = refs[len(segments) + 5 + carried :]
    normed, pages, streams = outs[0], outs[1], outs[2:]
    rows = normed.shape[0]
    features = gain.shape[1]
    width = features // count

    for start in range(0, rows, 128):
        at = pl.ds(start, 128)
        blocks = []
        for ref, (turn, begin, end) in zip(pieces, segments):
            if begin <= start < end:
                part = ref.at[turn] if len(ref.shape) == 3 else ref
                blocks.append((part, pl.ds(start - begin, 128), turn))
        square = 0.0
        for part, rows_at, turn in blocks:
            wide = part[rows_at, :].astype(jnp.float32)
            square = square + jnp.sum(wide * wide, axis=-1, keepdims=True)
        scale = lax.rsqrt(square * (1.0 / features) + norm_eps)
        for part, rows_at, turn in blocks:
            cols = pl.ds(pl.multiple_of(shards[turn] * width, 128), width)
            wide = part[rows_at, :].astype(jnp.float32)
            normed[at, cols] = (wide * scale * gain[:, cols]).astype(jnp.bfloat16)
    keys = jnp.dot(normed[...], wk[...], preferred_element_type=jnp.float32)
    values = jnp.dot(normed[...], wv[...], preferred_element_type=jnp.float32)
    kv_width = wk.shape[1]
    size = streams[0].shape[0]
    for start in range(0, rows, PAGE):
        at = slice(start, start + PAGE)
        slot = table[first_page + start // PAGE]
        out = streams[start // size]
        to = slice(start % size, start % size + PAGE)
        for head in range(kv_width // HD):
            cols = slice(head * HD, head * HD + HD)
            turned_keys = rope(keys[at, cols], cos[at, :], sin[at, :]).astype(jnp.bfloat16)
            out[to, cols] = turned_keys
            pages[slot, :, cols] = turned_keys
        rounded = values[at].astype(jnp.bfloat16)
        out[to, kv_width:] = rounded
        pages[slot, :, kv_width:] = rounded


def project_kv(shards, table, pieces, gain, wk, wv, cos, sin, size, first_page=0, pages=None):
    features = wk.shape[0]
    rows = cos.shape[0]
    width = 2 * wk.shape[1]
    segments = tuple(where for _, where in pieces)
    arrays = []
    for array, _ in pieces:
        arrays.append(array)
    carried = pages is not None
    operands = [shards, table, *arrays, gain, wk, wv, cos, sin] + ([pages] if carried else [])
    stream = jax.ShapeDtypeStruct((size, width), jnp.bfloat16)
    paged = jax.ShapeDtypeStruct((table.shape[0], PAGE, width), jnp.bfloat16)
    out_shape = (jax.ShapeDtypeStruct((rows, features), jnp.bfloat16), paged)
    out_shape = out_shape + (stream,) * (rows // size)
    specs = [whole(SMEM)] * 2 + [whole()] * (len(operands) - 2)
    return pl.pallas_call(
        functools.partial(kv_kernel, (segments, first_page, carried, shards.shape[0])),
        name="norm_project_kv",
        out_shape=out_shape,
        in_specs=specs,
        out_specs=(whole(),) * len(out_shape),
        input_output_aliases={len(operands) - 1: 1} if carried else {},
        compiler_params=pltpu.CompilerParams(vmem_limit_bytes=14 << 20),
        cost_estimate=pl.CostEstimate(
            flops=2 * rows * features * width,
            transcendentals=rows,
            bytes_accessed=2 * (2 * rows * features + features * width),
        ),
    )(*operands)


def q_kernel(count, *refs):
    normed = refs[:count]
    wq, cos, sin, out = refs[count:]
    start = 0
    for block in normed:
        at = slice(start, start + block.shape[0])
        raw = jnp.dot(block[...], wq[...], preferred_element_type=jnp.float32)
        for head in range(wq.shape[1] // HD):
            cols = slice(head * HD, head * HD + HD)
            out[at, cols] = rope(raw[:, cols], cos[at, :], sin[at, :]).astype(jnp.bfloat16)
        start += block.shape[0]


def project_q(normed, wq, cos, sin):
    rows = cos.shape[0]
    features, width = wq.shape
    return pl.pallas_call(
        functools.partial(q_kernel, len(normed)),
        name="project_q",
        out_shape=jax.ShapeDtypeStruct((rows, width), jnp.bfloat16),
        in_specs=[whole()] * (len(normed) + 3),
        out_specs=whole(),
        compiler_params=pltpu.CompilerParams(vmem_limit_bytes=10 << 20),
        cost_estimate=pl.CostEstimate(
            flops=10000000 * rows,
            transcendentals=0,
            bytes_accessed=rows * width,
        ),
    )(*normed, wq, cos, sin)


def attend_kernel(places, first, last, guarded, meta, low_ref, q_ref, *refs):
    count = len(places)
    blocks = refs[:count]
    refs = refs[count:]
    if first:
        acc, tot = refs[-2:]
        acc[...] = jnp.zeros_like(acc)
        tot[...] = jnp.zeros_like(tot)
    else:
        acc_in, tot_in = refs[:2]
        if last:
            out, acc, tot = refs[2:]
            acc[...] = acc_in[...]
            tot[...] = tot_in[...]
        else:
            acc, tot = refs[2:]
    rows = q_ref.shape[0]
    heads = q_ref.shape[1] // HD
    kv_width = blocks[0].shape[1] // 2
    repeat = heads * HD // kv_width

    def visit(block, index, top):
        span = block.shape[0]
        key_first = meta[index]
        at = slice(top or 0, rows)
        here = (at.stop - at.start, span)
        key_index = key_first + lax.broadcasted_iota(jnp.int32, here, 1)
        allowed = key_index >= low_ref[at, :]
        if top is not None:
            row = meta[0] + top + lax.broadcasted_iota(jnp.int32, here, 0)
            allowed = allowed & (key_index <= row)
        for head in range(heads):
            cols = slice(head * HD, head * HD + HD)
            group = head // repeat
            keys = block[:, group * HD : group * HD + HD]
            values = block[:, kv_width + group * HD : kv_width + group * HD + HD]
            raw = lax.dot_general(
                q_ref[at, cols],
                keys,
                (((1,), (1,)), ((), ())),
                preferred_element_type=jnp.float32,
            )
            capped = jnp.tanh(raw * (query_scale / logit_cap))
            weights = jnp.where(allowed, jnp.exp2(capped * (logit_cap * log2e)), 0.0)
            part = weights[:, :HD]
            for k in range(HD, span, HD):
                part = part + weights[:, k : k + HD]
            tot[at, cols] += part
            acc[at, cols] += jnp.dot(
                weights.astype(jnp.bfloat16), values, preferred_element_type=jnp.float32
            )

    def visit_all():
        for block, (index, top) in zip(blocks, places):
            visit(block, index, top)

    if guarded:
        key_first = meta[places[0][0]]
        pl.when((key_first <= meta[0]) & (key_first + rows > meta[0] - WIN))(visit_all)
    else:
        visit_all()
    if last:
        for head in range(heads):
            cols = slice(head * HD, head * HD + HD)
            total = jnp.sum(tot[:, cols], axis=-1, keepdims=True)
            out[:, cols] = (acc[:, cols] / total).astype(jnp.bfloat16)


def attend(meta, low, queries, parts, state=None, last=False, guarded=False):
    rows, width = queries.shape
    places = tuple((index, top) for _, index, top in parts)
    blocks = [block for block, _, _ in parts]
    wide = jax.ShapeDtypeStruct((rows, width), jnp.float32)
    first = state is None
    operands = [meta, low, queries, *blocks] + ([] if first else list(state))
    keys = sum(block.shape[0] for block in blocks)
    scratch = ()
    aliases = {}
    if last:
        out_shape = jax.ShapeDtypeStruct((rows, width), jnp.bfloat16)
        out_specs = whole()
        scratch = (VMEM((rows, width), jnp.float32), VMEM((rows, width), jnp.float32))
    else:
        out_shape = (wide, wide)
        out_specs = (whole(), whole())
        if not first:
            aliases = {len(operands) - 2: 0, len(operands) - 1: 1}
    return pl.pallas_call(
        functools.partial(attend_kernel, places, first, last, guarded),
        name="attend_last" if last else "attend",
        out_shape=out_shape,
        in_specs=[whole(SMEM)] + [whole()] * (len(operands) - 1),
        out_specs=out_specs,
        scratch_shapes=scratch,
        input_output_aliases=aliases,
        compiler_params=pltpu.CompilerParams(vmem_limit_bytes=8 << 20),
        cost_estimate=pl.CostEstimate(
            flops=10000000 * keys,
            transcendentals=0,
            bytes_accessed=width * keys,
        ),
    )(*operands)


def cache_kernel(received, out):
    width = received.shape[2] // 2
    for shard in range(received.shape[0]):
        cols = slice(shard * width, shard * width + width)
        for index in range(2):
            block = received[shard, :, index * width : index * width + width]
            out[0, :, index, cols] = block


def build_cache(received):
    ranks, rows, width = received.shape
    return pl.pallas_call(
        cache_kernel,
        name="build_cache",
        out_shape=jax.ShapeDtypeStruct((1, rows, 2, ranks * width // 2), received.dtype),
        in_specs=[whole()],
        out_specs=whole(),
        compiler_params=pltpu.CompilerParams(vmem_limit_bytes=8 << 20),
    )(received)


def after(value, *others):
    return lax.optimization_barrier((value, *others))[0]


def ring_gather(block):
    rows = block.shape[0]
    half = rows // 2
    left = turned(block, "tp", 1)
    right = turned(block, "tp", -1)
    far_a = turned(left[:half], "tp", 1)
    far_b = turned(right[half:], "tp", -1)
    return [
        (block, (0, 0, rows)),
        (left, (3, 0, rows)),
        (right, (1, 0, rows)),
        (far_a, (2, 0, half)),
        (far_b, (2, half, rows)),
    ]


def per_device(hidden, norm_gain, w_query, w_key, w_value, segment_ids, page_table):
    tokens = hidden.shape[0]
    place = lax.axis_index("seq")
    rank = lax.axis_index("tp")
    half = tokens // 2
    ranks = lax.axis_size("tp")
    shards = (rank + jnp.arange(ranks, dtype=jnp.int32)) % ranks
    table = page_table[0]

    pieces = ring_gather(hidden)
    marked = (segment_ids + 1).reshape(1, tokens)
    near = jnp.concatenate(
        [marked, shifted(marked, "seq", 1), shifted(marked, "seq", 2)], axis=0
    )
    earlier = jnp.concatenate(
        [near[1:], shifted(near, "seq", 3), shifted(near, "seq", 6)], axis=0
    ).reshape(1, -1)
    first_token = place * tokens
    own = segment_ids.reshape(tokens, 1) + 1
    before = jnp.sum((marked < own).astype(jnp.int32), axis=1, keepdims=True)
    same = jnp.sum((earlier == own).astype(jnp.int32), axis=1, keepdims=True)
    starts = first_token + before - same
    query_index = first_token + jnp.arange(tokens, dtype=jnp.int32)[:, None]
    low = jnp.maximum(starts, query_index - (WIN - 1))
    steps = WIN // tokens // 2
    core = place % 2
    backs = [jnp.int32(2 * step) for step in range(steps + 1)]
    backs += [2 * step - 1 + 2 * core for step in range(steps + 1)]
    firsts = jnp.stack(backs) * -tokens + first_token
    meta = jnp.concatenate([first_token.reshape(1), firsts, firsts + half])

    freqs = 10000.0 ** (-(jnp.arange(HD // 2, dtype=jnp.float32) * (2.0 / HD)))
    angles = (query_index - starts).astype(jnp.float32) * jnp.concatenate([freqs, freqs])[None, :]
    sign = np.where(np.arange(HD) < HD // 2, -1.0, 1.0).astype(np.float32)
    cos = jnp.cos(angles)
    sin = jnp.sin(angles) * sign[None, :]
    gain = norm_gain.reshape(1, -1)

    normed, pages, a0, b0 = project_kv(
        shards, table, pieces, gain, w_key, w_value, cos, sin, half
    )

    def hop(name, block):
        with jax.named_scope(name):
            return shifted(block, "seq", 2)

    def cross(name, block):
        with jax.named_scope(name):
            return swapped(block)

    look = functools.partial(attend, meta, low)
    straight = [1 + step for step in range(steps + 1)]
    turned_at = [2 + steps + step for step in range(steps + 1)]
    later = 2 * (steps + 1)

    a, b = [a0], [b0]
    ca, cb = [], []
    for step in range(steps + 1):
        if step:
            a.append(hop(f"hop_a{step}", a[-1]))
            b.append(hop(f"hop_b{step}", b[-1]))
        ca.append(cross(f"cross_a{step}", a[-1]))
        cb.append(cross(f"cross_b{step}", b[-1]))
    queries = project_q((normed,), w_query, cos, sin)
    state = look(queries, [(a[0], straight[0], 0), (b[0], straight[0] + later, half)])
    edge = [(ca[0], turned_at[0], None), (cb[0], turned_at[0] + later, None)]
    state = look(queries, edge, state, guarded=True)
    for step in range(1, steps):
        near, over = straight[step], turned_at[step]
        state = look(queries, [(a[step], near, None), (ca[step], over, None)], state)
        near, over = near + later, over + later
        state = look(queries, [(b[step], near, None), (cb[step], over, None)], state)
    near, over = straight[steps], turned_at[steps]
    state = look(queries, [(a[steps], near, None), (b[steps], near + later, None)], state)
    edge = [(ca[steps], over, None), (cb[steps], over + later, None)]
    attended = look(queries, edge, state, last=True, guarded=True)
    received = lax.all_to_all(after(pages, a[1]), "tp", split_axis=0, concat_axis=0, tiled=True)
    kv_cache = build_cache(received)
    return (attended, kv_cache)


def solution(mesh):
    placed = (
        P("seq", "tp"),
        P(),
        P(None, "tp"),
        P(None, "tp"),
        P(None, "tp"),
        P("seq"),
        P("seq", None),
    )
    return jax.shard_map(
        per_device,
        mesh=mesh,
        in_specs=placed,
        out_specs=(P("seq", "tp"), P(("seq", "tp"), None, None, None)),
        check_vma=False,
    )
```

profile of v0, /device:TPU:6, one launch (start us, length us, event | category | flops | bytes accessed | tf_op | source)
XLA Modules:
  0.0 147.8 jit_solution(18403334101432991656)
XLA Ops:
  1.4 1.9 %collective-permute-start = (s32[1,512]{1,0:T(1,128)S(1)}, s32[1,512]{1,0:T(1,128)S(1)}, u32[]{:S(2)}, u32[]{:S(2)}) collective-permute-start(s32[1,512]{1,0:T(1,128)S(1)} %bitcast.13), channel_id=1, source_target_pairs={{0,4},{4,8},{8,12},{12,16},{16,20},{20,24},{24,28},{28,32},{32,36}... | collective-permute-start | bytes 6152 | tf_op jit(solution)/shard_map/ppermute | solution.py:31
  3.3 3.8 %collective-permute-start.1 = (s32[1,512]{1,0:T(1,128)S(1)}, s32[1,512]{1,0:T(1,128)}, u32[]{:S(2)}, u32[]{:S(2)}) collective-permute-start(s32[1,512]{1,0:T(1,128)S(1)} %bitcast.14), channel_id=1, source_target_pairs={{0,8},{4,12},{8,16},{12,20},{16,24},{20,28},{24,32},{28,36},{32,40... | collective-permute-start | bytes 6152 | tf_op jit(solution)/shard_map/ppermute | solution.py:31
  7.2 1.7 %collective-permute-start.4 = (bf16[512,1152]{1,0:T(8,128)(2,1)}, bf16[512,1152]{1,0:T(8,128)(2,1)S(1)}, u32[]{:S(2)}, u32[]{:S(2)}) collective-permute-start(bf16[512,1152]{1,0:T(8,128)(2,1)} %refs_0_.1), channel_id=1, source_target_pairs={{0,1},{1,2},{2,3},{3,0},{4,5},{5,6},{6,7},{7,4},{8,9},{9,10},{10,1... | collective-permute-start | bytes 3538952 | tf_op jit(solution)/shard_map/ppermute | solution.py:36
  8.8 1.7 %collective-permute-start.5 = (bf16[512,1152]{1,0:T(8,128)(2,1)}, bf16[512,1152]{1,0:T(8,128)(2,1)S(1)}, u32[]{:S(2)}, u32[]{:S(2)}) collective-permute-start(bf16[512,1152]{1,0:T(8,128)(2,1)} %refs_0_.1), channel_id=1, source_target_pairs={{0,3},{1,0},{2,1},{3,2},{4,7},{5,4},{6,5},{7,6},{8,11},{9,8},{10,9... | collective-permute-start | bytes 3538952 | tf_op jit(solution)/shard_map/ppermute | solution.py:36
  11.2 1.3 pad_maximum_fusion
  13.7 4.5 %collective-permute-start.2 = (s32[3,512]{1,0:T(4,128)S(1)}, s32[3,512]{1,0:T(4,128)S(1)}, u32[]{:S(2)}, u32[]{:S(2)}) collective-permute-start(s32[3,512]{1,0:T(4,128)S(1)} %pad_add_fusion), channel_id=1, source_target_pairs={{0,12},{4,16},{8,20},{12,24},{16,28},{20,32},{24,36},{28,40},{32,4... | collective-permute-start | bytes 18440 | tf_op jit(solution)/shard_map/ppermute | solution.py:31
  18.2 5.9 %collective-permute-start.3 = (s32[3,512]{1,0:T(4,128)S(1)}, s32[3,512]{1,0:T(4,128)S(1)}, u32[]{:S(2)}, u32[]{:S(2)}) collective-permute-start(s32[3,512]{1,0:T(4,128)S(1)} %pad_add_fusion), channel_id=1, source_target_pairs={{0,24},{4,28},{8,32},{12,36},{16,40},{20,44},{24,48},{28,52},{32,5... | collective-permute-start | bytes 18440 | tf_op jit(solution)/shard_map/ppermute | solution.py:31
  24.3 1.3 reshape.66.refs_5_
  25.6 2.1 %collective-permute-done.3 = s32[3,512]{1,0:T(4,128)S(1)} collective-permute-done((s32[3,512]{1,0:T(4,128)S(1)}, s32[3,512]{1,0:T(4,128)S(1)}, u32[]{:S(2)}, u32[]{:S(2)}) %collective-permute-start.3) | collective-permute-done | bytes 6176 | tf_op jit(solution)/shard_map/ppermute | solution.py:31
  28.4 1.0 convert_reduce_fusion
  29.4 7.3 %collective-permute-done.4.refs_1_ = bf16[512,1152]{1,0:T(8,128)(2,1)S(1)} collective-permute-done((bf16[512,1152]{1,0:T(8,128)(2,1)}, bf16[512,1152]{1,0:T(8,128)(2,1)S(1)}, u32[]{:S(2)}, u32[]{:S(2)}) %collective-permute-start.4) | collective-permute-done | bytes 1179680 | tf_op jit(solution)/shard_map/ppermute | solution.py:36
  38.9 2.8 %collective-permute-start.7 = (bf16[256,1152]{1,0:T(8,128)(2,1)}, bf16[256,1152]{1,0:T(8,128)(2,1)}, u32[]{:S(2)}, u32[]{:S(2)}) collective-permute-start(bf16[256,1152]{1,0:T(8,128)(2,1)} %slice.11), channel_id=1, source_target_pairs={{0,3},{1,0},{2,1},{3,2},{4,7},{5,4},{6,5},{7,6},{8,11},{9,8},{10,9... | collective-permute-start | bytes 1769480 | tf_op jit(solution)/shard_map/ppermute | solution.py:36
  42.2 1.5 %copy.27 = s32[512,1]{1,0:T(8,128)} copy(s32[512,1]{0,1:T(1,128)} %bitcast.17) | data formatting | bytes 4096 | tf_op jit(solution)/shard_map/sub | solution.py:320
  44.8 1.7 %fusion = (f32[512,128]{1,0:T(8,128)S(1)}, f32[512,128]{1,0:T(8,128)S(1)}) fusion(f32[128]{0:T(128)} %constant.74, f32[128]{0:T(128)} %pad_maximum_fusion, f32[512]{0:T(512)S(1)} %get-tuple-element.48), kind=kLoop, calls=%fused_computation.4 | loop fusion | flops 131072 | bytes 527360 | tf_op jit(solution)/shard_map/mul | solution.py:334
  46.4 8.5 %collective-permute-done.6.refs_3_ = bf16[256,1152]{1,0:T(8,128)(2,1)} collective-permute-done((bf16[256,1152]{1,0:T(8,128)(2,1)}, bf16[256,1152]{1,0:T(8,128)(2,1)}, u32[]{:S(2)}, u32[]{:S(2)}) %collective-permute-start.6) | collective-permute-done | bytes 589856 | tf_op jit(solution)/shard_map/ppermute | solution.py:36
  55.1 1.7 %copy-done = bf16[4608,256]{1,0:T(8,128)(2,1)S(1)} copy-done((bf16[4608,256]{1,0:T(8,128)(2,1)S(1)}, bf16[4608,256]{1,0:T(8,128)(2,1)}, u32[]{:S(2)}) %copy-start) | copy-done | bytes 2359320
  56.8 1.7 %copy-done.1 = bf16[4608,256]{1,0:T(8,128)(2,1)S(1)} copy-done((bf16[4608,256]{1,0:T(8,128)(2,1)S(1)}, bf16[4608,256]{1,0:T(8,128)(2,1)}, u32[]{:S(2)}) %copy-start.1) | copy-done | bytes 2359320
  59.2 7.3 %norm_project_kv.1 = (bf16[512,4608]{1,0:T(8,128)(2,1)S(1)}, bf16[4,128,512]{2,1,0:T(8,128)(2,1)S(1)}, bf16[256,512]{1,0:T(8,128)(2,1)}, bf16[256,512]{1,0:T(8,128)(2,1)}) custom-call(s32[4]{0:T(128)S(1)} %and_select_fusion.shards, s32[4]{0:T(128)S(1)} %bitcast.12, bf16[512,1152]{1,0:T(8,128)(2,1)S(1)} %copy-done.2, ...), custom_call_target="tpu_custom_call" | custom-call | flops 2415919104 | bytes 14155776 | tf_op jit(solution)/shard_map/norm_project_kv/pallas_call | solution.py:107
  66.5 3.8 %collective-permute-start.8 = (bf16[256,512]{1,0:T(8,128)(2,1)}, bf16[256,512]{1,0:T(8,128)(2,1)S(1)}, u32[]{:S(2)}, u32[]{:S(2)}) collective-permute-start(bf16[256,512]{1,0:T(8,128)(2,1)} %get-tuple-element.26.refs_0_), channel_id=1, source_target_pairs={{0,8},{4,12},{8,16},{12,20},{16,24},{20,28},{24,32},{28,36},{32,40... | collective-permute-start | bytes 786440 | tf_op jit(solution)/shard_map/hop_a1/ppermute | solution.py:31
  70.6 3.2 %collective-permute-start.13 = (bf16[256,512]{1,0:T(8,128)(2,1)}, bf16[256,512]{1,0:T(8,128)(2,1)S(1)}, u32[]{:S(2)}, u32[]{:S(2)}) collective-permute-start(bf16[256,512]{1,0:T(8,128)(2,1)} %get-tuple-element.27.refs_1_), channel_id=1, source_target_pairs={{0,8},{4,12},{8,16},{12,20},{16,24},{20,28},{24,32},{28,36},{32,40... | collective-permute-start | bytes 786440 | tf_op jit(solution)/shard_map/hop_b1/ppermute | solution.py:31
  73.9 2.3 %copy-done.9 = bf16[4608,512]{1,0:T(8,128)(2,1)S(1)} copy-done((bf16[4608,512]{1,0:T(8,128)(2,1)S(1)}, bf16[4608,512]{1,0:T(8,128)(2,1)}, u32[]{:S(2)}) %copy-start.9) | copy-done | bytes 4718616
  76.2 2.8 %project_q.1.q_ref = bf16[512,512]{1,0:T(8,128)(2,1)S(1)} custom-call(bf16[512,4608]{1,0:T(8,128)(2,1)S(1)} %get-tuple-element.25.refs_0_, bf16[4608,512]{1,0:T(8,128)(2,1)S(1)} %copy-done.9, f32[512,128]{1,0:T(8,128)S(1)} %get-tuple-element.53.refs_8_.refs_2_, f32[512,128]{1,0:T(8,128)S(1)} %get-tuple-element.52.refs_9_.refs_3_), custom_call_target="tpu_custom_call" | custom-call | flops 5120000000 | bytes 262144 | tf_op jit(solution)/shard_map/project_q/pallas_call | solution.py:139
  79.0 2.5 %attend.9 = (f32[512,512]{1,0:T(8,128)S(1)}, f32[512,512]{1,0:T(8,128)S(1)}) custom-call(s32[21]{0:T(128)S(1)} %pad_add_fusion.1.meta, s32[512,1]{1,0:T(8,128)S(1)} %add_maximum_fusion.low_ref, bf16[512,512]{1,0:T(8,128)(2,1)S(1)} %project_q.1.q_ref, bf16[256,512]{1,0:T(8,128)(2,1)} %get-tuple-element.26.refs_0_, bf16[256,512]{1,0:T(8,128)(2,1)} %get-tuple-element.27.refs_1_), custom_call_target="tpu_custom_call" | custom-call | flops 5120000000 | bytes 262144 | tf_op jit(solution)/shard_map/attend/pallas_call | solution.py:241
  83.5 4.7 %all-to-all-start = ((bf16[4,128,512]{2,1,0:T(8,128)(2,1)}), bf16[4,128,512]{2,1,0:T(8,128)(2,1)S(1)}, u32[]{:S(2)}, u32[]{:S(2)}) async-start(bf16[4,128,512]{2,1,0:T(8,128)(2,1)} %copy-done.3), calls=%async_computation | async-start | bytes 1048576 | tf_op jit(solution)/shard_map/all_to_all | solution.py:375
  88.2 6.3 %collective-permute-start.9 = (bf16[256,512]{1,0:T(8,128)(2,1)S(1)}, bf16[256,512]{1,0:T(8,128)(2,1)S(1)}, u32[]{:S(2)}, u32[]{:S(2)}) collective-permute-start(bf16[256,512]{1,0:T(8,128)(2,1)S(1)} %collective-permute-done.8.refs_0_), channel_id=1, source_target_pairs={{0,8},{4,12},{8,16},{12,20},{16,24},{20,28},{24,32},{28,36},{32,40... | collective-permute-start | bytes 786440 | tf_op jit(solution)/shard_map/hop_a2/ppermute | solution.py:31
  94.8 2.9 %collective-permute-start.14 = (bf16[256,512]{1,0:T(8,128)(2,1)S(1)}, bf16[256,512]{1,0:T(8,128)(2,1)S(1)}, u32[]{:S(2)}, u32[]{:S(2)}) collective-permute-start(bf16[256,512]{1,0:T(8,128)(2,1)S(1)} %collective-permute-done.13.refs_0_), channel_id=1, source_target_pairs={{0,8},{4,12},{8,16},{12,20},{16,24},{20,28},{24,32},{28,36},{32,40... | collective-permute-start | bytes 786440 | tf_op jit(solution)/shard_map/hop_b2/ppermute | solution.py:31
  98.7 1.2 copy-done.14
  99.9 1.2 copy-done.18
  101.7 1.7 %collective-permute-start.21 = (bf16[256,512]{1,0:T(8,128)(2,1)S(1)}, bf16[256,512]{1,0:T(8,128)(2,1)S(1)}, u32[]{:S(2)}, u32[]{:S(2)}) collective-permute-start(bf16[256,512]{1,0:T(8,128)(2,1)S(1)} %collective-permute-done.9.refs_0_), channel_id=1, source_target_pairs={{0,4},{4,0},{8,12},{12,8},{16,20},{20,16},{24,28},{28,24},{32,36},... | collective-permute-start | bytes 786440 | tf_op jit(solution)/shard_map/cross_a2/ppermute | solution.py:40
  103.4 2.9 %collective-permute-start.10 = (bf16[256,512]{1,0:T(8,128)(2,1)S(1)}, bf16[256,512]{1,0:T(8,128)(2,1)S(1)}, u32[]{:S(2)}, u32[]{:S(2)}) collective-permute-start(bf16[256,512]{1,0:T(8,128)(2,1)S(1)} %collective-permute-done.9.refs_0_), channel_id=1, source_target_pairs={{0,8},{4,12},{8,16},{12,20},{16,24},{20,28},{24,32},{28,36},{32,40... | collective-permute-start | bytes 786440 | tf_op jit(solution)/shard_map/hop_a3/ppermute | solution.py:31
  107.3 3.4 %collective-permute-start.15 = (bf16[256,512]{1,0:T(8,128)(2,1)S(1)}, bf16[256,512]{1,0:T(8,128)(2,1)S(1)}, u32[]{:S(2)}, u32[]{:S(2)}) collective-permute-start(bf16[256,512]{1,0:T(8,128)(2,1)S(1)} %collective-permute-done.14.refs_0_), channel_id=1, source_target_pairs={{0,8},{4,12},{8,16},{12,20},{16,24},{20,28},{24,32},{28,36},{32,40... | collective-permute-start | bytes 786440 | tf_op jit(solution)/shard_map/hop_b3/ppermute | solution.py:31
  110.7 1.0 copy-done.11
  111.7 2.1 %attend.11 = (f32[512,512]{1,0:T(8,128)S(1)}, f32[512,512]{1,0:T(8,128)S(1)}) custom-call(s32[21]{0:T(128)S(1)} %pad_add_fusion.1.meta, s32[512,1]{1,0:T(8,128)S(1)} %copy-done.5, bf16[512,512]{1,0:T(8,128)(2,1)S(1)} %copy-done.11, bf16[256,512]{1,0:T(8,128)(2,1)S(1)} %collective-permute-done.8.refs_0_, ...), custom_call_target="tpu_custom_call", output_to_operand_aliasing={{0}: (5, {}), {1}: (6, {})} | custom-call | flops 5120000000 | bytes 262144 | tf_op jit(solution)/shard_map/attend/pallas_call | solution.py:241
  113.9 2.1 %attend.12 = (f32[512,512]{1,0:T(8,128)S(1)}, f32[512,512]{1,0:T(8,128)S(1)}) custom-call(s32[21]{0:T(128)S(1)} %pad_add_fusion.1.meta, s32[512,1]{1,0:T(8,128)S(1)} %copy-done.5, bf16[512,512]{1,0:T(8,128)(2,1)S(1)} %copy-done.11, bf16[256,512]{1,0:T(8,128)(2,1)S(1)} %collective-permute-done.13.refs_0_, ...), custom_call_target="tpu_custom_call", output_to_operand_aliasing={{0}: (5, {}), {1}: (6, {})} | custom-call | flops 5120000000 | bytes 262144 | tf_op jit(solution)/shard_map/attend/pallas_call | solution.py:241
  116.0 1.0 copy-done.15
  118.0 1.6 %build_cache.1 = bf16[1,128,2,1024]{3,2,1,0:T(2,128)(2,1)} custom-call(bf16[4,128,512]{2,1,0:T(8,128)(2,1)S(1)} %all-to-all-done.received), custom_call_target="tpu_custom_call" | custom-call | tf_op jit(solution)/shard_map/build_cache/pallas_call | solution.py:269
  119.9 3.1 %collective-permute-start.11 = (bf16[256,512]{1,0:T(8,128)(2,1)S(1)}, bf16[256,512]{1,0:T(8,128)(2,1)S(1)}, u32[]{:S(2)}, u32[]{:S(2)}) collective-permute-start(bf16[256,512]{1,0:T(8,128)(2,1)S(1)} %collective-permute-done.10.refs_0_), channel_id=1, source_target_pairs={{0,8},{4,12},{8,16},{12,20},{16,24},{20,28},{24,32},{28,36},{32,40... | collective-permute-start | bytes 786440 | tf_op jit(solution)/shard_map/hop_a4/ppermute | solution.py:31
  123.1 3.1 %collective-permute-start.16 = (bf16[256,512]{1,0:T(8,128)(2,1)S(1)}, bf16[256,512]{1,0:T(8,128)(2,1)S(1)}, u32[]{:S(2)}, u32[]{:S(2)}) collective-permute-start(bf16[256,512]{1,0:T(8,128)(2,1)S(1)} %collective-permute-done.15.refs_0_), channel_id=1, source_target_pairs={{0,8},{4,12},{8,16},{12,20},{16,24},{20,28},{24,32},{28,36},{32,40... | collective-permute-start | bytes 786440 | tf_op jit(solution)/shard_map/hop_b4/ppermute | solution.py:31
  126.3 1.0 copy-done.12
  127.3 1.2 copy-done.16
  128.5 1.2 copy-done.20
  129.8 2.1 %attend.13 = (f32[512,512]{1,0:T(8,128)S(1)}, f32[512,512]{1,0:T(8,128)S(1)}) custom-call(s32[21]{0:T(128)S(1)} %pad_add_fusion.1.meta, s32[512,1]{1,0:T(8,128)S(1)} %copy-done.6, bf16[512,512]{1,0:T(8,128)(2,1)S(1)} %copy-done.12, bf16[256,512]{1,0:T(8,128)(2,1)S(1)} %collective-permute-done.9.refs_0_, ...), custom_call_target="tpu_custom_call", output_to_operand_aliasing={{0}: (5, {}), {1}: (6, {})} | custom-call | flops 5120000000 | bytes 262144 | tf_op jit(solution)/shard_map/attend/pallas_call | solution.py:241
  131.9 2.1 %attend.14 = (f32[512,512]{1,0:T(8,128)S(1)}, f32[512,512]{1,0:T(8,128)S(1)}) custom-call(s32[21]{0:T(128)S(1)} %pad_add_fusion.1.meta, s32[512,1]{1,0:T(8,128)S(1)} %copy-done.6, bf16[512,512]{1,0:T(8,128)(2,1)S(1)} %copy-done.12, bf16[256,512]{1,0:T(8,128)(2,1)S(1)} %collective-permute-done.14.refs_0_, ...), custom_call_target="tpu_custom_call", output_to_operand_aliasing={{0}: (5, {}), {1}: (6, {})} | custom-call | flops 5120000000 | bytes 262144 | tf_op jit(solution)/shard_map/attend/pallas_call | solution.py:241
  134.3 3.7 %collective-permute-done.16.refs_1_ = bf16[256,512]{1,0:T(8,128)(2,1)S(1)} collective-permute-done((bf16[256,512]{1,0:T(8,128)(2,1)S(1)}, bf16[256,512]{1,0:T(8,128)(2,1)S(1)}, u32[]{:S(2)}, u32[]{:S(2)}) %collective-permute-start.16) | collective-permute-done | bytes 262176 | tf_op jit(solution)/shard_map/hop_b4/ppermute | solution.py:31
  138.0 2.1 %attend.15 = (f32[512,512]{1,0:T(8,128)S(1)}, f32[512,512]{1,0:T(8,128)S(1)}) custom-call(s32[21]{0:T(128)S(1)} %pad_add_fusion.1.meta, s32[512,1]{1,0:T(8,128)S(1)} %copy-done.6, bf16[512,512]{1,0:T(8,128)(2,1)S(1)} %copy-done.12, bf16[256,512]{1,0:T(8,128)(2,1)S(1)} %collective-permute-done.10.refs_0_, ...), custom_call_target="tpu_custom_call", output_to_operand_aliasing={{0}: (5, {}), {1}: (6, {})} | custom-call | flops 5120000000 | bytes 262144 | tf_op jit(solution)/shard_map/attend/pallas_call | solution.py:241
  140.1 2.1 %attend.16 = (f32[512,512]{1,0:T(8,128)S(1)}, f32[512,512]{1,0:T(8,128)S(1)}) custom-call(s32[21]{0:T(128)S(1)} %pad_add_fusion.1.meta, s32[512,1]{1,0:T(8,128)S(1)} %copy-done.6, bf16[512,512]{1,0:T(8,128)(2,1)S(1)} %copy-done.12, bf16[256,512]{1,0:T(8,128)(2,1)S(1)} %collective-permute-done.15.refs_0_, ...), custom_call_target="tpu_custom_call", output_to_operand_aliasing={{0}: (5, {}), {1}: (6, {})} | custom-call | flops 5120000000 | bytes 262144 | tf_op jit(solution)/shard_map/attend/pallas_call | solution.py:241
  142.2 2.1 %attend.17 = (f32[512,512]{1,0:T(8,128)S(1)}, f32[512,512]{1,0:T(8,128)S(1)}) custom-call(s32[21]{0:T(128)S(1)} %pad_add_fusion.1.meta, s32[512,1]{1,0:T(8,128)S(1)} %copy-done.6, bf16[512,512]{1,0:T(8,128)(2,1)S(1)} %copy-done.12, bf16[256,512]{1,0:T(8,128)(2,1)S(1)} %collective-permute-done.11.refs_0_, ...), custom_call_target="tpu_custom_call", output_to_operand_aliasing={{0}: (5, {}), {1}: (6, {})} | custom-call | flops 5120000000 | bytes 262144 | tf_op jit(solution)/shard_map/attend/pallas_call | solution.py:241
  144.4 3.4 %attend_last.1 = bf16[512,512]{1,0:T(8,128)(2,1)} custom-call(s32[21]{0:T(128)S(1)} %pad_add_fusion.1.meta, s32[512,1]{1,0:T(8,128)S(1)} %copy-done.6, bf16[512,512]{1,0:T(8,128)(2,1)S(1)} %copy-done.12, bf16[256,512]{1,0:T(8,128)(2,1)S(1)} %collective-permute-done.12.refs_0_, bf16[256,512]{1,0:T(8,128)(2,1)S(1)} %collective-permute-done.17.refs_1_, ...), custom_call_target="tpu_custom_call" | custom-call | flops 5120000000 | bytes 262144 | tf_op jit(solution)/shard_map/attend_last/pallas_call | solution.py:241
  (82 shorter events, 14.8 us)
Async XLA Ops:
  0.6 54.5 %copy-start.2 = (bf16[512,1152]{1,0:T(8,128)(2,1)S(1)}, bf16[512,1152]{1,0:T(8,128)(2,1)}, u32[]{:S(2)}) copy-start(bf16[512,1152]{1,0:T(8,128)(2,1)} %refs_0_.1) | copy-start | bytes 3538948
  0.6 54.5 %copy-start.8 = (s32[1,4]{1,0:T(1,128)S(1)}, s32[1,4]{1,0:T(1,128)}, u32[]{:S(2)}) copy-start(s32[1,4]{1,0:T(1,128)} %param.14) | copy-start | bytes 52
  1.4 11.3 %collective-permute-start = (s32[1,512]{1,0:T(1,128)S(1)}, s32[1,512]{1,0:T(1,128)S(1)}, u32[]{:S(2)}, u32[]{:S(2)}) collective-permute-start(s32[1,512]{1,0:T(1,128)S(1)} %bitcast.13), channel_id=1, source_target_pairs={{0,4},{4,8},{8,12},{12,16},{16,20},{20,24},{24,28},{28,32},{32,36}... | collective-permute-start | bytes 6152 | tf_op jit(solution)/shard_map/ppermute | solution.py:31
  3.3 9.7 %collective-permute-start.1 = (s32[1,512]{1,0:T(1,128)S(1)}, s32[1,512]{1,0:T(1,128)}, u32[]{:S(2)}, u32[]{:S(2)}) collective-permute-start(s32[1,512]{1,0:T(1,128)S(1)} %bitcast.14), channel_id=1, source_target_pairs={{0,8},{4,12},{8,16},{12,20},{16,24},{20,28},{24,32},{28,36},{32,40... | collective-permute-start | bytes 6152 | tf_op jit(solution)/shard_map/ppermute | solution.py:31
  7.2 29.5 %collective-permute-start.4 = (bf16[512,1152]{1,0:T(8,128)(2,1)}, bf16[512,1152]{1,0:T(8,128)(2,1)S(1)}, u32[]{:S(2)}, u32[]{:S(2)}) collective-permute-start(bf16[512,1152]{1,0:T(8,128)(2,1)} %refs_0_.1), channel_id=1, source_target_pairs={{0,1},{1,2},{2,3},{3,0},{4,5},{5,6},{6,7},{7,4},{8,9},{9,10},{10,1... | collective-permute-start | bytes 3538952 | tf_op jit(solution)/shard_map/ppermute | solution.py:36
  8.8 29.2 %collective-permute-start.5 = (bf16[512,1152]{1,0:T(8,128)(2,1)}, bf16[512,1152]{1,0:T(8,128)(2,1)S(1)}, u32[]{:S(2)}, u32[]{:S(2)}) collective-permute-start(bf16[512,1152]{1,0:T(8,128)(2,1)} %refs_0_.1), channel_id=1, source_target_pairs={{0,3},{1,0},{2,1},{3,2},{4,7},{5,4},{6,5},{7,6},{8,11},{9,8},{10,9... | collective-permute-start | bytes 3538952 | tf_op jit(solution)/shard_map/ppermute | solution.py:36
  12.7 11.4 %copy-start.21 = (s32[1,512]{1,0:T(1,128)}, s32[1,512]{1,0:T(1,128)S(1)}, u32[]{:S(2)}) copy-start(s32[1,512]{1,0:T(1,128)S(1)} %collective-permute-done) | copy-start | bytes 6148
  13.7 11.9 %collective-permute-start.2 = (s32[3,512]{1,0:T(4,128)S(1)}, s32[3,512]{1,0:T(4,128)S(1)}, u32[]{:S(2)}, u32[]{:S(2)}) collective-permute-start(s32[3,512]{1,0:T(4,128)S(1)} %pad_add_fusion), channel_id=1, source_target_pairs={{0,12},{4,16},{8,20},{12,24},{16,28},{20,32},{24,36},{28,40},{32,4... | collective-permute-start | bytes 18440 | tf_op jit(solution)/shard_map/ppermute | solution.py:31
  18.2 9.5 %collective-permute-start.3 = (s32[3,512]{1,0:T(4,128)S(1)}, s32[3,512]{1,0:T(4,128)S(1)}, u32[]{:S(2)}, u32[]{:S(2)}) collective-permute-start(s32[3,512]{1,0:T(4,128)S(1)} %pad_add_fusion), channel_id=1, source_target_pairs={{0,24},{4,28},{8,32},{12,36},{16,40},{20,44},{24,48},{28,52},{32,5... | collective-permute-start | bytes 18440 | tf_op jit(solution)/shard_map/ppermute | solution.py:31
  37.6 17.4 %collective-permute-start.6 = (bf16[256,1152]{1,0:T(8,128)(2,1)}, bf16[256,1152]{1,0:T(8,128)(2,1)}, u32[]{:S(2)}, u32[]{:S(2)}) collective-permute-start(bf16[256,1152]{1,0:T(8,128)(2,1)} %slice.10), channel_id=1, source_target_pairs={{0,1},{1,2},{2,3},{3,0},{4,5},{5,6},{6,7},{7,4},{8,9},{9,10},{10,1... | collective-permute-start | bytes 1769480 | tf_op jit(solution)/shard_map/ppermute | solution.py:36
  38.9 16.2 %collective-permute-start.7 = (bf16[256,1152]{1,0:T(8,128)(2,1)}, bf16[256,1152]{1,0:T(8,128)(2,1)}, u32[]{:S(2)}, u32[]{:S(2)}) collective-permute-start(bf16[256,1152]{1,0:T(8,128)(2,1)} %slice.11), channel_id=1, source_target_pairs={{0,3},{1,0},{2,1},{3,2},{4,7},{5,4},{6,5},{7,6},{8,11},{9,8},{10,9... | collective-permute-start | bytes 1769480 | tf_op jit(solution)/shard_map/ppermute | solution.py:36
  44.7 34.3 %copy-start.4 = (s32[512,1]{1,0:T(8,128)}, s32[512,1]{1,0:T(8,128)S(1)}, u32[]{:S(2)}) copy-start(s32[512,1]{1,0:T(8,128)S(1)} %add_maximum_fusion.low_ref) | copy-start | bytes 6148
  55.1 1.7 %copy-start = (bf16[4608,256]{1,0:T(8,128)(2,1)S(1)}, bf16[4608,256]{1,0:T(8,128)(2,1)}, u32[]{:S(2)}) copy-start(bf16[4608,256]{1,0:T(8,128)(2,1)} %refs_6_.1) | copy-start | bytes 7077892
  56.8 1.7 %copy-start.1 = (bf16[4608,256]{1,0:T(8,128)(2,1)S(1)}, bf16[4608,256]{1,0:T(8,128)(2,1)}, u32[]{:S(2)}) copy-start(bf16[4608,256]{1,0:T(8,128)(2,1)} %refs_7_.1) | copy-start | bytes 7077892
  66.5 12.5 %copy-start.3 = (bf16[4,128,512]{2,1,0:T(8,128)(2,1)}, bf16[4,128,512]{2,1,0:T(8,128)(2,1)S(1)}, u32[]{:S(2)}) copy-start(bf16[4,128,512]{2,1,0:T(8,128)(2,1)S(1)} %get-tuple-element.47) | copy-start | bytes 1572868
  66.5 28.3 %collective-permute-start.24 = (bf16[256,512]{1,0:T(8,128)(2,1)}, bf16[256,512]{1,0:T(8,128)(2,1)S(1)}, u32[]{:S(2)}, u32[]{:S(2)}) collective-permute-start(bf16[256,512]{1,0:T(8,128)(2,1)} %get-tuple-element.26.refs_0_), channel_id=1, source_target_pairs={{0,4},{4,0},{8,12},{12,8},{16,20},{20,16},{24,28},{28,24},{32,36},... | collective-permute-start | bytes 786440 | tf_op jit(solution)/shard_map/cross_a0/ppermute | solution.py:40
  66.5 17.0 %collective-permute-start.8 = (bf16[256,512]{1,0:T(8,128)(2,1)}, bf16[256,512]{1,0:T(8,128)(2,1)S(1)}, u32[]{:S(2)}, u32[]{:S(2)}) collective-permute-start(bf16[256,512]{1,0:T(8,128)(2,1)} %get-tuple-element.26.refs_0_), channel_id=1, source_target_pairs={{0,8},{4,12},{8,16},{12,20},{16,24},{20,28},{24,32},{28,36},{32,40... | collective-permute-start | bytes 786440 | tf_op jit(solution)/shard_map/hop_a1/ppermute | solution.py:31
  70.3 27.4 %collective-permute-start.25 = (bf16[256,512]{1,0:T(8,128)(2,1)}, bf16[256,512]{1,0:T(8,128)(2,1)S(1)}, u32[]{:S(2)}, u32[]{:S(2)}) collective-permute-start(bf16[256,512]{1,0:T(8,128)(2,1)} %get-tuple-element.27.refs_1_), channel_id=1, source_target_pairs={{0,4},{4,0},{8,12},{12,8},{16,20},{20,16},{24,28},{28,24},{32,36},... | collective-permute-start | bytes 786440 | tf_op jit(solution)/shard_map/cross_b0/ppermute | solution.py:40
  70.6 23.8 %collective-permute-start.13 = (bf16[256,512]{1,0:T(8,128)(2,1)}, bf16[256,512]{1,0:T(8,128)(2,1)S(1)}, u32[]{:S(2)}, u32[]{:S(2)}) collective-permute-start(bf16[256,512]{1,0:T(8,128)(2,1)} %get-tuple-element.27.refs_1_), channel_id=1, source_target_pairs={{0,8},{4,12},{8,16},{12,20},{16,24},{20,28},{24,32},{28,36},{32,40... | collective-permute-start | bytes 786440 | tf_op jit(solution)/shard_map/hop_b1/ppermute | solution.py:31
  73.9 2.3 %copy-start.9 = (bf16[4608,512]{1,0:T(8,128)(2,1)S(1)}, bf16[4608,512]{1,0:T(8,128)(2,1)}, u32[]{:S(2)}) copy-start(bf16[4608,512]{1,0:T(8,128)(2,1)} %refs_1_.1) | copy-start | bytes 14155780
  79.0 18.7 %copy-start.10 = (bf16[512,512]{1,0:T(8,128)(2,1)}, bf16[512,512]{1,0:T(8,128)(2,1)S(1)}, u32[]{:S(2)}) copy-start(bf16[512,512]{1,0:T(8,128)(2,1)S(1)} %project_q.1.q_ref) | copy-start | bytes 1572868
  81.5 1.0 copy-start.13
  82.5 1.0 copy-start.17
  83.5 34.5 %all-to-all-start = ((bf16[4,128,512]{2,1,0:T(8,128)(2,1)}), bf16[4,128,512]{2,1,0:T(8,128)(2,1)S(1)}, u32[]{:S(2)}, u32[]{:S(2)}) async-start(bf16[4,128,512]{2,1,0:T(8,128)(2,1)} %copy-done.3), calls=%async_computation | async-start | bytes 1048576 | tf_op jit(solution)/shard_map/all_to_all | solution.py:375
  88.2 19.1 %collective-permute-start.23 = (bf16[256,512]{1,0:T(8,128)(2,1)S(1)}, bf16[256,512]{1,0:T(8,128)(2,1)S(1)}, u32[]{:S(2)}, u32[]{:S(2)}) collective-permute-start(bf16[256,512]{1,0:T(8,128)(2,1)S(1)} %collective-permute-done.8.refs_0_), channel_id=1, source_target_pairs={{0,4},{4,0},{8,12},{12,8},{16,20},{20,16},{24,28},{28,24},{32,36},... | collective-permute-start | bytes 786440 | tf_op jit(solution)/shard_map/cross_a1/ppermute | solution.py:40
  88.2 13.5 %collective-permute-start.9 = (bf16[256,512]{1,0:T(8,128)(2,1)S(1)}, bf16[256,512]{1,0:T(8,128)(2,1)S(1)}, u32[]{:S(2)}, u32[]{:S(2)}) collective-permute-start(bf16[256,512]{1,0:T(8,128)(2,1)S(1)} %collective-permute-done.8.refs_0_), channel_id=1, source_target_pairs={{0,8},{4,12},{8,16},{12,20},{16,24},{20,28},{24,32},{28,36},{32,40... | collective-permute-start | bytes 786440 | tf_op jit(solution)/shard_map/hop_a2/ppermute | solution.py:31
  94.5 19.4 %collective-permute-start.22 = (bf16[256,512]{1,0:T(8,128)(2,1)S(1)}, bf16[256,512]{1,0:T(8,128)(2,1)S(1)}, u32[]{:S(2)}, u32[]{:S(2)}) collective-permute-start(bf16[256,512]{1,0:T(8,128)(2,1)S(1)} %collective-permute-done.13.refs_0_), channel_id=1, source_target_pairs={{0,4},{4,0},{8,12},{12,8},{16,20},{20,16},{24,28},{28,24},{32,36},... | collective-permute-start | bytes 786440 | tf_op jit(solution)/shard_map/cross_b1/ppermute | solution.py:40
  94.8 12.5 %collective-permute-start.14 = (bf16[256,512]{1,0:T(8,128)(2,1)S(1)}, bf16[256,512]{1,0:T(8,128)(2,1)S(1)}, u32[]{:S(2)}, u32[]{:S(2)}) collective-permute-start(bf16[256,512]{1,0:T(8,128)(2,1)S(1)} %collective-permute-done.13.refs_0_), channel_id=1, source_target_pairs={{0,8},{4,12},{8,16},{12,20},{16,24},{20,28},{24,32},{28,36},{32,40... | collective-permute-start | bytes 786440 | tf_op jit(solution)/shard_map/hop_b2/ppermute | solution.py:31
  97.7 1.0 copy-start.5
  98.7 1.2 copy-start.14
  99.9 1.2 copy-start.18
  101.7 21.4 %collective-permute-start.21 = (bf16[256,512]{1,0:T(8,128)(2,1)S(1)}, bf16[256,512]{1,0:T(8,128)(2,1)S(1)}, u32[]{:S(2)}, u32[]{:S(2)}) collective-permute-start(bf16[256,512]{1,0:T(8,128)(2,1)S(1)} %collective-permute-done.9.refs_0_), channel_id=1, source_target_pairs={{0,4},{4,0},{8,12},{12,8},{16,20},{20,16},{24,28},{28,24},{32,36},... | collective-permute-start | bytes 786440 | tf_op jit(solution)/shard_map/cross_a2/ppermute | solution.py:40
  103.4 16.3 %collective-permute-start.10 = (bf16[256,512]{1,0:T(8,128)(2,1)S(1)}, bf16[256,512]{1,0:T(8,128)(2,1)S(1)}, u32[]{:S(2)}, u32[]{:S(2)}) collective-permute-start(bf16[256,512]{1,0:T(8,128)(2,1)S(1)} %collective-permute-done.9.refs_0_), channel_id=1, source_target_pairs={{0,8},{4,12},{8,16},{12,20},{16,24},{20,28},{24,32},{28,36},{32,40... | collective-permute-start | bytes 786440 | tf_op jit(solution)/shard_map/hop_a3/ppermute | solution.py:31
  107.3 24.6 %collective-permute-start.20 = (bf16[256,512]{1,0:T(8,128)(2,1)S(1)}, bf16[256,512]{1,0:T(8,128)(2,1)S(1)}, u32[]{:S(2)}, u32[]{:S(2)}) collective-permute-start(bf16[256,512]{1,0:T(8,128)(2,1)S(1)} %collective-permute-done.14.refs_0_), channel_id=1, source_target_pairs={{0,4},{4,0},{8,12},{12,8},{16,20},{20,16},{24,28},{28,24},{32,36},... | collective-permute-start | bytes 786440 | tf_op jit(solution)/shard_map/cross_b2/ppermute | solution.py:40
  107.3 15.7 %collective-permute-start.15 = (bf16[256,512]{1,0:T(8,128)(2,1)S(1)}, bf16[256,512]{1,0:T(8,128)(2,1)S(1)}, u32[]{:S(2)}, u32[]{:S(2)}) collective-permute-start(bf16[256,512]{1,0:T(8,128)(2,1)S(1)} %collective-permute-done.14.refs_0_), channel_id=1, source_target_pairs={{0,8},{4,12},{8,16},{12,20},{16,24},{20,28},{24,32},{28,36},{32,40... | collective-permute-start | bytes 786440 | tf_op jit(solution)/shard_map/hop_b3/ppermute | solution.py:31
  110.7 1.0 copy-start.11
  113.9 12.4 %copy-start.6 = (s32[512,1]{1,0:T(8,128)S(1)}, s32[512,1]{1,0:T(8,128)}, u32[]{:S(2)}) copy-start(s32[512,1]{1,0:T(8,128)} %copy-done.4) | copy-start | bytes 6148
  116.0 1.0 copy-start.15
  117.0 1.0 copy-start.19
  119.6 18.3 %collective-permute-start.19 = (bf16[256,512]{1,0:T(8,128)(2,1)S(1)}, bf16[256,512]{1,0:T(8,128)(2,1)S(1)}, u32[]{:S(2)}, u32[]{:S(2)}) collective-permute-start(bf16[256,512]{1,0:T(8,128)(2,1)S(1)} %collective-permute-done.10.refs_0_), channel_id=1, source_target_pairs={{0,4},{4,0},{8,12},{12,8},{16,20},{20,16},{24,28},{28,24},{32,36},... | collective-permute-start | bytes 786440 | tf_op jit(solution)/shard_map/cross_a3/ppermute | solution.py:40
  119.9 14.2 %collective-permute-start.11 = (bf16[256,512]{1,0:T(8,128)(2,1)S(1)}, bf16[256,512]{1,0:T(8,128)(2,1)S(1)}, u32[]{:S(2)}, u32[]{:S(2)}) collective-permute-start(bf16[256,512]{1,0:T(8,128)(2,1)S(1)} %collective-permute-done.10.refs_0_), channel_id=1, source_target_pairs={{0,8},{4,12},{8,16},{12,20},{16,24},{20,28},{24,32},{28,36},{32,40... | collective-permute-start | bytes 786440 | tf_op jit(solution)/shard_map/hop_a4/ppermute | solution.py:31
  123.0 17.1 %collective-permute-start.18 = (bf16[256,512]{1,0:T(8,128)(2,1)S(1)}, bf16[256,512]{1,0:T(8,128)(2,1)S(1)}, u32[]{:S(2)}, u32[]{:S(2)}) collective-permute-start(bf16[256,512]{1,0:T(8,128)(2,1)S(1)} %collective-permute-done.15.refs_0_), channel_id=1, source_target_pairs={{0,4},{4,0},{8,12},{12,8},{16,20},{20,16},{24,28},{28,24},{32,36},... | collective-permute-start | bytes 786440 | tf_op jit(solution)/shard_map/cross_b3/ppermute | solution.py:40
  123.1 14.9 %collective-permute-start.16 = (bf16[256,512]{1,0:T(8,128)(2,1)S(1)}, bf16[256,512]{1,0:T(8,128)(2,1)S(1)}, u32[]{:S(2)}, u32[]{:S(2)}) collective-permute-start(bf16[256,512]{1,0:T(8,128)(2,1)S(1)} %collective-permute-done.15.refs_0_), channel_id=1, source_target_pairs={{0,8},{4,12},{8,16},{12,20},{16,24},{20,28},{24,32},{28,36},{32,40... | collective-permute-start | bytes 786440 | tf_op jit(solution)/shard_map/hop_b4/ppermute | solution.py:31
  126.3 1.0 copy-start.12
  127.3 1.2 copy-start.16
  128.5 1.2 copy-start.20
  134.0 10.3 %collective-permute-start.12 = (bf16[256,512]{1,0:T(8,128)(2,1)S(1)}, bf16[256,512]{1,0:T(8,128)(2,1)S(1)}, u32[]{:S(2)}, u32[]{:S(2)}) collective-permute-start(bf16[256,512]{1,0:T(8,128)(2,1)S(1)} %collective-permute-done.11.refs_0_), channel_id=1, source_target_pairs={{0,4},{4,0},{8,12},{12,8},{16,20},{20,16},{24,28},{28,24},{32,36},... | collective-permute-start | bytes 786440 | tf_op jit(solution)/shard_map/cross_a4/ppermute | solution.py:40
  138.0 6.4 %collective-permute-start.17 = (bf16[256,512]{1,0:T(8,128)(2,1)S(1)}, bf16[256,512]{1,0:T(8,128)(2,1)S(1)}, u32[]{:S(2)}, u32[]{:S(2)}) collective-permute-start(bf16[256,512]{1,0:T(8,128)(2,1)S(1)} %collective-permute-done.16.refs_1_), channel_id=1, source_target_pairs={{0,4},{4,0},{8,12},{12,8},{16,20},{20,16},{24,28},{28,24},{32,36},... | collective-permute-start | bytes 786440 | tf_op jit(solution)/shard_map/cross_b4/ppermute | solution.py:40
  (1 other events, 0.7 us)
where the time goes:
time: 149 us; the launch traced here: 148 us
  starting transfers between devices  59.1 us (40%)
  Pallas kernels  33 us (22%)
  local copies, waits for them, and re-layouts  23 us (15%)
  waiting for transfers between devices  23 us (15%)
  other arithmetic  8.62 us (6%)
    ppermute x12, starting transfers between devices, shifted(): return lax.ppermute(block, axis, route)  44.9 us
    pallas_call x10, Pallas kernels, attend(): pl.pallas_call(functools.partial(attend_kernel, places, first, last, guar...  21.2 us
    unnamed x45, local copies, waits for them, and re-layouts  18.3 us
    ppermute x4, waiting for transfers between devices, turned(): lax.ppermute(block, axis, [(i, (i + distance) % count) for i in range(cou...  16 us
    pallas_call x1, Pallas kernels, project_kv(): pl.pallas_call(functools.partial(kv_kernel, (segments, first_page, carrie...  7.34 us
    ppermute x12, waiting for transfers between devices, shifted(): return lax.ppermute(block, axis, route)  7 us
    ppermute x4, starting transfers between devices, turned(): lax.ppermute(block, axis, [(i, (i + distance) % count) for i in range(cou...  6.55 us
    all_to_all x1, starting transfers between devices, per_device(): lax.all_to_all(after(pages, a[1]), 'tp', split_axis=0, concat_axis=0, til...  4.66 us
  transfers between devices with their start and end apart: 27, of which 7 were waited for; matrix products, arithmetic and copies ran while one was open for 8% of the time, Pallas kernels for 15%

commit v1 on v0

--- a/solution.py
+++ b/solution.py
@@ -11,6 +11,7 @@
 HD = 128
 WIN = 4096
 PAGE = 128
+SPAN = 256
 
 logit_cap = 50.0
 query_scale = 144.0 ** (-0.5)
@@ -76,7 +77,7 @@
     size = streams[0].shape[0]
     for start in range(0, rows, PAGE):
         at = slice(start, start + PAGE)
-        slot = table[first_page + start // PAGE]
+        slot = lax.rem(table[first_page + start // PAGE] - shards[0] + count, count)
         out = streams[start // size]
         to = slice(start % size, start % size + PAGE)
         for head in range(kv_width // HD):
@@ -172,21 +173,23 @@
     kv_width = blocks[0].shape[1] // 2
     repeat = heads * HD // kv_width
 
-    def visit(block, index, top):
-        span = block.shape[0]
-        key_first = meta[index]
+    def visit(block, index, base, top):
+        span = SPAN
+        key_first = meta[index] + base
         at = slice(top or 0, rows)
         here = (at.stop - at.start, span)
         key_index = key_first + lax.broadcasted_iota(jnp.int32, here, 1)
-        allowed = key_index >= low_ref[at, :]
+        allowed = key_index >= jnp.concatenate([low_ref[at, :]] * (span // HD), axis=1)
         if top is not None:
             row = meta[0] + top + lax.broadcasted_iota(jnp.int32, here, 0)
             allowed = allowed & (key_index <= row)
         for head in range(heads):
             cols = slice(head * HD, head * HD + HD)
             group = head // repeat
-            keys = block[:, group * HD : group * HD + HD]
-            values = block[:, kv_width + group * HD : kv_width + group * HD + HD]
+            keys = block[base : base + span, group * HD : group * HD + HD]
+            values = block[
+                base : base + span, kv_width + group * HD : kv_width + group * HD + HD
+            ]
             raw = lax.dot_general(
                 q_ref[at, cols],
                 keys,
@@ -205,7 +208,8 @@
 
     def visit_all():
         for block, (index, top) in zip(blocks, places):
-            visit(block, index, top)
+            for base in range(0, block.shape[0], SPAN):
+                visit(block, index, base, None if top is None else top + base)
 
     if guarded:
         key_first = meta[places[0][0]]
@@ -255,29 +259,51 @@
     )(*operands)
 
 
-def cache_kernel(received, out):
-    width = received.shape[2] // 2
-    for shard in range(received.shape[0]):
-        cols = slice(shard * width, shard * width + width)
+def cache_kernel(shards, *refs):
+    out = refs[-1]
+    count = len(refs) - 1
+    width = refs[0].shape[1] // 2
+    for turn, received in enumerate(refs[:-1]):
+        shard = shards[(count - turn) % count]
+        cols = pl.ds(pl.multiple_of(shard * width, 128), width)
         for index in range(2):
-            block = received[shard, :, index * width : index * width + width]
-            out[0, :, index, cols] = block
-
-
-def build_cache(received):
-    ranks, rows, width = received.shape
+            out[0, :, index, cols] = received[:, index * width : index * width + width]
+
+
+def exchange_pages(shards, pages):
+    count, rows, width = pages.shape
+    received = [pages[0]]
+    for turn in range(1, count):
+        received.append(turned(pages[turn], "tp", turn))
     return pl.pallas_call(
         cache_kernel,
         name="build_cache",
-        out_shape=jax.ShapeDtypeStruct((1, rows, 2, ranks * width // 2), received.dtype),
-        in_specs=[whole()],
+        out_shape=jax.ShapeDtypeStruct((1, rows, 2, count * width // 2), pages.dtype),
+        in_specs=[whole(SMEM)] + [whole()] * count,
         out_specs=whole(),
         compiler_params=pltpu.CompilerParams(vmem_limit_bytes=8 << 20),
-    )(received)
-
-
-def after(value, *others):
-    return lax.optimization_barrier((value, *others))[0]
+        cost_estimate=pl.CostEstimate(flops=1000000000, transcendentals=0, bytes_accessed=1000),
+    )(shards, *received)
+
+
+def halves_kernel(left, right, left_out, right_out):
+    half = left_out.shape[0]
+    left_out[...] = left[:half, :]
+    right_out[...] = right[half:, :]
+
+
+def halves(left, right):
+    rows, width = left.shape
+    half = jax.ShapeDtypeStruct((rows // 2, width), left.dtype)
+    return pl.pallas_call(
+        halves_kernel,
+        name="halves",
+        out_shape=(half, half),
+        in_specs=[whole()] * 2,
+        out_specs=(whole(), whole()),
+        compiler_params=pltpu.CompilerParams(vmem_limit_bytes=8 << 20),
+        cost_estimate=pl.CostEstimate(flops=20000000000, transcendentals=0, bytes_accessed=4 * rows * width),
+    )(left, right)
 
 
 def ring_gather(block):
@@ -285,8 +311,9 @@
     half = rows // 2
     left = turned(block, "tp", 1)
     right = turned(block, "tp", -1)
-    far_a = turned(left[:half], "tp", 1)
-    far_b = turned(right[half:], "tp", -1)
+    left_half, right_half = halves(left, right)
+    far_a = turned(left_half, "tp", 1)
+    far_b = turned(right_half, "tp", -1)
     return [
         (block, (0, 0, rows)),
         (left, (3, 0, rows)),
@@ -319,13 +346,13 @@
     same = jnp.sum((earlier == own).astype(jnp.int32), axis=1, keepdims=True)
     starts = first_token + before - same
     query_index = first_token + jnp.arange(tokens, dtype=jnp.int32)[:, None]
-    low = jnp.maximum(starts, query_index - (WIN - 1))
+    low = jnp.maximum(starts, query_index - (WIN - 1)) + jnp.zeros((1, HD), jnp.int32)
     steps = WIN // tokens // 2
     core = place % 2
     backs = [jnp.int32(2 * step) for step in range(steps + 1)]
     backs += [2 * step - 1 + 2 * core for step in range(steps + 1)]
     firsts = jnp.stack(backs) * -tokens + first_token
-    meta = jnp.concatenate([first_token.reshape(1), firsts, firsts + half])
+    meta = jnp.concatenate([first_token.reshape(1), firsts])
 
     freqs = 10000.0 ** (-(jnp.arange(HD // 2, dtype=jnp.float32) * (2.0 / HD)))
     angles = (query_index - starts).astype(jnp.float32) * jnp.concatenate([freqs, freqs])[None, :]
@@ -334,46 +361,30 @@
     sin = jnp.sin(angles) * sign[None, :]
     gain = norm_gain.reshape(1, -1)
 
-    normed, pages, a0, b0 = project_kv(
-        shards, table, pieces, gain, w_key, w_value, cos, sin, half
+    normed, pages, stream = project_kv(
+        shards, table, pieces, gain, w_key, w_value, cos, sin, tokens
     )
-
-    def hop(name, block):
-        with jax.named_scope(name):
-            return shifted(block, "seq", 2)
-
-    def cross(name, block):
-        with jax.named_scope(name):
-            return swapped(block)
-
     look = functools.partial(attend, meta, low)
-    straight = [1 + step for step in range(steps + 1)]
-    turned_at = [2 + steps + step for step in range(steps + 1)]
-    later = 2 * (steps + 1)
-
-    a, b = [a0], [b0]
-    ca, cb = [], []
+    arrived = [stream]
+    crossed = []
     for step in range(steps + 1):
         if step:
-            a.append(hop(f"hop_a{step}", a[-1]))
-            b.append(hop(f"hop_b{step}", b[-1]))
-        ca.append(cross(f"cross_a{step}", a[-1]))
-        cb.append(cross(f"cross_b{step}", b[-1]))
+            with jax.named_scope(f"hop_{step}"):
+                arrived.append(shifted(arrived[-1], "seq", 2))
+        with jax.named_scope(f"cross_{step}"):
+            crossed.append(swapped(arrived[-1]))
+    straight = [1 + step for step in range(steps + 1)]
+    over = [2 + steps + step for step in range(steps + 1)]
     queries = project_q((normed,), w_query, cos, sin)
-    state = look(queries, [(a[0], straight[0], 0), (b[0], straight[0] + later, half)])
-    edge = [(ca[0], turned_at[0], None), (cb[0], turned_at[0] + later, None)]
-    state = look(queries, edge, state, guarded=True)
+    state = look(queries, [(arrived[0], straight[0], 0)])
+    state = look(queries, [(crossed[0], over[0], None)], state, guarded=True)
     for step in range(1, steps):
-        near, over = straight[step], turned_at[step]
-        state = look(queries, [(a[step], near, None), (ca[step], over, None)], state)
-        near, over = near + later, over + later
-        state = look(queries, [(b[step], near, None), (cb[step], over, None)], state)
-    near, over = straight[steps], turned_at[steps]
-    state = look(queries, [(a[steps], near, None), (b[steps], near + later, None)], state)
-    edge = [(ca[steps], over, None), (cb[steps], over + later, None)]
+        state = look(queries, [(arrived[step], straight[step], None)], state)
+        state = look(queries, [(crossed[step], over[step], None)], state)
+    state = look(queries, [(arrived[steps], straight[steps], None)], state)
+    edge = [(crossed[steps], over[steps], None)]
     attended = look(queries, edge, state, last=True, guarded=True)
-    received = lax.all_to_all(after(pages, a[1]), "tp", split_axis=0, concat_axis=0, tiled=True)
-    kv_cache = build_cache(received)
+    kv_cache = exchange_pages(shards, pages)
     return (attended, kv_cache)
 
 

time: 149 us -> 135 us (0.906)
  waiting for transfers between devices: 23 us -> 62.1 us
  starting transfers between devices: 59.1 us -> 36.3 us
  local copies, waits for them, and re-layouts: 23 us -> 1.03 us
  other arithmetic: 8.62 us -> 3.15 us
  Pallas kernels: 33 us -> 31.2 us
    ppermute x12 -> x8, waiting for transfers between devices: 7 us -> 48.9 us  [shifted(): return lax.ppermute(block, axis, route)]
    ppermute x12 -> x8, starting transfers between devices: 44.9 us -> 24 us  [shifted(): return lax.ppermute(block, axis, route)]
    unnamed x45 -> x13, local copies, waits for them, and re-layouts: 18.3 us -> 0.04 us
    ppermute x4 -> x7, starting transfers between devices: 6.55 us -> 12.1 us  [turned(): lax.ppermute(block, axis, [(i, (i + distance) % count) for i in range(cou...]
    all_to_all x1 -> x0, starting transfers between devices: 4.66 us -> none  [per_device(): lax.all_to_all(after(pages, a[1]), 'tp', split_axis=0, concat_axis=0, til...]
    ppermute x4 -> x7, waiting for transfers between devices: 16 us -> 13.1 us  [turned(): lax.ppermute(block, axis, [(i, (i + distance) % count) for i in range(cou...]
    ppermute x10 -> x5, starting transfers between devices: 2.9 us -> 0.1 us  [swapped(): lax.ppermute(block, 'seq', [(i, i ^ 1) for i in range(lax.axis_size('seq'...]
    slice x2 -> x0, local copies, waits for them, and re-layouts: 1.72 us -> none  [the longest x1 0.87 us: ring_gather(): far_b = turned(right[half:], 'tp', -1)]
  transfers between devices with their start and end apart: 27 -> 20, of which waited for: 7 -> 10; matrix products, arithmetic and copies ran while one was open for 8% -> 3% of each run, Pallas kernels for 15% -> 16%
where the time goes in v1:
time: 135 us
  waiting for transfers between devices  62.1 us (46%)
  starting transfers between devices  36.3 us (27%)
  Pallas kernels  31.2 us (23%)
  other arithmetic  3.15 us (2%)
    ppermute x8, waiting for transfers between devices, shifted(): return lax.ppermute(block, axis, route)  48.9 us
    ppermute x8, starting transfers between devices, shifted(): return lax.ppermute(block, axis, route)  24 us
    pallas_call x10, Pallas kernels, attend(): pl.pallas_call(functools.partial(attend_kernel, places, first, last, guar...  20.2 us
    ppermute x7, waiting for transfers between devices, turned(): lax.ppermute(block, axis, [(i, (i + distance) % count) for i in range(cou...  13.1 us
    ppermute x7, starting transfers between devices, turned(): lax.ppermute(block, axis, [(i, (i + distance) % count) for i in range(cou...  12.1 us
    pallas_call x1, Pallas kernels, project_kv(): pl.pallas_call(functools.partial(kv_kernel, (segments, first_page, carrie...  5.87 us
    pallas_call x1, Pallas kernels, project_q(): pl.pallas_call(functools.partial(q_kernel, len(normed)), name='project_q'...  2.81 us
  transfers between devices with their start and end apart: 20, of which 10 were waited for; matrix products, arithmetic and copies ran while one was open for 3% of the time, Pallas kernels for 16%

profile of v1, /device:TPU:6, one launch (start us, length us, event | category | flops | bytes accessed | tf_op | source)
XLA Modules:
  0.0 134.7 jit_solution(17181120264629977867)
XLA Ops:
  0.6 1.7 %collective-permute-start.4 = (bf16[512,1152]{1,0:T(8,128)(2,1)}, bf16[512,1152]{1,0:T(8,128)(2,1)S(1)}, u32[]{:S(2)}, u32[]{:S(2)}) collective-permute-start(bf16[512,1152]{1,0:T(8,128)(2,1)} %refs_0_.1), channel_id=1, source_target_pairs={{0,1},{1,2},{2,3},{3,0},{4,5},{5,6},{6,7},{7,4},{8,9},{9,10},{10,1... | collective-permute-start | bytes 3538952 | tf_op jit(solution)/shard_map/ppermute | solution.py:37
  2.3 1.7 %collective-permute-start.5 = (bf16[512,1152]{1,0:T(8,128)(2,1)}, bf16[512,1152]{1,0:T(8,128)(2,1)S(1)}, u32[]{:S(2)}, u32[]{:S(2)}) collective-permute-start(bf16[512,1152]{1,0:T(8,128)(2,1)} %refs_0_.1), channel_id=1, source_target_pairs={{0,3},{1,0},{2,1},{3,2},{4,7},{5,4},{6,5},{7,6},{8,11},{9,8},{10,9... | collective-permute-start | bytes 3538952 | tf_op jit(solution)/shard_map/ppermute | solution.py:37
  3.9 0.7 broadcast_add_fusion
  4.6 1.9 %collective-permute-start = (s32[1,512]{1,0:T(1,128)S(1)}, s32[1,512]{1,0:T(1,128)S(1)}, u32[]{:S(2)}, u32[]{:S(2)}) collective-permute-start(s32[1,512]{1,0:T(1,128)S(1)} %bitcast.20), channel_id=1, source_target_pairs={{0,4},{4,8},{8,12},{12,16},{16,20},{20,24},{24,28},{28,32},{32,36}... | collective-permute-start | bytes 6152 | tf_op jit(solution)/shard_map/ppermute | solution.py:32
  6.5 3.8 %collective-permute-start.1 = (s32[1,512]{1,0:T(1,128)S(1)}, s32[1,512]{1,0:T(1,128)S(1)}, u32[]{:S(2)}, u32[]{:S(2)}) collective-permute-start(s32[1,512]{1,0:T(1,128)S(1)} %bitcast.21), channel_id=1, source_target_pairs={{0,8},{4,12},{8,16},{12,20},{16,24},{20,28},{24,32},{28,36},{32,40... | collective-permute-start | bytes 6152 | tf_op jit(solution)/shard_map/ppermute | solution.py:32
  10.4 0.1 stack.23
  10.5 0.1 pad_maximum_fusion
  10.6 0.3 convert_reduce_fusion.1
  10.9 2.1 %collective-permute-done = s32[1,512]{1,0:T(1,128)S(1)} collective-permute-done((s32[1,512]{1,0:T(1,128)S(1)}, s32[1,512]{1,0:T(1,128)S(1)}, u32[]{:S(2)}, u32[]{:S(2)}) %collective-permute-start) | collective-permute-done | bytes 2080 | tf_op jit(solution)/shard_map/ppermute | solution.py:32
  12.9 3.2 %collective-permute-done.1 = s32[1,512]{1,0:T(1,128)S(1)} collective-permute-done((s32[1,512]{1,0:T(1,128)S(1)}, s32[1,512]{1,0:T(1,128)S(1)}, u32[]{:S(2)}, u32[]{:S(2)}) %collective-permute-start.1) | collective-permute-done | bytes 2080 | tf_op jit(solution)/shard_map/ppermute | solution.py:32
  16.1 1.9 %collective-permute-start.2 = (s32[3,512]{1,0:T(4,128)S(1)}, s32[3,512]{1,0:T(4,128)S(1)}, u32[]{:S(2)}, u32[]{:S(2)}) collective-permute-start(s32[3,512]{1,0:T(4,128)S(1)} %pad_add_fusion), channel_id=1, source_target_pairs={{0,12},{4,16},{8,20},{12,24},{16,28},{20,32},{24,36},{28,40},{32,4... | collective-permute-start | bytes 18440 | tf_op jit(solution)/shard_map/ppermute | solution.py:32
  18.1 6.6 %collective-permute-start.3 = (s32[3,512]{1,0:T(4,128)S(1)}, s32[3,512]{1,0:T(4,128)S(1)}, u32[]{:S(2)}, u32[]{:S(2)}) collective-permute-start(s32[3,512]{1,0:T(4,128)S(1)} %pad_add_fusion), channel_id=1, source_target_pairs={{0,24},{4,28},{8,32},{12,36},{16,40},{20,44},{24,48},{28,52},{32,5... | collective-permute-start | bytes 18440 | tf_op jit(solution)/shard_map/ppermute | solution.py:32
  24.8 0.7 reshape.48.refs_5_
  25.5 2.0 %collective-permute-done.3 = s32[3,512]{1,0:T(4,128)S(1)} collective-permute-done((s32[3,512]{1,0:T(4,128)S(1)}, s32[3,512]{1,0:T(4,128)S(1)}, u32[]{:S(2)}, u32[]{:S(2)}) %collective-permute-start.3) | collective-permute-done | bytes 6176 | tf_op jit(solution)/shard_map/ppermute | solution.py:32
  27.7 2.2 %collective-permute-done.4.left.refs_1_ = bf16[512,1152]{1,0:T(8,128)(2,1)S(1)} collective-permute-done((bf16[512,1152]{1,0:T(8,128)(2,1)}, bf16[512,1152]{1,0:T(8,128)(2,1)S(1)}, u32[]{:S(2)}, u32[]{:S(2)}) %collective-permute-start.4) | collective-permute-done | bytes 1179680 | tf_op jit(solution)/shard_map/ppermute | solution.py:37
  29.9 0.1 halves.1
  30.0 1.7 %collective-permute-start.6 = (bf16[256,1152]{1,0:T(8,128)(2,1)S(1)}, bf16[256,1152]{1,0:T(8,128)(2,1)S(1)}, u32[]{:S(2)}, u32[]{:S(2)}) collective-permute-start(bf16[256,1152]{1,0:T(8,128)(2,1)S(1)} %get-tuple-element.25), channel_id=1, source_target_pairs={{0,1},{1,2},{2,3},{3,0},{4,5},{5,6},{6,7},{7,4},{8,9},{9,10},{10,1... | collective-permute-start | bytes 1769480 | tf_op jit(solution)/shard_map/ppermute | solution.py:37
  31.7 1.7 %collective-permute-start.7 = (bf16[256,1152]{1,0:T(8,128)(2,1)S(1)}, bf16[256,1152]{1,0:T(8,128)(2,1)S(1)}, u32[]{:S(2)}, u32[]{:S(2)}) collective-permute-start(bf16[256,1152]{1,0:T(8,128)(2,1)S(1)} %get-tuple-element.26), channel_id=1, source_target_pairs={{0,3},{1,0},{2,1},{3,2},{4,7},{5,4},{6,5},{7,6},{8,11},{9,8},{10,9... | collective-permute-start | bytes 1769480 | tf_op jit(solution)/shard_map/ppermute | solution.py:37
  33.3 1.0 convert_reduce_fusion
  34.4 1.0 fusion
  35.4 10.2 %collective-permute-done.6.refs_3_ = bf16[256,1152]{1,0:T(8,128)(2,1)S(1)} collective-permute-done((bf16[256,1152]{1,0:T(8,128)(2,1)S(1)}, bf16[256,1152]{1,0:T(8,128)(2,1)S(1)}, u32[]{:S(2)}, u32[]{:S(2)}) %collective-permute-start.6) | collective-permute-done | bytes 589856 | tf_op jit(solution)/shard_map/ppermute | solution.py:37
  45.6 5.9 %norm_project_kv.1 = (bf16[512,4608]{1,0:T(8,128)(2,1)S(1)}, bf16[4,128,512]{2,1,0:T(8,128)(2,1)S(1)}, bf16[512,512]{1,0:T(8,128)(2,1)S(1)}) custom-call(s32[4]{0:T(128)S(1)} %and_select_fusion.shards, s32[4]{0:T(128)S(1)} %bitcast.19, bf16[512,1152]{1,0:T(8,128)(2,1)S(1)} %copy-done.2, bf16[512,1152]{1,0:T(8,128)(2,1)S(1)} %collective-permute-done.4.left.refs_1_, ...), custom_call_target="tpu_custom_call" | custom-call | flops 2415919104 | bytes 14155776 | tf_op jit(solution)/shard_map/norm_project_kv/pallas_call | solution.py:108
  51.5 0.1 collective-permute-start.16
  51.6 3.8 %collective-permute-start.8 = (bf16[512,512]{1,0:T(8,128)(2,1)S(1)}, bf16[512,512]{1,0:T(8,128)(2,1)S(1)}, u32[]{:S(2)}, u32[]{:S(2)}) collective-permute-start(bf16[512,512]{1,0:T(8,128)(2,1)S(1)} %get-tuple-element.28.refs_0_), channel_id=1, source_target_pairs={{0,8},{4,12},{8,16},{12,20},{16,24},{20,28},{24,32},{28,36},{32,40... | collective-permute-start | bytes 1572872 | tf_op jit(solution)/shard_map/hop_1/ppermute | solution.py:32
  55.4 1.1 collective-permute-start.17
  56.5 3.4 %collective-permute-start.18 = (bf16[128,512]{1,0:T(8,128)(2,1)S(1)}, bf16[128,512]{1,0:T(8,128)(2,1)S(1)}, u32[]{:S(2)}, u32[]{:S(2)}) collective-permute-start(bf16[128,512]{1,0:T(8,128)(2,1)S(1)} %get-tuple-element.49), channel_id=1, source_target_pairs={{0,2},{1,3},{2,0},{3,1},{4,6},{5,7},{6,4},{7,5},{8,10},{9,11},{10,... | collective-permute-start | bytes 393224 | tf_op jit(solution)/shard_map/ppermute | solution.py:37
  59.9 1.0 collective-permute-start.19
  60.9 2.8 %project_q.1.q_ref = bf16[512,512]{1,0:T(8,128)(2,1)S(1)} custom-call(bf16[512,4608]{1,0:T(8,128)(2,1)S(1)} %get-tuple-element.27.refs_0_, bf16[4608,512]{1,0:T(8,128)(2,1)S(1)} %copy-done.4, f32[512,128]{1,0:T(8,128)S(1)} %get-tuple-element.55.refs_8_.refs_2_, f32[512,128]{1,0:T(8,128)S(1)} %get-tuple-element.54.refs_9_.refs_3_), custom_call_target="tpu_custom_call" | custom-call | flops 5120000000 | bytes 262144 | tf_op jit(solution)/shard_map/project_q/pallas_call | solution.py:140
  63.8 0.1 add.80.low_ref
  63.9 1.8 %attend.9 = (f32[512,512]{1,0:T(8,128)S(1)}, f32[512,512]{1,0:T(8,128)S(1)}) custom-call(s32[11]{0:T(128)S(1)} %pad_add_fusion.1.meta, s32[512,128]{1,0:T(8,128)S(1)} %add.80.low_ref, bf16[512,512]{1,0:T(8,128)(2,1)S(1)} %project_q.1.q_ref, bf16[512,512]{1,0:T(8,128)(2,1)S(1)} %get-tuple-element.28.refs_0_), custom_call_target="tpu_custom_call" | custom-call | flops 5120000000 | bytes 262144 | tf_op jit(solution)/shard_map/attend/pallas_call | solution.py:245
  65.7 0.7 collective-permute-done.18.refs_2_
  66.3 2.2 %build_cache.1 = bf16[1,128,2,1024]{3,2,1,0:T(2,128)(2,1)} custom-call(s32[4]{0:T(128)S(1)} %and_select_fusion.shards, bf16[128,512]{1,0:T(8,128)(2,1)S(1)} %get-tuple-element.51.refs_0_, bf16[128,512]{1,0:T(8,128)(2,1)S(1)} %collective-permute-done.17.refs_1_, bf16[128,512]{1,0:T(8,128)(2,1)S(1)} %collective-permute-done.18.refs_2_, ...), custom_call_target="tpu_custom_call" | custom-call | flops 1000000000 | bytes 1000 | tf_op jit(solution)/shard_map/build_cache/pallas_call | solution.py:278
  68.5 3.6 %collective-permute-done.8.refs_0_ = bf16[512,512]{1,0:T(8,128)(2,1)S(1)} collective-permute-done((bf16[512,512]{1,0:T(8,128)(2,1)S(1)}, bf16[512,512]{1,0:T(8,128)(2,1)S(1)}, u32[]{:S(2)}, u32[]{:S(2)}) %collective-permute-start.8) | collective-permute-done | bytes 524320 | tf_op jit(solution)/shard_map/hop_1/ppermute | solution.py:32
  72.2 1.9 %collective-permute-start.9 = (bf16[512,512]{1,0:T(8,128)(2,1)S(1)}, bf16[512,512]{1,0:T(8,128)(2,1)S(1)}, u32[]{:S(2)}, u32[]{:S(2)}) collective-permute-start(bf16[512,512]{1,0:T(8,128)(2,1)S(1)} %collective-permute-done.8.refs_0_), channel_id=1, source_target_pairs={{0,8},{4,12},{8,16},{12,20},{16,24},{20,28},{24,32},{28,36},{32,40... | collective-permute-start | bytes 1572872 | tf_op jit(solution)/shard_map/hop_2/ppermute | solution.py:32
  74.1 0.6 attend.10
  74.7 2.1 %attend.11 = (f32[512,512]{1,0:T(8,128)S(1)}, f32[512,512]{1,0:T(8,128)S(1)}) custom-call(s32[11]{0:T(128)S(1)} %pad_add_fusion.1.meta, s32[512,128]{1,0:T(8,128)S(1)} %add.80.low_ref, bf16[512,512]{1,0:T(8,128)(2,1)S(1)} %project_q.1.q_ref, bf16[512,512]{1,0:T(8,128)(2,1)S(1)} %collective-permute-done.8.refs_0_, ...), custom_call_target="tpu_custom_call", output_to_operand_aliasing={{0}: (4, {}), {1}: (5, {})} | custom-call | flops 5120000000 | bytes 262144 | tf_op jit(solution)/shard_map/attend/pallas_call | solution.py:245
  76.7 13.8 %collective-permute-done.9.refs_0_ = bf16[512,512]{1,0:T(8,128)(2,1)S(1)} collective-permute-done((bf16[512,512]{1,0:T(8,128)(2,1)S(1)}, bf16[512,512]{1,0:T(8,128)(2,1)S(1)}, u32[]{:S(2)}, u32[]{:S(2)}) %collective-permute-start.9) | collective-permute-done | bytes 524320 | tf_op jit(solution)/shard_map/hop_2/ppermute | solution.py:32
  90.5 1.9 %collective-permute-start.10 = (bf16[512,512]{1,0:T(8,128)(2,1)S(1)}, bf16[512,512]{1,0:T(8,128)(2,1)S(1)}, u32[]{:S(2)}, u32[]{:S(2)}) collective-permute-start(bf16[512,512]{1,0:T(8,128)(2,1)S(1)} %collective-permute-done.9.refs_0_), channel_id=1, source_target_pairs={{0,8},{4,12},{8,16},{12,20},{16,24},{20,28},{24,32},{28,36},{32,40... | collective-permute-start | bytes 1572872 | tf_op jit(solution)/shard_map/hop_3/ppermute | solution.py:32
  92.4 2.1 %attend.12 = (f32[512,512]{1,0:T(8,128)S(1)}, f32[512,512]{1,0:T(8,128)S(1)}) custom-call(s32[11]{0:T(128)S(1)} %pad_add_fusion.1.meta, s32[512,128]{1,0:T(8,128)S(1)} %add.80.low_ref, bf16[512,512]{1,0:T(8,128)(2,1)S(1)} %project_q.1.q_ref, bf16[512,512]{1,0:T(8,128)(2,1)S(1)} %collective-permute-done.15.refs_0_, ...), custom_call_target="tpu_custom_call", output_to_operand_aliasing={{0}: (4, {}), {1}: (5, {})} | custom-call | flops 5120000000 | bytes 262144 | tf_op jit(solution)/shard_map/attend/pallas_call | solution.py:245
  94.5 2.1 %attend.13 = (f32[512,512]{1,0:T(8,128)S(1)}, f32[512,512]{1,0:T(8,128)S(1)}) custom-call(s32[11]{0:T(128)S(1)} %pad_add_fusion.1.meta, s32[512,128]{1,0:T(8,128)S(1)} %add.80.low_ref, bf16[512,512]{1,0:T(8,128)(2,1)S(1)} %project_q.1.q_ref, bf16[512,512]{1,0:T(8,128)(2,1)S(1)} %collective-permute-done.9.refs_0_, ...), custom_call_target="tpu_custom_call", output_to_operand_aliasing={{0}: (4, {}), {1}: (5, {})} | custom-call | flops 5120000000 | bytes 262144 | tf_op jit(solution)/shard_map/attend/pallas_call | solution.py:245
  96.6 12.2 %collective-permute-done.10.refs_0_ = bf16[512,512]{1,0:T(8,128)(2,1)S(1)} collective-permute-done((bf16[512,512]{1,0:T(8,128)(2,1)S(1)}, bf16[512,512]{1,0:T(8,128)(2,1)S(1)}, u32[]{:S(2)}, u32[]{:S(2)}) %collective-permute-start.10) | collective-permute-done | bytes 524320 | tf_op jit(solution)/shard_map/hop_3/ppermute | solution.py:32
  108.8 2.1 %collective-permute-start.11 = (bf16[512,512]{1,0:T(8,128)(2,1)S(1)}, bf16[512,512]{1,0:T(8,128)(2,1)S(1)}, u32[]{:S(2)}, u32[]{:S(2)}) collective-permute-start(bf16[512,512]{1,0:T(8,128)(2,1)S(1)} %collective-permute-done.10.refs_0_), channel_id=1, source_target_pairs={{0,8},{4,12},{8,16},{12,20},{16,24},{20,28},{24,32},{28,36},{32,40... | collective-permute-start | bytes 1572872 | tf_op jit(solution)/shard_map/hop_4/ppermute | solution.py:32
  111.0 2.1 %attend.14 = (f32[512,512]{1,0:T(8,128)S(1)}, f32[512,512]{1,0:T(8,128)S(1)}) custom-call(s32[11]{0:T(128)S(1)} %pad_add_fusion.1.meta, s32[512,128]{1,0:T(8,128)S(1)} %add.80.low_ref, bf16[512,512]{1,0:T(8,128)(2,1)S(1)} %project_q.1.q_ref, bf16[512,512]{1,0:T(8,128)(2,1)S(1)} %collective-permute-done.14.refs_0_, ...), custom_call_target="tpu_custom_call", output_to_operand_aliasing={{0}: (4, {}), {1}: (5, {})} | custom-call | flops 5120000000 | bytes 262144 | tf_op jit(solution)/shard_map/attend/pallas_call | solution.py:245
  113.1 2.1 %attend.15 = (f32[512,512]{1,0:T(8,128)S(1)}, f32[512,512]{1,0:T(8,128)S(1)}) custom-call(s32[11]{0:T(128)S(1)} %pad_add_fusion.1.meta, s32[512,128]{1,0:T(8,128)S(1)} %add.80.low_ref, bf16[512,512]{1,0:T(8,128)(2,1)S(1)} %project_q.1.q_ref, bf16[512,512]{1,0:T(8,128)(2,1)S(1)} %collective-permute-done.10.refs_0_, ...), custom_call_target="tpu_custom_call", output_to_operand_aliasing={{0}: (4, {}), {1}: (5, {})} | custom-call | flops 5120000000 | bytes 262144 | tf_op jit(solution)/shard_map/attend/pallas_call | solution.py:245
  115.1 12.0 %collective-permute-done.11.refs_0_ = bf16[512,512]{1,0:T(8,128)(2,1)S(1)} collective-permute-done((bf16[512,512]{1,0:T(8,128)(2,1)S(1)}, bf16[512,512]{1,0:T(8,128)(2,1)S(1)}, u32[]{:S(2)}, u32[]{:S(2)}) %collective-permute-start.11) | collective-permute-done | bytes 524320 | tf_op jit(solution)/shard_map/hop_4/ppermute | solution.py:32
  127.2 2.1 %attend.16 = (f32[512,512]{1,0:T(8,128)S(1)}, f32[512,512]{1,0:T(8,128)S(1)}) custom-call(s32[11]{0:T(128)S(1)} %pad_add_fusion.1.meta, s32[512,128]{1,0:T(8,128)S(1)} %add.80.low_ref, bf16[512,512]{1,0:T(8,128)(2,1)S(1)} %project_q.1.q_ref, bf16[512,512]{1,0:T(8,128)(2,1)S(1)} %collective-permute-done.13.refs_0_, ...), custom_call_target="tpu_custom_call", output_to_operand_aliasing={{0}: (4, {}), {1}: (5, {})} | custom-call | flops 5120000000 | bytes 262144 | tf_op jit(solution)/shard_map/attend/pallas_call | solution.py:245
  129.2 2.1 %attend.17 = (f32[512,512]{1,0:T(8,128)S(1)}, f32[512,512]{1,0:T(8,128)S(1)}) custom-call(s32[11]{0:T(128)S(1)} %pad_add_fusion.1.meta, s32[512,128]{1,0:T(8,128)S(1)} %add.80.low_ref, bf16[512,512]{1,0:T(8,128)(2,1)S(1)} %project_q.1.q_ref, bf16[512,512]{1,0:T(8,128)(2,1)S(1)} %collective-permute-done.11.refs_0_, ...), custom_call_target="tpu_custom_call", output_to_operand_aliasing={{0}: (4, {}), {1}: (5, {})} | custom-call | flops 5120000000 | bytes 262144 | tf_op jit(solution)/shard_map/attend/pallas_call | solution.py:245
  131.3 3.3 %attend_last.1 = bf16[512,512]{1,0:T(8,128)(2,1)} custom-call(s32[11]{0:T(128)S(1)} %pad_add_fusion.1.meta, s32[512,128]{1,0:T(8,128)S(1)} %add.80.low_ref, bf16[512,512]{1,0:T(8,128)(2,1)S(1)} %project_q.1.q_ref, bf16[512,512]{1,0:T(8,128)(2,1)S(1)} %collective-permute-done.12.refs_0_, f32[512,512]{1,0:T(8,128)S(1)} %get-tuple-element.45.refs_1_, ...), custom_call_target="tpu_custom_call" | custom-call | flops 5120000000 | bytes 262144 | tf_op jit(solution)/shard_map/attend_last/pallas_call | solution.py:245
  (35 shorter events, 0.3 us)
Async XLA Ops:
  0.6 29.3 %collective-permute-start.4 = (bf16[512,1152]{1,0:T(8,128)(2,1)}, bf16[512,1152]{1,0:T(8,128)(2,1)S(1)}, u32[]{:S(2)}, u32[]{:S(2)}) collective-permute-start(bf16[512,1152]{1,0:T(8,128)(2,1)} %refs_0_.1), channel_id=1, source_target_pairs={{0,1},{1,2},{2,3},{3,0},{4,5},{5,6},{6,7},{7,4},{8,9},{9,10},{10,1... | collective-permute-start | bytes 3538952 | tf_op jit(solution)/shard_map/ppermute | solution.py:37
  2.3 27.6 %collective-permute-start.5 = (bf16[512,1152]{1,0:T(8,128)(2,1)}, bf16[512,1152]{1,0:T(8,128)(2,1)S(1)}, u32[]{:S(2)}, u32[]{:S(2)}) collective-permute-start(bf16[512,1152]{1,0:T(8,128)(2,1)} %refs_0_.1), channel_id=1, source_target_pairs={{0,3},{1,0},{2,1},{3,2},{4,7},{5,4},{6,5},{7,6},{8,11},{9,8},{10,9... | collective-permute-start | bytes 3538952 | tf_op jit(solution)/shard_map/ppermute | solution.py:37
  4.6 8.3 %collective-permute-start = (s32[1,512]{1,0:T(1,128)S(1)}, s32[1,512]{1,0:T(1,128)S(1)}, u32[]{:S(2)}, u32[]{:S(2)}) collective-permute-start(s32[1,512]{1,0:T(1,128)S(1)} %bitcast.20), channel_id=1, source_target_pairs={{0,4},{4,8},{8,12},{12,16},{16,20},{20,24},{24,28},{28,32},{32,36}... | collective-permute-start | bytes 6152 | tf_op jit(solution)/shard_map/ppermute | solution.py:32
  6.5 9.6 %collective-permute-start.1 = (s32[1,512]{1,0:T(1,128)S(1)}, s32[1,512]{1,0:T(1,128)S(1)}, u32[]{:S(2)}, u32[]{:S(2)}) collective-permute-start(s32[1,512]{1,0:T(1,128)S(1)} %bitcast.21), channel_id=1, source_target_pairs={{0,8},{4,12},{8,16},{12,20},{16,24},{20,28},{24,32},{28,36},{32,40... | collective-permute-start | bytes 6152 | tf_op jit(solution)/shard_map/ppermute | solution.py:32
  16.1 9.4 %collective-permute-start.2 = (s32[3,512]{1,0:T(4,128)S(1)}, s32[3,512]{1,0:T(4,128)S(1)}, u32[]{:S(2)}, u32[]{:S(2)}) collective-permute-start(s32[3,512]{1,0:T(4,128)S(1)} %pad_add_fusion), channel_id=1, source_target_pairs={{0,12},{4,16},{8,20},{12,24},{16,28},{20,32},{24,36},{28,40},{32,4... | collective-permute-start | bytes 18440 | tf_op jit(solution)/shard_map/ppermute | solution.py:32
  18.1 9.5 %collective-permute-start.3 = (s32[3,512]{1,0:T(4,128)S(1)}, s32[3,512]{1,0:T(4,128)S(1)}, u32[]{:S(2)}, u32[]{:S(2)}) collective-permute-start(s32[3,512]{1,0:T(4,128)S(1)} %pad_add_fusion), channel_id=1, source_target_pairs={{0,24},{4,28},{8,32},{12,36},{16,40},{20,44},{24,48},{28,52},{32,5... | collective-permute-start | bytes 18440 | tf_op jit(solution)/shard_map/ppermute | solution.py:32
  27.6 6.7 %copy-start.5 = (f32[128]{0:T(128)S(1)}, f32[128]{0:T(128)}, u32[]{:S(2)}) copy-start(f32[128]{0:T(128)} %constant.72) | copy-start | bytes 1540
  27.6 17.9 %copy-start = (bf16[4608,256]{1,0:T(8,128)(2,1)S(1)}, bf16[4608,256]{1,0:T(8,128)(2,1)}, u32[]{:S(2)}) copy-start(bf16[4608,256]{1,0:T(8,128)(2,1)} %refs_6_.1) | copy-start | bytes 7077892
  27.6 17.9 %copy-start.1 = (bf16[4608,256]{1,0:T(8,128)(2,1)S(1)}, bf16[4608,256]{1,0:T(8,128)(2,1)}, u32[]{:S(2)}) copy-start(bf16[4608,256]{1,0:T(8,128)(2,1)} %refs_7_.1) | copy-start | bytes 7077892
  27.6 17.9 %copy-start.2 = (bf16[512,1152]{1,0:T(8,128)(2,1)S(1)}, bf16[512,1152]{1,0:T(8,128)(2,1)}, u32[]{:S(2)}) copy-start(bf16[512,1152]{1,0:T(8,128)(2,1)} %refs_0_.1) | copy-start | bytes 3538948
  27.7 17.9 %copy-start.3 = (s32[1,4]{1,0:T(1,128)S(1)}, s32[1,4]{1,0:T(1,128)}, u32[]{:S(2)}) copy-start(s32[1,4]{1,0:T(1,128)} %param.14) | copy-start | bytes 52
  30.0 15.5 %collective-permute-start.6 = (bf16[256,1152]{1,0:T(8,128)(2,1)S(1)}, bf16[256,1152]{1,0:T(8,128)(2,1)S(1)}, u32[]{:S(2)}, u32[]{:S(2)}) collective-permute-start(bf16[256,1152]{1,0:T(8,128)(2,1)S(1)} %get-tuple-element.25), channel_id=1, source_target_pairs={{0,1},{1,2},{2,3},{3,0},{4,5},{5,6},{6,7},{7,4},{8,9},{9,10},{10,1... | collective-permute-start | bytes 1769480 | tf_op jit(solution)/shard_map/ppermute | solution.py:37
  31.7 13.9 %collective-permute-start.7 = (bf16[256,1152]{1,0:T(8,128)(2,1)S(1)}, bf16[256,1152]{1,0:T(8,128)(2,1)S(1)}, u32[]{:S(2)}, u32[]{:S(2)}) collective-permute-start(bf16[256,1152]{1,0:T(8,128)(2,1)S(1)} %get-tuple-element.26), channel_id=1, source_target_pairs={{0,3},{1,0},{2,1},{3,2},{4,7},{5,4},{6,5},{7,6},{8,11},{9,8},{10,9... | collective-permute-start | bytes 1769480 | tf_op jit(solution)/shard_map/ppermute | solution.py:37
  45.6 15.3 %copy-start.4 = (bf16[4608,512]{1,0:T(8,128)(2,1)S(1)}, bf16[4608,512]{1,0:T(8,128)(2,1)}, u32[]{:S(2)}) copy-start(bf16[4608,512]{1,0:T(8,128)(2,1)} %refs_1_.1) | copy-start | bytes 14155780
  51.5 22.6 %collective-permute-start.16 = (bf16[512,512]{1,0:T(8,128)(2,1)S(1)}, bf16[512,512]{1,0:T(8,128)(2,1)S(1)}, u32[]{:S(2)}, u32[]{:S(2)}) collective-permute-start(bf16[512,512]{1,0:T(8,128)(2,1)S(1)} %get-tuple-element.28.refs_0_), channel_id=1, source_target_pairs={{0,4},{4,0},{8,12},{12,8},{16,20},{20,16},{24,28},{28,24},{32,36},... | collective-permute-start | bytes 1572872 | tf_op jit(solution)/shard_map/cross_0/ppermute | solution.py:41
  51.6 20.6 %collective-permute-start.8 = (bf16[512,512]{1,0:T(8,128)(2,1)S(1)}, bf16[512,512]{1,0:T(8,128)(2,1)S(1)}, u32[]{:S(2)}, u32[]{:S(2)}) collective-permute-start(bf16[512,512]{1,0:T(8,128)(2,1)S(1)} %get-tuple-element.28.refs_0_), channel_id=1, source_target_pairs={{0,8},{4,12},{8,16},{12,20},{16,24},{20,28},{24,32},{28,36},{32,40... | collective-permute-start | bytes 1572872 | tf_op jit(solution)/shard_map/hop_1/ppermute | solution.py:32
  55.4 10.2 %collective-permute-start.17 = (bf16[128,512]{1,0:T(8,128)(2,1)S(1)}, bf16[128,512]{1,0:T(8,128)(2,1)S(1)}, u32[]{:S(2)}, u32[]{:S(2)}) collective-permute-start(bf16[128,512]{1,0:T(8,128)(2,1)S(1)} %get-tuple-element.50), channel_id=1, source_target_pairs={{0,1},{1,2},{2,3},{3,0},{4,5},{5,6},{6,7},{7,4},{8,9},{9,10},{10,1... | collective-permute-start | bytes 393224 | tf_op jit(solution)/shard_map/ppermute | solution.py:37
  56.5 9.8 %collective-permute-start.18 = (bf16[128,512]{1,0:T(8,128)(2,1)S(1)}, bf16[128,512]{1,0:T(8,128)(2,1)S(1)}, u32[]{:S(2)}, u32[]{:S(2)}) collective-permute-start(bf16[128,512]{1,0:T(8,128)(2,1)S(1)} %get-tuple-element.49), channel_id=1, source_target_pairs={{0,2},{1,3},{2,0},{3,1},{4,6},{5,7},{6,4},{7,5},{8,10},{9,11},{10,... | collective-permute-start | bytes 393224 | tf_op jit(solution)/shard_map/ppermute | solution.py:37
  59.9 6.4 %collective-permute-start.19 = (bf16[128,512]{1,0:T(8,128)(2,1)S(1)}, bf16[128,512]{1,0:T(8,128)(2,1)S(1)}, u32[]{:S(2)}, u32[]{:S(2)}) collective-permute-start(bf16[128,512]{1,0:T(8,128)(2,1)S(1)} %get-tuple-element.48), channel_id=1, source_target_pairs={{0,3},{1,0},{2,1},{3,2},{4,7},{5,4},{6,5},{7,6},{8,11},{9,8},{10,9... | collective-permute-start | bytes 393224 | tf_op jit(solution)/shard_map/ppermute | solution.py:37
  72.2 20.3 %collective-permute-start.15 = (bf16[512,512]{1,0:T(8,128)(2,1)S(1)}, bf16[512,512]{1,0:T(8,128)(2,1)S(1)}, u32[]{:S(2)}, u32[]{:S(2)}) collective-permute-start(bf16[512,512]{1,0:T(8,128)(2,1)S(1)} %collective-permute-done.8.refs_0_), channel_id=1, source_target_pairs={{0,4},{4,0},{8,12},{12,8},{16,20},{20,16},{24,28},{28,24},{32,36},... | collective-permute-start | bytes 1572872 | tf_op jit(solution)/shard_map/cross_1/ppermute | solution.py:41
  72.2 18.3 %collective-permute-start.9 = (bf16[512,512]{1,0:T(8,128)(2,1)S(1)}, bf16[512,512]{1,0:T(8,128)(2,1)S(1)}, u32[]{:S(2)}, u32[]{:S(2)}) collective-permute-start(bf16[512,512]{1,0:T(8,128)(2,1)S(1)} %collective-permute-done.8.refs_0_), channel_id=1, source_target_pairs={{0,8},{4,12},{8,16},{12,20},{16,24},{20,28},{24,32},{28,36},{32,40... | collective-permute-start | bytes 1572872 | tf_op jit(solution)/shard_map/hop_2/ppermute | solution.py:32
  90.5 20.5 %collective-permute-start.14 = (bf16[512,512]{1,0:T(8,128)(2,1)S(1)}, bf16[512,512]{1,0:T(8,128)(2,1)S(1)}, u32[]{:S(2)}, u32[]{:S(2)}) collective-permute-start(bf16[512,512]{1,0:T(8,128)(2,1)S(1)} %collective-permute-done.9.refs_0_), channel_id=1, source_target_pairs={{0,4},{4,0},{8,12},{12,8},{16,20},{20,16},{24,28},{28,24},{32,36},... | collective-permute-start | bytes 1572872 | tf_op jit(solution)/shard_map/cross_2/ppermute | solution.py:41
  90.5 18.3 %collective-permute-start.10 = (bf16[512,512]{1,0:T(8,128)(2,1)S(1)}, bf16[512,512]{1,0:T(8,128)(2,1)S(1)}, u32[]{:S(2)}, u32[]{:S(2)}) collective-permute-start(bf16[512,512]{1,0:T(8,128)(2,1)S(1)} %collective-permute-done.9.refs_0_), channel_id=1, source_target_pairs={{0,8},{4,12},{8,16},{12,20},{16,24},{20,28},{24,32},{28,36},{32,40... | collective-permute-start | bytes 1572872 | tf_op jit(solution)/shard_map/hop_3/ppermute | solution.py:32
  108.8 18.3 %collective-permute-start.13 = (bf16[512,512]{1,0:T(8,128)(2,1)S(1)}, bf16[512,512]{1,0:T(8,128)(2,1)S(1)}, u32[]{:S(2)}, u32[]{:S(2)}) collective-permute-start(bf16[512,512]{1,0:T(8,128)(2,1)S(1)} %collective-permute-done.10.refs_0_), channel_id=1, source_target_pairs={{0,4},{4,0},{8,12},{12,8},{16,20},{20,16},{24,28},{28,24},{32,36},... | collective-permute-start | bytes 1572872 | tf_op jit(solution)/shard_map/cross_3/ppermute | solution.py:41
  108.8 18.3 %collective-permute-start.11 = (bf16[512,512]{1,0:T(8,128)(2,1)S(1)}, bf16[512,512]{1,0:T(8,128)(2,1)S(1)}, u32[]{:S(2)}, u32[]{:S(2)}) collective-permute-start(bf16[512,512]{1,0:T(8,128)(2,1)S(1)} %collective-permute-done.10.refs_0_), channel_id=1, source_target_pairs={{0,8},{4,12},{8,16},{12,20},{16,24},{20,28},{24,32},{28,36},{32,40... | collective-permute-start | bytes 1572872 | tf_op jit(solution)/shard_map/hop_4/ppermute | solution.py:32
  127.2 4.2 %collective-permute-start.12 = (bf16[512,512]{1,0:T(8,128)(2,1)S(1)}, bf16[512,512]{1,0:T(8,128)(2,1)S(1)}, u32[]{:S(2)}, u32[]{:S(2)}) collective-permute-start(bf16[512,512]{1,0:T(8,128)(2,1)S(1)} %collective-permute-done.11.refs_0_), channel_id=1, source_target_pairs={{0,4},{4,0},{8,12},{12,8},{16,20},{20,16},{24,28},{28,24},{32,36},... | collective-permute-start | bytes 1572872 | tf_op jit(solution)/shard_map/cross_4/ppermute | solution.py:41

commit v2 on v1

--- a/solution.py
+++ b/solution.py
@@ -45,80 +45,92 @@
     return x * cos + pltpu.roll(x, HD // 2, 1) * sin
 
 
-def kv_kernel(layout, shards, table, *refs):
-    segments, first_page, carried, count = layout
-    pieces = refs[: len(segments)]
-    gain, wk, wv, cos, sin = refs[len(segments) : len(segments) + 5]
-    outs = refs[len(segments) + 5 + carried :]
-    normed, pages, streams = outs[0], outs[1], outs[2:]
-    rows = normed.shape[0]
-    features = gain.shape[1]
-    width = features // count
+def squares_kernel(own, left, right, out):
+    def tile(index, carry):
+        at = pl.ds(pl.multiple_of(index * 64, 64), 64)
+        total = jnp.zeros((64, HD), jnp.float32)
+        for piece in (own, left, right):
+            wide = piece[at, :].astype(jnp.float32)
+            wide = wide * wide
+            for lane in range(0, wide.shape[1], HD):
+                total = total + wide[:, lane : lane + HD]
+        out[at, :] = total
+        return carry
+
+    lax.fori_loop(0, out.shape[0] // 64, tile, 0)
+
+
+def squares(own, left, right):
+    rows, width = own.shape
+    return pl.pallas_call(
+        squares_kernel,
+        name="squares",
+        out_shape=jax.ShapeDtypeStruct((rows, HD), jnp.float32),
+        in_specs=[whole()] * 3,
+        out_specs=whole(),
+        compiler_params=pltpu.CompilerParams(vmem_limit_bytes=8 << 20),
+        cost_estimate=pl.CostEstimate(
+            flops=6 * rows * width, transcendentals=0, bytes_accessed=6 * rows * width
+        ),
+    )(own, left, right)
+
+
+def kv_kernel(shards, table, *refs):
+    own, left, right, far_a, far_b, square_ref, gain, wk, wv, cos, sin = refs[:11]
+    normed, first, second, pages = refs[11:]
+    count = shards.shape[0]
+    rows, features = normed.shape
+    width = own.shape[1]
+    half = rows // 2
 
     for start in range(0, rows, 128):
         at = pl.ds(start, 128)
-        blocks = []
-        for ref, (turn, begin, end) in zip(pieces, segments):
-            if begin <= start < end:
-                part = ref.at[turn] if len(ref.shape) == 3 else ref
-                blocks.append((part, pl.ds(start - begin, 128), turn))
-        square = 0.0
-        for part, rows_at, turn in blocks:
-            wide = part[rows_at, :].astype(jnp.float32)
-            square = square + jnp.sum(wide * wide, axis=-1, keepdims=True)
+        far = far_a if start < half else far_b
+        pieces = ((far, pl.ds(start % half, 128), 2), (own, at, 0), (left, at, 3), (right, at, 1))
+        wide = far[pieces[0][1], :].astype(jnp.float32)
+        square = jnp.sum(wide * wide, axis=-1, keepdims=True)
+        square = square + jnp.sum(square_ref[at, :], axis=-1, keepdims=True)
         scale = lax.rsqrt(square * (1.0 / features) + norm_eps)
-        for part, rows_at, turn in blocks:
+        for part, rows_at, turn in pieces:
             cols = pl.ds(pl.multiple_of(shards[turn] * width, 128), width)
             wide = part[rows_at, :].astype(jnp.float32)
             normed[at, cols] = (wide * scale * gain[:, cols]).astype(jnp.bfloat16)
     keys = jnp.dot(normed[...], wk[...], preferred_element_type=jnp.float32)
     values = jnp.dot(normed[...], wv[...], preferred_element_type=jnp.float32)
     kv_width = wk.shape[1]
-    size = streams[0].shape[0]
-    for start in range(0, rows, PAGE):
-        at = slice(start, start + PAGE)
-        slot = lax.rem(table[first_page + start // PAGE] - shards[0] + count, count)
-        out = streams[start // size]
-        to = slice(start % size, start % size + PAGE)
+    for out, start in ((first, 0), (second, half)):
+        at = slice(start, start + half)
         for head in range(kv_width // HD):
             cols = slice(head * HD, head * HD + HD)
-            turned_keys = rope(keys[at, cols], cos[at, :], sin[at, :]).astype(jnp.bfloat16)
-            out[to, cols] = turned_keys
-            pages[slot, :, cols] = turned_keys
-        rounded = values[at].astype(jnp.bfloat16)
-        out[to, kv_width:] = rounded
-        pages[slot, :, kv_width:] = rounded
-
-
-def project_kv(shards, table, pieces, gain, wk, wv, cos, sin, size, first_page=0, pages=None):
+            out[:, cols] = rope(keys[at, cols], cos[at, :], sin[at, :]).astype(jnp.bfloat16)
+        out[:, kv_width:] = values[at].astype(jnp.bfloat16)
+        for page in range(half // PAGE):
+            slot = lax.rem(table[start // PAGE + page] - shards[0] + count, count)
+            pages[slot, :, :] = out[page * PAGE : page * PAGE + PAGE, :]
+
+
+def project_kv(shards, table, pieces, square, gain, wk, wv, cos, sin):
     features = wk.shape[0]
     rows = cos.shape[0]
     width = 2 * wk.shape[1]
-    segments = tuple(where for _, where in pieces)
-    arrays = []
-    for array, _ in pieces:
-        arrays.append(array)
-    carried = pages is not None
-    operands = [shards, table, *arrays, gain, wk, wv, cos, sin] + ([pages] if carried else [])
-    stream = jax.ShapeDtypeStruct((size, width), jnp.bfloat16)
-    paged = jax.ShapeDtypeStruct((table.shape[0], PAGE, width), jnp.bfloat16)
-    out_shape = (jax.ShapeDtypeStruct((rows, features), jnp.bfloat16), paged)
-    out_shape = out_shape + (stream,) * (rows // size)
-    specs = [whole(SMEM)] * 2 + [whole()] * (len(operands) - 2)
-    return pl.pallas_call(
-        functools.partial(kv_kernel, (segments, first_page, carried, shards.shape[0])),
+    out_shape = tuple(
+        jax.ShapeDtypeStruct(shape, jnp.bfloat16)
+        for shape in ((rows, features), (rows // 2, width), (rows // 2, width))
+    )
+    paged = jax.ShapeDtypeStruct((rows // PAGE, PAGE, width), jnp.bfloat16)
+    return pl.pallas_call(
+        kv_kernel,
         name="norm_project_kv",
-        out_shape=out_shape,
-        in_specs=specs,
-        out_specs=(whole(),) * len(out_shape),
-        input_output_aliases={len(operands) - 1: 1} if carried else {},
+        out_shape=(*out_shape, paged),
+        in_specs=[whole(SMEM)] * 2 + [whole()] * 11,
+        out_specs=(whole(),) * 4,
         compiler_params=pltpu.CompilerParams(vmem_limit_bytes=14 << 20),
         cost_estimate=pl.CostEstimate(
             flops=2 * rows * features * width,
             transcendentals=rows,
             bytes_accessed=2 * (2 * rows * features + features * width),
         ),
-    )(*operands)
+    )(shards, table, *pieces, square, gain, wk, wv, cos, sin)
 
 
 def q_kernel(count, *refs):
@@ -252,7 +264,7 @@
         input_output_aliases=aliases,
         compiler_params=pltpu.CompilerParams(vmem_limit_bytes=8 << 20),
         cost_estimate=pl.CostEstimate(
-            flops=10000000 * keys,
+            flops=5000000 * keys,
             transcendentals=0,
             bytes_accessed=width * keys,
         ),
@@ -352,7 +364,8 @@
     backs = [jnp.int32(2 * step) for step in range(steps + 1)]
     backs += [2 * step - 1 + 2 * core for step in range(steps + 1)]
     firsts = jnp.stack(backs) * -tokens + first_token
-    meta = jnp.concatenate([first_token.reshape(1), firsts])
+    meta = jnp.concatenate([first_token.reshape(1), firsts, firsts + half])
+    later = 2 * (steps + 1)
 
     freqs = 10000.0 ** (-(jnp.arange(HD // 2, dtype=jnp.float32) * (2.0 / HD)))
     angles = (query_index - starts).astype(jnp.float32) * jnp.concatenate([freqs, freqs])[None, :]
@@ -361,28 +374,39 @@
     sin = jnp.sin(angles) * sign[None, :]
     gain = norm_gain.reshape(1, -1)
 
-    normed, pages, stream = project_kv(
-        shards, table, pieces, gain, w_key, w_value, cos, sin, tokens
+    arrays = [array for array, _ in pieces]
+    square = squares(*arrays[:3])
+    normed, a0, b0, pages = project_kv(
+        shards, table, arrays, square, gain, w_key, w_value, cos, sin
     )
+
+    def chain(name, block):
+        arrived, crossed = [block], []
+        for step in range(steps + 1):
+            if step:
+                with jax.named_scope(f"hop_{name}{step}"):
+                    arrived.append(shifted(arrived[-1], "seq", 2))
+            with jax.named_scope(f"cross_{name}{step}"):
+                crossed.append(swapped(arrived[-1]))
+        return arrived, crossed
+
+    a, ca = chain("a", a0)
+    b, cb = chain("b", b0)
     look = functools.partial(attend, meta, low)
-    arrived = [stream]
-    crossed = []
-    for step in range(steps + 1):
-        if step:
-            with jax.named_scope(f"hop_{step}"):
-                arrived.append(shifted(arrived[-1], "seq", 2))
-        with jax.named_scope(f"cross_{step}"):
-            crossed.append(swapped(arrived[-1]))
     straight = [1 + step for step in range(steps + 1)]
     over = [2 + steps + step for step in range(steps + 1)]
     queries = project_q((normed,), w_query, cos, sin)
-    state = look(queries, [(arrived[0], straight[0], 0)])
-    state = look(queries, [(crossed[0], over[0], None)], state, guarded=True)
+    state = look(queries, [(a[0], straight[0], 0), (b[0], straight[0] + later, half)])
+    edge = [(ca[0], over[0], None), (cb[0], over[0] + later, None)]
+    state = look(queries, edge, state, guarded=True)
     for step in range(1, steps):
-        state = look(queries, [(arrived[step], straight[step], None)], state)
-        state = look(queries, [(crossed[step], over[step], None)], state)
-    state = look(queries, [(arrived[steps], straight[steps], None)], state)
-    edge = [(crossed[steps], over[steps], None)]
+        near, far = straight[step], over[step]
+        first = [(a[step], near, None), (ca[step], far, None)]
+        second = [(b[step], near + later, None), (cb[step], far + later, None)]
+        state = look(queries, first + second, state)
+    near, far = straight[steps], over[steps]
+    state = look(queries, [(a[steps], near, None), (b[steps], near + later, None)], state)
+    edge = [(ca[steps], far, None), (cb[steps], far + later, None)]
     attended = look(queries, edge, state, last=True, guarded=True)
     kv_cache = exchange_pages(shards, pages)
     return (attended, kv_cache)

time: 135 us -> 127 us (0.941)
  waiting for transfers between devices: 62.1 us -> 37.4 us
  starting transfers between devices: 36.3 us -> 54.4 us
  Pallas kernels: 31.2 us -> 29.2 us
    ppermute x8 -> x12, waiting for transfers between devices: 48.9 us -> 23 us  [shifted(): return lax.ppermute(block, axis, route)]
    ppermute x8 -> x12, starting transfers between devices: 24 us -> 40.7 us  [shifted(): return lax.ppermute(block, axis, route)]
    pallas_call x10 -> x7, Pallas kernels: 20.2 us -> 18 us  [attend(): pl.pallas_call(functools.partial(attend_kernel, places, first, last, guar...]
    ppermute x5 -> x10, starting transfers between devices: 0.1 us -> 1.54 us  [swapped(): lax.ppermute(block, 'seq', [(i, i ^ 1) for i in range(lax.axis_size('seq'...]
    pallas_call x1 -> x2, Pallas kernels: 5.87 us -> 6.07 us  [the longest x1 5.27 us: project_kv(): pl.pallas_call(kv_kernel, name='norm_project_kv', out_shape=(*out_shape,...]
  transfers between devices with their start and end apart: 20 -> 29, of which waited for: 10 -> 12; matrix products, arithmetic and copies ran while one was open for 3% -> 3% of each run, Pallas kernels for 16% -> 16%
where the time goes in v2:
time: 127 us; the launch traced here: 126 us
  starting transfers between devices  54.4 us (43%)
  waiting for transfers between devices  37.4 us (29%)
  Pallas kernels  29.2 us (23%)
  other arithmetic  3.15 us (2%)
    ppermute x12, starting transfers between devices, shifted(): return lax.ppermute(block, axis, route)  40.7 us
    ppermute x12, waiting for transfers between devices, shifted(): return lax.ppermute(block, axis, route)  23 us
    pallas_call x7, Pallas kernels, attend(): pl.pallas_call(functools.partial(attend_kernel, places, first, last, guar...  18 us
    ppermute x7, waiting for transfers between devices, turned(): lax.ppermute(block, axis, [(i, (i + distance) % count) for i in range(cou...  14.3 us
    ppermute x7, starting transfers between devices, turned(): lax.ppermute(block, axis, [(i, (i + distance) % count) for i in range(cou...  12.2 us
    pallas_call x1, Pallas kernels, project_kv(): pl.pallas_call(kv_kernel, name='norm_project_kv', out_shape=(*out_shape,...  5.27 us
    pallas_call x1, Pallas kernels, project_q(): pl.pallas_call(functools.partial(q_kernel, len(normed)), name='project_q'...  2.81 us
  transfers between devices with their start and end apart: 29, of which 12 were waited for; matrix products, arithmetic and copies ran while one was open for 3% of the time, Pallas kernels for 16%

profile of v2, /device:TPU:6, one launch (start us, length us, event | category | flops | bytes accessed | tf_op | source)
XLA Modules:
  0.0 126.2 jit_solution(11560120670011343778)
XLA Ops:
  0.6 1.7 %collective-permute-start.4 = (bf16[512,1152]{1,0:T(8,128)(2,1)}, bf16[512,1152]{1,0:T(8,128)(2,1)S(1)}, u32[]{:S(2)}, u32[]{:S(2)}) collective-permute-start(bf16[512,1152]{1,0:T(8,128)(2,1)} %refs_0_.1), channel_id=1, source_target_pairs={{0,1},{1,2},{2,3},{3,0},{4,5},{5,6},{6,7},{7,4},{8,9},{9,10},{10,1... | collective-permute-start | bytes 3538952 | tf_op jit(solution)/shard_map/ppermute | solution.py:37
  2.3 1.7 %collective-permute-start.5 = (bf16[512,1152]{1,0:T(8,128)(2,1)}, bf16[512,1152]{1,0:T(8,128)(2,1)S(1)}, u32[]{:S(2)}, u32[]{:S(2)}) collective-permute-start(bf16[512,1152]{1,0:T(8,128)(2,1)} %refs_0_.1), channel_id=1, source_target_pairs={{0,3},{1,0},{2,1},{3,2},{4,7},{5,4},{6,5},{7,6},{8,11},{9,8},{10,9... | collective-permute-start | bytes 3538952 | tf_op jit(solution)/shard_map/ppermute | solution.py:37
  3.9 0.7 broadcast_add_fusion
  4.6 1.9 %collective-permute-start = (s32[1,512]{1,0:T(1,128)S(1)}, s32[1,512]{1,0:T(1,128)S(1)}, u32[]{:S(2)}, u32[]{:S(2)}) collective-permute-start(s32[1,512]{1,0:T(1,128)S(1)} %bitcast.22), channel_id=1, source_target_pairs={{0,4},{4,8},{8,12},{12,16},{16,20},{20,24},{24,28},{28,32},{32,36}... | collective-permute-start | bytes 6152 | tf_op jit(solution)/shard_map/ppermute | solution.py:32
  6.5 3.8 %collective-permute-start.1 = (s32[1,512]{1,0:T(1,128)S(1)}, s32[1,512]{1,0:T(1,128)S(1)}, u32[]{:S(2)}, u32[]{:S(2)}) collective-permute-start(s32[1,512]{1,0:T(1,128)S(1)} %bitcast.23), channel_id=1, source_target_pairs={{0,8},{4,12},{8,16},{12,20},{16,24},{20,28},{24,32},{28,36},{32,40... | collective-permute-start | bytes 6152 | tf_op jit(solution)/shard_map/ppermute | solution.py:32
  10.6 0.3 convert_reduce_fusion.1
  10.9 2.1 %collective-permute-done = s32[1,512]{1,0:T(1,128)S(1)} collective-permute-done((s32[1,512]{1,0:T(1,128)S(1)}, s32[1,512]{1,0:T(1,128)S(1)}, u32[]{:S(2)}, u32[]{:S(2)}) %collective-permute-start) | collective-permute-done | bytes 2080 | tf_op jit(solution)/shard_map/ppermute | solution.py:32
  12.9 3.2 %collective-permute-done.1 = s32[1,512]{1,0:T(1,128)S(1)} collective-permute-done((s32[1,512]{1,0:T(1,128)S(1)}, s32[1,512]{1,0:T(1,128)S(1)}, u32[]{:S(2)}, u32[]{:S(2)}) %collective-permute-start.1) | collective-permute-done | bytes 2080 | tf_op jit(solution)/shard_map/ppermute | solution.py:32
  16.1 1.9 %collective-permute-start.2 = (s32[3,512]{1,0:T(4,128)S(1)}, s32[3,512]{1,0:T(4,128)S(1)}, u32[]{:S(2)}, u32[]{:S(2)}) collective-permute-start(s32[3,512]{1,0:T(4,128)S(1)} %pad_add_fusion), channel_id=1, source_target_pairs={{0,12},{4,16},{8,20},{12,24},{16,28},{20,32},{24,36},{28,40},{32,4... | collective-permute-start | bytes 18440 | tf_op jit(solution)/shard_map/ppermute | solution.py:32
  18.1 6.6 %collective-permute-start.3 = (s32[3,512]{1,0:T(4,128)S(1)}, s32[3,512]{1,0:T(4,128)S(1)}, u32[]{:S(2)}, u32[]{:S(2)}) collective-permute-start(s32[3,512]{1,0:T(4,128)S(1)} %pad_add_fusion), channel_id=1, source_target_pairs={{0,24},{4,28},{8,32},{12,36},{16,40},{20,44},{24,48},{28,52},{32,5... | collective-permute-start | bytes 18440 | tf_op jit(solution)/shard_map/ppermute | solution.py:32
  24.8 0.7 reshape.48.refs_6_
  25.5 2.0 %collective-permute-done.3 = s32[3,512]{1,0:T(4,128)S(1)} collective-permute-done((s32[3,512]{1,0:T(4,128)S(1)}, s32[3,512]{1,0:T(4,128)S(1)}, u32[]{:S(2)}, u32[]{:S(2)}) %collective-permute-start.3) | collective-permute-done | bytes 6176 | tf_op jit(solution)/shard_map/ppermute | solution.py:32
  27.6 2.3 %collective-permute-done.4.left.refs_1_ = bf16[512,1152]{1,0:T(8,128)(2,1)S(1)} collective-permute-done((bf16[512,1152]{1,0:T(8,128)(2,1)}, bf16[512,1152]{1,0:T(8,128)(2,1)S(1)}, u32[]{:S(2)}, u32[]{:S(2)}) %collective-permute-start.4) | collective-permute-done | bytes 1179680 | tf_op jit(solution)/shard_map/ppermute | solution.py:37
  30.0 1.7 %collective-permute-start.6 = (bf16[256,1152]{1,0:T(8,128)(2,1)S(1)}, bf16[256,1152]{1,0:T(8,128)(2,1)S(1)}, u32[]{:S(2)}, u32[]{:S(2)}) collective-permute-start(bf16[256,1152]{1,0:T(8,128)(2,1)S(1)} %get-tuple-element.20), channel_id=1, source_target_pairs={{0,1},{1,2},{2,3},{3,0},{4,5},{5,6},{6,7},{7,4},{8,9},{9,10},{10,1... | collective-permute-start | bytes 1769480 | tf_op jit(solution)/shard_map/ppermute | solution.py:37
  31.7 1.7 %collective-permute-start.7 = (bf16[256,1152]{1,0:T(8,128)(2,1)S(1)}, bf16[256,1152]{1,0:T(8,128)(2,1)S(1)}, u32[]{:S(2)}, u32[]{:S(2)}) collective-permute-start(bf16[256,1152]{1,0:T(8,128)(2,1)S(1)} %get-tuple-element.21), channel_id=1, source_target_pairs={{0,3},{1,0},{2,1},{3,2},{4,7},{5,4},{6,5},{7,6},{8,11},{9,8},{10,9... | collective-permute-start | bytes 1769480 | tf_op jit(solution)/shard_map/ppermute | solution.py:37
  33.4 1.0 convert_reduce_fusion
  34.4 1.0 fusion
  35.4 0.8 squares.1.refs_5_
  36.2 9.4 %collective-permute-done.6.refs_3_ = bf16[256,1152]{1,0:T(8,128)(2,1)S(1)} collective-permute-done((bf16[256,1152]{1,0:T(8,128)(2,1)S(1)}, bf16[256,1152]{1,0:T(8,128)(2,1)S(1)}, u32[]{:S(2)}, u32[]{:S(2)}) %collective-permute-start.6) | collective-permute-done | bytes 589856 | tf_op jit(solution)/shard_map/ppermute | solution.py:37
  45.6 5.3 %norm_project_kv.1 = (bf16[512,4608]{1,0:T(8,128)(2,1)S(1)}, bf16[256,512]{1,0:T(8,128)(2,1)S(1)}, bf16[256,512]{1,0:T(8,128)(2,1)S(1)}, bf16[4,128,512]{2,1,0:T(8,128)(2,1)S(1)}) custom-call(s32[4]{0:T(128)S(1)} %and_select_fusion.shards, s32[4]{0:T(128)S(1)} %bitcast.19, bf16[512,1152]{1,0:T(8,128)(2,1)S(1)} %copy-done, ...), custom_call_target="tpu_custom_call" | custom-call | flops 2415919104 | bytes 14155776 | tf_op jit(solution)/shard_map/norm_project_kv/pallas_call | solution.py:121
  51.0 3.8 %collective-permute-start.8 = (bf16[256,512]{1,0:T(8,128)(2,1)S(1)}, bf16[256,512]{1,0:T(8,128)(2,1)S(1)}, u32[]{:S(2)}, u32[]{:S(2)}) collective-permute-start(bf16[256,512]{1,0:T(8,128)(2,1)S(1)} %get-tuple-element.23.refs_0_), channel_id=1, source_target_pairs={{0,8},{4,12},{8,16},{12,20},{16,24},{20,28},{24,32},{28,36},{32,40... | collective-permute-start | bytes 786440 | tf_op jit(solution)/shard_map/hop_a1/ppermute | solution.py:32
  54.9 1.1 collective-permute-start.26
  55.9 3.4 %collective-permute-start.27 = (bf16[128,512]{1,0:T(8,128)(2,1)S(1)}, bf16[128,512]{1,0:T(8,128)(2,1)S(1)}, u32[]{:S(2)}, u32[]{:S(2)}) collective-permute-start(bf16[128,512]{1,0:T(8,128)(2,1)S(1)} %get-tuple-element.41), channel_id=1, source_target_pairs={{0,2},{1,3},{2,0},{3,1},{4,6},{5,7},{6,4},{7,5},{8,10},{9,11},{10,... | collective-permute-start | bytes 393224 | tf_op jit(solution)/shard_map/ppermute | solution.py:37
  59.3 4.0 %collective-permute-start.13 = (bf16[256,512]{1,0:T(8,128)(2,1)S(1)}, bf16[256,512]{1,0:T(8,128)(2,1)S(1)}, u32[]{:S(2)}, u32[]{:S(2)}) collective-permute-start(bf16[256,512]{1,0:T(8,128)(2,1)S(1)} %get-tuple-element.24.refs_1_), channel_id=1, source_target_pairs={{0,8},{4,12},{8,16},{12,20},{16,24},{20,28},{24,32},{28,36},{32,40... | collective-permute-start | bytes 786440 | tf_op jit(solution)/shard_map/hop_b1/ppermute | solution.py:32
  63.4 2.8 %project_q.1.q_ref = bf16[512,512]{1,0:T(8,128)(2,1)S(1)} custom-call(bf16[512,4608]{1,0:T(8,128)(2,1)S(1)} %get-tuple-element.22.refs_0_, bf16[4608,512]{1,0:T(8,128)(2,1)S(1)} %bitcast.21, f32[512,128]{1,0:T(8,128)S(1)} %get-tuple-element.47.refs_9_.refs_2_, f32[512,128]{1,0:T(8,128)S(1)} %get-tuple-element.46.refs_10_.refs_3_), custom_call_target="tpu_custom_call" | custom-call | flops 5120000000 | bytes 262144 | tf_op jit(solution)/shard_map/project_q/pallas_call | solution.py:152
  66.3 1.1 collective-permute-start.28
  67.5 1.8 %attend.6 = (f32[512,512]{1,0:T(8,128)S(1)}, f32[512,512]{1,0:T(8,128)S(1)}) custom-call(s32[21]{0:T(128)S(1)} %pad_add_fusion.1.meta, s32[512,128]{1,0:T(8,128)S(1)} %add.84.low_ref, bf16[512,512]{1,0:T(8,128)(2,1)S(1)} %project_q.1.q_ref, bf16[256,512]{1,0:T(8,128)(2,1)S(1)} %get-tuple-element.23.refs_0_, bf16[256,512]{1,0:T(8,128)(2,1)S(1)} %get-tuple-element.24.refs_1_), custom_call_target="tpu_custom_call" | custom-call | flops 2560000000 | bytes 262144 | tf_op jit(solution)/shard_map/attend/pallas_call | solution.py:257
  69.6 2.7 %collective-permute-done.28.refs_3_ = bf16[128,512]{1,0:T(8,128)(2,1)S(1)} collective-permute-done((bf16[128,512]{1,0:T(8,128)(2,1)S(1)}, bf16[128,512]{1,0:T(8,128)(2,1)S(1)}, u32[]{:S(2)}, u32[]{:S(2)}) %collective-permute-start.28) | collective-permute-done | bytes 131104 | tf_op jit(solution)/shard_map/ppermute | solution.py:37
  72.2 3.8 %collective-permute-start.9 = (bf16[256,512]{1,0:T(8,128)(2,1)S(1)}, bf16[256,512]{1,0:T(8,128)(2,1)S(1)}, u32[]{:S(2)}, u32[]{:S(2)}) collective-permute-start(bf16[256,512]{1,0:T(8,128)(2,1)S(1)} %collective-permute-done.8.refs_0_), channel_id=1, source_target_pairs={{0,8},{4,12},{8,16},{12,20},{16,24},{20,28},{24,32},{28,36},{32,40... | collective-permute-start | bytes 786440 | tf_op jit(solution)/shard_map/hop_a2/ppermute | solution.py:32
  76.2 5.0 %collective-permute-start.14 = (bf16[256,512]{1,0:T(8,128)(2,1)S(1)}, bf16[256,512]{1,0:T(8,128)(2,1)S(1)}, u32[]{:S(2)}, u32[]{:S(2)}) collective-permute-start(bf16[256,512]{1,0:T(8,128)(2,1)S(1)} %collective-permute-done.13.refs_2_), channel_id=1, source_target_pairs={{0,8},{4,12},{8,16},{12,20},{16,24},{20,28},{24,32},{28,36},{32,40... | collective-permute-start | bytes 786440 | tf_op jit(solution)/shard_map/hop_b2/ppermute | solution.py:32
  81.2 2.2 %build_cache.1 = bf16[1,128,2,1024]{3,2,1,0:T(2,128)(2,1)} custom-call(s32[4]{0:T(128)S(1)} %and_select_fusion.shards, bf16[128,512]{1,0:T(8,128)(2,1)S(1)} %get-tuple-element.43.refs_0_, bf16[128,512]{1,0:T(8,128)(2,1)S(1)} %collective-permute-done.26.refs_1_, bf16[128,512]{1,0:T(8,128)(2,1)S(1)} %collective-permute-done.27.refs_2_, ...), custom_call_target="tpu_custom_call" | custom-call | flops 1000000000 | bytes 1000 | tf_op jit(solution)/shard_map/build_cache/pallas_call | solution.py:290
  83.4 0.6 attend.7
  84.0 0.8 collective-permute-done.9.refs_0_
  84.8 1.0 collective-permute-start.20
  85.8 2.9 %collective-permute-start.10 = (bf16[256,512]{1,0:T(8,128)(2,1)S(1)}, bf16[256,512]{1,0:T(8,128)(2,1)S(1)}, u32[]{:S(2)}, u32[]{:S(2)}) collective-permute-start(bf16[256,512]{1,0:T(8,128)(2,1)S(1)} %collective-permute-done.9.refs_0_), channel_id=1, source_target_pairs={{0,8},{4,12},{8,16},{12,20},{16,24},{20,28},{24,32},{28,36},{32,40... | collective-permute-start | bytes 786440 | tf_op jit(solution)/shard_map/hop_a3/ppermute | solution.py:32
  88.7 0.9 collective-permute-done.14.refs_2_
  89.7 2.8 %collective-permute-start.15 = (bf16[256,512]{1,0:T(8,128)(2,1)S(1)}, bf16[256,512]{1,0:T(8,128)(2,1)S(1)}, u32[]{:S(2)}, u32[]{:S(2)}) collective-permute-start(bf16[256,512]{1,0:T(8,128)(2,1)S(1)} %collective-permute-done.14.refs_2_), channel_id=1, source_target_pairs={{0,8},{4,12},{8,16},{12,20},{16,24},{20,28},{24,32},{28,36},{32,40... | collective-permute-start | bytes 786440 | tf_op jit(solution)/shard_map/hop_b3/ppermute | solution.py:32
  92.5 3.4 %attend.8 = (f32[512,512]{1,0:T(8,128)S(1)}, f32[512,512]{1,0:T(8,128)S(1)}) custom-call(s32[21]{0:T(128)S(1)} %pad_add_fusion.1.meta, s32[512,128]{1,0:T(8,128)S(1)} %add.84.low_ref, bf16[512,512]{1,0:T(8,128)(2,1)S(1)} %project_q.1.q_ref, bf16[256,512]{1,0:T(8,128)(2,1)S(1)} %collective-permute-done.8.refs_0_, ...), custom_call_target="tpu_custom_call", output_to_operand_aliasing={{0}: (7, {}), {1}: (8, {})} | custom-call | flops 5120000000 | bytes 524288 | tf_op jit(solution)/shard_map/attend/pallas_call | solution.py:257
  95.9 3.1 %collective-permute-done.10.refs_0_ = bf16[256,512]{1,0:T(8,128)(2,1)S(1)} collective-permute-done((bf16[256,512]{1,0:T(8,128)(2,1)S(1)}, bf16[256,512]{1,0:T(8,128)(2,1)S(1)}, u32[]{:S(2)}, u32[]{:S(2)}) %collective-permute-start.10) | collective-permute-done | bytes 262176 | tf_op jit(solution)/shard_map/hop_a3/ppermute | solution.py:32
  99.0 2.1 %collective-permute-start.11 = (bf16[256,512]{1,0:T(8,128)(2,1)S(1)}, bf16[256,512]{1,0:T(8,128)(2,1)S(1)}, u32[]{:S(2)}, u32[]{:S(2)}) collective-permute-start(bf16[256,512]{1,0:T(8,128)(2,1)S(1)} %collective-permute-done.10.refs_0_), channel_id=1, source_target_pairs={{0,8},{4,12},{8,16},{12,20},{16,24},{20,28},{24,32},{28,36},{32,40... | collective-permute-start | bytes 786440 | tf_op jit(solution)/shard_map/hop_a4/ppermute | solution.py:32
  101.1 2.5 %collective-permute-done.15.refs_2_ = bf16[256,512]{1,0:T(8,128)(2,1)S(1)} collective-permute-done((bf16[256,512]{1,0:T(8,128)(2,1)S(1)}, bf16[256,512]{1,0:T(8,128)(2,1)S(1)}, u32[]{:S(2)}, u32[]{:S(2)}) %collective-permute-start.15) | collective-permute-done | bytes 262176 | tf_op jit(solution)/shard_map/hop_b3/ppermute | solution.py:32
  103.7 1.9 %collective-permute-start.16 = (bf16[256,512]{1,0:T(8,128)(2,1)S(1)}, bf16[256,512]{1,0:T(8,128)(2,1)S(1)}, u32[]{:S(2)}, u32[]{:S(2)}) collective-permute-start(bf16[256,512]{1,0:T(8,128)(2,1)S(1)} %collective-permute-done.15.refs_2_), channel_id=1, source_target_pairs={{0,8},{4,12},{8,16},{12,20},{16,24},{20,28},{24,32},{28,36},{32,40... | collective-permute-start | bytes 786440 | tf_op jit(solution)/shard_map/hop_b4/ppermute | solution.py:32
  105.6 3.4 %attend.9 = (f32[512,512]{1,0:T(8,128)S(1)}, f32[512,512]{1,0:T(8,128)S(1)}) custom-call(s32[21]{0:T(128)S(1)} %pad_add_fusion.1.meta, s32[512,128]{1,0:T(8,128)S(1)} %add.84.low_ref, bf16[512,512]{1,0:T(8,128)(2,1)S(1)} %project_q.1.q_ref, bf16[256,512]{1,0:T(8,128)(2,1)S(1)} %collective-permute-done.9.refs_0_, ...), custom_call_target="tpu_custom_call", output_to_operand_aliasing={{0}: (7, {}), {1}: (8, {})} | custom-call | flops 5120000000 | bytes 524288 | tf_op jit(solution)/shard_map/attend/pallas_call | solution.py:257
  109.0 3.1 %collective-permute-done.11.refs_0_ = bf16[256,512]{1,0:T(8,128)(2,1)S(1)} collective-permute-done((bf16[256,512]{1,0:T(8,128)(2,1)S(1)}, bf16[256,512]{1,0:T(8,128)(2,1)S(1)}, u32[]{:S(2)}, u32[]{:S(2)}) %collective-permute-start.11) | collective-permute-done | bytes 262176 | tf_op jit(solution)/shard_map/hop_a4/ppermute | solution.py:32
  112.1 5.2 %collective-permute-done.16.refs_1_ = bf16[256,512]{1,0:T(8,128)(2,1)S(1)} collective-permute-done((bf16[256,512]{1,0:T(8,128)(2,1)S(1)}, bf16[256,512]{1,0:T(8,128)(2,1)S(1)}, u32[]{:S(2)}, u32[]{:S(2)}) %collective-permute-start.16) | collective-permute-done | bytes 262176 | tf_op jit(solution)/shard_map/hop_b4/ppermute | solution.py:32
  117.3 3.4 %attend.10 = (f32[512,512]{1,0:T(8,128)S(1)}, f32[512,512]{1,0:T(8,128)S(1)}) custom-call(s32[21]{0:T(128)S(1)} %pad_add_fusion.1.meta, s32[512,128]{1,0:T(8,128)S(1)} %add.84.low_ref, bf16[512,512]{1,0:T(8,128)(2,1)S(1)} %project_q.1.q_ref, bf16[256,512]{1,0:T(8,128)(2,1)S(1)} %collective-permute-done.10.refs_0_, ...), custom_call_target="tpu_custom_call", output_to_operand_aliasing={{0}: (7, {}), {1}: (8, {})} | custom-call | flops 5120000000 | bytes 524288 | tf_op jit(solution)/shard_map/attend/pallas_call | solution.py:257
  120.7 2.1 %attend.11 = (f32[512,512]{1,0:T(8,128)S(1)}, f32[512,512]{1,0:T(8,128)S(1)}) custom-call(s32[21]{0:T(128)S(1)} %pad_add_fusion.1.meta, s32[512,128]{1,0:T(8,128)S(1)} %add.84.low_ref, bf16[512,512]{1,0:T(8,128)(2,1)S(1)} %project_q.1.q_ref, bf16[256,512]{1,0:T(8,128)(2,1)S(1)} %collective-permute-done.11.refs_0_, ...), custom_call_target="tpu_custom_call", output_to_operand_aliasing={{0}: (5, {}), {1}: (6, {})} | custom-call | flops 2560000000 | bytes 262144 | tf_op jit(solution)/shard_map/attend/pallas_call | solution.py:257
  122.9 3.4 %attend_last.1 = bf16[512,512]{1,0:T(8,128)(2,1)} custom-call(s32[21]{0:T(128)S(1)} %pad_add_fusion.1.meta, s32[512,128]{1,0:T(8,128)S(1)} %add.84.low_ref, bf16[512,512]{1,0:T(8,128)(2,1)S(1)} %project_q.1.q_ref, bf16[256,512]{1,0:T(8,128)(2,1)S(1)} %collective-permute-done.12.refs_0_, bf16[256,512]{1,0:T(8,128)(2,1)S(1)} %collective-permute-done.17.refs_1_, ...), custom_call_target="tpu_custom_call" | custom-call | flops 2560000000 | bytes 262144 | tf_op jit(solution)/shard_map/attend_last/pallas_call | solution.py:257
  (54 shorter events, 1.2 us)
Async XLA Ops:
  0.6 29.3 %collective-permute-start.4 = (bf16[512,1152]{1,0:T(8,128)(2,1)}, bf16[512,1152]{1,0:T(8,128)(2,1)S(1)}, u32[]{:S(2)}, u32[]{:S(2)}) collective-permute-start(bf16[512,1152]{1,0:T(8,128)(2,1)} %refs_0_.1), channel_id=1, source_target_pairs={{0,1},{1,2},{2,3},{3,0},{4,5},{5,6},{6,7},{7,4},{8,9},{9,10},{10,1... | collective-permute-start | bytes 3538952 | tf_op jit(solution)/shard_map/ppermute | solution.py:37
  2.3 27.6 %collective-permute-start.5 = (bf16[512,1152]{1,0:T(8,128)(2,1)}, bf16[512,1152]{1,0:T(8,128)(2,1)S(1)}, u32[]{:S(2)}, u32[]{:S(2)}) collective-permute-start(bf16[512,1152]{1,0:T(8,128)(2,1)} %refs_0_.1), channel_id=1, source_target_pairs={{0,3},{1,0},{2,1},{3,2},{4,7},{5,4},{6,5},{7,6},{8,11},{9,8},{10,9... | collective-permute-start | bytes 3538952 | tf_op jit(solution)/shard_map/ppermute | solution.py:37
  4.6 8.3 %collective-permute-start = (s32[1,512]{1,0:T(1,128)S(1)}, s32[1,512]{1,0:T(1,128)S(1)}, u32[]{:S(2)}, u32[]{:S(2)}) collective-permute-start(s32[1,512]{1,0:T(1,128)S(1)} %bitcast.22), channel_id=1, source_target_pairs={{0,4},{4,8},{8,12},{12,16},{16,20},{20,24},{24,28},{28,32},{32,36}... | collective-permute-start | bytes 6152 | tf_op jit(solution)/shard_map/ppermute | solution.py:32
  6.5 9.6 %collective-permute-start.1 = (s32[1,512]{1,0:T(1,128)S(1)}, s32[1,512]{1,0:T(1,128)S(1)}, u32[]{:S(2)}, u32[]{:S(2)}) collective-permute-start(s32[1,512]{1,0:T(1,128)S(1)} %bitcast.23), channel_id=1, source_target_pairs={{0,8},{4,12},{8,16},{12,20},{16,24},{20,28},{24,32},{28,36},{32,40... | collective-permute-start | bytes 6152 | tf_op jit(solution)/shard_map/ppermute | solution.py:32
  16.1 9.4 %collective-permute-start.2 = (s32[3,512]{1,0:T(4,128)S(1)}, s32[3,512]{1,0:T(4,128)S(1)}, u32[]{:S(2)}, u32[]{:S(2)}) collective-permute-start(s32[3,512]{1,0:T(4,128)S(1)} %pad_add_fusion), channel_id=1, source_target_pairs={{0,12},{4,16},{8,20},{12,24},{16,28},{20,32},{24,36},{28,40},{32,4... | collective-permute-start | bytes 18440 | tf_op jit(solution)/shard_map/ppermute | solution.py:32
  18.1 9.5 %collective-permute-start.3 = (s32[3,512]{1,0:T(4,128)S(1)}, s32[3,512]{1,0:T(4,128)S(1)}, u32[]{:S(2)}, u32[]{:S(2)}) collective-permute-start(s32[3,512]{1,0:T(4,128)S(1)} %pad_add_fusion), channel_id=1, source_target_pairs={{0,24},{4,28},{8,32},{12,36},{16,40},{20,44},{24,48},{28,52},{32,5... | collective-permute-start | bytes 18440 | tf_op jit(solution)/shard_map/ppermute | solution.py:32
  27.6 6.8 %copy-start.4 = (f32[128]{0:T(128)S(1)}, f32[128]{0:T(128)}, u32[]{:S(2)}) copy-start(f32[128]{0:T(128)} %constant.74) | copy-start | bytes 1540
  27.6 7.8 %copy-start = (bf16[512,1152]{1,0:T(8,128)(2,1)S(1)}, bf16[512,1152]{1,0:T(8,128)(2,1)}, u32[]{:S(2)}) copy-start(bf16[512,1152]{1,0:T(8,128)(2,1)} %refs_0_.1) | copy-start | bytes 3538948
  29.9 15.7 %copy-start.2 = (bf16[4608,256]{1,0:T(8,128)(2,1)S(1)}, bf16[4608,256]{1,0:T(8,128)(2,1)}, u32[]{:S(2)}) copy-start(bf16[4608,256]{1,0:T(8,128)(2,1)} %refs_8_.1) | copy-start | bytes 7077892
  30.0 15.6 %copy-start.1 = (bf16[4608,256]{1,0:T(8,128)(2,1)S(1)}, bf16[4608,256]{1,0:T(8,128)(2,1)}, u32[]{:S(2)}) copy-start(bf16[4608,256]{1,0:T(8,128)(2,1)} %refs_7_.1) | copy-start | bytes 7077892
  30.0 15.6 %copy-start.3 = (s32[1,4]{1,0:T(1,128)S(1)}, s32[1,4]{1,0:T(1,128)}, u32[]{:S(2)}) copy-start(s32[1,4]{1,0:T(1,128)} %param.14) | copy-start | bytes 52
  30.0 15.5 %collective-permute-start.6 = (bf16[256,1152]{1,0:T(8,128)(2,1)S(1)}, bf16[256,1152]{1,0:T(8,128)(2,1)S(1)}, u32[]{:S(2)}, u32[]{:S(2)}) collective-permute-start(bf16[256,1152]{1,0:T(8,128)(2,1)S(1)} %get-tuple-element.20), channel_id=1, source_target_pairs={{0,1},{1,2},{2,3},{3,0},{4,5},{5,6},{6,7},{7,4},{8,9},{9,10},{10,1... | collective-permute-start | bytes 1769480 | tf_op jit(solution)/shard_map/ppermute | solution.py:37
  31.7 13.9 %collective-permute-start.7 = (bf16[256,1152]{1,0:T(8,128)(2,1)S(1)}, bf16[256,1152]{1,0:T(8,128)(2,1)S(1)}, u32[]{:S(2)}, u32[]{:S(2)}) collective-permute-start(bf16[256,1152]{1,0:T(8,128)(2,1)S(1)} %get-tuple-element.21), channel_id=1, source_target_pairs={{0,3},{1,0},{2,1},{3,2},{4,7},{5,4},{6,5},{7,6},{8,11},{9,8},{10,9... | collective-permute-start | bytes 1769480 | tf_op jit(solution)/shard_map/ppermute | solution.py:37
  35.4 28.0 %slice-start = ((s8[4718592]{0:T(1024)(128)(4,1)}), s8[4194304]{0:T(1024)(128)(4,1)S(1)}, s32[]{:S(2)}) async-start(s8[4718592]{0:T(1024)(128)(4,1)} %bitcast.20), calls=%async_computation | async-start | bytes 8388608
  45.6 17.8 %slice-start.1 = ((s8[4718592]{0:T(1024)(128)(4,1)}), s8[524288]{0:T(1024)(128)(4,1)S(1)}, s32[]{:S(2)}) async-start(s8[4718592]{0:T(1024)(128)(4,1)} %bitcast.20), calls=%async_computation.1 | async-start | bytes 1048576
  50.9 25.3 %collective-permute-start.24 = (bf16[256,512]{1,0:T(8,128)(2,1)S(1)}, bf16[256,512]{1,0:T(8,128)(2,1)S(1)}, u32[]{:S(2)}, u32[]{:S(2)}) collective-permute-start(bf16[256,512]{1,0:T(8,128)(2,1)S(1)} %get-tuple-element.23.refs_0_), channel_id=1, source_target_pairs={{0,4},{4,0},{8,12},{12,8},{16,20},{20,16},{24,28},{28,24},{32,36},... | collective-permute-start | bytes 786440 | tf_op jit(solution)/shard_map/cross_a0/ppermute | solution.py:41
  51.0 18.3 %collective-permute-start.8 = (bf16[256,512]{1,0:T(8,128)(2,1)S(1)}, bf16[256,512]{1,0:T(8,128)(2,1)S(1)}, u32[]{:S(2)}, u32[]{:S(2)}) collective-permute-start(bf16[256,512]{1,0:T(8,128)(2,1)S(1)} %get-tuple-element.23.refs_0_), channel_id=1, source_target_pairs={{0,8},{4,12},{8,16},{12,20},{16,24},{20,28},{24,32},{28,36},{32,40... | collective-permute-start | bytes 786440 | tf_op jit(solution)/shard_map/hop_a1/ppermute | solution.py:32
  54.9 11.3 %collective-permute-start.26 = (bf16[128,512]{1,0:T(8,128)(2,1)S(1)}, bf16[128,512]{1,0:T(8,128)(2,1)S(1)}, u32[]{:S(2)}, u32[]{:S(2)}) collective-permute-start(bf16[128,512]{1,0:T(8,128)(2,1)S(1)} %get-tuple-element.42), channel_id=1, source_target_pairs={{0,1},{1,2},{2,3},{3,0},{4,5},{5,6},{6,7},{7,4},{8,9},{9,10},{10,1... | collective-permute-start | bytes 393224 | tf_op jit(solution)/shard_map/ppermute | solution.py:37
  55.9 10.4 %collective-permute-start.27 = (bf16[128,512]{1,0:T(8,128)(2,1)S(1)}, bf16[128,512]{1,0:T(8,128)(2,1)S(1)}, u32[]{:S(2)}, u32[]{:S(2)}) collective-permute-start(bf16[128,512]{1,0:T(8,128)(2,1)S(1)} %get-tuple-element.41), channel_id=1, source_target_pairs={{0,2},{1,3},{2,0},{3,1},{4,6},{5,7},{6,4},{7,5},{8,10},{9,11},{10,... | collective-permute-start | bytes 393224 | tf_op jit(solution)/shard_map/ppermute | solution.py:37
  59.3 16.7 %collective-permute-start.13 = (bf16[256,512]{1,0:T(8,128)(2,1)S(1)}, bf16[256,512]{1,0:T(8,128)(2,1)S(1)}, u32[]{:S(2)}, u32[]{:S(2)}) collective-permute-start(bf16[256,512]{1,0:T(8,128)(2,1)S(1)} %get-tuple-element.24.refs_1_), channel_id=1, source_target_pairs={{0,8},{4,12},{8,16},{12,20},{16,24},{20,28},{24,32},{28,36},{32,40... | collective-permute-start | bytes 786440 | tf_op jit(solution)/shard_map/hop_b1/ppermute | solution.py:32
  66.2 17.2 %collective-permute-start.25 = (bf16[256,512]{1,0:T(8,128)(2,1)S(1)}, bf16[256,512]{1,0:T(8,128)(2,1)S(1)}, u32[]{:S(2)}, u32[]{:S(2)}) collective-permute-start(bf16[256,512]{1,0:T(8,128)(2,1)S(1)} %get-tuple-element.24.refs_1_), channel_id=1, source_target_pairs={{0,4},{4,0},{8,12},{12,8},{16,20},{20,16},{24,28},{28,24},{32,36},... | collective-permute-start | bytes 786440 | tf_op jit(solution)/shard_map/cross_b0/ppermute | solution.py:41
  66.3 5.9 %collective-permute-start.28 = (bf16[128,512]{1,0:T(8,128)(2,1)S(1)}, bf16[128,512]{1,0:T(8,128)(2,1)S(1)}, u32[]{:S(2)}, u32[]{:S(2)}) collective-permute-start(bf16[128,512]{1,0:T(8,128)(2,1)S(1)} %get-tuple-element.40), channel_id=1, source_target_pairs={{0,3},{1,0},{2,1},{3,2},{4,7},{5,4},{6,5},{7,6},{8,11},{9,8},{10,9... | collective-permute-start | bytes 393224 | tf_op jit(solution)/shard_map/ppermute | solution.py:37
  69.3 20.4 %collective-permute-start.22 = (bf16[256,512]{1,0:T(8,128)(2,1)S(1)}, bf16[256,512]{1,0:T(8,128)(2,1)S(1)}, u32[]{:S(2)}, u32[]{:S(2)}) collective-permute-start(bf16[256,512]{1,0:T(8,128)(2,1)S(1)} %collective-permute-done.8.refs_0_), channel_id=1, source_target_pairs={{0,4},{4,0},{8,12},{12,8},{16,20},{20,16},{24,28},{28,24},{32,36},... | collective-permute-start | bytes 786440 | tf_op jit(solution)/shard_map/cross_a1/ppermute | solution.py:41
  72.2 12.6 %collective-permute-start.9 = (bf16[256,512]{1,0:T(8,128)(2,1)S(1)}, bf16[256,512]{1,0:T(8,128)(2,1)S(1)}, u32[]{:S(2)}, u32[]{:S(2)}) collective-permute-start(bf16[256,512]{1,0:T(8,128)(2,1)S(1)} %collective-permute-done.8.refs_0_), channel_id=1, source_target_pairs={{0,8},{4,12},{8,16},{12,20},{16,24},{20,28},{24,32},{28,36},{32,40... | collective-permute-start | bytes 786440 | tf_op jit(solution)/shard_map/hop_a2/ppermute | solution.py:32
  76.0 16.5 %collective-permute-start.23 = (bf16[256,512]{1,0:T(8,128)(2,1)S(1)}, bf16[256,512]{1,0:T(8,128)(2,1)S(1)}, u32[]{:S(2)}, u32[]{:S(2)}) collective-permute-start(bf16[256,512]{1,0:T(8,128)(2,1)S(1)} %collective-permute-done.13.refs_2_), channel_id=1, source_target_pairs={{0,4},{4,0},{8,12},{12,8},{16,20},{20,16},{24,28},{28,24},{32,36},... | collective-permute-start | bytes 786440 | tf_op jit(solution)/shard_map/cross_b1/ppermute | solution.py:41
  76.2 13.5 %collective-permute-start.14 = (bf16[256,512]{1,0:T(8,128)(2,1)S(1)}, bf16[256,512]{1,0:T(8,128)(2,1)S(1)}, u32[]{:S(2)}, u32[]{:S(2)}) collective-permute-start(bf16[256,512]{1,0:T(8,128)(2,1)S(1)} %collective-permute-done.13.refs_2_), channel_id=1, source_target_pairs={{0,8},{4,12},{8,16},{12,20},{16,24},{20,28},{24,32},{28,36},{32,40... | collective-permute-start | bytes 786440 | tf_op jit(solution)/shard_map/hop_b2/ppermute | solution.py:32
  84.8 18.9 %collective-permute-start.20 = (bf16[256,512]{1,0:T(8,128)(2,1)S(1)}, bf16[256,512]{1,0:T(8,128)(2,1)S(1)}, u32[]{:S(2)}, u32[]{:S(2)}) collective-permute-start(bf16[256,512]{1,0:T(8,128)(2,1)S(1)} %collective-permute-done.9.refs_0_), channel_id=1, source_target_pairs={{0,4},{4,0},{8,12},{12,8},{16,20},{20,16},{24,28},{28,24},{32,36},... | collective-permute-start | bytes 786440 | tf_op jit(solution)/shard_map/cross_a2/ppermute | solution.py:41
  85.8 13.2 %collective-permute-start.10 = (bf16[256,512]{1,0:T(8,128)(2,1)S(1)}, bf16[256,512]{1,0:T(8,128)(2,1)S(1)}, u32[]{:S(2)}, u32[]{:S(2)}) collective-permute-start(bf16[256,512]{1,0:T(8,128)(2,1)S(1)} %collective-permute-done.9.refs_0_), channel_id=1, source_target_pairs={{0,8},{4,12},{8,16},{12,20},{16,24},{20,28},{24,32},{28,36},{32,40... | collective-permute-start | bytes 786440 | tf_op jit(solution)/shard_map/hop_a3/ppermute | solution.py:32
  89.7 15.9 %collective-permute-start.21 = (bf16[256,512]{1,0:T(8,128)(2,1)S(1)}, bf16[256,512]{1,0:T(8,128)(2,1)S(1)}, u32[]{:S(2)}, u32[]{:S(2)}) collective-permute-start(bf16[256,512]{1,0:T(8,128)(2,1)S(1)} %collective-permute-done.14.refs_2_), channel_id=1, source_target_pairs={{0,4},{4,0},{8,12},{12,8},{16,20},{20,16},{24,28},{28,24},{32,36},... | collective-permute-start | bytes 786440 | tf_op jit(solution)/shard_map/cross_b2/ppermute | solution.py:41
  89.7 14.0 %collective-permute-start.15 = (bf16[256,512]{1,0:T(8,128)(2,1)S(1)}, bf16[256,512]{1,0:T(8,128)(2,1)S(1)}, u32[]{:S(2)}, u32[]{:S(2)}) collective-permute-start(bf16[256,512]{1,0:T(8,128)(2,1)S(1)} %collective-permute-done.14.refs_2_), channel_id=1, source_target_pairs={{0,8},{4,12},{8,16},{12,20},{16,24},{20,28},{24,32},{28,36},{32,40... | collective-permute-start | bytes 786440 | tf_op jit(solution)/shard_map/hop_b3/ppermute | solution.py:32
  99.0 18.3 %collective-permute-start.18 = (bf16[256,512]{1,0:T(8,128)(2,1)S(1)}, bf16[256,512]{1,0:T(8,128)(2,1)S(1)}, u32[]{:S(2)}, u32[]{:S(2)}) collective-permute-start(bf16[256,512]{1,0:T(8,128)(2,1)S(1)} %collective-permute-done.10.refs_0_), channel_id=1, source_target_pairs={{0,4},{4,0},{8,12},{12,8},{16,20},{20,16},{24,28},{28,24},{32,36},... | collective-permute-start | bytes 786440 | tf_op jit(solution)/shard_map/cross_a3/ppermute | solution.py:41
  99.0 13.1 %collective-permute-start.11 = (bf16[256,512]{1,0:T(8,128)(2,1)S(1)}, bf16[256,512]{1,0:T(8,128)(2,1)S(1)}, u32[]{:S(2)}, u32[]{:S(2)}) collective-permute-start(bf16[256,512]{1,0:T(8,128)(2,1)S(1)} %collective-permute-done.10.refs_0_), channel_id=1, source_target_pairs={{0,8},{4,12},{8,16},{12,20},{16,24},{20,28},{24,32},{28,36},{32,40... | collective-permute-start | bytes 786440 | tf_op jit(solution)/shard_map/hop_a4/ppermute | solution.py:32
  103.7 13.7 %collective-permute-start.19 = (bf16[256,512]{1,0:T(8,128)(2,1)S(1)}, bf16[256,512]{1,0:T(8,128)(2,1)S(1)}, u32[]{:S(2)}, u32[]{:S(2)}) collective-permute-start(bf16[256,512]{1,0:T(8,128)(2,1)S(1)} %collective-permute-done.15.refs_2_), channel_id=1, source_target_pairs={{0,4},{4,0},{8,12},{12,8},{16,20},{20,16},{24,28},{28,24},{32,36},... | collective-permute-start | bytes 786440 | tf_op jit(solution)/shard_map/cross_b3/ppermute | solution.py:41
  103.7 13.6 %collective-permute-start.16 = (bf16[256,512]{1,0:T(8,128)(2,1)S(1)}, bf16[256,512]{1,0:T(8,128)(2,1)S(1)}, u32[]{:S(2)}, u32[]{:S(2)}) collective-permute-start(bf16[256,512]{1,0:T(8,128)(2,1)S(1)} %collective-permute-done.15.refs_2_), channel_id=1, source_target_pairs={{0,8},{4,12},{8,16},{12,20},{16,24},{20,28},{24,32},{28,36},{32,40... | collective-permute-start | bytes 786440 | tf_op jit(solution)/shard_map/hop_b4/ppermute | solution.py:32
  112.1 10.8 %collective-permute-start.12 = (bf16[256,512]{1,0:T(8,128)(2,1)S(1)}, bf16[256,512]{1,0:T(8,128)(2,1)S(1)}, u32[]{:S(2)}, u32[]{:S(2)}) collective-permute-start(bf16[256,512]{1,0:T(8,128)(2,1)S(1)} %collective-permute-done.11.refs_0_), channel_id=1, source_target_pairs={{0,4},{4,0},{8,12},{12,8},{16,20},{20,16},{24,28},{28,24},{32,36},... | collective-permute-start | bytes 786440 | tf_op jit(solution)/shard_map/cross_a4/ppermute | solution.py:41
  117.3 5.5 %collective-permute-start.17 = (bf16[256,512]{1,0:T(8,128)(2,1)S(1)}, bf16[256,512]{1,0:T(8,128)(2,1)S(1)}, u32[]{:S(2)}, u32[]{:S(2)}) collective-permute-start(bf16[256,512]{1,0:T(8,128)(2,1)S(1)} %collective-permute-done.16.refs_1_), channel_id=1, source_target_pairs={{0,4},{4,0},{8,12},{12,8},{16,20},{20,16},{24,28},{28,24},{32,36},... | collective-permute-start | bytes 786440 | tf_op jit(solution)/shard_map/cross_b4/ppermute | solution.py:41

commit v3 on v2

--- a/solution.py
+++ b/solution.py
@@ -77,7 +77,7 @@
 
 def kv_kernel(shards, table, *refs):
     own, left, right, far_a, far_b, square_ref, gain, wk, wv, cos, sin = refs[:11]
-    normed, first, second, pages = refs[11:]
+    normed, block, first, second, pages = refs[11:]
     count = shards.shape[0]
     rows, features = normed.shape
     width = own.shape[1]
@@ -104,6 +104,7 @@
             cols = slice(head * HD, head * HD + HD)
             out[:, cols] = rope(keys[at, cols], cos[at, :], sin[at, :]).astype(jnp.bfloat16)
         out[:, kv_width:] = values[at].astype(jnp.bfloat16)
+        block[at, :] = out[...]
         for page in range(half // PAGE):
             slot = lax.rem(table[start // PAGE + page] - shards[0] + count, count)
             pages[slot, :, :] = out[page * PAGE : page * PAGE + PAGE, :]
@@ -115,7 +116,7 @@
     width = 2 * wk.shape[1]
     out_shape = tuple(
         jax.ShapeDtypeStruct(shape, jnp.bfloat16)
-        for shape in ((rows, features), (rows // 2, width), (rows // 2, width))
+        for shape in ((rows, features), (rows, width), (rows // 2, width), (rows // 2, width))
     )
     paged = jax.ShapeDtypeStruct((rows // PAGE, PAGE, width), jnp.bfloat16)
     return pl.pallas_call(
@@ -123,7 +124,7 @@
         name="norm_project_kv",
         out_shape=(*out_shape, paged),
         in_specs=[whole(SMEM)] * 2 + [whole()] * 11,
-        out_specs=(whole(),) * 4,
+        out_specs=(whole(),) * 5,
         compiler_params=pltpu.CompilerParams(vmem_limit_bytes=14 << 20),
         cost_estimate=pl.CostEstimate(
             flops=2 * rows * features * width,
@@ -376,39 +377,50 @@
 
     arrays = [array for array, _ in pieces]
     square = squares(*arrays[:3])
-    normed, a0, b0, pages = project_kv(
+    normed, block, a0, b0, pages = project_kv(
         shards, table, arrays, square, gain, w_key, w_value, cos, sin
     )
 
+    def after(value, *others):
+        return lax.optimization_barrier((value, *others))[0]
+
     def chain(name, block):
-        arrived, crossed = [block], []
-        for step in range(steps + 1):
-            if step:
-                with jax.named_scope(f"hop_{name}{step}"):
-                    arrived.append(shifted(arrived[-1], "seq", 2))
-            with jax.named_scope(f"cross_{name}{step}"):
-                crossed.append(swapped(arrived[-1]))
-        return arrived, crossed
-
-    a, ca = chain("a", a0)
-    b, cb = chain("b", b0)
+        arrived = [block]
+        for step in range(1, steps + 1):
+            with jax.named_scope(f"hop_{name}{step}"):
+                arrived.append(shifted(arrived[-1], "seq", 2))
+        return arrived
+
+    def cross(name, block):
+        with jax.named_scope(f"cross_{name}"):
+            return swapped(block)
+
+    a = chain("a", a0)
+    b = chain("b", b0)
     look = functools.partial(attend, meta, low)
     straight = [1 + step for step in range(steps + 1)]
     over = [2 + steps + step for step in range(steps + 1)]
     queries = project_q((normed,), w_query, cos, sin)
-    state = look(queries, [(a[0], straight[0], 0), (b[0], straight[0] + later, half)])
-    edge = [(ca[0], over[0], None), (cb[0], over[0] + later, None)]
-    state = look(queries, edge, state, guarded=True)
+    crossed = cross("own", after(block, queries))
+    state = look(queries, [(block, straight[0], 0)])
+    state = look(queries, [(crossed, over[0], None)], state, guarded=True)
     for step in range(1, steps):
         near, far = straight[step], over[step]
-        first = [(a[step], near, None), (ca[step], far, None)]
-        second = [(b[step], near + later, None), (cb[step], far + later, None)]
-        state = look(queries, first + second, state)
+        parts = [
+            (a[step], near, None),
+            (cross(f"a{step}", a[step]), far, None),
+            (b[step], near + later, None),
+            (cross(f"b{step}", b[step]), far + later, None),
+        ]
+        state = look(queries, parts, state)
+    kv_cache = exchange_pages(shards, after(pages, b[2]))
     near, far = straight[steps], over[steps]
+    edge = [
+        (cross(f"a{steps}", a[steps]), far, None),
+        (cross(f"b{steps}", after(b[steps], *state, kv_cache)), far + later, None),
+    ]
     state = look(queries, [(a[steps], near, None), (b[steps], near + later, None)], state)
-    edge = [(ca[steps], far, None), (cb[steps], far + later, None)]
     attended = look(queries, edge, state, last=True, guarded=True)
-    kv_cache = exchange_pages(shards, pages)
     return (attended, kv_cache)
 
 

time: 127 us -> 121 us (0.953)
  starting transfers between devices: 54.4 us -> 48.1 us
    ppermute x12, starting transfers between devices: 40.7 us -> 34.7 us  [shifted(): return lax.ppermute(block, axis, route)]
    ppermute x12, waiting for transfers between devices: 23 us -> 25.2 us  [shifted(): return lax.ppermute(block, axis, route)]
    ppermute x7, waiting for transfers between devices: 14.3 us -> 13 us  [turned(): lax.ppermute(block, axis, [(i, (i + distance) % count) for i in range(cou...]
  transfers between devices with their start and end apart: 29 -> 28, of which waited for: 12 -> 13; matrix products, arithmetic and copies ran while one was open for 3% -> 3% of each run, Pallas kernels for 16% -> 17%
where the time goes in v3:
time: 121 us
  starting transfers between devices  48.1 us (40%)
  waiting for transfers between devices  38.2 us (32%)
  Pallas kernels  29.1 us (24%)
  other arithmetic  3.15 us (3%)
    ppermute x12, starting transfers between devices, shifted(): return lax.ppermute(block, axis, route)  34.7 us
    ppermute x12, waiting for transfers between devices, shifted(): return lax.ppermute(block, axis, route)  25.2 us
    pallas_call x7, Pallas kernels, attend(): pl.pallas_call(functools.partial(attend_kernel, places, first, last, guar...  17.9 us
    ppermute x7, waiting for transfers between devices, turned(): lax.ppermute(block, axis, [(i, (i + distance) % count) for i in range(cou...  13 us
    ppermute x7, starting transfers between devices, turned(): lax.ppermute(block, axis, [(i, (i + distance) % count) for i in range(cou...  12.2 us
    pallas_call x1, Pallas kernels, project_kv(): pl.pallas_call(kv_kernel, name='norm_project_kv', out_shape=(*out_shape,...  5.27 us
    pallas_call x1, Pallas kernels, project_q(): pl.pallas_call(functools.partial(q_kernel, len(normed)), name='project_q'...  2.81 us
  transfers between devices with their start and end apart: 28, of which 13 were waited for; matrix products, arithmetic and copies ran while one was open for 3% of the time, Pallas kernels for 17%

profile of v3, /device:TPU:6, one launch (start us, length us, event | category | flops | bytes accessed | tf_op | source)
XLA Modules:
  0.0 120.7 jit_solution(13011655456813020317)
XLA Ops:
  0.6 1.7 %collective-permute-start.4 = (bf16[512,1152]{1,0:T(8,128)(2,1)}, bf16[512,1152]{1,0:T(8,128)(2,1)S(1)}, u32[]{:S(2)}, u32[]{:S(2)}) collective-permute-start(bf16[512,1152]{1,0:T(8,128)(2,1)} %refs_0_.1), channel_id=1, source_target_pairs={{0,1},{1,2},{2,3},{3,0},{4,5},{5,6},{6,7},{7,4},{8,9},{9,10},{10,1... | collective-permute-start | bytes 3538952 | tf_op jit(solution)/shard_map/ppermute | solution.py:37
  2.3 1.7 %collective-permute-start.5 = (bf16[512,1152]{1,0:T(8,128)(2,1)}, bf16[512,1152]{1,0:T(8,128)(2,1)S(1)}, u32[]{:S(2)}, u32[]{:S(2)}) collective-permute-start(bf16[512,1152]{1,0:T(8,128)(2,1)} %refs_0_.1), channel_id=1, source_target_pairs={{0,3},{1,0},{2,1},{3,2},{4,7},{5,4},{6,5},{7,6},{8,11},{9,8},{10,9... | collective-permute-start | bytes 3538952 | tf_op jit(solution)/shard_map/ppermute | solution.py:37
  3.9 0.7 broadcast_add_fusion
  4.6 1.9 %collective-permute-start = (s32[1,512]{1,0:T(1,128)S(1)}, s32[1,512]{1,0:T(1,128)S(1)}, u32[]{:S(2)}, u32[]{:S(2)}) collective-permute-start(s32[1,512]{1,0:T(1,128)S(1)} %bitcast.22), channel_id=1, source_target_pairs={{0,4},{4,8},{8,12},{12,16},{16,20},{20,24},{24,28},{28,32},{32,36}... | collective-permute-start | bytes 6152 | tf_op jit(solution)/shard_map/ppermute | solution.py:32
  6.5 3.8 %collective-permute-start.1 = (s32[1,512]{1,0:T(1,128)S(1)}, s32[1,512]{1,0:T(1,128)S(1)}, u32[]{:S(2)}, u32[]{:S(2)}) collective-permute-start(s32[1,512]{1,0:T(1,128)S(1)} %bitcast.23), channel_id=1, source_target_pairs={{0,8},{4,12},{8,16},{12,20},{16,24},{20,28},{24,32},{28,36},{32,40... | collective-permute-start | bytes 6152 | tf_op jit(solution)/shard_map/ppermute | solution.py:32
  10.8 2.1 %collective-permute-done = s32[1,512]{1,0:T(1,128)S(1)} collective-permute-done((s32[1,512]{1,0:T(1,128)S(1)}, s32[1,512]{1,0:T(1,128)S(1)}, u32[]{:S(2)}, u32[]{:S(2)}) %collective-permute-start) | collective-permute-done | bytes 2080 | tf_op jit(solution)/shard_map/ppermute | solution.py:32
  12.9 3.2 %collective-permute-done.1 = s32[1,512]{1,0:T(1,128)S(1)} collective-permute-done((s32[1,512]{1,0:T(1,128)S(1)}, s32[1,512]{1,0:T(1,128)S(1)}, u32[]{:S(2)}, u32[]{:S(2)}) %collective-permute-start.1) | collective-permute-done | bytes 2080 | tf_op jit(solution)/shard_map/ppermute | solution.py:32
  16.1 1.9 %collective-permute-start.2 = (s32[3,512]{1,0:T(4,128)S(1)}, s32[3,512]{1,0:T(4,128)S(1)}, u32[]{:S(2)}, u32[]{:S(2)}) collective-permute-start(s32[3,512]{1,0:T(4,128)S(1)} %pad_add_fusion), channel_id=1, source_target_pairs={{0,12},{4,16},{8,20},{12,24},{16,28},{20,32},{24,36},{28,40},{32,4... | collective-permute-start | bytes 18440 | tf_op jit(solution)/shard_map/ppermute | solution.py:32
  18.1 6.6 %collective-permute-start.3 = (s32[3,512]{1,0:T(4,128)S(1)}, s32[3,512]{1,0:T(4,128)S(1)}, u32[]{:S(2)}, u32[]{:S(2)}) collective-permute-start(s32[3,512]{1,0:T(4,128)S(1)} %pad_add_fusion), channel_id=1, source_target_pairs={{0,24},{4,28},{8,32},{12,36},{16,40},{20,44},{24,48},{28,52},{32,5... | collective-permute-start | bytes 18440 | tf_op jit(solution)/shard_map/ppermute | solution.py:32
  24.7 0.7 reshape.48.refs_6_
  25.5 2.1 %collective-permute-done.3 = s32[3,512]{1,0:T(4,128)S(1)} collective-permute-done((s32[3,512]{1,0:T(4,128)S(1)}, s32[3,512]{1,0:T(4,128)S(1)}, u32[]{:S(2)}, u32[]{:S(2)}) %collective-permute-start.3) | collective-permute-done | bytes 6176 | tf_op jit(solution)/shard_map/ppermute | solution.py:32
  27.6 2.3 %collective-permute-done.4.left.refs_1_ = bf16[512,1152]{1,0:T(8,128)(2,1)S(1)} collective-permute-done((bf16[512,1152]{1,0:T(8,128)(2,1)}, bf16[512,1152]{1,0:T(8,128)(2,1)S(1)}, u32[]{:S(2)}, u32[]{:S(2)}) %collective-permute-start.4) | collective-permute-done | bytes 1179680 | tf_op jit(solution)/shard_map/ppermute | solution.py:37
  30.0 1.7 %collective-permute-start.6 = (bf16[256,1152]{1,0:T(8,128)(2,1)S(1)}, bf16[256,1152]{1,0:T(8,128)(2,1)S(1)}, u32[]{:S(2)}, u32[]{:S(2)}) collective-permute-start(bf16[256,1152]{1,0:T(8,128)(2,1)S(1)} %get-tuple-element.24), channel_id=1, source_target_pairs={{0,1},{1,2},{2,3},{3,0},{4,5},{5,6},{6,7},{7,4},{8,9},{9,10},{10,1... | collective-permute-start | bytes 1769480 | tf_op jit(solution)/shard_map/ppermute | solution.py:37
  31.7 1.7 %collective-permute-start.7 = (bf16[256,1152]{1,0:T(8,128)(2,1)S(1)}, bf16[256,1152]{1,0:T(8,128)(2,1)S(1)}, u32[]{:S(2)}, u32[]{:S(2)}) collective-permute-start(bf16[256,1152]{1,0:T(8,128)(2,1)S(1)} %get-tuple-element.25), channel_id=1, source_target_pairs={{0,3},{1,0},{2,1},{3,2},{4,7},{5,4},{6,5},{7,6},{8,11},{9,8},{10,9... | collective-permute-start | bytes 1769480 | tf_op jit(solution)/shard_map/ppermute | solution.py:37
  33.4 1.0 convert_reduce_fusion
  34.4 1.0 fusion
  35.4 0.8 squares.1.refs_5_
  36.2 9.4 %collective-permute-done.6.refs_3_ = bf16[256,1152]{1,0:T(8,128)(2,1)S(1)} collective-permute-done((bf16[256,1152]{1,0:T(8,128)(2,1)S(1)}, bf16[256,1152]{1,0:T(8,128)(2,1)S(1)}, u32[]{:S(2)}, u32[]{:S(2)}) %collective-permute-start.6) | collective-permute-done | bytes 589856 | tf_op jit(solution)/shard_map/ppermute | solution.py:37
  45.6 5.3 %norm_project_kv.1 = (bf16[512,4608]{1,0:T(8,128)(2,1)S(1)}, bf16[512,512]{1,0:T(8,128)(2,1)S(1)}, bf16[256,512]{1,0:T(8,128)(2,1)S(1)}, bf16[256,512]{1,0:T(8,128)(2,1)S(1)}, bf16[4,128,512]{2,1,0:T(8,128)(2,1)S(1)}) custom-call(s32[4]{0:T(128)S(1)} %and_select_fusion.shards, s32[4]{0:T(128)S(1)} %bitcast.19, bf16[512,1152]{1,0:T(8,128)(2,1)S(1)} %copy-done, ...), custom_call_target="tpu_custom_call" | custom-call | flops 2415919104 | bytes 14155776 | tf_op jit(solution)/shard_map/norm_project_kv/pallas_call | solution.py:122
  50.9 3.8 %collective-permute-start.13 = (bf16[256,512]{1,0:T(8,128)(2,1)S(1)}, bf16[256,512]{1,0:T(8,128)(2,1)S(1)}, u32[]{:S(2)}, u32[]{:S(2)}) collective-permute-start(bf16[256,512]{1,0:T(8,128)(2,1)S(1)} %get-tuple-element.28), channel_id=1, source_target_pairs={{0,8},{4,12},{8,16},{12,20},{16,24},{20,28},{24,32},{28,36},{32,40... | collective-permute-start | bytes 786440 | tf_op jit(solution)/shard_map/hop_b1/ppermute | solution.py:32
  54.7 2.8 %project_q.1.q_ref = bf16[512,512]{1,0:T(8,128)(2,1)S(1)} custom-call(bf16[512,4608]{1,0:T(8,128)(2,1)S(1)} %get-tuple-element.26.refs_0_, bf16[4608,512]{1,0:T(8,128)(2,1)S(1)} %bitcast.21, f32[512,128]{1,0:T(8,128)S(1)} %get-tuple-element.55.refs_9_.refs_2_, f32[512,128]{1,0:T(8,128)S(1)} %get-tuple-element.54.refs_10_.refs_3_), custom_call_target="tpu_custom_call" | custom-call | flops 5120000000 | bytes 262144 | tf_op jit(solution)/shard_map/project_q/pallas_call | solution.py:153
  57.7 3.8 %collective-permute-start.8 = (bf16[256,512]{1,0:T(8,128)(2,1)S(1)}, bf16[256,512]{1,0:T(8,128)(2,1)S(1)}, u32[]{:S(2)}, u32[]{:S(2)}) collective-permute-start(bf16[256,512]{1,0:T(8,128)(2,1)S(1)} %get-tuple-element.27), channel_id=1, source_target_pairs={{0,8},{4,12},{8,16},{12,20},{16,24},{20,28},{24,32},{28,36},{32,40... | collective-permute-start | bytes 786440 | tf_op jit(solution)/shard_map/hop_a1/ppermute | solution.py:32
  61.5 2.0 %collective-permute-done.13.refs_2_ = bf16[256,512]{1,0:T(8,128)(2,1)S(1)} collective-permute-done((bf16[256,512]{1,0:T(8,128)(2,1)S(1)}, bf16[256,512]{1,0:T(8,128)(2,1)S(1)}, u32[]{:S(2)}, u32[]{:S(2)}) %collective-permute-start.13) | collective-permute-done | bytes 262176 | tf_op jit(solution)/shard_map/hop_b1/ppermute | solution.py:32
  63.5 2.1 %collective-permute-start.14 = (bf16[256,512]{1,0:T(8,128)(2,1)S(1)}, bf16[256,512]{1,0:T(8,128)(2,1)S(1)}, u32[]{:S(2)}, u32[]{:S(2)}) collective-permute-start(bf16[256,512]{1,0:T(8,128)(2,1)S(1)} %collective-permute-done.13.refs_2_), channel_id=1, source_target_pairs={{0,8},{4,12},{8,16},{12,20},{16,24},{20,28},{24,32},{28,36},{32,40... | collective-permute-start | bytes 786440 | tf_op jit(solution)/shard_map/hop_b2/ppermute | solution.py:32
  65.8 1.8 %attend.6 = (f32[512,512]{1,0:T(8,128)S(1)}, f32[512,512]{1,0:T(8,128)S(1)}) custom-call(s32[21]{0:T(128)S(1)} %pad_add_fusion.1.meta, s32[512,128]{1,0:T(8,128)S(1)} %add.84.low_ref, bf16[512,512]{1,0:T(8,128)(2,1)S(1)} %project_q.1.q_ref, bf16[512,512]{1,0:T(8,128)(2,1)S(1)} %get-tuple-element.30.refs_0_), custom_call_target="tpu_custom_call" | custom-call | flops 2560000000 | bytes 262144 | tf_op jit(solution)/shard_map/attend/pallas_call | solution.py:258
  67.7 3.3 %collective-permute-done.8.refs_0_ = bf16[256,512]{1,0:T(8,128)(2,1)S(1)} collective-permute-done((bf16[256,512]{1,0:T(8,128)(2,1)S(1)}, bf16[256,512]{1,0:T(8,128)(2,1)S(1)}, u32[]{:S(2)}, u32[]{:S(2)}) %collective-permute-start.8) | collective-permute-done | bytes 262176 | tf_op jit(solution)/shard_map/hop_a1/ppermute | solution.py:32
  70.9 2.2 %collective-permute-start.9 = (bf16[256,512]{1,0:T(8,128)(2,1)S(1)}, bf16[256,512]{1,0:T(8,128)(2,1)S(1)}, u32[]{:S(2)}, u32[]{:S(2)}) collective-permute-start(bf16[256,512]{1,0:T(8,128)(2,1)S(1)} %collective-permute-done.8.refs_0_), channel_id=1, source_target_pairs={{0,8},{4,12},{8,16},{12,20},{16,24},{20,28},{24,32},{28,36},{32,40... | collective-permute-start | bytes 786440 | tf_op jit(solution)/shard_map/hop_a2/ppermute | solution.py:32
  73.1 3.2 %collective-permute-done.14.refs_2_ = bf16[256,512]{1,0:T(8,128)(2,1)S(1)} collective-permute-done((bf16[256,512]{1,0:T(8,128)(2,1)S(1)}, bf16[256,512]{1,0:T(8,128)(2,1)S(1)}, u32[]{:S(2)}, u32[]{:S(2)}) %collective-permute-start.14) | collective-permute-done | bytes 262176 | tf_op jit(solution)/shard_map/hop_b2/ppermute | solution.py:32
  76.4 1.1 collective-permute-start.24
  77.5 3.4 %collective-permute-start.25 = (bf16[128,512]{1,0:T(8,128)(2,1)S(1)}, bf16[128,512]{1,0:T(8,128)(2,1)S(1)}, u32[]{:S(2)}, u32[]{:S(2)}) collective-permute-start(bf16[128,512]{1,0:T(8,128)(2,1)S(1)} %get-tuple-element.49), channel_id=1, source_target_pairs={{0,2},{1,3},{2,0},{3,1},{4,6},{5,7},{6,4},{7,5},{8,10},{9,11},{10,... | collective-permute-start | bytes 393224 | tf_op jit(solution)/shard_map/ppermute | solution.py:37
  80.9 0.5 attend.7
  81.4 1.1 collective-permute-start.26
  82.5 0.6 collective-permute-start.20
  83.2 0.5 collective-permute-done.9.refs_0_
  83.7 1.9 %collective-permute-start.15 = (bf16[256,512]{1,0:T(8,128)(2,1)S(1)}, bf16[256,512]{1,0:T(8,128)(2,1)S(1)}, u32[]{:S(2)}, u32[]{:S(2)}) collective-permute-start(bf16[256,512]{1,0:T(8,128)(2,1)S(1)} %collective-permute-done.14.refs_2_), channel_id=1, source_target_pairs={{0,8},{4,12},{8,16},{12,20},{16,24},{20,28},{24,32},{28,36},{32,40... | collective-permute-start | bytes 786440 | tf_op jit(solution)/shard_map/hop_b3/ppermute | solution.py:32
  85.7 1.3 %collective-permute-done.25.refs_2_ = bf16[128,512]{1,0:T(8,128)(2,1)S(1)} collective-permute-done((bf16[128,512]{1,0:T(8,128)(2,1)S(1)}, bf16[128,512]{1,0:T(8,128)(2,1)S(1)}, u32[]{:S(2)}, u32[]{:S(2)}) %collective-permute-start.25) | collective-permute-done | bytes 131104 | tf_op jit(solution)/shard_map/ppermute | solution.py:37
  87.0 1.9 %collective-permute-start.10 = (bf16[256,512]{1,0:T(8,128)(2,1)S(1)}, bf16[256,512]{1,0:T(8,128)(2,1)S(1)}, u32[]{:S(2)}, u32[]{:S(2)}) collective-permute-start(bf16[256,512]{1,0:T(8,128)(2,1)S(1)} %collective-permute-done.9.refs_0_), channel_id=1, source_target_pairs={{0,8},{4,12},{8,16},{12,20},{16,24},{20,28},{24,32},{28,36},{32,40... | collective-permute-start | bytes 786440 | tf_op jit(solution)/shard_map/hop_a3/ppermute | solution.py:32
  88.9 3.4 %attend.8 = (f32[512,512]{1,0:T(8,128)S(1)}, f32[512,512]{1,0:T(8,128)S(1)}) custom-call(s32[21]{0:T(128)S(1)} %pad_add_fusion.1.meta, s32[512,128]{1,0:T(8,128)S(1)} %add.84.low_ref, bf16[512,512]{1,0:T(8,128)(2,1)S(1)} %project_q.1.q_ref, bf16[256,512]{1,0:T(8,128)(2,1)S(1)} %collective-permute-done.8.refs_0_, ...), custom_call_target="tpu_custom_call", output_to_operand_aliasing={{0}: (7, {}), {1}: (8, {})} | custom-call | flops 5120000000 | bytes 524288 | tf_op jit(solution)/shard_map/attend/pallas_call | solution.py:258
  92.3 2.2 %build_cache.1 = bf16[1,128,2,1024]{3,2,1,0:T(2,128)(2,1)} custom-call(s32[4]{0:T(128)S(1)} %and_select_fusion.shards, bf16[128,512]{1,0:T(8,128)(2,1)S(1)} %get-tuple-element.51.refs_0_, bf16[128,512]{1,0:T(8,128)(2,1)S(1)} %collective-permute-done.24.refs_1_, bf16[128,512]{1,0:T(8,128)(2,1)S(1)} %collective-permute-done.25.refs_2_, ...), custom_call_target="tpu_custom_call" | custom-call | flops 1000000000 | bytes 1000 | tf_op jit(solution)/shard_map/build_cache/pallas_call | solution.py:291
  94.5 2.3 %collective-permute-done.15.refs_2_ = bf16[256,512]{1,0:T(8,128)(2,1)S(1)} collective-permute-done((bf16[256,512]{1,0:T(8,128)(2,1)S(1)}, bf16[256,512]{1,0:T(8,128)(2,1)S(1)}, u32[]{:S(2)}, u32[]{:S(2)}) %collective-permute-start.15) | collective-permute-done | bytes 262176 | tf_op jit(solution)/shard_map/hop_b3/ppermute | solution.py:32
  96.9 2.2 %collective-permute-start.16 = (bf16[256,512]{1,0:T(8,128)(2,1)S(1)}, bf16[256,512]{1,0:T(8,128)(2,1)S(1)}, u32[]{:S(2)}, u32[]{:S(2)}) collective-permute-start(bf16[256,512]{1,0:T(8,128)(2,1)S(1)} %collective-permute-done.15.refs_2_), channel_id=1, source_target_pairs={{0,8},{4,12},{8,16},{12,20},{16,24},{20,28},{24,32},{28,36},{32,40... | collective-permute-start | bytes 786440 | tf_op jit(solution)/shard_map/hop_b4/ppermute | solution.py:32
  99.1 2.1 %collective-permute-done.10.refs_0_ = bf16[256,512]{1,0:T(8,128)(2,1)S(1)} collective-permute-done((bf16[256,512]{1,0:T(8,128)(2,1)S(1)}, bf16[256,512]{1,0:T(8,128)(2,1)S(1)}, u32[]{:S(2)}, u32[]{:S(2)}) %collective-permute-start.10) | collective-permute-done | bytes 262176 | tf_op jit(solution)/shard_map/hop_a3/ppermute | solution.py:32
  101.2 2.4 %collective-permute-start.11 = (bf16[256,512]{1,0:T(8,128)(2,1)S(1)}, bf16[256,512]{1,0:T(8,128)(2,1)S(1)}, u32[]{:S(2)}, u32[]{:S(2)}) collective-permute-start(bf16[256,512]{1,0:T(8,128)(2,1)S(1)} %collective-permute-done.10.refs_0_), channel_id=1, source_target_pairs={{0,8},{4,12},{8,16},{12,20},{16,24},{20,28},{24,32},{28,36},{32,40... | collective-permute-start | bytes 786440 | tf_op jit(solution)/shard_map/hop_a4/ppermute | solution.py:32
  103.6 3.4 %attend.9 = (f32[512,512]{1,0:T(8,128)S(1)}, f32[512,512]{1,0:T(8,128)S(1)}) custom-call(s32[21]{0:T(128)S(1)} %pad_add_fusion.1.meta, s32[512,128]{1,0:T(8,128)S(1)} %add.84.low_ref, bf16[512,512]{1,0:T(8,128)(2,1)S(1)} %project_q.1.q_ref, bf16[256,512]{1,0:T(8,128)(2,1)S(1)} %collective-permute-done.9.refs_0_, ...), custom_call_target="tpu_custom_call", output_to_operand_aliasing={{0}: (7, {}), {1}: (8, {})} | custom-call | flops 5120000000 | bytes 524288 | tf_op jit(solution)/shard_map/attend/pallas_call | solution.py:258
  107.0 3.4 %attend.10 = (f32[512,512]{1,0:T(8,128)S(1)}, f32[512,512]{1,0:T(8,128)S(1)}) custom-call(s32[21]{0:T(128)S(1)} %pad_add_fusion.1.meta, s32[512,128]{1,0:T(8,128)S(1)} %add.84.low_ref, bf16[512,512]{1,0:T(8,128)(2,1)S(1)} %project_q.1.q_ref, bf16[256,512]{1,0:T(8,128)(2,1)S(1)} %collective-permute-done.10.refs_0_, ...), custom_call_target="tpu_custom_call", output_to_operand_aliasing={{0}: (7, {}), {1}: (8, {})} | custom-call | flops 5120000000 | bytes 524288 | tf_op jit(solution)/shard_map/attend/pallas_call | solution.py:258
  110.8 4.4 %collective-permute-done.11.refs_0_ = bf16[256,512]{1,0:T(8,128)(2,1)S(1)} collective-permute-done((bf16[256,512]{1,0:T(8,128)(2,1)S(1)}, bf16[256,512]{1,0:T(8,128)(2,1)S(1)}, u32[]{:S(2)}, u32[]{:S(2)}) %collective-permute-start.11) | collective-permute-done | bytes 262176 | tf_op jit(solution)/shard_map/hop_a4/ppermute | solution.py:32
  115.2 2.1 %attend.11 = (f32[512,512]{1,0:T(8,128)S(1)}, f32[512,512]{1,0:T(8,128)S(1)}) custom-call(s32[21]{0:T(128)S(1)} %pad_add_fusion.1.meta, s32[512,128]{1,0:T(8,128)S(1)} %add.84.low_ref, bf16[512,512]{1,0:T(8,128)(2,1)S(1)} %project_q.1.q_ref, bf16[256,512]{1,0:T(8,128)(2,1)S(1)} %collective-permute-done.11.refs_0_, ...), custom_call_target="tpu_custom_call", output_to_operand_aliasing={{0}: (5, {}), {1}: (6, {})} | custom-call | flops 2560000000 | bytes 262144 | tf_op jit(solution)/shard_map/attend/pallas_call | solution.py:258
  117.3 3.3 %attend_last.1 = bf16[512,512]{1,0:T(8,128)(2,1)} custom-call(s32[21]{0:T(128)S(1)} %pad_add_fusion.1.meta, s32[512,128]{1,0:T(8,128)S(1)} %add.84.low_ref, bf16[512,512]{1,0:T(8,128)(2,1)S(1)} %project_q.1.q_ref, bf16[256,512]{1,0:T(8,128)(2,1)S(1)} %collective-permute-done.12.refs_0_, bf16[256,512]{1,0:T(8,128)(2,1)S(1)} %collective-permute-done.27.refs_1_, ...), custom_call_target="tpu_custom_call" | custom-call | flops 2560000000 | bytes 262144 | tf_op jit(solution)/shard_map/attend_last/pallas_call | solution.py:258
  (52 shorter events, 1.5 us)
Async XLA Ops:
  0.6 29.3 %collective-permute-start.4 = (bf16[512,1152]{1,0:T(8,128)(2,1)}, bf16[512,1152]{1,0:T(8,128)(2,1)S(1)}, u32[]{:S(2)}, u32[]{:S(2)}) collective-permute-start(bf16[512,1152]{1,0:T(8,128)(2,1)} %refs_0_.1), channel_id=1, source_target_pairs={{0,1},{1,2},{2,3},{3,0},{4,5},{5,6},{6,7},{7,4},{8,9},{9,10},{10,1... | collective-permute-start | bytes 3538952 | tf_op jit(solution)/shard_map/ppermute | solution.py:37
  2.3 27.6 %collective-permute-start.5 = (bf16[512,1152]{1,0:T(8,128)(2,1)}, bf16[512,1152]{1,0:T(8,128)(2,1)S(1)}, u32[]{:S(2)}, u32[]{:S(2)}) collective-permute-start(bf16[512,1152]{1,0:T(8,128)(2,1)} %refs_0_.1), channel_id=1, source_target_pairs={{0,3},{1,0},{2,1},{3,2},{4,7},{5,4},{6,5},{7,6},{8,11},{9,8},{10,9... | collective-permute-start | bytes 3538952 | tf_op jit(solution)/shard_map/ppermute | solution.py:37
  4.6 8.3 %collective-permute-start = (s32[1,512]{1,0:T(1,128)S(1)}, s32[1,512]{1,0:T(1,128)S(1)}, u32[]{:S(2)}, u32[]{:S(2)}) collective-permute-start(s32[1,512]{1,0:T(1,128)S(1)} %bitcast.22), channel_id=1, source_target_pairs={{0,4},{4,8},{8,12},{12,16},{16,20},{20,24},{24,28},{28,32},{32,36}... | collective-permute-start | bytes 6152 | tf_op jit(solution)/shard_map/ppermute | solution.py:32
  6.5 9.6 %collective-permute-start.1 = (s32[1,512]{1,0:T(1,128)S(1)}, s32[1,512]{1,0:T(1,128)S(1)}, u32[]{:S(2)}, u32[]{:S(2)}) collective-permute-start(s32[1,512]{1,0:T(1,128)S(1)} %bitcast.23), channel_id=1, source_target_pairs={{0,8},{4,12},{8,16},{12,20},{16,24},{20,28},{24,32},{28,36},{32,40... | collective-permute-start | bytes 6152 | tf_op jit(solution)/shard_map/ppermute | solution.py:32
  16.1 9.3 %collective-permute-start.2 = (s32[3,512]{1,0:T(4,128)S(1)}, s32[3,512]{1,0:T(4,128)S(1)}, u32[]{:S(2)}, u32[]{:S(2)}) collective-permute-start(s32[3,512]{1,0:T(4,128)S(1)} %pad_add_fusion), channel_id=1, source_target_pairs={{0,12},{4,16},{8,20},{12,24},{16,28},{20,32},{24,36},{28,40},{32,4... | collective-permute-start | bytes 18440 | tf_op jit(solution)/shard_map/ppermute | solution.py:32
  18.1 9.5 %collective-permute-start.3 = (s32[3,512]{1,0:T(4,128)S(1)}, s32[3,512]{1,0:T(4,128)S(1)}, u32[]{:S(2)}, u32[]{:S(2)}) collective-permute-start(s32[3,512]{1,0:T(4,128)S(1)} %pad_add_fusion), channel_id=1, source_target_pairs={{0,24},{4,28},{8,32},{12,36},{16,40},{20,44},{24,48},{28,52},{32,5... | collective-permute-start | bytes 18440 | tf_op jit(solution)/shard_map/ppermute | solution.py:32
  27.6 6.8 %copy-start.4 = (f32[128]{0:T(128)S(1)}, f32[128]{0:T(128)}, u32[]{:S(2)}) copy-start(f32[128]{0:T(128)} %constant.74) | copy-start | bytes 1540
  27.6 7.8 %copy-start = (bf16[512,1152]{1,0:T(8,128)(2,1)S(1)}, bf16[512,1152]{1,0:T(8,128)(2,1)}, u32[]{:S(2)}) copy-start(bf16[512,1152]{1,0:T(8,128)(2,1)} %refs_0_.1) | copy-start | bytes 3538948
  29.9 15.7 %copy-start.2 = (bf16[4608,256]{1,0:T(8,128)(2,1)S(1)}, bf16[4608,256]{1,0:T(8,128)(2,1)}, u32[]{:S(2)}) copy-start(bf16[4608,256]{1,0:T(8,128)(2,1)} %refs_8_.1) | copy-start | bytes 7077892
  30.0 15.6 %copy-start.1 = (bf16[4608,256]{1,0:T(8,128)(2,1)S(1)}, bf16[4608,256]{1,0:T(8,128)(2,1)}, u32[]{:S(2)}) copy-start(bf16[4608,256]{1,0:T(8,128)(2,1)} %refs_7_.1) | copy-start | bytes 7077892
  30.0 15.6 %copy-start.3 = (s32[1,4]{1,0:T(1,128)S(1)}, s32[1,4]{1,0:T(1,128)}, u32[]{:S(2)}) copy-start(s32[1,4]{1,0:T(1,128)} %param.14) | copy-start | bytes 52
  30.0 15.5 %collective-permute-start.6 = (bf16[256,1152]{1,0:T(8,128)(2,1)S(1)}, bf16[256,1152]{1,0:T(8,128)(2,1)S(1)}, u32[]{:S(2)}, u32[]{:S(2)}) collective-permute-start(bf16[256,1152]{1,0:T(8,128)(2,1)S(1)} %get-tuple-element.24), channel_id=1, source_target_pairs={{0,1},{1,2},{2,3},{3,0},{4,5},{5,6},{6,7},{7,4},{8,9},{9,10},{10,1... | collective-permute-start | bytes 1769480 | tf_op jit(solution)/shard_map/ppermute | solution.py:37
  31.7 13.9 %collective-permute-start.7 = (bf16[256,1152]{1,0:T(8,128)(2,1)S(1)}, bf16[256,1152]{1,0:T(8,128)(2,1)S(1)}, u32[]{:S(2)}, u32[]{:S(2)}) collective-permute-start(bf16[256,1152]{1,0:T(8,128)(2,1)S(1)} %get-tuple-element.25), channel_id=1, source_target_pairs={{0,3},{1,0},{2,1},{3,2},{4,7},{5,4},{6,5},{7,6},{8,11},{9,8},{10,9... | collective-permute-start | bytes 1769480 | tf_op jit(solution)/shard_map/ppermute | solution.py:37
  35.4 19.3 %slice-start = ((s8[4718592]{0:T(1024)(128)(4,1)}), s8[4194304]{0:T(1024)(128)(4,1)S(1)}, s32[]{:S(2)}) async-start(s8[4718592]{0:T(1024)(128)(4,1)} %bitcast.20), calls=%async_computation | async-start | bytes 8388608
  45.6 9.1 %slice-start.1 = ((s8[4718592]{0:T(1024)(128)(4,1)}), s8[524288]{0:T(1024)(128)(4,1)S(1)}, s32[]{:S(2)}) async-start(s8[4718592]{0:T(1024)(128)(4,1)} %bitcast.20), calls=%async_computation.1 | async-start | bytes 1048576
  50.9 12.6 %collective-permute-start.13 = (bf16[256,512]{1,0:T(8,128)(2,1)S(1)}, bf16[256,512]{1,0:T(8,128)(2,1)S(1)}, u32[]{:S(2)}, u32[]{:S(2)}) collective-permute-start(bf16[256,512]{1,0:T(8,128)(2,1)S(1)} %get-tuple-element.28), channel_id=1, source_target_pairs={{0,8},{4,12},{8,16},{12,20},{16,24},{20,28},{24,32},{28,36},{32,40... | collective-permute-start | bytes 786440 | tf_op jit(solution)/shard_map/hop_b1/ppermute | solution.py:32
  57.6 19.9 %collective-permute-start.23 = (bf16[512,512]{1,0:T(8,128)(2,1)S(1)}, bf16[512,512]{1,0:T(8,128)(2,1)S(1)}, u32[]{:S(2)}, u32[]{:S(2)}) collective-permute-start(bf16[512,512]{1,0:T(8,128)(2,1)S(1)} %get-tuple-element.30.refs_0_), channel_id=1, source_target_pairs={{0,4},{4,0},{8,12},{12,8},{16,20},{20,16},{24,28},{28,24},{32,36},... | collective-permute-start | bytes 1572872 | tf_op jit(solution)/shard_map/cross_own/ppermute | solution.py:41
  57.7 13.3 %collective-permute-start.8 = (bf16[256,512]{1,0:T(8,128)(2,1)S(1)}, bf16[256,512]{1,0:T(8,128)(2,1)S(1)}, u32[]{:S(2)}, u32[]{:S(2)}) collective-permute-start(bf16[256,512]{1,0:T(8,128)(2,1)S(1)} %get-tuple-element.27), channel_id=1, source_target_pairs={{0,8},{4,12},{8,16},{12,20},{16,24},{20,28},{24,32},{28,36},{32,40... | collective-permute-start | bytes 786440 | tf_op jit(solution)/shard_map/hop_a1/ppermute | solution.py:32
  63.5 12.9 %collective-permute-start.14 = (bf16[256,512]{1,0:T(8,128)(2,1)S(1)}, bf16[256,512]{1,0:T(8,128)(2,1)S(1)}, u32[]{:S(2)}, u32[]{:S(2)}) collective-permute-start(bf16[256,512]{1,0:T(8,128)(2,1)S(1)} %collective-permute-done.13.refs_2_), channel_id=1, source_target_pairs={{0,8},{4,12},{8,16},{12,20},{16,24},{20,28},{24,32},{28,36},{32,40... | collective-permute-start | bytes 786440 | tf_op jit(solution)/shard_map/hop_b2/ppermute | solution.py:32
  67.6 15.0 %collective-permute-start.22 = (bf16[256,512]{1,0:T(8,128)(2,1)S(1)}, bf16[256,512]{1,0:T(8,128)(2,1)S(1)}, u32[]{:S(2)}, u32[]{:S(2)}) collective-permute-start(bf16[256,512]{1,0:T(8,128)(2,1)S(1)} %collective-permute-done.13.refs_2_), channel_id=1, source_target_pairs={{0,4},{4,0},{8,12},{12,8},{16,20},{20,16},{24,28},{28,24},{32,36},... | collective-permute-start | bytes 786440 | tf_op jit(solution)/shard_map/cross_b1/ppermute | solution.py:41
  70.9 10.5 %collective-permute-start.21 = (bf16[256,512]{1,0:T(8,128)(2,1)S(1)}, bf16[256,512]{1,0:T(8,128)(2,1)S(1)}, u32[]{:S(2)}, u32[]{:S(2)}) collective-permute-start(bf16[256,512]{1,0:T(8,128)(2,1)S(1)} %collective-permute-done.8.refs_0_), channel_id=1, source_target_pairs={{0,4},{4,0},{8,12},{12,8},{16,20},{20,16},{24,28},{28,24},{32,36},... | collective-permute-start | bytes 786440 | tf_op jit(solution)/shard_map/cross_a1/ppermute | solution.py:41
  70.9 12.7 %collective-permute-start.9 = (bf16[256,512]{1,0:T(8,128)(2,1)S(1)}, bf16[256,512]{1,0:T(8,128)(2,1)S(1)}, u32[]{:S(2)}, u32[]{:S(2)}) collective-permute-start(bf16[256,512]{1,0:T(8,128)(2,1)S(1)} %collective-permute-done.8.refs_0_), channel_id=1, source_target_pairs={{0,8},{4,12},{8,16},{12,20},{16,24},{20,28},{24,32},{28,36},{32,40... | collective-permute-start | bytes 786440 | tf_op jit(solution)/shard_map/hop_a2/ppermute | solution.py:32
  76.4 9.2 %collective-permute-start.24 = (bf16[128,512]{1,0:T(8,128)(2,1)S(1)}, bf16[128,512]{1,0:T(8,128)(2,1)S(1)}, u32[]{:S(2)}, u32[]{:S(2)}) collective-permute-start(bf16[128,512]{1,0:T(8,128)(2,1)S(1)} %get-tuple-element.50), channel_id=1, source_target_pairs={{0,1},{1,2},{2,3},{3,0},{4,5},{5,6},{6,7},{7,4},{8,9},{9,10},{10,1... | collective-permute-start | bytes 393224 | tf_op jit(solution)/shard_map/ppermute | solution.py:37
  77.5 9.5 %collective-permute-start.25 = (bf16[128,512]{1,0:T(8,128)(2,1)S(1)}, bf16[128,512]{1,0:T(8,128)(2,1)S(1)}, u32[]{:S(2)}, u32[]{:S(2)}) collective-permute-start(bf16[128,512]{1,0:T(8,128)(2,1)S(1)} %get-tuple-element.49), channel_id=1, source_target_pairs={{0,2},{1,3},{2,0},{3,1},{4,6},{5,7},{6,4},{7,5},{8,10},{9,11},{10,... | collective-permute-start | bytes 393224 | tf_op jit(solution)/shard_map/ppermute | solution.py:37
  81.4 10.9 %collective-permute-start.26 = (bf16[128,512]{1,0:T(8,128)(2,1)S(1)}, bf16[128,512]{1,0:T(8,128)(2,1)S(1)}, u32[]{:S(2)}, u32[]{:S(2)}) collective-permute-start(bf16[128,512]{1,0:T(8,128)(2,1)S(1)} %get-tuple-element.48), channel_id=1, source_target_pairs={{0,3},{1,0},{2,1},{3,2},{4,7},{5,4},{6,5},{7,6},{8,11},{9,8},{10,9... | collective-permute-start | bytes 393224 | tf_op jit(solution)/shard_map/ppermute | solution.py:37
  82.5 18.7 %collective-permute-start.20 = (bf16[256,512]{1,0:T(8,128)(2,1)S(1)}, bf16[256,512]{1,0:T(8,128)(2,1)S(1)}, u32[]{:S(2)}, u32[]{:S(2)}) collective-permute-start(bf16[256,512]{1,0:T(8,128)(2,1)S(1)} %collective-permute-done.14.refs_2_), channel_id=1, source_target_pairs={{0,4},{4,0},{8,12},{12,8},{16,20},{20,16},{24,28},{28,24},{32,36},... | collective-permute-start | bytes 786440 | tf_op jit(solution)/shard_map/cross_b2/ppermute | solution.py:41
  83.7 13.2 %collective-permute-start.15 = (bf16[256,512]{1,0:T(8,128)(2,1)S(1)}, bf16[256,512]{1,0:T(8,128)(2,1)S(1)}, u32[]{:S(2)}, u32[]{:S(2)}) collective-permute-start(bf16[256,512]{1,0:T(8,128)(2,1)S(1)} %collective-permute-done.14.refs_2_), channel_id=1, source_target_pairs={{0,8},{4,12},{8,16},{12,20},{16,24},{20,28},{24,32},{28,36},{32,40... | collective-permute-start | bytes 786440 | tf_op jit(solution)/shard_map/hop_b3/ppermute | solution.py:32
  85.6 18.0 %collective-permute-start.19 = (bf16[256,512]{1,0:T(8,128)(2,1)S(1)}, bf16[256,512]{1,0:T(8,128)(2,1)S(1)}, u32[]{:S(2)}, u32[]{:S(2)}) collective-permute-start(bf16[256,512]{1,0:T(8,128)(2,1)S(1)} %collective-permute-done.9.refs_0_), channel_id=1, source_target_pairs={{0,4},{4,0},{8,12},{12,8},{16,20},{20,16},{24,28},{28,24},{32,36},... | collective-permute-start | bytes 786440 | tf_op jit(solution)/shard_map/cross_a2/ppermute | solution.py:41
  87.0 14.2 %collective-permute-start.10 = (bf16[256,512]{1,0:T(8,128)(2,1)S(1)}, bf16[256,512]{1,0:T(8,128)(2,1)S(1)}, u32[]{:S(2)}, u32[]{:S(2)}) collective-permute-start(bf16[256,512]{1,0:T(8,128)(2,1)S(1)} %collective-permute-done.9.refs_0_), channel_id=1, source_target_pairs={{0,8},{4,12},{8,16},{12,20},{16,24},{20,28},{24,32},{28,36},{32,40... | collective-permute-start | bytes 786440 | tf_op jit(solution)/shard_map/hop_a3/ppermute | solution.py:32
  96.9 10.1 %collective-permute-start.18 = (bf16[256,512]{1,0:T(8,128)(2,1)S(1)}, bf16[256,512]{1,0:T(8,128)(2,1)S(1)}, u32[]{:S(2)}, u32[]{:S(2)}) collective-permute-start(bf16[256,512]{1,0:T(8,128)(2,1)S(1)} %collective-permute-done.15.refs_2_), channel_id=1, source_target_pairs={{0,4},{4,0},{8,12},{12,8},{16,20},{20,16},{24,28},{28,24},{32,36},... | collective-permute-start | bytes 786440 | tf_op jit(solution)/shard_map/cross_b3/ppermute | solution.py:41
  96.9 13.6 %collective-permute-start.16 = (bf16[256,512]{1,0:T(8,128)(2,1)S(1)}, bf16[256,512]{1,0:T(8,128)(2,1)S(1)}, u32[]{:S(2)}, u32[]{:S(2)}) collective-permute-start(bf16[256,512]{1,0:T(8,128)(2,1)S(1)} %collective-permute-done.15.refs_2_), channel_id=1, source_target_pairs={{0,8},{4,12},{8,16},{12,20},{16,24},{20,28},{24,32},{28,36},{32,40... | collective-permute-start | bytes 786440 | tf_op jit(solution)/shard_map/hop_b4/ppermute | solution.py:32
  101.2 5.8 %collective-permute-start.17 = (bf16[256,512]{1,0:T(8,128)(2,1)S(1)}, bf16[256,512]{1,0:T(8,128)(2,1)S(1)}, u32[]{:S(2)}, u32[]{:S(2)}) collective-permute-start(bf16[256,512]{1,0:T(8,128)(2,1)S(1)} %collective-permute-done.10.refs_0_), channel_id=1, source_target_pairs={{0,4},{4,0},{8,12},{12,8},{16,20},{20,16},{24,28},{28,24},{32,36},... | collective-permute-start | bytes 786440 | tf_op jit(solution)/shard_map/cross_a3/ppermute | solution.py:41
  101.2 14.0 %collective-permute-start.11 = (bf16[256,512]{1,0:T(8,128)(2,1)S(1)}, bf16[256,512]{1,0:T(8,128)(2,1)S(1)}, u32[]{:S(2)}, u32[]{:S(2)}) collective-permute-start(bf16[256,512]{1,0:T(8,128)(2,1)S(1)} %collective-permute-done.10.refs_0_), channel_id=1, source_target_pairs={{0,8},{4,12},{8,16},{12,20},{16,24},{20,28},{24,32},{28,36},{32,40... | collective-permute-start | bytes 786440 | tf_op jit(solution)/shard_map/hop_a4/ppermute | solution.py:32
  110.4 6.9 %collective-permute-start.27 = (bf16[256,512]{1,0:T(8,128)(2,1)S(1)}, bf16[256,512]{1,0:T(8,128)(2,1)S(1)}, u32[]{:S(2)}, u32[]{:S(2)}) collective-permute-start(bf16[256,512]{1,0:T(8,128)(2,1)S(1)} %collective-permute-done.16.refs_1_), channel_id=1, source_target_pairs={{0,4},{4,0},{8,12},{12,8},{16,20},{20,16},{24,28},{28,24},{32,36},... | collective-permute-start | bytes 786440 | tf_op jit(solution)/shard_map/cross_b4/ppermute | solution.py:41
  115.2 2.1 %collective-permute-start.12 = (bf16[256,512]{1,0:T(8,128)(2,1)S(1)}, bf16[256,512]{1,0:T(8,128)(2,1)S(1)}, u32[]{:S(2)}, u32[]{:S(2)}) collective-permute-start(bf16[256,512]{1,0:T(8,128)(2,1)S(1)} %collective-permute-done.11.refs_0_), channel_id=1, source_target_pairs={{0,4},{4,0},{8,12},{12,8},{16,20},{20,16},{24,28},{28,24},{32,36},... | collective-permute-start | bytes 786440 | tf_op jit(solution)/shard_map/cross_a4/ppermute | solution.py:41

commit v4 on v3

--- a/solution.py
+++ b/solution.py
@@ -45,58 +45,73 @@
     return x * cos + pltpu.roll(x, HD // 2, 1) * sin
 
 
-def squares_kernel(own, left, right, out):
-    def tile(index, carry):
-        at = pl.ds(pl.multiple_of(index * 64, 64), 64)
-        total = jnp.zeros((64, HD), jnp.float32)
-        for piece in (own, left, right):
+def early_kernel(shards, own, left, right, far_square, gain, wq, wk, wv, *refs):
+    scale_out, q_part, k_part, v_part, normed = refs
+    rows, width = own.shape
+    features = wk.shape[0]
+    pieces = ((own, 0), (left, 3), (right, 1))
+
+    for start in range(0, rows, 128):
+        at = pl.ds(start, 128)
+        square = jnp.zeros((128, HD), jnp.float32)
+        for piece, turn in pieces:
             wide = piece[at, :].astype(jnp.float32)
             wide = wide * wide
-            for lane in range(0, wide.shape[1], HD):
-                total = total + wide[:, lane : lane + HD]
-        out[at, :] = total
-        return carry
-
-    lax.fori_loop(0, out.shape[0] // 64, tile, 0)
-
-
-def squares(own, left, right):
+            for lane in range(0, width, HD):
+                square = square + wide[:, lane : lane + HD]
+        square = jnp.sum(square, axis=-1, keepdims=True) + far_square[at, :1]
+        scale = lax.rsqrt(square * (1.0 / features) + norm_eps)
+        scale_out[at, :] = jnp.broadcast_to(scale, (128, HD))
+        for index, (piece, turn) in enumerate(pieces):
+            cols = pl.ds(pl.multiple_of(shards[turn] * width, 128), width)
+            wide = piece[at, :].astype(jnp.float32)
+            normed[index, at, :] = (wide * scale * gain[:, cols]).astype(jnp.bfloat16)
+    for weights, out in ((wk, k_part), (wv, v_part), (wq, q_part)):
+        total = 0.0
+        for index, (piece, turn) in enumerate(pieces):
+            at = pl.ds(pl.multiple_of(shards[turn] * width, 128), width)
+            total = total + jnp.dot(
+                normed[index], weights[at, :], preferred_element_type=jnp.float32
+            )
+        out[...] = total
+
+
+def project_early(shards, own, left, right, far_square, gain, wq, wk, wv):
     rows, width = own.shape
-    return pl.pallas_call(
-        squares_kernel,
-        name="squares",
-        out_shape=jax.ShapeDtypeStruct((rows, HD), jnp.float32),
-        in_specs=[whole()] * 3,
-        out_specs=whole(),
-        compiler_params=pltpu.CompilerParams(vmem_limit_bytes=8 << 20),
+    columns = (wq.shape[1], wk.shape[1], wv.shape[1])
+    return pl.pallas_call(
+        early_kernel,
+        name="project_early",
+        out_shape=tuple(
+            jax.ShapeDtypeStruct((rows, n), jnp.float32) for n in (HD, *columns)
+        ),
+        in_specs=[whole(SMEM)] + [whole()] * 8,
+        out_specs=(whole(),) * 4,
+        scratch_shapes=(VMEM((3, rows, width), jnp.bfloat16),),
+        compiler_params=pltpu.CompilerParams(vmem_limit_bytes=16 << 20),
         cost_estimate=pl.CostEstimate(
-            flops=6 * rows * width, transcendentals=0, bytes_accessed=6 * rows * width
+            flops=6 * rows * width * sum(columns),
+            transcendentals=rows,
+            bytes_accessed=6 * rows * width,
         ),
-    )(own, left, right)
+    )(shards, own, left, right, far_square, gain, wq, wk, wv)
 
 
 def kv_kernel(shards, table, *refs):
-    own, left, right, far_a, far_b, square_ref, gain, wk, wv, cos, sin = refs[:11]
-    normed, block, first, second, pages = refs[11:]
+    far_a, far_b, scale, gain, wk, wv, k_part, v_part, cos, sin = refs[:10]
+    normed, block, first, second, pages = refs[10:]
     count = shards.shape[0]
-    rows, features = normed.shape
-    width = own.shape[1]
+    rows, width = normed.shape
     half = rows // 2
+    mine = pl.ds(pl.multiple_of(shards[2] * width, 128), width)
 
     for start in range(0, rows, 128):
         at = pl.ds(start, 128)
         far = far_a if start < half else far_b
-        pieces = ((far, pl.ds(start % half, 128), 2), (own, at, 0), (left, at, 3), (right, at, 1))
-        wide = far[pieces[0][1], :].astype(jnp.float32)
-        square = jnp.sum(wide * wide, axis=-1, keepdims=True)
-        square = square + jnp.sum(square_ref[at, :], axis=-1, keepdims=True)
-        scale = lax.rsqrt(square * (1.0 / features) + norm_eps)
-        for part, rows_at, turn in pieces:
-            cols = pl.ds(pl.multiple_of(shards[turn] * width, 128), width)
-            wide = part[rows_at, :].astype(jnp.float32)
-            normed[at, cols] = (wide * scale * gain[:, cols]).astype(jnp.bfloat16)
-    keys = jnp.dot(normed[...], wk[...], preferred_element_type=jnp.float32)
-    values = jnp.dot(normed[...], wv[...], preferred_element_type=jnp.float32)
+        wide = far[pl.ds(start % half, 128), :].astype(jnp.float32)
+        normed[at, :] = (wide * scale[at, :1] * gain[:, mine]).astype(jnp.bfloat16)
+    keys = k_part[...] + jnp.dot(normed[...], wk[mine, :], preferred_element_type=jnp.float32)
+    values = v_part[...] + jnp.dot(normed[...], wv[mine, :], preferred_element_type=jnp.float32)
     kv_width = wk.shape[1]
     for out, start in ((first, 0), (second, half)):
         at = slice(start, start + half)
@@ -110,59 +125,49 @@
             pages[slot, :, :] = out[page * PAGE : page * PAGE + PAGE, :]
 
 
-def project_kv(shards, table, pieces, square, gain, wk, wv, cos, sin):
-    features = wk.shape[0]
+def project_kv(shards, table, far, scale, gain, wk, wv, k_part, v_part, cos, sin):
     rows = cos.shape[0]
+    far_width = far[0].shape[1]
     width = 2 * wk.shape[1]
-    out_shape = tuple(
-        jax.ShapeDtypeStruct(shape, jnp.bfloat16)
-        for shape in ((rows, features), (rows, width), (rows // 2, width), (rows // 2, width))
-    )
-    paged = jax.ShapeDtypeStruct((rows // PAGE, PAGE, width), jnp.bfloat16)
+    shapes = ((rows, far_width), (rows, width), (rows // 2, width), (rows // 2, width))
+    shapes += ((rows // PAGE, PAGE, width),)
     return pl.pallas_call(
         kv_kernel,
-        name="norm_project_kv",
-        out_shape=(*out_shape, paged),
-        in_specs=[whole(SMEM)] * 2 + [whole()] * 11,
+        name="project_kv",
+        out_shape=tuple(jax.ShapeDtypeStruct(shape, jnp.bfloat16) for shape in shapes),
+        in_specs=[whole(SMEM)] * 2 + [whole()] * 10,
         out_specs=(whole(),) * 5,
-        compiler_params=pltpu.CompilerParams(vmem_limit_bytes=14 << 20),
+        compiler_params=pltpu.CompilerParams(vmem_limit_bytes=10 << 20),
         cost_estimate=pl.CostEstimate(
-            flops=2 * rows * features * width,
-            transcendentals=rows,
-            bytes_accessed=2 * (2 * rows * features + features * width),
+            flops=2 * rows * far_width * width,
+            transcendentals=0,
+            bytes_accessed=2 * rows * far_width,
         ),
-    )(shards, table, *pieces, square, gain, wk, wv, cos, sin)
-
-
-def q_kernel(count, *refs):
-    normed = refs[:count]
-    wq, cos, sin, out = refs[count:]
-    start = 0
-    for block in normed:
-        at = slice(start, start + block.shape[0])
-        raw = jnp.dot(block[...], wq[...], preferred_element_type=jnp.float32)
-        for head in range(wq.shape[1] // HD):
-            cols = slice(head * HD, head * HD + HD)
-            out[at, cols] = rope(raw[:, cols], cos[at, :], sin[at, :]).astype(jnp.bfloat16)
-        start += block.shape[0]
-
-
-def project_q(normed, wq, cos, sin):
-    rows = cos.shape[0]
-    features, width = wq.shape
-    return pl.pallas_call(
-        functools.partial(q_kernel, len(normed)),
+    )(shards, table, *far, scale, gain, wk, wv, k_part, v_part, cos, sin)
+
+
+def q_kernel(shards, normed, wq, part, cos, sin, out):
+    width = normed.shape[1]
+    mine = pl.ds(pl.multiple_of(shards[2] * width, 128), width)
+    raw = part[...] + jnp.dot(normed[...], wq[mine, :], preferred_element_type=jnp.float32)
+    for head in range(wq.shape[1] // HD):
+        cols = slice(head * HD, head * HD + HD)
+        out[:, cols] = rope(raw[:, cols], cos[...], sin[...]).astype(jnp.bfloat16)
+
+
+def project_q(shards, normed, wq, part, cos, sin):
+    rows, width = part.shape
+    return pl.pallas_call(
+        q_kernel,
         name="project_q",
         out_shape=jax.ShapeDtypeStruct((rows, width), jnp.bfloat16),
-        in_specs=[whole()] * (len(normed) + 3),
+        in_specs=[whole(SMEM)] + [whole()] * 5,
         out_specs=whole(),
-        compiler_params=pltpu.CompilerParams(vmem_limit_bytes=10 << 20),
+        compiler_params=pltpu.CompilerParams(vmem_limit_bytes=8 << 20),
         cost_estimate=pl.CostEstimate(
-            flops=10000000 * rows,
-            transcendentals=0,
-            bytes_accessed=rows * width,
+            flops=10000000 * rows, transcendentals=0, bytes_accessed=rows * width
         ),
-    )(*normed, wq, cos, sin)
+    )(shards, normed, wq, part, cos, sin)
 
 
 def attend_kernel(places, first, last, guarded, meta, low_ref, q_ref, *refs):
@@ -327,13 +332,7 @@
     left_half, right_half = halves(left, right)
     far_a = turned(left_half, "tp", 1)
     far_b = turned(right_half, "tp", -1)
-    return [
-        (block, (0, 0, rows)),
-        (left, (3, 0, rows)),
-        (right, (1, 0, rows)),
-        (far_a, (2, 0, half)),
-        (far_b, (2, half, rows)),
-    ]
+    return left, right, (far_a, far_b), left_half
 
 
 def per_device(hidden, norm_gain, w_query, w_key, w_value, segment_ids, page_table):
@@ -345,7 +344,11 @@
     shards = (rank + jnp.arange(ranks, dtype=jnp.int32)) % ranks
     table = page_table[0]
 
-    pieces = ring_gather(hidden)
+    left, right, far, forwarded = ring_gather(hidden)
+    wide = hidden.astype(jnp.float32)
+    with jax.named_scope("far_square"):
+        far_square = turned(jnp.sum(wide * wide, axis=-1).reshape(1, tokens), "tp", 2)
+    far_square = far_square.reshape(tokens, 1) + jnp.zeros((1, HD), jnp.float32)
     marked = (segment_ids + 1).reshape(1, tokens)
     near = jnp.concatenate(
         [marked, shifted(marked, "seq", 1), shifted(marked, "seq", 2)], axis=0
@@ -353,6 +356,7 @@
     earlier = jnp.concatenate(
         [near[1:], shifted(near, "seq", 3), shifted(near, "seq", 6)], axis=0
     ).reshape(1, -1)
+    earlier = lax.optimization_barrier((earlier, forwarded))[0]
     first_token = place * tokens
     own = segment_ids.reshape(tokens, 1) + 1
     before = jnp.sum((marked < own).astype(jnp.int32), axis=1, keepdims=True)
@@ -375,10 +379,11 @@
     sin = jnp.sin(angles) * sign[None, :]
     gain = norm_gain.reshape(1, -1)
 
-    arrays = [array for array, _ in pieces]
-    square = squares(*arrays[:3])
+    scale, q_part, k_part, v_part = project_early(
+        shards, hidden, left, right, far_square, gain, w_query, w_key, w_value
+    )
     normed, block, a0, b0, pages = project_kv(
-        shards, table, arrays, square, gain, w_key, w_value, cos, sin
+        shards, table, far, scale, gain, w_key, w_value, k_part, v_part, cos, sin
     )
 
     def after(value, *others):
@@ -400,7 +405,7 @@
     look = functools.partial(attend, meta, low)
     straight = [1 + step for step in range(steps + 1)]
     over = [2 + steps + step for step in range(steps + 1)]
-    queries = project_q((normed,), w_query, cos, sin)
+    queries = project_q(shards, normed, w_query, q_part, cos, sin)
     crossed = cross("own", after(block, queries))
     state = look(queries, [(block, straight[0], 0)])
     state = look(queries, [(crossed, over[0], None)], state, guarded=True)

time: 121 us -> 118 us (0.975)
  waiting for transfers between devices: 38.2 us -> 28.3 us
  starting transfers between devices: 48.1 us -> 51.9 us
  other arithmetic: 3.15 us -> 4.72 us
    ppermute x7 -> x8, waiting for transfers between devices: 13 us -> 6.84 us  [turned(): lax.ppermute(block, axis, [(i, (i + distance) % count) for i in range(cou...]
    ppermute x12, waiting for transfers between devices: 25.2 us -> 21.5 us  [shifted(): return lax.ppermute(block, axis, route)]
    ppermute x7 -> x8, starting transfers between devices: 12.2 us -> 14.6 us  [turned(): lax.ppermute(block, axis, [(i, (i + distance) % count) for i in range(cou...]
    ppermute x12, starting transfers between devices: 34.7 us -> 36.7 us  [shifted(): return lax.ppermute(block, axis, route)]
    reduce_sum x0 -> x1, other arithmetic: none -> 1.58 us  [per_device(): jnp.sum(wide * wide, axis=-1).reshape(1, tokens)]
  transfers between devices with their start and end apart: 28 -> 29, of which waited for: 13 -> 13; matrix products, arithmetic and copies ran while one was open for 3% -> 5% of each run, Pallas kernels for 17% -> 21%
where the time goes in v4:
time: 118 us; the launch traced here: 117 us
  starting transfers between devices  51.9 us (44%)
  Pallas kernels  29.7 us (25%)
  waiting for transfers between devices  28.3 us (24%)
  other arithmetic  4.72 us (4%)
    ppermute x12, starting transfers between devices, shifted(): return lax.ppermute(block, axis, route)  36.7 us
    ppermute x12, waiting for transfers between devices, shifted(): return lax.ppermute(block, axis, route)  21.5 us
    pallas_call x7, Pallas kernels, attend(): pl.pallas_call(functools.partial(attend_kernel, places, first, last, guar...  18.2 us
    ppermute x8, starting transfers between devices, turned(): lax.ppermute(block, axis, [(i, (i + distance) % count) for i in range(cou...  14.6 us
    ppermute x8, waiting for transfers between devices, turned(): lax.ppermute(block, axis, [(i, (i + distance) % count) for i in range(cou...  6.84 us
    pallas_call x1, Pallas kernels, project_early(): pl.pallas_call(early_kernel, name='project_early', out_shape=tuple((jax.S...  5.76 us
  transfers between devices with their start and end apart: 29, of which 13 were waited for; matrix products, arithmetic and copies ran while one was open for 5% of the time, Pallas kernels for 21%

profile of v4, /device:TPU:6, one launch (start us, length us, event | category | flops | bytes accessed | tf_op | source)
XLA Modules:
  0.0 116.9 jit_solution(13533748292178509100)
XLA Ops:
  0.6 1.7 %collective-permute-start.4 = (bf16[512,1152]{1,0:T(8,128)(2,1)}, bf16[512,1152]{1,0:T(8,128)(2,1)S(1)}, u32[]{:S(2)}, u32[]{:S(2)}) collective-permute-start(bf16[512,1152]{1,0:T(8,128)(2,1)} %own.1), channel_id=1, source_target_pairs={{0,1},{1,2},{2,3},{3,0},{4,5},{5,6},{6,7},{7,4},{8,9},{9,10},{10,1... | collective-permute-start | bytes 3538952 | tf_op jit(solution)/shard_map/ppermute | solution.py:37
  2.3 1.7 %collective-permute-start.5 = (bf16[512,1152]{1,0:T(8,128)(2,1)}, bf16[512,1152]{1,0:T(8,128)(2,1)S(1)}, u32[]{:S(2)}, u32[]{:S(2)}) collective-permute-start(bf16[512,1152]{1,0:T(8,128)(2,1)} %own.1), channel_id=1, source_target_pairs={{0,3},{1,0},{2,1},{3,2},{4,7},{5,4},{6,5},{7,6},{8,11},{9,8},{10,9... | collective-permute-start | bytes 3538952 | tf_op jit(solution)/shard_map/ppermute | solution.py:37
  3.9 0.7 broadcast_add_fusion
  4.6 1.9 %collective-permute-start = (s32[1,512]{1,0:T(1,128)S(1)}, s32[1,512]{1,0:T(1,128)S(1)}, u32[]{:S(2)}, u32[]{:S(2)}) collective-permute-start(s32[1,512]{1,0:T(1,128)S(1)} %bitcast.26), channel_id=1, source_target_pairs={{0,4},{4,8},{8,12},{12,16},{16,20},{20,24},{24,28},{28,32},{32,36}... | collective-permute-start | bytes 6152 | tf_op jit(solution)/shard_map/ppermute | solution.py:32
  6.5 3.8 %collective-permute-start.1 = (s32[1,512]{1,0:T(1,128)S(1)}, s32[1,512]{1,0:T(1,128)S(1)}, u32[]{:S(2)}, u32[]{:S(2)}) collective-permute-start(s32[1,512]{1,0:T(1,128)S(1)} %bitcast.27), channel_id=1, source_target_pairs={{0,8},{4,12},{8,16},{12,20},{16,24},{20,28},{24,32},{28,36},{32,40... | collective-permute-start | bytes 6152 | tf_op jit(solution)/shard_map/ppermute | solution.py:32
  10.4 1.6 %multiply_reduce_fusion = f32[512]{0:T(512)S(1)} fusion(bf16[512,1152]{1,0:T(8,128)(2,1)} %own.1), kind=kLoop, calls=%fused_computation.1 | loop fusion | flops 1768960 | bytes 1181696 | tf_op jit(solution)/shard_map/far_square/reduce_sum | solution.py:350
  12.0 2.1 %collective-permute-start.8 = (f32[1,512]{1,0:T(1,128)S(1)}, f32[1,512]{1,0:T(1,128)S(1)}, u32[]{:S(2)}, u32[]{:S(2)}) collective-permute-start(f32[1,512]{1,0:T(1,128)S(1)} %bitcast.31), channel_id=1, source_target_pairs={{0,2},{1,3},{2,0},{3,1},{4,6},{5,7},{6,4},{7,5},{8,10},{9,11},{10,... | collective-permute-start | bytes 6152 | tf_op jit(solution)/shard_map/far_square/ppermute | solution.py:37
  14.5 1.7 %collective-permute-done.1 = s32[1,512]{1,0:T(1,128)S(1)} collective-permute-done((s32[1,512]{1,0:T(1,128)S(1)}, s32[1,512]{1,0:T(1,128)S(1)}, u32[]{:S(2)}, u32[]{:S(2)}) %collective-permute-start.1) | collective-permute-done | bytes 2080 | tf_op jit(solution)/shard_map/ppermute | solution.py:32
  16.1 3.2 %collective-permute-start.2 = (s32[3,512]{1,0:T(4,128)S(1)}, s32[3,512]{1,0:T(4,128)S(1)}, u32[]{:S(2)}, u32[]{:S(2)}) collective-permute-start(s32[3,512]{1,0:T(4,128)S(1)} %pad_add_fusion), channel_id=1, source_target_pairs={{0,12},{4,16},{8,20},{12,24},{16,28},{20,32},{24,36},{28,40},{32,4... | collective-permute-start | bytes 18440 | tf_op jit(solution)/shard_map/ppermute | solution.py:32
  19.4 5.9 %collective-permute-start.3 = (s32[3,512]{1,0:T(4,128)S(1)}, s32[3,512]{1,0:T(4,128)S(1)}, u32[]{:S(2)}, u32[]{:S(2)}) collective-permute-start(s32[3,512]{1,0:T(4,128)S(1)} %pad_add_fusion), channel_id=1, source_target_pairs={{0,24},{4,28},{8,32},{12,36},{16,40},{20,44},{24,48},{28,52},{32,5... | collective-permute-start | bytes 18440 | tf_op jit(solution)/shard_map/ppermute | solution.py:32
  25.4 0.7 reshape.56.gain.refs_3_
  26.1 2.7 %collective-permute-done.3 = s32[3,512]{1,0:T(4,128)S(1)} collective-permute-done((s32[3,512]{1,0:T(4,128)S(1)}, s32[3,512]{1,0:T(4,128)S(1)}, u32[]{:S(2)}, u32[]{:S(2)}) %collective-permute-start.3) | collective-permute-done | bytes 6176 | tf_op jit(solution)/shard_map/ppermute | solution.py:32
  29.0 0.9 collective-permute-done.4.left
  30.0 1.7 %collective-permute-start.6 = (bf16[256,1152]{1,0:T(8,128)(2,1)S(1)}, bf16[256,1152]{1,0:T(8,128)(2,1)S(1)}, u32[]{:S(2)}, u32[]{:S(2)}) collective-permute-start(bf16[256,1152]{1,0:T(8,128)(2,1)S(1)} %get-tuple-element.29), channel_id=1, source_target_pairs={{0,1},{1,2},{2,3},{3,0},{4,5},{5,6},{6,7},{7,4},{8,9},{9,10},{10,1... | collective-permute-start | bytes 1769480 | tf_op jit(solution)/shard_map/ppermute | solution.py:37
  31.7 1.0 convert_reduce_fusion
  32.7 1.7 %collective-permute-start.7 = (bf16[256,1152]{1,0:T(8,128)(2,1)S(1)}, bf16[256,1152]{1,0:T(8,128)(2,1)S(1)}, u32[]{:S(2)}, u32[]{:S(2)}) collective-permute-start(bf16[256,1152]{1,0:T(8,128)(2,1)S(1)} %get-tuple-element.31), channel_id=1, source_target_pairs={{0,3},{1,0},{2,1},{3,2},{4,7},{5,4},{6,5},{7,6},{8,11},{9,8},{10,9... | collective-permute-start | bytes 1769480 | tf_op jit(solution)/shard_map/ppermute | solution.py:37
  34.4 1.0 fusion
  35.6 5.8 %project_early.1 = (f32[512,128]{1,0:T(8,128)S(1)}, f32[512,512]{1,0:T(8,128)S(1)}, f32[512,256]{1,0:T(8,128)S(1)}, f32[512,256]{1,0:T(8,128)S(1)}) custom-call(s32[4]{0:T(128)S(1)} %and_select_fusion.shards, bf16[512,1152]{1,0:T(8,128)(2,1)S(1)} %copy-done.2, bf16[512,1152]{1,0:T(8,128)(2,1)S(1)} %collective-permute-done.4.left, ...), custom_call_target="tpu_custom_call" | custom-call | flops 3623878656 | bytes 3538944 | tf_op jit(solution)/shard_map/project_early/pallas_call | solution.py:82
  41.4 4.1 %collective-permute-done.6.refs_0_ = bf16[256,1152]{1,0:T(8,128)(2,1)S(1)} collective-permute-done((bf16[256,1152]{1,0:T(8,128)(2,1)S(1)}, bf16[256,1152]{1,0:T(8,128)(2,1)S(1)}, u32[]{:S(2)}, u32[]{:S(2)}) %collective-permute-start.6) | collective-permute-done | bytes 589856 | tf_op jit(solution)/shard_map/ppermute | solution.py:37
  45.6 0.8 collective-permute-done.7.refs_1_
  46.3 1.8 %project_kv.1 = (bf16[512,1152]{1,0:T(8,128)(2,1)S(1)}, bf16[512,512]{1,0:T(8,128)(2,1)S(1)}, bf16[256,512]{1,0:T(8,128)(2,1)S(1)}, bf16[256,512]{1,0:T(8,128)(2,1)S(1)}, bf16[4,128,512]{2,1,0:T(8,128)(2,1)S(1)}) custom-call(s32[4]{0:T(128)S(1)} %and_select_fusion.shards, s32[4]{0:T(128)S(1)} %bitcast.23, ...), custom_call_target="tpu_custom_call" | custom-call | flops 603979776 | bytes 1179648 | tf_op jit(solution)/shard_map/project_kv/pallas_call | solution.py:134
  48.1 3.9 %collective-permute-start.14 = (bf16[256,512]{1,0:T(8,128)(2,1)S(1)}, bf16[256,512]{1,0:T(8,128)(2,1)S(1)}, u32[]{:S(2)}, u32[]{:S(2)}) collective-permute-start(bf16[256,512]{1,0:T(8,128)(2,1)S(1)} %get-tuple-element.38), channel_id=1, source_target_pairs={{0,8},{4,12},{8,16},{12,20},{16,24},{20,28},{24,32},{28,36},{32,40... | collective-permute-start | bytes 786440 | tf_op jit(solution)/shard_map/hop_b1/ppermute | solution.py:32
  52.0 1.6 %project_q.1.q_ref = bf16[512,512]{1,0:T(8,128)(2,1)S(1)} custom-call(s32[4]{0:T(128)S(1)} %and_select_fusion.shards, bf16[512,1152]{1,0:T(8,128)(2,1)S(1)} %get-tuple-element.35.normed, bf16[4608,512]{1,0:T(8,128)(2,1)S(1)} %bitcast.25, f32[512,512]{1,0:T(8,128)S(1)} %get-tuple-element.36.part, f32[512,128]{1,0:T(8,128)S(1)} %get-tuple-element.65.refs_8_.cos, ...), custom_call_target="tpu_custom_call" | custom-call | flops 5120000000 | bytes 262144 | tf_op jit(solution)/shard_map/project_q/pallas_call | solution.py:160
  53.7 3.9 %collective-permute-start.9 = (bf16[256,512]{1,0:T(8,128)(2,1)S(1)}, bf16[256,512]{1,0:T(8,128)(2,1)S(1)}, u32[]{:S(2)}, u32[]{:S(2)}) collective-permute-start(bf16[256,512]{1,0:T(8,128)(2,1)S(1)} %get-tuple-element.37), channel_id=1, source_target_pairs={{0,8},{4,12},{8,16},{12,20},{16,24},{20,28},{24,32},{28,36},{32,40... | collective-permute-start | bytes 786440 | tf_op jit(solution)/shard_map/hop_a1/ppermute | solution.py:32
  57.7 2.8 %collective-permute-done.14.refs_2_ = bf16[256,512]{1,0:T(8,128)(2,1)S(1)} collective-permute-done((bf16[256,512]{1,0:T(8,128)(2,1)S(1)}, bf16[256,512]{1,0:T(8,128)(2,1)S(1)}, u32[]{:S(2)}, u32[]{:S(2)}) %collective-permute-start.14) | collective-permute-done | bytes 262176 | tf_op jit(solution)/shard_map/hop_b1/ppermute | solution.py:32
  60.5 1.9 %collective-permute-start.15 = (bf16[256,512]{1,0:T(8,128)(2,1)S(1)}, bf16[256,512]{1,0:T(8,128)(2,1)S(1)}, u32[]{:S(2)}, u32[]{:S(2)}) collective-permute-start(bf16[256,512]{1,0:T(8,128)(2,1)S(1)} %collective-permute-done.14.refs_2_), channel_id=1, source_target_pairs={{0,8},{4,12},{8,16},{12,20},{16,24},{20,28},{24,32},{28,36},{32,40... | collective-permute-start | bytes 786440 | tf_op jit(solution)/shard_map/hop_b2/ppermute | solution.py:32
  62.6 1.8 %attend.6 = (f32[512,512]{1,0:T(8,128)S(1)}, f32[512,512]{1,0:T(8,128)S(1)}) custom-call(s32[21]{0:T(128)S(1)} %pad_add_fusion.1.meta, s32[512,128]{1,0:T(8,128)S(1)} %add.91.low_ref, bf16[512,512]{1,0:T(8,128)(2,1)S(1)} %project_q.1.q_ref, bf16[512,512]{1,0:T(8,128)(2,1)S(1)} %get-tuple-element.40.refs_0_), custom_call_target="tpu_custom_call" | custom-call | flops 2560000000 | bytes 262144 | tf_op jit(solution)/shard_map/attend/pallas_call | solution.py:263
  64.5 2.6 %collective-permute-done.9.refs_0_ = bf16[256,512]{1,0:T(8,128)(2,1)S(1)} collective-permute-done((bf16[256,512]{1,0:T(8,128)(2,1)S(1)}, bf16[256,512]{1,0:T(8,128)(2,1)S(1)}, u32[]{:S(2)}, u32[]{:S(2)}) %collective-permute-start.9) | collective-permute-done | bytes 262176 | tf_op jit(solution)/shard_map/hop_a1/ppermute | solution.py:32
  67.1 2.0 %collective-permute-start.10 = (bf16[256,512]{1,0:T(8,128)(2,1)S(1)}, bf16[256,512]{1,0:T(8,128)(2,1)S(1)}, u32[]{:S(2)}, u32[]{:S(2)}) collective-permute-start(bf16[256,512]{1,0:T(8,128)(2,1)S(1)} %collective-permute-done.9.refs_0_), channel_id=1, source_target_pairs={{0,8},{4,12},{8,16},{12,20},{16,24},{20,28},{24,32},{28,36},{32,40... | collective-permute-start | bytes 786440 | tf_op jit(solution)/shard_map/hop_a2/ppermute | solution.py:32
  69.2 3.4 %collective-permute-done.15.refs_2_ = bf16[256,512]{1,0:T(8,128)(2,1)S(1)} collective-permute-done((bf16[256,512]{1,0:T(8,128)(2,1)S(1)}, bf16[256,512]{1,0:T(8,128)(2,1)S(1)}, u32[]{:S(2)}, u32[]{:S(2)}) %collective-permute-start.15) | collective-permute-done | bytes 262176 | tf_op jit(solution)/shard_map/hop_b2/ppermute | solution.py:32
  72.6 1.4 %collective-permute-start.25 = (bf16[128,512]{1,0:T(8,128)(2,1)S(1)}, bf16[128,512]{1,0:T(8,128)(2,1)S(1)}, u32[]{:S(2)}, u32[]{:S(2)}) collective-permute-start(bf16[128,512]{1,0:T(8,128)(2,1)S(1)} %get-tuple-element.60), channel_id=1, source_target_pairs={{0,1},{1,2},{2,3},{3,0},{4,5},{5,6},{6,7},{7,4},{8,9},{9,10},{10,1... | collective-permute-start | bytes 393224 | tf_op jit(solution)/shard_map/ppermute | solution.py:37
  74.0 3.6 %collective-permute-start.26 = (bf16[128,512]{1,0:T(8,128)(2,1)S(1)}, bf16[128,512]{1,0:T(8,128)(2,1)S(1)}, u32[]{:S(2)}, u32[]{:S(2)}) collective-permute-start(bf16[128,512]{1,0:T(8,128)(2,1)S(1)} %get-tuple-element.59), channel_id=1, source_target_pairs={{0,2},{1,3},{2,0},{3,1},{4,6},{5,7},{6,4},{7,5},{8,10},{9,11},{10,... | collective-permute-start | bytes 393224 | tf_op jit(solution)/shard_map/ppermute | solution.py:37
  78.1 0.9 collective-permute-start.27
  79.0 0.8 collective-permute-done.10.refs_0_
  79.8 1.9 %collective-permute-start.16 = (bf16[256,512]{1,0:T(8,128)(2,1)S(1)}, bf16[256,512]{1,0:T(8,128)(2,1)S(1)}, u32[]{:S(2)}, u32[]{:S(2)}) collective-permute-start(bf16[256,512]{1,0:T(8,128)(2,1)S(1)} %collective-permute-done.15.refs_2_), channel_id=1, source_target_pairs={{0,8},{4,12},{8,16},{12,20},{16,24},{20,28},{24,32},{28,36},{32,40... | collective-permute-start | bytes 786440 | tf_op jit(solution)/shard_map/hop_b3/ppermute | solution.py:32
  81.9 0.9 collective-permute-done.26.refs_2_
  82.8 2.7 %collective-permute-start.11 = (bf16[256,512]{1,0:T(8,128)(2,1)S(1)}, bf16[256,512]{1,0:T(8,128)(2,1)S(1)}, u32[]{:S(2)}, u32[]{:S(2)}) collective-permute-start(bf16[256,512]{1,0:T(8,128)(2,1)S(1)} %collective-permute-done.10.refs_0_), channel_id=1, source_target_pairs={{0,8},{4,12},{8,16},{12,20},{16,24},{20,28},{24,32},{28,36},{32,40... | collective-permute-start | bytes 786440 | tf_op jit(solution)/shard_map/hop_a3/ppermute | solution.py:32
  85.4 3.5 %attend.8 = (f32[512,512]{1,0:T(8,128)S(1)}, f32[512,512]{1,0:T(8,128)S(1)}) custom-call(s32[21]{0:T(128)S(1)} %pad_add_fusion.1.meta, s32[512,128]{1,0:T(8,128)S(1)} %add.91.low_ref, bf16[512,512]{1,0:T(8,128)(2,1)S(1)} %project_q.1.q_ref, bf16[256,512]{1,0:T(8,128)(2,1)S(1)} %collective-permute-done.9.refs_0_, ...), custom_call_target="tpu_custom_call", output_to_operand_aliasing={{0}: (7, {}), {1}: (8, {})} | custom-call | flops 5120000000 | bytes 524288 | tf_op jit(solution)/shard_map/attend/pallas_call | solution.py:263
  88.9 2.2 %build_cache.1 = bf16[1,128,2,1024]{3,2,1,0:T(2,128)(2,1)} custom-call(s32[4]{0:T(128)S(1)} %and_select_fusion.shards, bf16[128,512]{1,0:T(8,128)(2,1)S(1)} %get-tuple-element.61.refs_0_, bf16[128,512]{1,0:T(8,128)(2,1)S(1)} %collective-permute-done.25.refs_1_, bf16[128,512]{1,0:T(8,128)(2,1)S(1)} %collective-permute-done.26.refs_2_, ...), custom_call_target="tpu_custom_call" | custom-call | flops 1000000000 | bytes 1000 | tf_op jit(solution)/shard_map/build_cache/pallas_call | solution.py:296
  91.1 1.9 %collective-permute-done.16.refs_2_ = bf16[256,512]{1,0:T(8,128)(2,1)S(1)} collective-permute-done((bf16[256,512]{1,0:T(8,128)(2,1)S(1)}, bf16[256,512]{1,0:T(8,128)(2,1)S(1)}, u32[]{:S(2)}, u32[]{:S(2)}) %collective-permute-start.16) | collective-permute-done | bytes 262176 | tf_op jit(solution)/shard_map/hop_b3/ppermute | solution.py:32
  93.0 2.7 %collective-permute-start.17 = (bf16[256,512]{1,0:T(8,128)(2,1)S(1)}, bf16[256,512]{1,0:T(8,128)(2,1)S(1)}, u32[]{:S(2)}, u32[]{:S(2)}) collective-permute-start(bf16[256,512]{1,0:T(8,128)(2,1)S(1)} %collective-permute-done.16.refs_2_), channel_id=1, source_target_pairs={{0,8},{4,12},{8,16},{12,20},{16,24},{20,28},{24,32},{28,36},{32,40... | collective-permute-start | bytes 786440 | tf_op jit(solution)/shard_map/hop_b4/ppermute | solution.py:32
  95.7 1.7 %collective-permute-done.11.refs_0_ = bf16[256,512]{1,0:T(8,128)(2,1)S(1)} collective-permute-done((bf16[256,512]{1,0:T(8,128)(2,1)S(1)}, bf16[256,512]{1,0:T(8,128)(2,1)S(1)}, u32[]{:S(2)}, u32[]{:S(2)}) %collective-permute-start.11) | collective-permute-done | bytes 262176 | tf_op jit(solution)/shard_map/hop_a3/ppermute | solution.py:32
  97.4 2.8 %collective-permute-start.12 = (bf16[256,512]{1,0:T(8,128)(2,1)S(1)}, bf16[256,512]{1,0:T(8,128)(2,1)S(1)}, u32[]{:S(2)}, u32[]{:S(2)}) collective-permute-start(bf16[256,512]{1,0:T(8,128)(2,1)S(1)} %collective-permute-done.11.refs_0_), channel_id=1, source_target_pairs={{0,8},{4,12},{8,16},{12,20},{16,24},{20,28},{24,32},{28,36},{32,40... | collective-permute-start | bytes 786440 | tf_op jit(solution)/shard_map/hop_a4/ppermute | solution.py:32
  100.2 3.5 %attend.9 = (f32[512,512]{1,0:T(8,128)S(1)}, f32[512,512]{1,0:T(8,128)S(1)}) custom-call(s32[21]{0:T(128)S(1)} %pad_add_fusion.1.meta, s32[512,128]{1,0:T(8,128)S(1)} %add.91.low_ref, bf16[512,512]{1,0:T(8,128)(2,1)S(1)} %project_q.1.q_ref, bf16[256,512]{1,0:T(8,128)(2,1)S(1)} %collective-permute-done.10.refs_0_, ...), custom_call_target="tpu_custom_call", output_to_operand_aliasing={{0}: (7, {}), {1}: (8, {})} | custom-call | flops 5120000000 | bytes 524288 | tf_op jit(solution)/shard_map/attend/pallas_call | solution.py:263
  103.7 3.5 %attend.10 = (f32[512,512]{1,0:T(8,128)S(1)}, f32[512,512]{1,0:T(8,128)S(1)}) custom-call(s32[21]{0:T(128)S(1)} %pad_add_fusion.1.meta, s32[512,128]{1,0:T(8,128)S(1)} %add.91.low_ref, bf16[512,512]{1,0:T(8,128)(2,1)S(1)} %project_q.1.q_ref, bf16[256,512]{1,0:T(8,128)(2,1)S(1)} %collective-permute-done.11.refs_0_, ...), custom_call_target="tpu_custom_call", output_to_operand_aliasing={{0}: (7, {}), {1}: (8, {})} | custom-call | flops 5120000000 | bytes 524288 | tf_op jit(solution)/shard_map/attend/pallas_call | solution.py:263
  107.5 3.9 %collective-permute-done.12.refs_0_ = bf16[256,512]{1,0:T(8,128)(2,1)S(1)} collective-permute-done((bf16[256,512]{1,0:T(8,128)(2,1)S(1)}, bf16[256,512]{1,0:T(8,128)(2,1)S(1)}, u32[]{:S(2)}, u32[]{:S(2)}) %collective-permute-start.12) | collective-permute-done | bytes 262176 | tf_op jit(solution)/shard_map/hop_a4/ppermute | solution.py:32
  111.4 2.1 %attend.11 = (f32[512,512]{1,0:T(8,128)S(1)}, f32[512,512]{1,0:T(8,128)S(1)}) custom-call(s32[21]{0:T(128)S(1)} %pad_add_fusion.1.meta, s32[512,128]{1,0:T(8,128)S(1)} %add.91.low_ref, bf16[512,512]{1,0:T(8,128)(2,1)S(1)} %project_q.1.q_ref, bf16[256,512]{1,0:T(8,128)(2,1)S(1)} %collective-permute-done.12.refs_0_, ...), custom_call_target="tpu_custom_call", output_to_operand_aliasing={{0}: (5, {}), {1}: (6, {})} | custom-call | flops 2560000000 | bytes 262144 | tf_op jit(solution)/shard_map/attend/pallas_call | solution.py:263
  113.5 3.4 %attend_last.1 = bf16[512,512]{1,0:T(8,128)(2,1)} custom-call(s32[21]{0:T(128)S(1)} %pad_add_fusion.1.meta, s32[512,128]{1,0:T(8,128)S(1)} %add.91.low_ref, bf16[512,512]{1,0:T(8,128)(2,1)S(1)} %project_q.1.q_ref, bf16[256,512]{1,0:T(8,128)(2,1)S(1)} %collective-permute-done.13.refs_0_, bf16[256,512]{1,0:T(8,128)(2,1)S(1)} %collective-permute-done.28.refs_1_, ...), custom_call_target="tpu_custom_call" | custom-call | flops 2560000000 | bytes 262144 | tf_op jit(solution)/shard_map/attend_last/pallas_call | solution.py:263
  (56 shorter events, 2.2 us)
Async XLA Ops:
  0.6 29.3 %collective-permute-start.4 = (bf16[512,1152]{1,0:T(8,128)(2,1)}, bf16[512,1152]{1,0:T(8,128)(2,1)S(1)}, u32[]{:S(2)}, u32[]{:S(2)}) collective-permute-start(bf16[512,1152]{1,0:T(8,128)(2,1)} %own.1), channel_id=1, source_target_pairs={{0,1},{1,2},{2,3},{3,0},{4,5},{5,6},{6,7},{7,4},{8,9},{9,10},{10,1... | collective-permute-start | bytes 3538952 | tf_op jit(solution)/shard_map/ppermute | solution.py:37
  2.3 27.7 %collective-permute-start.5 = (bf16[512,1152]{1,0:T(8,128)(2,1)}, bf16[512,1152]{1,0:T(8,128)(2,1)S(1)}, u32[]{:S(2)}, u32[]{:S(2)}) collective-permute-start(bf16[512,1152]{1,0:T(8,128)(2,1)} %own.1), channel_id=1, source_target_pairs={{0,3},{1,0},{2,1},{3,2},{4,7},{5,4},{6,5},{7,6},{8,11},{9,8},{10,9... | collective-permute-start | bytes 3538952 | tf_op jit(solution)/shard_map/ppermute | solution.py:37
  4.6 9.8 %collective-permute-start = (s32[1,512]{1,0:T(1,128)S(1)}, s32[1,512]{1,0:T(1,128)S(1)}, u32[]{:S(2)}, u32[]{:S(2)}) collective-permute-start(s32[1,512]{1,0:T(1,128)S(1)} %bitcast.26), channel_id=1, source_target_pairs={{0,4},{4,8},{8,12},{12,16},{16,20},{20,24},{24,28},{28,32},{32,36}... | collective-permute-start | bytes 6152 | tf_op jit(solution)/shard_map/ppermute | solution.py:32
  6.5 9.6 %collective-permute-start.1 = (s32[1,512]{1,0:T(1,128)S(1)}, s32[1,512]{1,0:T(1,128)S(1)}, u32[]{:S(2)}, u32[]{:S(2)}) collective-permute-start(s32[1,512]{1,0:T(1,128)S(1)} %bitcast.27), channel_id=1, source_target_pairs={{0,8},{4,12},{8,16},{12,20},{16,24},{20,28},{24,32},{28,36},{32,40... | collective-permute-start | bytes 6152 | tf_op jit(solution)/shard_map/ppermute | solution.py:32
  12.0 23.5 %collective-permute-start.8 = (f32[1,512]{1,0:T(1,128)S(1)}, f32[1,512]{1,0:T(1,128)S(1)}, u32[]{:S(2)}, u32[]{:S(2)}) collective-permute-start(f32[1,512]{1,0:T(1,128)S(1)} %bitcast.31), channel_id=1, source_target_pairs={{0,2},{1,3},{2,0},{3,1},{4,6},{5,7},{6,4},{7,5},{8,10},{9,11},{10,... | collective-permute-start | bytes 6152 | tf_op jit(solution)/shard_map/far_square/ppermute | solution.py:37
  16.1 10.0 %collective-permute-start.2 = (s32[3,512]{1,0:T(4,128)S(1)}, s32[3,512]{1,0:T(4,128)S(1)}, u32[]{:S(2)}, u32[]{:S(2)}) collective-permute-start(s32[3,512]{1,0:T(4,128)S(1)} %pad_add_fusion), channel_id=1, source_target_pairs={{0,12},{4,16},{8,20},{12,24},{16,28},{20,32},{24,36},{28,40},{32,4... | collective-permute-start | bytes 18440 | tf_op jit(solution)/shard_map/ppermute | solution.py:32
  19.4 9.5 %collective-permute-start.3 = (s32[3,512]{1,0:T(4,128)S(1)}, s32[3,512]{1,0:T(4,128)S(1)}, u32[]{:S(2)}, u32[]{:S(2)}) collective-permute-start(s32[3,512]{1,0:T(4,128)S(1)} %pad_add_fusion), channel_id=1, source_target_pairs={{0,24},{4,28},{8,32},{12,36},{16,40},{20,44},{24,48},{28,52},{32,5... | collective-permute-start | bytes 18440 | tf_op jit(solution)/shard_map/ppermute | solution.py:32
  28.9 6.7 %slice-start = ((s8[4718592]{0:T(1024)(128)(4,1)}), s8[4194304]{0:T(1024)(128)(4,1)S(1)}, s32[]{:S(2)}) async-start(s8[4718592]{0:T(1024)(128)(4,1)} %bitcast.24), calls=%async_computation | async-start | bytes 8388608
  28.9 5.5 %copy-start.4 = (f32[128]{0:T(128)S(1)}, f32[128]{0:T(128)}, u32[]{:S(2)}) copy-start(f32[128]{0:T(128)} %constant.76) | copy-start | bytes 1540
  28.9 6.7 %copy-start = (bf16[4608,256]{1,0:T(8,128)(2,1)S(1)}, bf16[4608,256]{1,0:T(8,128)(2,1)}, u32[]{:S(2)}) copy-start(bf16[4608,256]{1,0:T(8,128)(2,1)} %refs_4_.1) | copy-start | bytes 7077892
  28.9 6.7 %copy-start.1 = (bf16[4608,256]{1,0:T(8,128)(2,1)S(1)}, bf16[4608,256]{1,0:T(8,128)(2,1)}, u32[]{:S(2)}) copy-start(bf16[4608,256]{1,0:T(8,128)(2,1)} %refs_5_.1) | copy-start | bytes 7077892
  28.9 6.7 %copy-start.2 = (bf16[512,1152]{1,0:T(8,128)(2,1)S(1)}, bf16[512,1152]{1,0:T(8,128)(2,1)}, u32[]{:S(2)}) copy-start(bf16[512,1152]{1,0:T(8,128)(2,1)} %own.1) | copy-start | bytes 3538948
  28.9 6.7 %slice-start.1 = ((s8[4718592]{0:T(1024)(128)(4,1)}), s8[524288]{0:T(1024)(128)(4,1)S(1)}, s32[]{:S(2)}) async-start(s8[4718592]{0:T(1024)(128)(4,1)} %bitcast.24), calls=%async_computation.1 | async-start | bytes 1048576
  30.0 15.5 %collective-permute-start.6 = (bf16[256,1152]{1,0:T(8,128)(2,1)S(1)}, bf16[256,1152]{1,0:T(8,128)(2,1)S(1)}, u32[]{:S(2)}, u32[]{:S(2)}) collective-permute-start(bf16[256,1152]{1,0:T(8,128)(2,1)S(1)} %get-tuple-element.29), channel_id=1, source_target_pairs={{0,1},{1,2},{2,3},{3,0},{4,5},{5,6},{6,7},{7,4},{8,9},{9,10},{10,1... | collective-permute-start | bytes 1769480 | tf_op jit(solution)/shard_map/ppermute | solution.py:37
  32.7 13.7 %collective-permute-start.7 = (bf16[256,1152]{1,0:T(8,128)(2,1)S(1)}, bf16[256,1152]{1,0:T(8,128)(2,1)S(1)}, u32[]{:S(2)}, u32[]{:S(2)}) collective-permute-start(bf16[256,1152]{1,0:T(8,128)(2,1)S(1)} %get-tuple-element.31), channel_id=1, source_target_pairs={{0,3},{1,0},{2,1},{3,2},{4,7},{5,4},{6,5},{7,6},{8,11},{9,8},{10,9... | collective-permute-start | bytes 1769480 | tf_op jit(solution)/shard_map/ppermute | solution.py:37
  35.6 10.7 %copy-start.3 = (s32[1,4]{1,0:T(1,128)S(1)}, s32[1,4]{1,0:T(1,128)}, u32[]{:S(2)}) copy-start(s32[1,4]{1,0:T(1,128)} %param.14) | copy-start | bytes 52
  48.1 12.4 %collective-permute-start.14 = (bf16[256,512]{1,0:T(8,128)(2,1)S(1)}, bf16[256,512]{1,0:T(8,128)(2,1)S(1)}, u32[]{:S(2)}, u32[]{:S(2)}) collective-permute-start(bf16[256,512]{1,0:T(8,128)(2,1)S(1)} %get-tuple-element.38), channel_id=1, source_target_pairs={{0,8},{4,12},{8,16},{12,20},{16,24},{20,28},{24,32},{28,36},{32,40... | collective-permute-start | bytes 786440 | tf_op jit(solution)/shard_map/hop_b1/ppermute | solution.py:32
  53.6 20.3 %collective-permute-start.24 = (bf16[512,512]{1,0:T(8,128)(2,1)S(1)}, bf16[512,512]{1,0:T(8,128)(2,1)S(1)}, u32[]{:S(2)}, u32[]{:S(2)}) collective-permute-start(bf16[512,512]{1,0:T(8,128)(2,1)S(1)} %get-tuple-element.40.refs_0_), channel_id=1, source_target_pairs={{0,4},{4,0},{8,12},{12,8},{16,20},{20,16},{24,28},{28,24},{32,36},... | collective-permute-start | bytes 1572872 | tf_op jit(solution)/shard_map/cross_own/ppermute | solution.py:41
  53.7 13.4 %collective-permute-start.9 = (bf16[256,512]{1,0:T(8,128)(2,1)S(1)}, bf16[256,512]{1,0:T(8,128)(2,1)S(1)}, u32[]{:S(2)}, u32[]{:S(2)}) collective-permute-start(bf16[256,512]{1,0:T(8,128)(2,1)S(1)} %get-tuple-element.37), channel_id=1, source_target_pairs={{0,8},{4,12},{8,16},{12,20},{16,24},{20,28},{24,32},{28,36},{32,40... | collective-permute-start | bytes 786440 | tf_op jit(solution)/shard_map/hop_a1/ppermute | solution.py:32
  60.5 12.0 %collective-permute-start.15 = (bf16[256,512]{1,0:T(8,128)(2,1)S(1)}, bf16[256,512]{1,0:T(8,128)(2,1)S(1)}, u32[]{:S(2)}, u32[]{:S(2)}) collective-permute-start(bf16[256,512]{1,0:T(8,128)(2,1)S(1)} %collective-permute-done.14.refs_2_), channel_id=1, source_target_pairs={{0,8},{4,12},{8,16},{12,20},{16,24},{20,28},{24,32},{28,36},{32,40... | collective-permute-start | bytes 786440 | tf_op jit(solution)/shard_map/hop_b2/ppermute | solution.py:32
  64.4 14.6 %collective-permute-start.23 = (bf16[256,512]{1,0:T(8,128)(2,1)S(1)}, bf16[256,512]{1,0:T(8,128)(2,1)S(1)}, u32[]{:S(2)}, u32[]{:S(2)}) collective-permute-start(bf16[256,512]{1,0:T(8,128)(2,1)S(1)} %collective-permute-done.14.refs_2_), channel_id=1, source_target_pairs={{0,4},{4,0},{8,12},{12,8},{16,20},{20,16},{24,28},{28,24},{32,36},... | collective-permute-start | bytes 786440 | tf_op jit(solution)/shard_map/cross_b1/ppermute | solution.py:41
  67.1 11.0 %collective-permute-start.22 = (bf16[256,512]{1,0:T(8,128)(2,1)S(1)}, bf16[256,512]{1,0:T(8,128)(2,1)S(1)}, u32[]{:S(2)}, u32[]{:S(2)}) collective-permute-start(bf16[256,512]{1,0:T(8,128)(2,1)S(1)} %collective-permute-done.9.refs_0_), channel_id=1, source_target_pairs={{0,4},{4,0},{8,12},{12,8},{16,20},{20,16},{24,28},{28,24},{32,36},... | collective-permute-start | bytes 786440 | tf_op jit(solution)/shard_map/cross_a1/ppermute | solution.py:41
  67.1 12.7 %collective-permute-start.10 = (bf16[256,512]{1,0:T(8,128)(2,1)S(1)}, bf16[256,512]{1,0:T(8,128)(2,1)S(1)}, u32[]{:S(2)}, u32[]{:S(2)}) collective-permute-start(bf16[256,512]{1,0:T(8,128)(2,1)S(1)} %collective-permute-done.9.refs_0_), channel_id=1, source_target_pairs={{0,8},{4,12},{8,16},{12,20},{16,24},{20,28},{24,32},{28,36},{32,40... | collective-permute-start | bytes 786440 | tf_op jit(solution)/shard_map/hop_a2/ppermute | solution.py:32
  72.6 9.2 %collective-permute-start.25 = (bf16[128,512]{1,0:T(8,128)(2,1)S(1)}, bf16[128,512]{1,0:T(8,128)(2,1)S(1)}, u32[]{:S(2)}, u32[]{:S(2)}) collective-permute-start(bf16[128,512]{1,0:T(8,128)(2,1)S(1)} %get-tuple-element.60), channel_id=1, source_target_pairs={{0,1},{1,2},{2,3},{3,0},{4,5},{5,6},{6,7},{7,4},{8,9},{9,10},{10,1... | collective-permute-start | bytes 393224 | tf_op jit(solution)/shard_map/ppermute | solution.py:37
  74.0 8.8 %collective-permute-start.26 = (bf16[128,512]{1,0:T(8,128)(2,1)S(1)}, bf16[128,512]{1,0:T(8,128)(2,1)S(1)}, u32[]{:S(2)}, u32[]{:S(2)}) collective-permute-start(bf16[128,512]{1,0:T(8,128)(2,1)S(1)} %get-tuple-element.59), channel_id=1, source_target_pairs={{0,2},{1,3},{2,0},{3,1},{4,6},{5,7},{6,4},{7,5},{8,10},{9,11},{10,... | collective-permute-start | bytes 393224 | tf_op jit(solution)/shard_map/ppermute | solution.py:37
  78.1 10.8 %collective-permute-start.27 = (bf16[128,512]{1,0:T(8,128)(2,1)S(1)}, bf16[128,512]{1,0:T(8,128)(2,1)S(1)}, u32[]{:S(2)}, u32[]{:S(2)}) collective-permute-start(bf16[128,512]{1,0:T(8,128)(2,1)S(1)} %get-tuple-element.58), channel_id=1, source_target_pairs={{0,3},{1,0},{2,1},{3,2},{4,7},{5,4},{6,5},{7,6},{8,11},{9,8},{10,9... | collective-permute-start | bytes 393224 | tf_op jit(solution)/shard_map/ppermute | solution.py:37
  79.0 18.4 %collective-permute-start.21 = (bf16[256,512]{1,0:T(8,128)(2,1)S(1)}, bf16[256,512]{1,0:T(8,128)(2,1)S(1)}, u32[]{:S(2)}, u32[]{:S(2)}) collective-permute-start(bf16[256,512]{1,0:T(8,128)(2,1)S(1)} %collective-permute-done.15.refs_2_), channel_id=1, source_target_pairs={{0,4},{4,0},{8,12},{12,8},{16,20},{20,16},{24,28},{28,24},{32,36},... | collective-permute-start | bytes 786440 | tf_op jit(solution)/shard_map/cross_b2/ppermute | solution.py:41
  79.8 13.2 %collective-permute-start.16 = (bf16[256,512]{1,0:T(8,128)(2,1)S(1)}, bf16[256,512]{1,0:T(8,128)(2,1)S(1)}, u32[]{:S(2)}, u32[]{:S(2)}) collective-permute-start(bf16[256,512]{1,0:T(8,128)(2,1)S(1)} %collective-permute-done.15.refs_2_), channel_id=1, source_target_pairs={{0,8},{4,12},{8,16},{12,20},{16,24},{20,28},{24,32},{28,36},{32,40... | collective-permute-start | bytes 786440 | tf_op jit(solution)/shard_map/hop_b3/ppermute | solution.py:32
  81.8 18.4 %collective-permute-start.20 = (bf16[256,512]{1,0:T(8,128)(2,1)S(1)}, bf16[256,512]{1,0:T(8,128)(2,1)S(1)}, u32[]{:S(2)}, u32[]{:S(2)}) collective-permute-start(bf16[256,512]{1,0:T(8,128)(2,1)S(1)} %collective-permute-done.10.refs_0_), channel_id=1, source_target_pairs={{0,4},{4,0},{8,12},{12,8},{16,20},{20,16},{24,28},{28,24},{32,36},... | collective-permute-start | bytes 786440 | tf_op jit(solution)/shard_map/cross_a2/ppermute | solution.py:41
  82.8 14.6 %collective-permute-start.11 = (bf16[256,512]{1,0:T(8,128)(2,1)S(1)}, bf16[256,512]{1,0:T(8,128)(2,1)S(1)}, u32[]{:S(2)}, u32[]{:S(2)}) collective-permute-start(bf16[256,512]{1,0:T(8,128)(2,1)S(1)} %collective-permute-done.10.refs_0_), channel_id=1, source_target_pairs={{0,8},{4,12},{8,16},{12,20},{16,24},{20,28},{24,32},{28,36},{32,40... | collective-permute-start | bytes 786440 | tf_op jit(solution)/shard_map/hop_a3/ppermute | solution.py:32
  93.0 10.6 %collective-permute-start.19 = (bf16[256,512]{1,0:T(8,128)(2,1)S(1)}, bf16[256,512]{1,0:T(8,128)(2,1)S(1)}, u32[]{:S(2)}, u32[]{:S(2)}) collective-permute-start(bf16[256,512]{1,0:T(8,128)(2,1)S(1)} %collective-permute-done.16.refs_2_), channel_id=1, source_target_pairs={{0,4},{4,0},{8,12},{12,8},{16,20},{20,16},{24,28},{28,24},{32,36},... | collective-permute-start | bytes 786440 | tf_op jit(solution)/shard_map/cross_b3/ppermute | solution.py:41
  93.0 14.1 %collective-permute-start.17 = (bf16[256,512]{1,0:T(8,128)(2,1)S(1)}, bf16[256,512]{1,0:T(8,128)(2,1)S(1)}, u32[]{:S(2)}, u32[]{:S(2)}) collective-permute-start(bf16[256,512]{1,0:T(8,128)(2,1)S(1)} %collective-permute-done.16.refs_2_), channel_id=1, source_target_pairs={{0,8},{4,12},{8,16},{12,20},{16,24},{20,28},{24,32},{28,36},{32,40... | collective-permute-start | bytes 786440 | tf_op jit(solution)/shard_map/hop_b4/ppermute | solution.py:32
  97.4 6.3 %collective-permute-start.18 = (bf16[256,512]{1,0:T(8,128)(2,1)S(1)}, bf16[256,512]{1,0:T(8,128)(2,1)S(1)}, u32[]{:S(2)}, u32[]{:S(2)}) collective-permute-start(bf16[256,512]{1,0:T(8,128)(2,1)S(1)} %collective-permute-done.11.refs_0_), channel_id=1, source_target_pairs={{0,4},{4,0},{8,12},{12,8},{16,20},{20,16},{24,28},{28,24},{32,36},... | collective-permute-start | bytes 786440 | tf_op jit(solution)/shard_map/cross_a3/ppermute | solution.py:41
  97.4 14.0 %collective-permute-start.12 = (bf16[256,512]{1,0:T(8,128)(2,1)S(1)}, bf16[256,512]{1,0:T(8,128)(2,1)S(1)}, u32[]{:S(2)}, u32[]{:S(2)}) collective-permute-start(bf16[256,512]{1,0:T(8,128)(2,1)S(1)} %collective-permute-done.11.refs_0_), channel_id=1, source_target_pairs={{0,8},{4,12},{8,16},{12,20},{16,24},{20,28},{24,32},{28,36},{32,40... | collective-permute-start | bytes 786440 | tf_op jit(solution)/shard_map/hop_a4/ppermute | solution.py:32
  107.2 6.3 %collective-permute-start.28 = (bf16[256,512]{1,0:T(8,128)(2,1)S(1)}, bf16[256,512]{1,0:T(8,128)(2,1)S(1)}, u32[]{:S(2)}, u32[]{:S(2)}) collective-permute-start(bf16[256,512]{1,0:T(8,128)(2,1)S(1)} %collective-permute-done.17.refs_1_), channel_id=1, source_target_pairs={{0,4},{4,0},{8,12},{12,8},{16,20},{20,16},{24,28},{28,24},{32,36},... | collective-permute-start | bytes 786440 | tf_op jit(solution)/shard_map/cross_b4/ppermute | solution.py:41
  111.4 2.2 %collective-permute-start.13 = (bf16[256,512]{1,0:T(8,128)(2,1)S(1)}, bf16[256,512]{1,0:T(8,128)(2,1)S(1)}, u32[]{:S(2)}, u32[]{:S(2)}) collective-permute-start(bf16[256,512]{1,0:T(8,128)(2,1)S(1)} %collective-permute-done.12.refs_0_), channel_id=1, source_target_pairs={{0,4},{4,0},{8,12},{12,8},{16,20},{20,16},{24,28},{28,24},{32,36},... | collective-permute-start | bytes 786440 | tf_op jit(solution)/shard_map/cross_a4/ppermute | solution.py:41

commit v5 on v4

--- a/solution.py
+++ b/solution.py
@@ -165,7 +165,7 @@
         out_specs=whole(),
         compiler_params=pltpu.CompilerParams(vmem_limit_bytes=8 << 20),
         cost_estimate=pl.CostEstimate(
-            flops=10000000 * rows, transcendentals=0, bytes_accessed=rows * width
+            flops=1000000 * rows, transcendentals=0, bytes_accessed=rows * width
         ),
     )(shards, normed, wq, part, cos, sin)
 
@@ -270,7 +270,7 @@
         input_output_aliases=aliases,
         compiler_params=pltpu.CompilerParams(vmem_limit_bytes=8 << 20),
         cost_estimate=pl.CostEstimate(
-            flops=5000000 * keys,
+            flops=2000000 * keys,
             transcendentals=0,
             bytes_accessed=width * keys,
         ),
@@ -349,7 +349,16 @@
     with jax.named_scope("far_square"):
         far_square = turned(jnp.sum(wide * wide, axis=-1).reshape(1, tokens), "tp", 2)
     far_square = far_square.reshape(tokens, 1) + jnp.zeros((1, HD), jnp.float32)
+    first_token = place * tokens
+    steps = WIN // tokens // 2
+    core = place % 2
+    backs = [jnp.int32(2 * step) for step in range(steps + 1)]
+    backs += [2 * step - 1 + 2 * core for step in range(steps + 1)]
+    firsts = jnp.stack(backs) * -tokens + first_token
+    meta = jnp.concatenate([first_token.reshape(1), firsts, firsts + half])
+    later = 2 * (steps + 1)
     marked = (segment_ids + 1).reshape(1, tokens)
+    marked, meta = lax.optimization_barrier((marked, meta))
     near = jnp.concatenate(
         [marked, shifted(marked, "seq", 1), shifted(marked, "seq", 2)], axis=0
     )
@@ -357,21 +366,12 @@
         [near[1:], shifted(near, "seq", 3), shifted(near, "seq", 6)], axis=0
     ).reshape(1, -1)
     earlier = lax.optimization_barrier((earlier, forwarded))[0]
-    first_token = place * tokens
     own = segment_ids.reshape(tokens, 1) + 1
     before = jnp.sum((marked < own).astype(jnp.int32), axis=1, keepdims=True)
     same = jnp.sum((earlier == own).astype(jnp.int32), axis=1, keepdims=True)
     starts = first_token + before - same
     query_index = first_token + jnp.arange(tokens, dtype=jnp.int32)[:, None]
     low = jnp.maximum(starts, query_index - (WIN - 1)) + jnp.zeros((1, HD), jnp.int32)
-    steps = WIN // tokens // 2
-    core = place % 2
-    backs = [jnp.int32(2 * step) for step in range(steps + 1)]
-    backs += [2 * step - 1 + 2 * core for step in range(steps + 1)]
-    firsts = jnp.stack(backs) * -tokens + first_token
-    meta = jnp.concatenate([first_token.reshape(1), firsts, firsts + half])
-    later = 2 * (steps + 1)
-
     freqs = 10000.0 ** (-(jnp.arange(HD // 2, dtype=jnp.float32) * (2.0 / HD)))
     angles = (query_index - starts).astype(jnp.float32) * jnp.concatenate([freqs, freqs])[None, :]
     sign = np.where(np.arange(HD) < HD // 2, -1.0, 1.0).astype(np.float32)
@@ -389,23 +389,24 @@
     def after(value, *others):
         return lax.optimization_barrier((value, *others))[0]
 
-    def chain(name, block):
+    def chain(name, block, ahead):
         arrived = [block]
         for step in range(1, steps + 1):
+            moving = after(arrived[-1], ahead) if step == 2 else arrived[-1]
             with jax.named_scope(f"hop_{name}{step}"):
-                arrived.append(shifted(arrived[-1], "seq", 2))
+                arrived.append(shifted(moving, "seq", 2))
         return arrived
 
     def cross(name, block):
         with jax.named_scope(f"cross_{name}"):
             return swapped(block)
 
-    a = chain("a", a0)
-    b = chain("b", b0)
+    queries = project_q(shards, normed, w_query, q_part, cos, sin)
+    a = chain("a", a0, queries)
+    b = chain("b", b0, queries)
     look = functools.partial(attend, meta, low)
     straight = [1 + step for step in range(steps + 1)]
     over = [2 + steps + step for step in range(steps + 1)]
-    queries = project_q(shards, normed, w_query, q_part, cos, sin)
     crossed = cross("own", after(block, queries))
     state = look(queries, [(block, straight[0], 0)])
     state = look(queries, [(crossed, over[0], None)], state, guarded=True)

time: 118 us -> 125 us (1.059)
  waiting for transfers between devices: 28.3 us -> 33 us
  starting transfers between devices: 51.9 us -> 54.5 us
    ppermute x12, waiting for transfers between devices: 21.5 us -> 27.2 us  [shifted(): return lax.ppermute(block, axis, route)]
    ppermute x8, starting transfers between devices: 14.6 us -> 17.5 us  [turned(): lax.ppermute(block, axis, [(i, (i + distance) % count) for i in range(cou...]
    ppermute x12, starting transfers between devices: 36.7 us -> 35 us  [shifted(): return lax.ppermute(block, axis, route)]
    ppermute x9, starting transfers between devices: 0.58 us -> 1.97 us  [swapped(): lax.ppermute(block, 'seq', [(i, i ^ 1) for i in range(lax.axis_size('seq'...]
  transfers between devices with their start and end apart: 29 -> 29, of which waited for: 13 -> 12; matrix products, arithmetic and copies ran while one was open for 5% -> 5% of each run, Pallas kernels for 21% -> 20%
where the time goes in v5:
time: 125 us; the launch traced here: 124 us
  starting transfers between devices  54.5 us (44%)
  waiting for transfers between devices  33 us (26%)
  Pallas kernels  29.4 us (24%)
  other arithmetic  4.73 us (4%)
    ppermute x12, starting transfers between devices, shifted(): return lax.ppermute(block, axis, route)  35 us
    ppermute x12, waiting for transfers between devices, shifted(): return lax.ppermute(block, axis, route)  27.2 us
    pallas_call x7, Pallas kernels, attend(): pl.pallas_call(functools.partial(attend_kernel, places, first, last, guar...  17.9 us
    ppermute x8, starting transfers between devices, turned(): lax.ppermute(block, axis, [(i, (i + distance) % count) for i in range(cou...  17.5 us
    ppermute x8, waiting for transfers between devices, turned(): lax.ppermute(block, axis, [(i, (i + distance) % count) for i in range(cou...  5.83 us
    pallas_call x1, Pallas kernels, project_early(): pl.pallas_call(early_kernel, name='project_early', out_shape=tuple((jax.S...  5.78 us
  transfers between devices with their start and end apart: 29, of which 12 were waited for; matrix products, arithmetic and copies ran while one was open for 5% of the time, Pallas kernels for 20%

profile of v5, /device:TPU:6, one launch (start us, length us, event | category | flops | bytes accessed | tf_op | source)
XLA Modules:
  0.0 123.9 jit_solution(15470897609963999155)
XLA Ops:
  0.6 1.7 %collective-permute-start.4 = (bf16[512,1152]{1,0:T(8,128)(2,1)}, bf16[512,1152]{1,0:T(8,128)(2,1)S(1)}, u32[]{:S(2)}, u32[]{:S(2)}) collective-permute-start(bf16[512,1152]{1,0:T(8,128)(2,1)} %own.1), channel_id=1, source_target_pairs={{0,1},{1,2},{2,3},{3,0},{4,5},{5,6},{6,7},{7,4},{8,9},{9,10},{10,1... | collective-permute-start | bytes 3538952 | tf_op jit(solution)/shard_map/ppermute | solution.py:37
  2.3 1.7 %collective-permute-start.5 = (bf16[512,1152]{1,0:T(8,128)(2,1)}, bf16[512,1152]{1,0:T(8,128)(2,1)S(1)}, u32[]{:S(2)}, u32[]{:S(2)}) collective-permute-start(bf16[512,1152]{1,0:T(8,128)(2,1)} %own.1), channel_id=1, source_target_pairs={{0,3},{1,0},{2,1},{3,2},{4,7},{5,4},{6,5},{7,6},{8,11},{9,8},{10,9... | collective-permute-start | bytes 3538952 | tf_op jit(solution)/shard_map/ppermute | solution.py:37
  4.1 0.7 broadcast_add_fusion
  4.8 1.9 %collective-permute-start = (s32[1,512]{1,0:T(1,128)S(1)}, s32[1,512]{1,0:T(1,128)S(1)}, u32[]{:S(2)}, u32[]{:S(2)}) collective-permute-start(s32[1,512]{1,0:T(1,128)S(1)} %bitcast.27), channel_id=1, source_target_pairs={{0,4},{4,8},{8,12},{12,16},{16,20},{20,24},{24,28},{28,32},{32,36}... | collective-permute-start | bytes 6152 | tf_op jit(solution)/shard_map/ppermute | solution.py:32
  6.7 3.8 %collective-permute-start.1 = (s32[1,512]{1,0:T(1,128)S(1)}, s32[1,512]{1,0:T(1,128)S(1)}, u32[]{:S(2)}, u32[]{:S(2)}) collective-permute-start(s32[1,512]{1,0:T(1,128)S(1)} %bitcast.28), channel_id=1, source_target_pairs={{0,8},{4,12},{8,16},{12,20},{16,24},{20,28},{24,32},{28,36},{32,40... | collective-permute-start | bytes 6152 | tf_op jit(solution)/shard_map/ppermute | solution.py:32
  10.6 1.6 %multiply_reduce_fusion = f32[512]{0:T(512)S(1)} fusion(bf16[512,1152]{1,0:T(8,128)(2,1)} %own.1), kind=kLoop, calls=%fused_computation.1 | loop fusion | flops 1768960 | bytes 1181696 | tf_op jit(solution)/shard_map/far_square/reduce_sum | solution.py:350
  12.1 2.1 %collective-permute-start.8 = (f32[1,512]{1,0:T(1,128)S(1)}, f32[1,512]{1,0:T(1,128)S(1)}, u32[]{:S(2)}, u32[]{:S(2)}) collective-permute-start(f32[1,512]{1,0:T(1,128)S(1)} %bitcast.32), channel_id=1, source_target_pairs={{0,2},{1,3},{2,0},{3,1},{4,6},{5,7},{6,4},{7,5},{8,10},{9,11},{10,... | collective-permute-start | bytes 6152 | tf_op jit(solution)/shard_map/far_square/ppermute | solution.py:37
  14.5 1.8 %collective-permute-done.1 = s32[1,512]{1,0:T(1,128)S(1)} collective-permute-done((s32[1,512]{1,0:T(1,128)S(1)}, s32[1,512]{1,0:T(1,128)S(1)}, u32[]{:S(2)}, u32[]{:S(2)}) %collective-permute-start.1) | collective-permute-done | bytes 2080 | tf_op jit(solution)/shard_map/ppermute | solution.py:32
  16.3 3.1 %collective-permute-start.2 = (s32[3,512]{1,0:T(4,128)S(1)}, s32[3,512]{1,0:T(4,128)S(1)}, u32[]{:S(2)}, u32[]{:S(2)}) collective-permute-start(s32[3,512]{1,0:T(4,128)S(1)} %pad_add_fusion), channel_id=1, source_target_pairs={{0,12},{4,16},{8,20},{12,24},{16,28},{20,32},{24,36},{28,40},{32,4... | collective-permute-start | bytes 18440 | tf_op jit(solution)/shard_map/ppermute | solution.py:32
  19.5 5.9 %collective-permute-start.3 = (s32[3,512]{1,0:T(4,128)S(1)}, s32[3,512]{1,0:T(4,128)S(1)}, u32[]{:S(2)}, u32[]{:S(2)}) collective-permute-start(s32[3,512]{1,0:T(4,128)S(1)} %pad_add_fusion), channel_id=1, source_target_pairs={{0,24},{4,28},{8,32},{12,36},{16,40},{20,44},{24,48},{28,52},{32,5... | collective-permute-start | bytes 18440 | tf_op jit(solution)/shard_map/ppermute | solution.py:32
  25.4 0.7 reshape.55.gain.refs_3_
  26.2 2.7 %collective-permute-done.3 = s32[3,512]{1,0:T(4,128)S(1)} collective-permute-done((s32[3,512]{1,0:T(4,128)S(1)}, s32[3,512]{1,0:T(4,128)S(1)}, u32[]{:S(2)}, u32[]{:S(2)}) %collective-permute-start.3) | collective-permute-done | bytes 6176 | tf_op jit(solution)/shard_map/ppermute | solution.py:32
  29.0 0.9 collective-permute-done.4.left
  30.0 1.7 %collective-permute-start.6 = (bf16[256,1152]{1,0:T(8,128)(2,1)S(1)}, bf16[256,1152]{1,0:T(8,128)(2,1)S(1)}, u32[]{:S(2)}, u32[]{:S(2)}) collective-permute-start(bf16[256,1152]{1,0:T(8,128)(2,1)S(1)} %get-tuple-element.35), channel_id=1, source_target_pairs={{0,1},{1,2},{2,3},{3,0},{4,5},{5,6},{6,7},{7,4},{8,9},{9,10},{10,1... | collective-permute-start | bytes 1769480 | tf_op jit(solution)/shard_map/ppermute | solution.py:37
  31.7 1.0 convert_reduce_fusion
  32.7 1.7 %collective-permute-start.7 = (bf16[256,1152]{1,0:T(8,128)(2,1)S(1)}, bf16[256,1152]{1,0:T(8,128)(2,1)S(1)}, u32[]{:S(2)}, u32[]{:S(2)}) collective-permute-start(bf16[256,1152]{1,0:T(8,128)(2,1)S(1)} %get-tuple-element.37), channel_id=1, source_target_pairs={{0,3},{1,0},{2,1},{3,2},{4,7},{5,4},{6,5},{7,6},{8,11},{9,8},{10,9... | collective-permute-start | bytes 1769480 | tf_op jit(solution)/shard_map/ppermute | solution.py:37
  34.4 1.0 fusion
  35.6 5.8 %project_early.1 = (f32[512,128]{1,0:T(8,128)S(1)}, f32[512,512]{1,0:T(8,128)S(1)}, f32[512,256]{1,0:T(8,128)S(1)}, f32[512,256]{1,0:T(8,128)S(1)}) custom-call(s32[4]{0:T(128)S(1)} %and_select_fusion.shards, bf16[512,1152]{1,0:T(8,128)(2,1)S(1)} %copy-done.2, bf16[512,1152]{1,0:T(8,128)(2,1)S(1)} %collective-permute-done.4.left, ...), custom_call_target="tpu_custom_call" | custom-call | flops 3623878656 | bytes 3538944 | tf_op jit(solution)/shard_map/project_early/pallas_call | solution.py:82
  41.4 4.1 %collective-permute-done.6.refs_0_ = bf16[256,1152]{1,0:T(8,128)(2,1)S(1)} collective-permute-done((bf16[256,1152]{1,0:T(8,128)(2,1)S(1)}, bf16[256,1152]{1,0:T(8,128)(2,1)S(1)}, u32[]{:S(2)}, u32[]{:S(2)}) %collective-permute-start.6) | collective-permute-done | bytes 589856 | tf_op jit(solution)/shard_map/ppermute | solution.py:37
  45.6 0.8 collective-permute-done.7.refs_1_
  46.3 1.8 %project_kv.1 = (bf16[512,1152]{1,0:T(8,128)(2,1)S(1)}, bf16[512,512]{1,0:T(8,128)(2,1)S(1)}, bf16[256,512]{1,0:T(8,128)(2,1)S(1)}, bf16[256,512]{1,0:T(8,128)(2,1)S(1)}, bf16[4,128,512]{2,1,0:T(8,128)(2,1)S(1)}) custom-call(s32[4]{0:T(128)S(1)} %and_select_fusion.shards, s32[4]{0:T(128)S(1)} %bitcast.26, ...), custom_call_target="tpu_custom_call" | custom-call | flops 603979776 | bytes 1179648 | tf_op jit(solution)/shard_map/project_kv/pallas_call | solution.py:134
  48.1 4.0 %collective-permute-start.14 = (bf16[256,512]{1,0:T(8,128)(2,1)S(1)}, bf16[256,512]{1,0:T(8,128)(2,1)S(1)}, u32[]{:S(2)}, u32[]{:S(2)}) collective-permute-start(bf16[256,512]{1,0:T(8,128)(2,1)S(1)} %get-tuple-element.45), channel_id=1, source_target_pairs={{0,8},{4,12},{8,16},{12,20},{16,24},{20,28},{24,32},{28,36},{32,40... | collective-permute-start | bytes 786440 | tf_op jit(solution)/shard_map/hop_b1/ppermute | solution.py:32
  52.1 3.7 %collective-permute-start.9 = (bf16[256,512]{1,0:T(8,128)(2,1)S(1)}, bf16[256,512]{1,0:T(8,128)(2,1)S(1)}, u32[]{:S(2)}, u32[]{:S(2)}) collective-permute-start(bf16[256,512]{1,0:T(8,128)(2,1)S(1)} %get-tuple-element.43), channel_id=1, source_target_pairs={{0,8},{4,12},{8,16},{12,20},{16,24},{20,28},{24,32},{28,36},{32,40... | collective-permute-start | bytes 786440 | tf_op jit(solution)/shard_map/hop_a1/ppermute | solution.py:32
  55.8 1.6 %project_q.1.q_ref = bf16[512,512]{1,0:T(8,128)(2,1)S(1)} custom-call(s32[4]{0:T(128)S(1)} %and_select_fusion.shards, bf16[512,1152]{1,0:T(8,128)(2,1)S(1)} %get-tuple-element.41.normed, bf16[4608,512]{1,0:T(8,128)(2,1)S(1)} %bitcast.25, f32[512,512]{1,0:T(8,128)S(1)} %get-tuple-element.42.part, f32[512,128]{1,0:T(8,128)S(1)} %get-tuple-element.73.refs_8_.cos, ...), custom_call_target="tpu_custom_call" | custom-call | flops 512000000 | bytes 262144 | tf_op jit(solution)/shard_map/project_q/pallas_call | solution.py:160
  57.4 5.4 %collective-permute-done.14.refs_2_ = bf16[256,512]{1,0:T(8,128)(2,1)S(1)} collective-permute-done((bf16[256,512]{1,0:T(8,128)(2,1)S(1)}, bf16[256,512]{1,0:T(8,128)(2,1)S(1)}, u32[]{:S(2)}, u32[]{:S(2)}) %collective-permute-start.14) | collective-permute-done | bytes 262176 | tf_op jit(solution)/shard_map/hop_b1/ppermute | solution.py:32
  62.8 1.9 %collective-permute-start.15 = (bf16[256,512]{1,0:T(8,128)(2,1)S(1)}, bf16[256,512]{1,0:T(8,128)(2,1)S(1)}, u32[]{:S(2)}, u32[]{:S(2)}) collective-permute-start(bf16[256,512]{1,0:T(8,128)(2,1)S(1)} %collective-permute-done.14.refs_2_), channel_id=1, source_target_pairs={{0,8},{4,12},{8,16},{12,20},{16,24},{20,28},{24,32},{28,36},{32,40... | collective-permute-start | bytes 786440 | tf_op jit(solution)/shard_map/hop_b2/ppermute | solution.py:32
  65.0 2.6 %collective-permute-done.9.refs_0_ = bf16[256,512]{1,0:T(8,128)(2,1)S(1)} collective-permute-done((bf16[256,512]{1,0:T(8,128)(2,1)S(1)}, bf16[256,512]{1,0:T(8,128)(2,1)S(1)}, u32[]{:S(2)}, u32[]{:S(2)}) %collective-permute-start.9) | collective-permute-done | bytes 262176 | tf_op jit(solution)/shard_map/hop_a1/ppermute | solution.py:32
  67.6 1.9 %collective-permute-start.10 = (bf16[256,512]{1,0:T(8,128)(2,1)S(1)}, bf16[256,512]{1,0:T(8,128)(2,1)S(1)}, u32[]{:S(2)}, u32[]{:S(2)}) collective-permute-start(bf16[256,512]{1,0:T(8,128)(2,1)S(1)} %collective-permute-done.9.refs_0_), channel_id=1, source_target_pairs={{0,8},{4,12},{8,16},{12,20},{16,24},{20,28},{24,32},{28,36},{32,40... | collective-permute-start | bytes 786440 | tf_op jit(solution)/shard_map/hop_a2/ppermute | solution.py:32
  70.1 3.1 %collective-permute-done.15.refs_2_ = bf16[256,512]{1,0:T(8,128)(2,1)S(1)} collective-permute-done((bf16[256,512]{1,0:T(8,128)(2,1)S(1)}, bf16[256,512]{1,0:T(8,128)(2,1)S(1)}, u32[]{:S(2)}, u32[]{:S(2)}) %collective-permute-start.15) | collective-permute-done | bytes 262176 | tf_op jit(solution)/shard_map/hop_b2/ppermute | solution.py:32
  73.2 1.4 %collective-permute-start.25 = (bf16[128,512]{1,0:T(8,128)(2,1)S(1)}, bf16[128,512]{1,0:T(8,128)(2,1)S(1)}, u32[]{:S(2)}, u32[]{:S(2)}) collective-permute-start(bf16[128,512]{1,0:T(8,128)(2,1)S(1)} %get-tuple-element.68), channel_id=1, source_target_pairs={{0,1},{1,2},{2,3},{3,0},{4,5},{5,6},{6,7},{7,4},{8,9},{9,10},{10,1... | collective-permute-start | bytes 393224 | tf_op jit(solution)/shard_map/ppermute | solution.py:37
  74.7 3.7 %collective-permute-start.26 = (bf16[128,512]{1,0:T(8,128)(2,1)S(1)}, bf16[128,512]{1,0:T(8,128)(2,1)S(1)}, u32[]{:S(2)}, u32[]{:S(2)}) collective-permute-start(bf16[128,512]{1,0:T(8,128)(2,1)S(1)} %get-tuple-element.67), channel_id=1, source_target_pairs={{0,2},{1,3},{2,0},{3,1},{4,6},{5,7},{6,4},{7,5},{8,10},{9,11},{10,... | collective-permute-start | bytes 393224 | tf_op jit(solution)/shard_map/ppermute | solution.py:37
  78.5 1.8 %attend.6 = (f32[512,512]{1,0:T(8,128)S(1)}, f32[512,512]{1,0:T(8,128)S(1)}) custom-call(s32[21]{0:T(128)S(1)} %pad_add_fusion.1.meta, s32[512,128]{1,0:T(8,128)S(1)} %add.91.low_ref, bf16[512,512]{1,0:T(8,128)(2,1)S(1)} %project_q.1.q_ref, bf16[512,512]{1,0:T(8,128)(2,1)S(1)} %get-tuple-element.48.refs_0_), custom_call_target="tpu_custom_call" | custom-call | flops 1024000000 | bytes 262144 | tf_op jit(solution)/shard_map/attend/pallas_call | solution.py:263
  80.3 1.9 %collective-permute-start.16 = (bf16[256,512]{1,0:T(8,128)(2,1)S(1)}, bf16[256,512]{1,0:T(8,128)(2,1)S(1)}, u32[]{:S(2)}, u32[]{:S(2)}) collective-permute-start(bf16[256,512]{1,0:T(8,128)(2,1)S(1)} %collective-permute-done.15.refs_2_), channel_id=1, source_target_pairs={{0,8},{4,12},{8,16},{12,20},{16,24},{20,28},{24,32},{28,36},{32,40... | collective-permute-start | bytes 786440 | tf_op jit(solution)/shard_map/hop_b3/ppermute | solution.py:32
  82.3 2.0 %collective-permute-start.11 = (bf16[256,512]{1,0:T(8,128)(2,1)S(1)}, bf16[256,512]{1,0:T(8,128)(2,1)S(1)}, u32[]{:S(2)}, u32[]{:S(2)}) collective-permute-start(bf16[256,512]{1,0:T(8,128)(2,1)S(1)} %collective-permute-done.10.refs_0_), channel_id=1, source_target_pairs={{0,8},{4,12},{8,16},{12,20},{16,24},{20,28},{24,32},{28,36},{32,40... | collective-permute-start | bytes 786440 | tf_op jit(solution)/shard_map/hop_a3/ppermute | solution.py:32
  84.8 3.6 %collective-permute-start.27 = (bf16[128,512]{1,0:T(8,128)(2,1)S(1)}, bf16[128,512]{1,0:T(8,128)(2,1)S(1)}, u32[]{:S(2)}, u32[]{:S(2)}) collective-permute-start(bf16[128,512]{1,0:T(8,128)(2,1)S(1)} %get-tuple-element.66), channel_id=1, source_target_pairs={{0,3},{1,0},{2,1},{3,2},{4,7},{5,4},{6,5},{7,6},{8,11},{9,8},{10,9... | collective-permute-start | bytes 393224 | tf_op jit(solution)/shard_map/ppermute | solution.py:37
  88.4 1.0 collective-permute-start.21
  89.5 3.4 %attend.8 = (f32[512,512]{1,0:T(8,128)S(1)}, f32[512,512]{1,0:T(8,128)S(1)}) custom-call(s32[21]{0:T(128)S(1)} %pad_add_fusion.1.meta, s32[512,128]{1,0:T(8,128)S(1)} %add.91.low_ref, bf16[512,512]{1,0:T(8,128)(2,1)S(1)} %project_q.1.q_ref, bf16[256,512]{1,0:T(8,128)(2,1)S(1)} %collective-permute-done.9.refs_0_, ...), custom_call_target="tpu_custom_call", output_to_operand_aliasing={{0}: (7, {}), {1}: (8, {})} | custom-call | flops 2048000000 | bytes 524288 | tf_op jit(solution)/shard_map/attend/pallas_call | solution.py:263
  92.9 0.6 collective-permute-done.16.refs_2_
  93.6 4.3 %collective-permute-done.11.refs_0_ = bf16[256,512]{1,0:T(8,128)(2,1)S(1)} collective-permute-done((bf16[256,512]{1,0:T(8,128)(2,1)S(1)}, bf16[256,512]{1,0:T(8,128)(2,1)S(1)}, u32[]{:S(2)}, u32[]{:S(2)}) %collective-permute-start.11) | collective-permute-done | bytes 262176 | tf_op jit(solution)/shard_map/hop_a3/ppermute | solution.py:32
  97.9 2.2 %build_cache.1 = bf16[1,128,2,1024]{3,2,1,0:T(2,128)(2,1)} custom-call(s32[4]{0:T(128)S(1)} %and_select_fusion.shards, bf16[128,512]{1,0:T(8,128)(2,1)S(1)} %get-tuple-element.69.refs_0_, bf16[128,512]{1,0:T(8,128)(2,1)S(1)} %collective-permute-done.25.refs_1_, bf16[128,512]{1,0:T(8,128)(2,1)S(1)} %collective-permute-done.26.refs_2_, ...), custom_call_target="tpu_custom_call" | custom-call | flops 1000000000 | bytes 1000 | tf_op jit(solution)/shard_map/build_cache/pallas_call | solution.py:296
  100.1 1.9 %collective-permute-start.17 = (bf16[256,512]{1,0:T(8,128)(2,1)S(1)}, bf16[256,512]{1,0:T(8,128)(2,1)S(1)}, u32[]{:S(2)}, u32[]{:S(2)}) collective-permute-start(bf16[256,512]{1,0:T(8,128)(2,1)S(1)} %collective-permute-done.16.refs_2_), channel_id=1, source_target_pairs={{0,8},{4,12},{8,16},{12,20},{16,24},{20,28},{24,32},{28,36},{32,40... | collective-permute-start | bytes 786440 | tf_op jit(solution)/shard_map/hop_b4/ppermute | solution.py:32
  102.0 2.9 %collective-permute-start.12 = (bf16[256,512]{1,0:T(8,128)(2,1)S(1)}, bf16[256,512]{1,0:T(8,128)(2,1)S(1)}, u32[]{:S(2)}, u32[]{:S(2)}) collective-permute-start(bf16[256,512]{1,0:T(8,128)(2,1)S(1)} %collective-permute-done.11.refs_0_), channel_id=1, source_target_pairs={{0,8},{4,12},{8,16},{12,20},{16,24},{20,28},{24,32},{28,36},{32,40... | collective-permute-start | bytes 786440 | tf_op jit(solution)/shard_map/hop_a4/ppermute | solution.py:32
  104.9 3.4 %attend.9 = (f32[512,512]{1,0:T(8,128)S(1)}, f32[512,512]{1,0:T(8,128)S(1)}) custom-call(s32[21]{0:T(128)S(1)} %pad_add_fusion.1.meta, s32[512,128]{1,0:T(8,128)S(1)} %add.91.low_ref, bf16[512,512]{1,0:T(8,128)(2,1)S(1)} %project_q.1.q_ref, bf16[256,512]{1,0:T(8,128)(2,1)S(1)} %collective-permute-done.10.refs_0_, ...), custom_call_target="tpu_custom_call", output_to_operand_aliasing={{0}: (7, {}), {1}: (8, {})} | custom-call | flops 2048000000 | bytes 524288 | tf_op jit(solution)/shard_map/attend/pallas_call | solution.py:263
  108.3 3.4 %attend.10 = (f32[512,512]{1,0:T(8,128)S(1)}, f32[512,512]{1,0:T(8,128)S(1)}) custom-call(s32[21]{0:T(128)S(1)} %pad_add_fusion.1.meta, s32[512,128]{1,0:T(8,128)S(1)} %add.91.low_ref, bf16[512,512]{1,0:T(8,128)(2,1)S(1)} %project_q.1.q_ref, bf16[256,512]{1,0:T(8,128)(2,1)S(1)} %collective-permute-done.11.refs_0_, ...), custom_call_target="tpu_custom_call", output_to_operand_aliasing={{0}: (7, {}), {1}: (8, {})} | custom-call | flops 2048000000 | bytes 524288 | tf_op jit(solution)/shard_map/attend/pallas_call | solution.py:263
  111.7 1.4 %collective-permute-done.17.refs_1_ = bf16[256,512]{1,0:T(8,128)(2,1)S(1)} collective-permute-done((bf16[256,512]{1,0:T(8,128)(2,1)S(1)}, bf16[256,512]{1,0:T(8,128)(2,1)S(1)}, u32[]{:S(2)}, u32[]{:S(2)}) %collective-permute-start.17) | collective-permute-done | bytes 262176 | tf_op jit(solution)/shard_map/hop_b4/ppermute | solution.py:32
  113.2 5.2 %collective-permute-done.12.refs_0_ = bf16[256,512]{1,0:T(8,128)(2,1)S(1)} collective-permute-done((bf16[256,512]{1,0:T(8,128)(2,1)S(1)}, bf16[256,512]{1,0:T(8,128)(2,1)S(1)}, u32[]{:S(2)}, u32[]{:S(2)}) %collective-permute-start.12) | collective-permute-done | bytes 262176 | tf_op jit(solution)/shard_map/hop_a4/ppermute | solution.py:32
  118.4 2.1 %attend.11 = (f32[512,512]{1,0:T(8,128)S(1)}, f32[512,512]{1,0:T(8,128)S(1)}) custom-call(s32[21]{0:T(128)S(1)} %pad_add_fusion.1.meta, s32[512,128]{1,0:T(8,128)S(1)} %add.91.low_ref, bf16[512,512]{1,0:T(8,128)(2,1)S(1)} %project_q.1.q_ref, bf16[256,512]{1,0:T(8,128)(2,1)S(1)} %collective-permute-done.12.refs_0_, ...), custom_call_target="tpu_custom_call", output_to_operand_aliasing={{0}: (5, {}), {1}: (6, {})} | custom-call | flops 1024000000 | bytes 262144 | tf_op jit(solution)/shard_map/attend/pallas_call | solution.py:263
  120.5 3.3 %attend_last.1 = bf16[512,512]{1,0:T(8,128)(2,1)} custom-call(s32[21]{0:T(128)S(1)} %pad_add_fusion.1.meta, s32[512,128]{1,0:T(8,128)S(1)} %add.91.low_ref, bf16[512,512]{1,0:T(8,128)(2,1)S(1)} %project_q.1.q_ref, bf16[256,512]{1,0:T(8,128)(2,1)S(1)} %collective-permute-done.13.refs_0_, bf16[256,512]{1,0:T(8,128)(2,1)S(1)} %collective-permute-done.28.refs_1_, ...), custom_call_target="tpu_custom_call" | custom-call | flops 1024000000 | bytes 262144 | tf_op jit(solution)/shard_map/attend_last/pallas_call | solution.py:263
  (56 shorter events, 2.6 us)
Async XLA Ops:
  0.6 29.3 %collective-permute-start.4 = (bf16[512,1152]{1,0:T(8,128)(2,1)}, bf16[512,1152]{1,0:T(8,128)(2,1)S(1)}, u32[]{:S(2)}, u32[]{:S(2)}) collective-permute-start(bf16[512,1152]{1,0:T(8,128)(2,1)} %own.1), channel_id=1, source_target_pairs={{0,1},{1,2},{2,3},{3,0},{4,5},{5,6},{6,7},{7,4},{8,9},{9,10},{10,1... | collective-permute-start | bytes 3538952 | tf_op jit(solution)/shard_map/ppermute | solution.py:37
  2.3 27.7 %collective-permute-start.5 = (bf16[512,1152]{1,0:T(8,128)(2,1)}, bf16[512,1152]{1,0:T(8,128)(2,1)S(1)}, u32[]{:S(2)}, u32[]{:S(2)}) collective-permute-start(bf16[512,1152]{1,0:T(8,128)(2,1)} %own.1), channel_id=1, source_target_pairs={{0,3},{1,0},{2,1},{3,2},{4,7},{5,4},{6,5},{7,6},{8,11},{9,8},{10,9... | collective-permute-start | bytes 3538952 | tf_op jit(solution)/shard_map/ppermute | solution.py:37
  4.8 9.7 %collective-permute-start = (s32[1,512]{1,0:T(1,128)S(1)}, s32[1,512]{1,0:T(1,128)S(1)}, u32[]{:S(2)}, u32[]{:S(2)}) collective-permute-start(s32[1,512]{1,0:T(1,128)S(1)} %bitcast.27), channel_id=1, source_target_pairs={{0,4},{4,8},{8,12},{12,16},{16,20},{20,24},{24,28},{28,32},{32,36}... | collective-permute-start | bytes 6152 | tf_op jit(solution)/shard_map/ppermute | solution.py:32
  6.7 9.6 %collective-permute-start.1 = (s32[1,512]{1,0:T(1,128)S(1)}, s32[1,512]{1,0:T(1,128)S(1)}, u32[]{:S(2)}, u32[]{:S(2)}) collective-permute-start(s32[1,512]{1,0:T(1,128)S(1)} %bitcast.28), channel_id=1, source_target_pairs={{0,8},{4,12},{8,16},{12,20},{16,24},{20,28},{24,32},{28,36},{32,40... | collective-permute-start | bytes 6152 | tf_op jit(solution)/shard_map/ppermute | solution.py:32
  12.1 23.3 %collective-permute-start.8 = (f32[1,512]{1,0:T(1,128)S(1)}, f32[1,512]{1,0:T(1,128)S(1)}, u32[]{:S(2)}, u32[]{:S(2)}) collective-permute-start(f32[1,512]{1,0:T(1,128)S(1)} %bitcast.32), channel_id=1, source_target_pairs={{0,2},{1,3},{2,0},{3,1},{4,6},{5,7},{6,4},{7,5},{8,10},{9,11},{10,... | collective-permute-start | bytes 6152 | tf_op jit(solution)/shard_map/far_square/ppermute | solution.py:37
  16.3 9.9 %collective-permute-start.2 = (s32[3,512]{1,0:T(4,128)S(1)}, s32[3,512]{1,0:T(4,128)S(1)}, u32[]{:S(2)}, u32[]{:S(2)}) collective-permute-start(s32[3,512]{1,0:T(4,128)S(1)} %pad_add_fusion), channel_id=1, source_target_pairs={{0,12},{4,16},{8,20},{12,24},{16,28},{20,32},{24,36},{28,40},{32,4... | collective-permute-start | bytes 18440 | tf_op jit(solution)/shard_map/ppermute | solution.py:32
  19.5 9.5 %collective-permute-start.3 = (s32[3,512]{1,0:T(4,128)S(1)}, s32[3,512]{1,0:T(4,128)S(1)}, u32[]{:S(2)}, u32[]{:S(2)}) collective-permute-start(s32[3,512]{1,0:T(4,128)S(1)} %pad_add_fusion), channel_id=1, source_target_pairs={{0,24},{4,28},{8,32},{12,36},{16,40},{20,44},{24,48},{28,52},{32,5... | collective-permute-start | bytes 18440 | tf_op jit(solution)/shard_map/ppermute | solution.py:32
  28.9 6.6 %slice-start = ((s8[4718592]{0:T(1024)(128)(4,1)}), s8[4194304]{0:T(1024)(128)(4,1)S(1)}, s32[]{:S(2)}) async-start(s8[4718592]{0:T(1024)(128)(4,1)} %bitcast.24), calls=%async_computation | async-start | bytes 8388608
  29.0 5.5 %copy-start.4 = (f32[128]{0:T(128)S(1)}, f32[128]{0:T(128)}, u32[]{:S(2)}) copy-start(f32[128]{0:T(128)} %constant.76) | copy-start | bytes 1540
  29.0 6.6 %slice-start.1 = ((s8[4718592]{0:T(1024)(128)(4,1)}), s8[524288]{0:T(1024)(128)(4,1)S(1)}, s32[]{:S(2)}) async-start(s8[4718592]{0:T(1024)(128)(4,1)} %bitcast.24), calls=%async_computation.1 | async-start | bytes 1048576
  29.0 6.6 %copy-start = (bf16[4608,256]{1,0:T(8,128)(2,1)S(1)}, bf16[4608,256]{1,0:T(8,128)(2,1)}, u32[]{:S(2)}) copy-start(bf16[4608,256]{1,0:T(8,128)(2,1)} %refs_4_.1) | copy-start | bytes 7077892
  29.0 6.6 %copy-start.1 = (bf16[4608,256]{1,0:T(8,128)(2,1)S(1)}, bf16[4608,256]{1,0:T(8,128)(2,1)}, u32[]{:S(2)}) copy-start(bf16[4608,256]{1,0:T(8,128)(2,1)} %refs_5_.1) | copy-start | bytes 7077892
  29.0 6.6 %copy-start.2 = (bf16[512,1152]{1,0:T(8,128)(2,1)S(1)}, bf16[512,1152]{1,0:T(8,128)(2,1)}, u32[]{:S(2)}) copy-start(bf16[512,1152]{1,0:T(8,128)(2,1)} %own.1) | copy-start | bytes 3538948
  30.0 15.5 %collective-permute-start.6 = (bf16[256,1152]{1,0:T(8,128)(2,1)S(1)}, bf16[256,1152]{1,0:T(8,128)(2,1)S(1)}, u32[]{:S(2)}, u32[]{:S(2)}) collective-permute-start(bf16[256,1152]{1,0:T(8,128)(2,1)S(1)} %get-tuple-element.35), channel_id=1, source_target_pairs={{0,1},{1,2},{2,3},{3,0},{4,5},{5,6},{6,7},{7,4},{8,9},{9,10},{10,1... | collective-permute-start | bytes 1769480 | tf_op jit(solution)/shard_map/ppermute | solution.py:37
  32.7 13.7 %collective-permute-start.7 = (bf16[256,1152]{1,0:T(8,128)(2,1)S(1)}, bf16[256,1152]{1,0:T(8,128)(2,1)S(1)}, u32[]{:S(2)}, u32[]{:S(2)}) collective-permute-start(bf16[256,1152]{1,0:T(8,128)(2,1)S(1)} %get-tuple-element.37), channel_id=1, source_target_pairs={{0,3},{1,0},{2,1},{3,2},{4,7},{5,4},{6,5},{7,6},{8,11},{9,8},{10,9... | collective-permute-start | bytes 1769480 | tf_op jit(solution)/shard_map/ppermute | solution.py:37
  35.6 10.7 %copy-start.3 = (s32[1,4]{1,0:T(1,128)S(1)}, s32[1,4]{1,0:T(1,128)}, u32[]{:S(2)}) copy-start(s32[1,4]{1,0:T(1,128)} %param.14) | copy-start | bytes 52
  48.1 14.7 %collective-permute-start.14 = (bf16[256,512]{1,0:T(8,128)(2,1)S(1)}, bf16[256,512]{1,0:T(8,128)(2,1)S(1)}, u32[]{:S(2)}, u32[]{:S(2)}) collective-permute-start(bf16[256,512]{1,0:T(8,128)(2,1)S(1)} %get-tuple-element.45), channel_id=1, source_target_pairs={{0,8},{4,12},{8,16},{12,20},{16,24},{20,28},{24,32},{28,36},{32,40... | collective-permute-start | bytes 786440 | tf_op jit(solution)/shard_map/hop_b1/ppermute | solution.py:32
  52.1 15.5 %collective-permute-start.9 = (bf16[256,512]{1,0:T(8,128)(2,1)S(1)}, bf16[256,512]{1,0:T(8,128)(2,1)S(1)}, u32[]{:S(2)}, u32[]{:S(2)}) collective-permute-start(bf16[256,512]{1,0:T(8,128)(2,1)S(1)} %get-tuple-element.43), channel_id=1, source_target_pairs={{0,8},{4,12},{8,16},{12,20},{16,24},{20,28},{24,32},{28,36},{32,40... | collective-permute-start | bytes 786440 | tf_op jit(solution)/shard_map/hop_a1/ppermute | solution.py:32
  62.8 10.4 %collective-permute-start.15 = (bf16[256,512]{1,0:T(8,128)(2,1)S(1)}, bf16[256,512]{1,0:T(8,128)(2,1)S(1)}, u32[]{:S(2)}, u32[]{:S(2)}) collective-permute-start(bf16[256,512]{1,0:T(8,128)(2,1)S(1)} %collective-permute-done.14.refs_2_), channel_id=1, source_target_pairs={{0,8},{4,12},{8,16},{12,20},{16,24},{20,28},{24,32},{28,36},{32,40... | collective-permute-start | bytes 786440 | tf_op jit(solution)/shard_map/hop_b2/ppermute | solution.py:32
  64.8 17.5 %collective-permute-start.24 = (bf16[512,512]{1,0:T(8,128)(2,1)S(1)}, bf16[512,512]{1,0:T(8,128)(2,1)S(1)}, u32[]{:S(2)}, u32[]{:S(2)}) collective-permute-start(bf16[512,512]{1,0:T(8,128)(2,1)S(1)} %get-tuple-element.48.refs_0_), channel_id=1, source_target_pairs={{0,4},{4,0},{8,12},{12,8},{16,20},{20,16},{24,28},{28,24},{32,36},... | collective-permute-start | bytes 1572872 | tf_op jit(solution)/shard_map/cross_own/ppermute | solution.py:41
  67.6 7.1 %collective-permute-start.22 = (bf16[256,512]{1,0:T(8,128)(2,1)S(1)}, bf16[256,512]{1,0:T(8,128)(2,1)S(1)}, u32[]{:S(2)}, u32[]{:S(2)}) collective-permute-start(bf16[256,512]{1,0:T(8,128)(2,1)S(1)} %collective-permute-done.9.refs_0_), channel_id=1, source_target_pairs={{0,4},{4,0},{8,12},{12,8},{16,20},{20,16},{24,28},{28,24},{32,36},... | collective-permute-start | bytes 786440 | tf_op jit(solution)/shard_map/cross_a1/ppermute | solution.py:41
  67.6 12.7 %collective-permute-start.10 = (bf16[256,512]{1,0:T(8,128)(2,1)S(1)}, bf16[256,512]{1,0:T(8,128)(2,1)S(1)}, u32[]{:S(2)}, u32[]{:S(2)}) collective-permute-start(bf16[256,512]{1,0:T(8,128)(2,1)S(1)} %collective-permute-done.9.refs_0_), channel_id=1, source_target_pairs={{0,8},{4,12},{8,16},{12,20},{16,24},{20,28},{24,32},{28,36},{32,40... | collective-permute-start | bytes 786440 | tf_op jit(solution)/shard_map/hop_a2/ppermute | solution.py:32
  69.5 15.3 %collective-permute-start.23 = (bf16[256,512]{1,0:T(8,128)(2,1)S(1)}, bf16[256,512]{1,0:T(8,128)(2,1)S(1)}, u32[]{:S(2)}, u32[]{:S(2)}) collective-permute-start(bf16[256,512]{1,0:T(8,128)(2,1)S(1)} %collective-permute-done.14.refs_2_), channel_id=1, source_target_pairs={{0,4},{4,0},{8,12},{12,8},{16,20},{20,16},{24,28},{28,24},{32,36},... | collective-permute-start | bytes 786440 | tf_op jit(solution)/shard_map/cross_b1/ppermute | solution.py:41
  73.2 15.2 %collective-permute-start.25 = (bf16[128,512]{1,0:T(8,128)(2,1)S(1)}, bf16[128,512]{1,0:T(8,128)(2,1)S(1)}, u32[]{:S(2)}, u32[]{:S(2)}) collective-permute-start(bf16[128,512]{1,0:T(8,128)(2,1)S(1)} %get-tuple-element.68), channel_id=1, source_target_pairs={{0,1},{1,2},{2,3},{3,0},{4,5},{5,6},{6,7},{7,4},{8,9},{9,10},{10,1... | collective-permute-start | bytes 393224 | tf_op jit(solution)/shard_map/ppermute | solution.py:37
  74.7 14.8 %collective-permute-start.26 = (bf16[128,512]{1,0:T(8,128)(2,1)S(1)}, bf16[128,512]{1,0:T(8,128)(2,1)S(1)}, u32[]{:S(2)}, u32[]{:S(2)}) collective-permute-start(bf16[128,512]{1,0:T(8,128)(2,1)S(1)} %get-tuple-element.67), channel_id=1, source_target_pairs={{0,2},{1,3},{2,0},{3,1},{4,6},{5,7},{6,4},{7,5},{8,10},{9,11},{10,... | collective-permute-start | bytes 393224 | tf_op jit(solution)/shard_map/ppermute | solution.py:37
  80.3 13.2 %collective-permute-start.16 = (bf16[256,512]{1,0:T(8,128)(2,1)S(1)}, bf16[256,512]{1,0:T(8,128)(2,1)S(1)}, u32[]{:S(2)}, u32[]{:S(2)}) collective-permute-start(bf16[256,512]{1,0:T(8,128)(2,1)S(1)} %collective-permute-done.15.refs_2_), channel_id=1, source_target_pairs={{0,8},{4,12},{8,16},{12,20},{16,24},{20,28},{24,32},{28,36},{32,40... | collective-permute-start | bytes 786440 | tf_op jit(solution)/shard_map/hop_b3/ppermute | solution.py:32
  82.3 15.6 %collective-permute-start.11 = (bf16[256,512]{1,0:T(8,128)(2,1)S(1)}, bf16[256,512]{1,0:T(8,128)(2,1)S(1)}, u32[]{:S(2)}, u32[]{:S(2)}) collective-permute-start(bf16[256,512]{1,0:T(8,128)(2,1)S(1)} %collective-permute-done.10.refs_0_), channel_id=1, source_target_pairs={{0,8},{4,12},{8,16},{12,20},{16,24},{20,28},{24,32},{28,36},{32,40... | collective-permute-start | bytes 786440 | tf_op jit(solution)/shard_map/hop_a3/ppermute | solution.py:32
  84.8 13.0 %collective-permute-start.27 = (bf16[128,512]{1,0:T(8,128)(2,1)S(1)}, bf16[128,512]{1,0:T(8,128)(2,1)S(1)}, u32[]{:S(2)}, u32[]{:S(2)}) collective-permute-start(bf16[128,512]{1,0:T(8,128)(2,1)S(1)} %get-tuple-element.66), channel_id=1, source_target_pairs={{0,3},{1,0},{2,1},{3,2},{4,7},{5,4},{6,5},{7,6},{8,11},{9,8},{10,9... | collective-permute-start | bytes 393224 | tf_op jit(solution)/shard_map/ppermute | solution.py:37
  88.4 13.5 %collective-permute-start.21 = (bf16[256,512]{1,0:T(8,128)(2,1)S(1)}, bf16[256,512]{1,0:T(8,128)(2,1)S(1)}, u32[]{:S(2)}, u32[]{:S(2)}) collective-permute-start(bf16[256,512]{1,0:T(8,128)(2,1)S(1)} %collective-permute-done.15.refs_2_), channel_id=1, source_target_pairs={{0,4},{4,0},{8,12},{12,8},{16,20},{20,16},{24,28},{28,24},{32,36},... | collective-permute-start | bytes 786440 | tf_op jit(solution)/shard_map/cross_b2/ppermute | solution.py:41
  89.5 15.5 %collective-permute-start.20 = (bf16[256,512]{1,0:T(8,128)(2,1)S(1)}, bf16[256,512]{1,0:T(8,128)(2,1)S(1)}, u32[]{:S(2)}, u32[]{:S(2)}) collective-permute-start(bf16[256,512]{1,0:T(8,128)(2,1)S(1)} %collective-permute-done.10.refs_0_), channel_id=1, source_target_pairs={{0,4},{4,0},{8,12},{12,8},{16,20},{20,16},{24,28},{28,24},{32,36},... | collective-permute-start | bytes 786440 | tf_op jit(solution)/shard_map/cross_a2/ppermute | solution.py:41
  93.6 14.8 %collective-permute-start.19 = (bf16[256,512]{1,0:T(8,128)(2,1)S(1)}, bf16[256,512]{1,0:T(8,128)(2,1)S(1)}, u32[]{:S(2)}, u32[]{:S(2)}) collective-permute-start(bf16[256,512]{1,0:T(8,128)(2,1)S(1)} %collective-permute-done.16.refs_2_), channel_id=1, source_target_pairs={{0,4},{4,0},{8,12},{12,8},{16,20},{20,16},{24,28},{28,24},{32,36},... | collective-permute-start | bytes 786440 | tf_op jit(solution)/shard_map/cross_b3/ppermute | solution.py:41
  97.9 10.5 %collective-permute-start.18 = (bf16[256,512]{1,0:T(8,128)(2,1)S(1)}, bf16[256,512]{1,0:T(8,128)(2,1)S(1)}, u32[]{:S(2)}, u32[]{:S(2)}) collective-permute-start(bf16[256,512]{1,0:T(8,128)(2,1)S(1)} %collective-permute-done.11.refs_0_), channel_id=1, source_target_pairs={{0,4},{4,0},{8,12},{12,8},{16,20},{20,16},{24,28},{28,24},{32,36},... | collective-permute-start | bytes 786440 | tf_op jit(solution)/shard_map/cross_a3/ppermute | solution.py:41
  100.1 13.1 %collective-permute-start.17 = (bf16[256,512]{1,0:T(8,128)(2,1)S(1)}, bf16[256,512]{1,0:T(8,128)(2,1)S(1)}, u32[]{:S(2)}, u32[]{:S(2)}) collective-permute-start(bf16[256,512]{1,0:T(8,128)(2,1)S(1)} %collective-permute-done.16.refs_2_), channel_id=1, source_target_pairs={{0,8},{4,12},{8,16},{12,20},{16,24},{20,28},{24,32},{28,36},{32,40... | collective-permute-start | bytes 786440 | tf_op jit(solution)/shard_map/hop_b4/ppermute | solution.py:32
  102.0 16.4 %collective-permute-start.12 = (bf16[256,512]{1,0:T(8,128)(2,1)S(1)}, bf16[256,512]{1,0:T(8,128)(2,1)S(1)}, u32[]{:S(2)}, u32[]{:S(2)}) collective-permute-start(bf16[256,512]{1,0:T(8,128)(2,1)S(1)} %collective-permute-done.11.refs_0_), channel_id=1, source_target_pairs={{0,8},{4,12},{8,16},{12,20},{16,24},{20,28},{24,32},{28,36},{32,40... | collective-permute-start | bytes 786440 | tf_op jit(solution)/shard_map/hop_a4/ppermute | solution.py:32
  113.2 7.3 %collective-permute-start.28 = (bf16[256,512]{1,0:T(8,128)(2,1)S(1)}, bf16[256,512]{1,0:T(8,128)(2,1)S(1)}, u32[]{:S(2)}, u32[]{:S(2)}) collective-permute-start(bf16[256,512]{1,0:T(8,128)(2,1)S(1)} %collective-permute-done.17.refs_1_), channel_id=1, source_target_pairs={{0,4},{4,0},{8,12},{12,8},{16,20},{20,16},{24,28},{28,24},{32,36},... | collective-permute-start | bytes 786440 | tf_op jit(solution)/shard_map/cross_b4/ppermute | solution.py:41
  118.4 2.1 %collective-permute-start.13 = (bf16[256,512]{1,0:T(8,128)(2,1)S(1)}, bf16[256,512]{1,0:T(8,128)(2,1)S(1)}, u32[]{:S(2)}, u32[]{:S(2)}) collective-permute-start(bf16[256,512]{1,0:T(8,128)(2,1)S(1)} %collective-permute-done.12.refs_0_), channel_id=1, source_target_pairs={{0,4},{4,0},{8,12},{12,8},{16,20},{20,16},{24,28},{28,24},{32,36},... | collective-permute-start | bytes 786440 | tf_op jit(solution)/shard_map/cross_a4/ppermute | solution.py:41

commit v6 on v4

--- a/solution.py
+++ b/solution.py
@@ -270,7 +270,7 @@
         input_output_aliases=aliases,
         compiler_params=pltpu.CompilerParams(vmem_limit_bytes=8 << 20),
         cost_estimate=pl.CostEstimate(
-            flops=5000000 * keys,
+            flops=10000000 * keys,
             transcendentals=0,
             bytes_accessed=width * keys,
         ),
@@ -389,19 +389,18 @@
     def after(value, *others):
         return lax.optimization_barrier((value, *others))[0]
 
-    def chain(name, block):
-        arrived = [block]
-        for step in range(1, steps + 1):
-            with jax.named_scope(f"hop_{name}{step}"):
-                arrived.append(shifted(arrived[-1], "seq", 2))
-        return arrived
+    def hop(name, block, distance):
+        with jax.named_scope(f"hop_{name}"):
+            return shifted(block, "seq", distance)
 
     def cross(name, block):
         with jax.named_scope(f"cross_{name}"):
             return swapped(block)
 
-    a = chain("a", a0)
-    b = chain("b", b0)
+    arrived = [block]
+    for step in range(1, steps):
+        arrived.append(hop(step, arrived[-1], 2))
+    arrived.append(hop("direct", block, 2 * steps))
     look = functools.partial(attend, meta, low)
     straight = [1 + step for step in range(steps + 1)]
     over = [2 + steps + step for step in range(steps + 1)]
@@ -409,23 +408,19 @@
     crossed = cross("own", after(block, queries))
     state = look(queries, [(block, straight[0], 0)])
     state = look(queries, [(crossed, over[0], None)], state, guarded=True)
-    for step in range(1, steps):
-        near, far = straight[step], over[step]
-        parts = [
-            (a[step], near, None),
-            (cross(f"a{step}", a[step]), far, None),
-            (b[step], near + later, None),
-            (cross(f"b{step}", b[step]), far + later, None),
-        ]
-        state = look(queries, parts, state)
-    kv_cache = exchange_pages(shards, after(pages, b[2]))
-    near, far = straight[steps], over[steps]
-    edge = [
-        (cross(f"a{steps}", a[steps]), far, None),
-        (cross(f"b{steps}", after(b[steps], *state, kv_cache)), far + later, None),
-    ]
-    state = look(queries, [(a[steps], near, None), (b[steps], near + later, None)], state)
-    attended = look(queries, edge, state, last=True, guarded=True)
+    kv_cache = exchange_pages(shards, after(pages, arrived[1]))
+    for step in range(1, steps - 1):
+        crossed = cross(step, arrived[step])
+        state = look(queries, [(arrived[step], straight[step], None)], state)
+        if step == steps - 2:
+            far_block = after(arrived[steps], *state)
+        state = look(queries, [(crossed, over[step], None)], state)
+    crossed = cross(steps, far_block)
+    state = look(queries, [(far_block, straight[steps], None)], state)
+    state = look(queries, [(crossed, over[steps], None)], state, guarded=True)
+    crossed = cross(steps - 1, after(arrived[steps - 1], kv_cache))
+    state = look(queries, [(arrived[steps - 1], straight[steps - 1], None)], state)
+    attended = look(queries, [(crossed, over[steps - 1], None)], state, last=True)
     return (attended, kv_cache)
 
 

time: 118 us -> 152 us (1.29)
  waiting for transfers between devices: 28.3 us -> 67.2 us
  starting transfers between devices: 51.9 us -> 44.8 us
  Pallas kernels: 29.7 us -> 32.2 us
    ppermute x12 -> x8, waiting for transfers between devices: 21.5 us -> 51.6 us  [shifted(): return lax.ppermute(block, axis, route)]
    ppermute x8, waiting for transfers between devices: 6.84 us -> 15.7 us  [turned(): lax.ppermute(block, axis, [(i, (i + distance) % count) for i in range(cou...]
    ppermute x12 -> x8, starting transfers between devices: 36.7 us -> 30 us  [shifted(): return lax.ppermute(block, axis, route)]
    pallas_call x7 -> x10, Pallas kernels: 18.2 us -> 20.1 us  [attend(): pl.pallas_call(functools.partial(attend_kernel, places, first, last, guar...]
  transfers between devices with their start and end apart: 29 -> 21, of which waited for: 13 -> 8; matrix products, arithmetic and copies ran while one was open for 5% -> 3% of each run, Pallas kernels for 21% -> 18%
where the time goes in v6:
time: 152 us; the launch traced here: 151 us
  waiting for transfers between devices  67.2 us (44%)
  starting transfers between devices  44.8 us (29%)
  Pallas kernels  32.2 us (21%)
  other arithmetic  4.76 us (3%)
    ppermute x8, waiting for transfers between devices, shifted(): return lax.ppermute(block, axis, route)  51.6 us
    ppermute x8, starting transfers between devices, shifted(): return lax.ppermute(block, axis, route)  30 us
    pallas_call x10, Pallas kernels, attend(): pl.pallas_call(functools.partial(attend_kernel, places, first, last, guar...  20.1 us
    ppermute x8, waiting for transfers between devices, turned(): lax.ppermute(block, axis, [(i, (i + distance) % count) for i in range(cou...  15.7 us
    ppermute x8, starting transfers between devices, turned(): lax.ppermute(block, axis, [(i, (i + distance) % count) for i in range(cou...  13.9 us
    pallas_call x1, Pallas kernels, project_early(): pl.pallas_call(early_kernel, name='project_early', out_shape=tuple((jax.S...  5.76 us
  transfers between devices with their start and end apart: 21, of which 8 were waited for; matrix products, arithmetic and copies ran while one was open for 3% of the time, Pallas kernels for 18%

profile of v6, /device:TPU:6, one launch (start us, length us, event | category | flops | bytes accessed | tf_op | source)
XLA Modules:
  0.0 151.2 jit_solution(13144044836518540763)
XLA Ops:
  0.6 0.7 broadcast_add_fusion
  1.3 1.9 %collective-permute-start = (s32[1,512]{1,0:T(1,128)S(1)}, s32[1,512]{1,0:T(1,128)S(1)}, u32[]{:S(2)}, u32[]{:S(2)}) collective-permute-start(s32[1,512]{1,0:T(1,128)S(1)} %bitcast.26), channel_id=1, source_target_pairs={{0,4},{4,8},{8,12},{12,16},{16,20},{20,24},{24,28},{28,32},{32,36}... | collective-permute-start | bytes 6152 | tf_op jit(solution)/shard_map/ppermute | solution.py:32
  3.2 3.8 %collective-permute-start.1 = (s32[1,512]{1,0:T(1,128)S(1)}, s32[1,512]{1,0:T(1,128)S(1)}, u32[]{:S(2)}, u32[]{:S(2)}) collective-permute-start(s32[1,512]{1,0:T(1,128)S(1)} %bitcast.27), channel_id=1, source_target_pairs={{0,8},{4,12},{8,16},{12,20},{16,24},{20,28},{24,32},{28,36},{32,40... | collective-permute-start | bytes 6152 | tf_op jit(solution)/shard_map/ppermute | solution.py:32
  7.1 1.7 %collective-permute-start.4 = (bf16[512,1152]{1,0:T(8,128)(2,1)}, bf16[512,1152]{1,0:T(8,128)(2,1)S(1)}, u32[]{:S(2)}, u32[]{:S(2)}) collective-permute-start(bf16[512,1152]{1,0:T(8,128)(2,1)} %own.1), channel_id=1, source_target_pairs={{0,1},{1,2},{2,3},{3,0},{4,5},{5,6},{6,7},{7,4},{8,9},{9,10},{10,1... | collective-permute-start | bytes 3538952 | tf_op jit(solution)/shard_map/ppermute | solution.py:37
  8.7 1.7 %collective-permute-start.5 = (bf16[512,1152]{1,0:T(8,128)(2,1)}, bf16[512,1152]{1,0:T(8,128)(2,1)S(1)}, u32[]{:S(2)}, u32[]{:S(2)}) collective-permute-start(bf16[512,1152]{1,0:T(8,128)(2,1)} %own.1), channel_id=1, source_target_pairs={{0,3},{1,0},{2,1},{3,2},{4,7},{5,4},{6,5},{7,6},{8,11},{9,8},{10,9... | collective-permute-start | bytes 3538952 | tf_op jit(solution)/shard_map/ppermute | solution.py:37
  10.4 1.6 %multiply_reduce_fusion = f32[512]{0:T(512)S(1)} fusion(bf16[512,1152]{1,0:T(8,128)(2,1)} %own.1), kind=kLoop, calls=%fused_computation.1 | loop fusion | flops 1768960 | bytes 1181696 | tf_op jit(solution)/shard_map/far_square/reduce_sum | solution.py:350
  12.0 2.1 %collective-permute-start.8 = (f32[1,512]{1,0:T(1,128)S(1)}, f32[1,512]{1,0:T(1,128)S(1)}, u32[]{:S(2)}, u32[]{:S(2)}) collective-permute-start(f32[1,512]{1,0:T(1,128)S(1)} %bitcast.31), channel_id=1, source_target_pairs={{0,2},{1,3},{2,0},{3,1},{4,6},{5,7},{6,4},{7,5},{8,10},{9,11},{10,... | collective-permute-start | bytes 6152 | tf_op jit(solution)/shard_map/far_square/ppermute | solution.py:37
  14.2 0.3 convert_reduce_fusion.1
  14.6 4.3 %collective-permute-start.2 = (s32[3,512]{1,0:T(4,128)S(1)}, s32[3,512]{1,0:T(4,128)S(1)}, u32[]{:S(2)}, u32[]{:S(2)}) collective-permute-start(s32[3,512]{1,0:T(4,128)S(1)} %pad_add_fusion), channel_id=1, source_target_pairs={{0,12},{4,16},{8,20},{12,24},{16,28},{20,32},{24,36},{28,40},{32,4... | collective-permute-start | bytes 18440 | tf_op jit(solution)/shard_map/ppermute | solution.py:32
  18.9 5.9 %collective-permute-start.3 = (s32[3,512]{1,0:T(4,128)S(1)}, s32[3,512]{1,0:T(4,128)S(1)}, u32[]{:S(2)}, u32[]{:S(2)}) collective-permute-start(s32[3,512]{1,0:T(4,128)S(1)} %pad_add_fusion), channel_id=1, source_target_pairs={{0,24},{4,28},{8,32},{12,36},{16,40},{20,44},{24,48},{28,52},{32,5... | collective-permute-start | bytes 18440 | tf_op jit(solution)/shard_map/ppermute | solution.py:32
  24.9 0.7 reshape.56.gain.refs_3_
  25.7 2.7 %collective-permute-done.3 = s32[3,512]{1,0:T(4,128)S(1)} collective-permute-done((s32[3,512]{1,0:T(4,128)S(1)}, s32[3,512]{1,0:T(4,128)S(1)}, u32[]{:S(2)}, u32[]{:S(2)}) %collective-permute-start.3) | collective-permute-done | bytes 6176 | tf_op jit(solution)/shard_map/ppermute | solution.py:32
  28.5 8.1 %collective-permute-done.4.left = bf16[512,1152]{1,0:T(8,128)(2,1)S(1)} collective-permute-done((bf16[512,1152]{1,0:T(8,128)(2,1)}, bf16[512,1152]{1,0:T(8,128)(2,1)S(1)}, u32[]{:S(2)}, u32[]{:S(2)}) %collective-permute-start.4) | collective-permute-done | bytes 1179680 | tf_op jit(solution)/shard_map/ppermute | solution.py:37
  36.6 0.8 collective-permute-done.5.right
  37.4 1.7 %collective-permute-start.6 = (bf16[256,1152]{1,0:T(8,128)(2,1)S(1)}, bf16[256,1152]{1,0:T(8,128)(2,1)S(1)}, u32[]{:S(2)}, u32[]{:S(2)}) collective-permute-start(bf16[256,1152]{1,0:T(8,128)(2,1)S(1)} %get-tuple-element.34), channel_id=1, source_target_pairs={{0,1},{1,2},{2,3},{3,0},{4,5},{5,6},{6,7},{7,4},{8,9},{9,10},{10,1... | collective-permute-start | bytes 1769480 | tf_op jit(solution)/shard_map/ppermute | solution.py:37
  39.1 1.0 convert_reduce_fusion
  40.1 1.7 %collective-permute-start.7 = (bf16[256,1152]{1,0:T(8,128)(2,1)S(1)}, bf16[256,1152]{1,0:T(8,128)(2,1)S(1)}, u32[]{:S(2)}, u32[]{:S(2)}) collective-permute-start(bf16[256,1152]{1,0:T(8,128)(2,1)S(1)} %get-tuple-element.36), channel_id=1, source_target_pairs={{0,3},{1,0},{2,1},{3,2},{4,7},{5,4},{6,5},{7,6},{8,11},{9,8},{10,9... | collective-permute-start | bytes 1769480 | tf_op jit(solution)/shard_map/ppermute | solution.py:37
  41.8 1.0 fusion
  42.9 0.1 add.96.far_square
  43.1 5.8 %project_early.1 = (f32[512,128]{1,0:T(8,128)S(1)}, f32[512,512]{1,0:T(8,128)S(1)}, f32[512,256]{1,0:T(8,128)S(1)}, f32[512,256]{1,0:T(8,128)S(1)}) custom-call(s32[4]{0:T(128)S(1)} %and_select_fusion.shards, bf16[512,1152]{1,0:T(8,128)(2,1)S(1)} %copy-done.2, bf16[512,1152]{1,0:T(8,128)(2,1)S(1)} %collective-permute-done.4.left, ...), custom_call_target="tpu_custom_call" | custom-call | flops 3623878656 | bytes 3538944 | tf_op jit(solution)/shard_map/project_early/pallas_call | solution.py:82
  48.8 5.7 %collective-permute-done.6.refs_0_ = bf16[256,1152]{1,0:T(8,128)(2,1)S(1)} collective-permute-done((bf16[256,1152]{1,0:T(8,128)(2,1)S(1)}, bf16[256,1152]{1,0:T(8,128)(2,1)S(1)}, u32[]{:S(2)}, u32[]{:S(2)}) %collective-permute-start.6) | collective-permute-done | bytes 589856 | tf_op jit(solution)/shard_map/ppermute | solution.py:37
  54.5 1.1 collective-permute-done.7.refs_1_
  55.7 2.5 %project_kv.1 = (bf16[512,1152]{1,0:T(8,128)(2,1)S(1)}, bf16[512,512]{1,0:T(8,128)(2,1)S(1)}, bf16[256,512]{1,0:T(8,128)(2,1)}, bf16[256,512]{1,0:T(8,128)(2,1)}, bf16[4,128,512]{2,1,0:T(8,128)(2,1)S(1)}) custom-call(s32[4]{0:T(128)S(1)} %and_select_fusion.shards, s32[4]{0:T(128)S(1)} %bitcast.23, bf16[256,1152]{1,0:T(8,128)(2,1)S(1)} %collective-permute-done.6.refs_0_, ...), custom_call_target="tpu_custom_call" | custom-call | flops 603979776 | bytes 1179648 | tf_op jit(solution)/shard_map/project_kv/pallas_call | solution.py:134
  58.1 3.8 %collective-permute-start.9 = (bf16[512,512]{1,0:T(8,128)(2,1)S(1)}, bf16[512,512]{1,0:T(8,128)(2,1)S(1)}, u32[]{:S(2)}, u32[]{:S(2)}) collective-permute-start(bf16[512,512]{1,0:T(8,128)(2,1)S(1)} %get-tuple-element.46.refs_0_), channel_id=1, source_target_pairs={{0,8},{4,12},{8,16},{12,20},{16,24},{20,28},{24,32},{28,36},{32,40... | collective-permute-start | bytes 1572872 | tf_op jit(solution)/shard_map/hop_1/ppermute | solution.py:32
  62.0 1.6 %project_q.1.q_ref = bf16[512,512]{1,0:T(8,128)(2,1)S(1)} custom-call(s32[4]{0:T(128)S(1)} %and_select_fusion.shards, bf16[512,1152]{1,0:T(8,128)(2,1)S(1)} %get-tuple-element.40.normed, bf16[4608,512]{1,0:T(8,128)(2,1)S(1)} %bitcast.25, f32[512,512]{1,0:T(8,128)S(1)} %get-tuple-element.41.part, f32[512,128]{1,0:T(8,128)S(1)} %get-tuple-element.75.refs_8_.cos, ...), custom_call_target="tpu_custom_call" | custom-call | flops 5120000000 | bytes 262144 | tf_op jit(solution)/shard_map/project_q/pallas_call | solution.py:160
  63.6 0.3 collective-permute-start.18
  63.9 0.1 add.91.low_ref
  64.0 1.8 %attend.9 = (f32[512,512]{1,0:T(8,128)S(1)}, f32[512,512]{1,0:T(8,128)S(1)}) custom-call(s32[21]{0:T(128)S(1)} %pad_add_fusion.1.meta, s32[512,128]{1,0:T(8,128)S(1)} %add.91.low_ref, bf16[512,512]{1,0:T(8,128)(2,1)S(1)} %project_q.1.q_ref, bf16[512,512]{1,0:T(8,128)(2,1)S(1)} %get-tuple-element.46.refs_0_), custom_call_target="tpu_custom_call" | custom-call | flops 5120000000 | bytes 262144 | tf_op jit(solution)/shard_map/attend/pallas_call | solution.py:263
  65.8 9.6 %collective-permute-done.9.refs_0_ = bf16[512,512]{1,0:T(8,128)(2,1)S(1)} collective-permute-done((bf16[512,512]{1,0:T(8,128)(2,1)S(1)}, bf16[512,512]{1,0:T(8,128)(2,1)S(1)}, u32[]{:S(2)}, u32[]{:S(2)}) %collective-permute-start.9) | collective-permute-done | bytes 524320 | tf_op jit(solution)/shard_map/hop_1/ppermute | solution.py:32
  75.5 0.8 collective-permute-start.12
  76.2 3.7 %collective-permute-start.13 = (bf16[128,512]{1,0:T(8,128)(2,1)S(1)}, bf16[128,512]{1,0:T(8,128)(2,1)S(1)}, u32[]{:S(2)}, u32[]{:S(2)}) collective-permute-start(bf16[128,512]{1,0:T(8,128)(2,1)S(1)} %get-tuple-element.69), channel_id=1, source_target_pairs={{0,2},{1,3},{2,0},{3,1},{4,6},{5,7},{6,4},{7,5},{8,10},{9,11},{10,... | collective-permute-start | bytes 393224 | tf_op jit(solution)/shard_map/ppermute | solution.py:37
  79.9 0.7 collective-permute-start.14
  80.6 1.9 %collective-permute-start.10 = (bf16[512,512]{1,0:T(8,128)(2,1)S(1)}, bf16[512,512]{1,0:T(8,128)(2,1)S(1)}, u32[]{:S(2)}, u32[]{:S(2)}) collective-permute-start(bf16[512,512]{1,0:T(8,128)(2,1)S(1)} %collective-permute-done.9.refs_0_), channel_id=1, source_target_pairs={{0,8},{4,12},{8,16},{12,20},{16,24},{20,28},{24,32},{28,36},{32,40... | collective-permute-start | bytes 1572872 | tf_op jit(solution)/shard_map/hop_2/ppermute | solution.py:32
  82.5 0.6 attend.10
  83.1 2.1 %attend.11 = (f32[512,512]{1,0:T(8,128)S(1)}, f32[512,512]{1,0:T(8,128)S(1)}) custom-call(s32[21]{0:T(128)S(1)} %pad_add_fusion.1.meta, s32[512,128]{1,0:T(8,128)S(1)} %add.91.low_ref, bf16[512,512]{1,0:T(8,128)(2,1)S(1)} %project_q.1.q_ref, bf16[512,512]{1,0:T(8,128)(2,1)S(1)} %collective-permute-done.9.refs_0_, ...), custom_call_target="tpu_custom_call", output_to_operand_aliasing={{0}: (4, {}), {1}: (5, {})} | custom-call | flops 5120000000 | bytes 262144 | tf_op jit(solution)/shard_map/attend/pallas_call | solution.py:263
  85.2 6.4 %collective-permute-start.16 = (bf16[512,512]{1,0:T(8,128)(2,1)S(1)}, bf16[512,512]{1,0:T(8,128)(2,1)S(1)}, u32[]{:S(2)}, u32[]{:S(2)}) collective-permute-start(bf16[512,512]{1,0:T(8,128)(2,1)S(1)} %get-tuple-element.46.refs_0_), channel_id=1, source_target_pairs={{0,32},{4,36},{8,40},{12,44},{16,48},{20,52},{24,56},{28,60},{32,6... | collective-permute-start | bytes 1572872 | tf_op jit(solution)/shard_map/hop_direct/ppermute | solution.py:32
  91.6 2.2 %build_cache.1 = bf16[1,128,2,1024]{3,2,1,0:T(2,128)(2,1)} custom-call(s32[4]{0:T(128)S(1)} %and_select_fusion.shards, bf16[128,512]{1,0:T(8,128)(2,1)S(1)} %get-tuple-element.71.refs_0_, bf16[128,512]{1,0:T(8,128)(2,1)S(1)} %collective-permute-done.12.refs_1_, bf16[128,512]{1,0:T(8,128)(2,1)S(1)} %collective-permute-done.13.refs_2_, ...), custom_call_target="tpu_custom_call" | custom-call | flops 1000000000 | bytes 1000 | tf_op jit(solution)/shard_map/build_cache/pallas_call | solution.py:296
  93.8 27.6 %collective-permute-done.10.refs_0_ = bf16[512,512]{1,0:T(8,128)(2,1)S(1)} collective-permute-done((bf16[512,512]{1,0:T(8,128)(2,1)S(1)}, bf16[512,512]{1,0:T(8,128)(2,1)S(1)}, u32[]{:S(2)}, u32[]{:S(2)}) %collective-permute-start.10) | collective-permute-done | bytes 524320 | tf_op jit(solution)/shard_map/hop_2/ppermute | solution.py:32
  121.4 1.9 %collective-permute-start.11 = (bf16[512,512]{1,0:T(8,128)(2,1)S(1)}, bf16[512,512]{1,0:T(8,128)(2,1)S(1)}, u32[]{:S(2)}, u32[]{:S(2)}) collective-permute-start(bf16[512,512]{1,0:T(8,128)(2,1)S(1)} %collective-permute-done.10.refs_0_), channel_id=1, source_target_pairs={{0,8},{4,12},{8,16},{12,20},{16,24},{20,28},{24,32},{28,36},{32,40... | collective-permute-start | bytes 1572872 | tf_op jit(solution)/shard_map/hop_3/ppermute | solution.py:32
  123.3 2.1 %attend.12 = (f32[512,512]{1,0:T(8,128)S(1)}, f32[512,512]{1,0:T(8,128)S(1)}) custom-call(s32[21]{0:T(128)S(1)} %pad_add_fusion.1.meta, s32[512,128]{1,0:T(8,128)S(1)} %add.91.low_ref, bf16[512,512]{1,0:T(8,128)(2,1)S(1)} %project_q.1.q_ref, bf16[512,512]{1,0:T(8,128)(2,1)S(1)} %collective-permute-done.17.refs_0_, ...), custom_call_target="tpu_custom_call", output_to_operand_aliasing={{0}: (4, {}), {1}: (5, {})} | custom-call | flops 5120000000 | bytes 262144 | tf_op jit(solution)/shard_map/attend/pallas_call | solution.py:263
  125.4 2.1 %attend.13 = (f32[512,512]{1,0:T(8,128)S(1)}, f32[512,512]{1,0:T(8,128)S(1)}) custom-call(s32[21]{0:T(128)S(1)} %pad_add_fusion.1.meta, s32[512,128]{1,0:T(8,128)S(1)} %add.91.low_ref, bf16[512,512]{1,0:T(8,128)(2,1)S(1)} %project_q.1.q_ref, bf16[512,512]{1,0:T(8,128)(2,1)S(1)} %collective-permute-done.10.refs_0_, ...), custom_call_target="tpu_custom_call", output_to_operand_aliasing={{0}: (4, {}), {1}: (5, {})} | custom-call | flops 5120000000 | bytes 262144 | tf_op jit(solution)/shard_map/attend/pallas_call | solution.py:263
  127.5 0.6 collective-permute-start.19
  128.1 11.6 %collective-permute-done.11.refs_0_ = bf16[512,512]{1,0:T(8,128)(2,1)S(1)} collective-permute-done((bf16[512,512]{1,0:T(8,128)(2,1)S(1)}, bf16[512,512]{1,0:T(8,128)(2,1)S(1)}, u32[]{:S(2)}, u32[]{:S(2)}) %collective-permute-start.11) | collective-permute-done | bytes 524320 | tf_op jit(solution)/shard_map/hop_3/ppermute | solution.py:32
  139.7 2.1 %attend.14 = (f32[512,512]{1,0:T(8,128)S(1)}, f32[512,512]{1,0:T(8,128)S(1)}) custom-call(s32[21]{0:T(128)S(1)} %pad_add_fusion.1.meta, s32[512,128]{1,0:T(8,128)S(1)} %add.91.low_ref, bf16[512,512]{1,0:T(8,128)(2,1)S(1)} %project_q.1.q_ref, bf16[512,512]{1,0:T(8,128)(2,1)S(1)} %collective-permute-done.20.refs_0_, ...), custom_call_target="tpu_custom_call", output_to_operand_aliasing={{0}: (4, {}), {1}: (5, {})} | custom-call | flops 5120000000 | bytes 262144 | tf_op jit(solution)/shard_map/attend/pallas_call | solution.py:263
  141.8 2.1 %attend.15 = (f32[512,512]{1,0:T(8,128)S(1)}, f32[512,512]{1,0:T(8,128)S(1)}) custom-call(s32[21]{0:T(128)S(1)} %pad_add_fusion.1.meta, s32[512,128]{1,0:T(8,128)S(1)} %add.91.low_ref, bf16[512,512]{1,0:T(8,128)(2,1)S(1)} %project_q.1.q_ref, bf16[512,512]{1,0:T(8,128)(2,1)S(1)} %collective-permute-done.16.refs_0_, ...), custom_call_target="tpu_custom_call", output_to_operand_aliasing={{0}: (4, {}), {1}: (5, {})} | custom-call | flops 5120000000 | bytes 262144 | tf_op jit(solution)/shard_map/attend/pallas_call | solution.py:263
  143.9 2.1 %attend.16 = (f32[512,512]{1,0:T(8,128)S(1)}, f32[512,512]{1,0:T(8,128)S(1)}) custom-call(s32[21]{0:T(128)S(1)} %pad_add_fusion.1.meta, s32[512,128]{1,0:T(8,128)S(1)} %add.91.low_ref, bf16[512,512]{1,0:T(8,128)(2,1)S(1)} %project_q.1.q_ref, bf16[512,512]{1,0:T(8,128)(2,1)S(1)} %collective-permute-done.19.refs_0_, ...), custom_call_target="tpu_custom_call", output_to_operand_aliasing={{0}: (4, {}), {1}: (5, {})} | custom-call | flops 5120000000 | bytes 262144 | tf_op jit(solution)/shard_map/attend/pallas_call | solution.py:263
  146.1 2.1 %attend.17 = (f32[512,512]{1,0:T(8,128)S(1)}, f32[512,512]{1,0:T(8,128)S(1)}) custom-call(s32[21]{0:T(128)S(1)} %pad_add_fusion.1.meta, s32[512,128]{1,0:T(8,128)S(1)} %add.91.low_ref, bf16[512,512]{1,0:T(8,128)(2,1)S(1)} %project_q.1.q_ref, bf16[512,512]{1,0:T(8,128)(2,1)S(1)} %collective-permute-done.11.refs_0_, ...), custom_call_target="tpu_custom_call", output_to_operand_aliasing={{0}: (4, {}), {1}: (5, {})} | custom-call | flops 5120000000 | bytes 262144 | tf_op jit(solution)/shard_map/attend/pallas_call | solution.py:263
  148.2 3.0 %attend_last.1 = bf16[512,512]{1,0:T(8,128)(2,1)} custom-call(s32[21]{0:T(128)S(1)} %pad_add_fusion.1.meta, s32[512,128]{1,0:T(8,128)S(1)} %add.91.low_ref, bf16[512,512]{1,0:T(8,128)(2,1)S(1)} %project_q.1.q_ref, bf16[512,512]{1,0:T(8,128)(2,1)S(1)} %collective-permute-done.15.refs_0_, f32[512,512]{1,0:T(8,128)S(1)} %get-tuple-element.64.refs_1_, ...), custom_call_target="tpu_custom_call" | custom-call | flops 5120000000 | bytes 262144 | tf_op jit(solution)/shard_map/attend_last/pallas_call | solution.py:263
  (43 shorter events, 0.5 us)
Async XLA Ops:
  1.3 13.2 %collective-permute-start = (s32[1,512]{1,0:T(1,128)S(1)}, s32[1,512]{1,0:T(1,128)S(1)}, u32[]{:S(2)}, u32[]{:S(2)}) collective-permute-start(s32[1,512]{1,0:T(1,128)S(1)} %bitcast.26), channel_id=1, source_target_pairs={{0,4},{4,8},{8,12},{12,16},{16,20},{20,24},{24,28},{28,32},{32,36}... | collective-permute-start | bytes 6152 | tf_op jit(solution)/shard_map/ppermute | solution.py:32
  3.2 11.3 %collective-permute-start.1 = (s32[1,512]{1,0:T(1,128)S(1)}, s32[1,512]{1,0:T(1,128)S(1)}, u32[]{:S(2)}, u32[]{:S(2)}) collective-permute-start(s32[1,512]{1,0:T(1,128)S(1)} %bitcast.27), channel_id=1, source_target_pairs={{0,8},{4,12},{8,16},{12,20},{16,24},{20,28},{24,32},{28,36},{32,40... | collective-permute-start | bytes 6152 | tf_op jit(solution)/shard_map/ppermute | solution.py:32
  7.1 29.5 %collective-permute-start.4 = (bf16[512,1152]{1,0:T(8,128)(2,1)}, bf16[512,1152]{1,0:T(8,128)(2,1)S(1)}, u32[]{:S(2)}, u32[]{:S(2)}) collective-permute-start(bf16[512,1152]{1,0:T(8,128)(2,1)} %own.1), channel_id=1, source_target_pairs={{0,1},{1,2},{2,3},{3,0},{4,5},{5,6},{6,7},{7,4},{8,9},{9,10},{10,1... | collective-permute-start | bytes 3538952 | tf_op jit(solution)/shard_map/ppermute | solution.py:37
  8.7 28.6 %collective-permute-start.5 = (bf16[512,1152]{1,0:T(8,128)(2,1)}, bf16[512,1152]{1,0:T(8,128)(2,1)S(1)}, u32[]{:S(2)}, u32[]{:S(2)}) collective-permute-start(bf16[512,1152]{1,0:T(8,128)(2,1)} %own.1), channel_id=1, source_target_pairs={{0,3},{1,0},{2,1},{3,2},{4,7},{5,4},{6,5},{7,6},{8,11},{9,8},{10,9... | collective-permute-start | bytes 3538952 | tf_op jit(solution)/shard_map/ppermute | solution.py:37
  12.0 30.9 %collective-permute-start.8 = (f32[1,512]{1,0:T(1,128)S(1)}, f32[1,512]{1,0:T(1,128)S(1)}, u32[]{:S(2)}, u32[]{:S(2)}) collective-permute-start(f32[1,512]{1,0:T(1,128)S(1)} %bitcast.31), channel_id=1, source_target_pairs={{0,2},{1,3},{2,0},{3,1},{4,6},{5,7},{6,4},{7,5},{8,10},{9,11},{10,... | collective-permute-start | bytes 6152 | tf_op jit(solution)/shard_map/far_square/ppermute | solution.py:37
  14.6 11.1 %collective-permute-start.2 = (s32[3,512]{1,0:T(4,128)S(1)}, s32[3,512]{1,0:T(4,128)S(1)}, u32[]{:S(2)}, u32[]{:S(2)}) collective-permute-start(s32[3,512]{1,0:T(4,128)S(1)} %pad_add_fusion), channel_id=1, source_target_pairs={{0,12},{4,16},{8,20},{12,24},{16,28},{20,32},{24,36},{28,40},{32,4... | collective-permute-start | bytes 18440 | tf_op jit(solution)/shard_map/ppermute | solution.py:32
  18.9 9.5 %collective-permute-start.3 = (s32[3,512]{1,0:T(4,128)S(1)}, s32[3,512]{1,0:T(4,128)S(1)}, u32[]{:S(2)}, u32[]{:S(2)}) collective-permute-start(s32[3,512]{1,0:T(4,128)S(1)} %pad_add_fusion), channel_id=1, source_target_pairs={{0,24},{4,28},{8,32},{12,36},{16,40},{20,44},{24,48},{28,52},{32,5... | collective-permute-start | bytes 18440 | tf_op jit(solution)/shard_map/ppermute | solution.py:32
  28.4 14.5 %slice-start = ((s8[4718592]{0:T(1024)(128)(4,1)}), s8[4194304]{0:T(1024)(128)(4,1)S(1)}, s32[]{:S(2)}) async-start(s8[4718592]{0:T(1024)(128)(4,1)} %bitcast.24), calls=%async_computation | async-start | bytes 8388608
  28.5 13.4 %copy-start.4 = (f32[128]{0:T(128)S(1)}, f32[128]{0:T(128)}, u32[]{:S(2)}) copy-start(f32[128]{0:T(128)} %constant.76) | copy-start | bytes 1540
  28.5 14.5 %copy-start = (bf16[4608,256]{1,0:T(8,128)(2,1)S(1)}, bf16[4608,256]{1,0:T(8,128)(2,1)}, u32[]{:S(2)}) copy-start(bf16[4608,256]{1,0:T(8,128)(2,1)} %refs_4_.1) | copy-start | bytes 7077892
  28.5 14.5 %copy-start.1 = (bf16[4608,256]{1,0:T(8,128)(2,1)S(1)}, bf16[4608,256]{1,0:T(8,128)(2,1)}, u32[]{:S(2)}) copy-start(bf16[4608,256]{1,0:T(8,128)(2,1)} %refs_5_.1) | copy-start | bytes 7077892
  28.5 14.5 %copy-start.2 = (bf16[512,1152]{1,0:T(8,128)(2,1)S(1)}, bf16[512,1152]{1,0:T(8,128)(2,1)}, u32[]{:S(2)}) copy-start(bf16[512,1152]{1,0:T(8,128)(2,1)} %own.1) | copy-start | bytes 3538948
  28.5 14.5 %slice-start.1 = ((s8[4718592]{0:T(1024)(128)(4,1)}), s8[524288]{0:T(1024)(128)(4,1)S(1)}, s32[]{:S(2)}) async-start(s8[4718592]{0:T(1024)(128)(4,1)} %bitcast.24), calls=%async_computation.1 | async-start | bytes 1048576
  37.4 17.1 %collective-permute-start.6 = (bf16[256,1152]{1,0:T(8,128)(2,1)S(1)}, bf16[256,1152]{1,0:T(8,128)(2,1)S(1)}, u32[]{:S(2)}, u32[]{:S(2)}) collective-permute-start(bf16[256,1152]{1,0:T(8,128)(2,1)S(1)} %get-tuple-element.34), channel_id=1, source_target_pairs={{0,1},{1,2},{2,3},{3,0},{4,5},{5,6},{6,7},{7,4},{8,9},{9,10},{10,1... | collective-permute-start | bytes 1769480 | tf_op jit(solution)/shard_map/ppermute | solution.py:37
  40.1 15.6 %collective-permute-start.7 = (bf16[256,1152]{1,0:T(8,128)(2,1)S(1)}, bf16[256,1152]{1,0:T(8,128)(2,1)S(1)}, u32[]{:S(2)}, u32[]{:S(2)}) collective-permute-start(bf16[256,1152]{1,0:T(8,128)(2,1)S(1)} %get-tuple-element.36), channel_id=1, source_target_pairs={{0,3},{1,0},{2,1},{3,2},{4,7},{5,4},{6,5},{7,6},{8,11},{9,8},{10,9... | collective-permute-start | bytes 1769480 | tf_op jit(solution)/shard_map/ppermute | solution.py:37
  43.0 12.6 %copy-start.3 = (s32[1,4]{1,0:T(1,128)S(1)}, s32[1,4]{1,0:T(1,128)}, u32[]{:S(2)}) copy-start(s32[1,4]{1,0:T(1,128)} %param.14) | copy-start | bytes 52
  58.1 17.3 %collective-permute-start.9 = (bf16[512,512]{1,0:T(8,128)(2,1)S(1)}, bf16[512,512]{1,0:T(8,128)(2,1)S(1)}, u32[]{:S(2)}, u32[]{:S(2)}) collective-permute-start(bf16[512,512]{1,0:T(8,128)(2,1)S(1)} %get-tuple-element.46.refs_0_), channel_id=1, source_target_pairs={{0,8},{4,12},{8,16},{12,20},{16,24},{20,28},{24,32},{28,36},{32,40... | collective-permute-start | bytes 1572872 | tf_op jit(solution)/shard_map/hop_1/ppermute | solution.py:32
  63.6 17.0 %collective-permute-start.18 = (bf16[512,512]{1,0:T(8,128)(2,1)S(1)}, bf16[512,512]{1,0:T(8,128)(2,1)S(1)}, u32[]{:S(2)}, u32[]{:S(2)}) collective-permute-start(bf16[512,512]{1,0:T(8,128)(2,1)S(1)} %get-tuple-element.46.refs_0_), channel_id=1, source_target_pairs={{0,4},{4,0},{8,12},{12,8},{16,20},{20,16},{24,28},{28,24},{32,36},... | collective-permute-start | bytes 1572872 | tf_op jit(solution)/shard_map/cross_own/ppermute | solution.py:41
  75.5 9.7 %collective-permute-start.12 = (bf16[128,512]{1,0:T(8,128)(2,1)S(1)}, bf16[128,512]{1,0:T(8,128)(2,1)S(1)}, u32[]{:S(2)}, u32[]{:S(2)}) collective-permute-start(bf16[128,512]{1,0:T(8,128)(2,1)S(1)} %get-tuple-element.70), channel_id=1, source_target_pairs={{0,1},{1,2},{2,3},{3,0},{4,5},{5,6},{6,7},{7,4},{8,9},{9,10},{10,1... | collective-permute-start | bytes 393224 | tf_op jit(solution)/shard_map/ppermute | solution.py:37
  76.2 15.3 %collective-permute-start.13 = (bf16[128,512]{1,0:T(8,128)(2,1)S(1)}, bf16[128,512]{1,0:T(8,128)(2,1)S(1)}, u32[]{:S(2)}, u32[]{:S(2)}) collective-permute-start(bf16[128,512]{1,0:T(8,128)(2,1)S(1)} %get-tuple-element.69), channel_id=1, source_target_pairs={{0,2},{1,3},{2,0},{3,1},{4,6},{5,7},{6,4},{7,5},{8,10},{9,11},{10,... | collective-permute-start | bytes 393224 | tf_op jit(solution)/shard_map/ppermute | solution.py:37
  79.9 11.7 %collective-permute-start.14 = (bf16[128,512]{1,0:T(8,128)(2,1)S(1)}, bf16[128,512]{1,0:T(8,128)(2,1)S(1)}, u32[]{:S(2)}, u32[]{:S(2)}) collective-permute-start(bf16[128,512]{1,0:T(8,128)(2,1)S(1)} %get-tuple-element.68), channel_id=1, source_target_pairs={{0,3},{1,0},{2,1},{3,2},{4,7},{5,4},{6,5},{7,6},{8,11},{9,8},{10,9... | collective-permute-start | bytes 393224 | tf_op jit(solution)/shard_map/ppermute | solution.py:37
  80.6 42.7 %collective-permute-start.17 = (bf16[512,512]{1,0:T(8,128)(2,1)S(1)}, bf16[512,512]{1,0:T(8,128)(2,1)S(1)}, u32[]{:S(2)}, u32[]{:S(2)}) collective-permute-start(bf16[512,512]{1,0:T(8,128)(2,1)S(1)} %collective-permute-done.9.refs_0_), channel_id=1, source_target_pairs={{0,4},{4,0},{8,12},{12,8},{16,20},{20,16},{24,28},{28,24},{32,36},... | collective-permute-start | bytes 1572872 | tf_op jit(solution)/shard_map/cross_1/ppermute | solution.py:41
  80.6 40.8 %collective-permute-start.10 = (bf16[512,512]{1,0:T(8,128)(2,1)S(1)}, bf16[512,512]{1,0:T(8,128)(2,1)S(1)}, u32[]{:S(2)}, u32[]{:S(2)}) collective-permute-start(bf16[512,512]{1,0:T(8,128)(2,1)S(1)} %collective-permute-done.9.refs_0_), channel_id=1, source_target_pairs={{0,8},{4,12},{8,16},{12,20},{16,24},{20,28},{24,32},{28,36},{32,40... | collective-permute-start | bytes 1572872 | tf_op jit(solution)/shard_map/hop_2/ppermute | solution.py:32
  85.2 42.4 %collective-permute-start.16 = (bf16[512,512]{1,0:T(8,128)(2,1)S(1)}, bf16[512,512]{1,0:T(8,128)(2,1)S(1)}, u32[]{:S(2)}, u32[]{:S(2)}) collective-permute-start(bf16[512,512]{1,0:T(8,128)(2,1)S(1)} %get-tuple-element.46.refs_0_), channel_id=1, source_target_pairs={{0,32},{4,36},{8,40},{12,44},{16,48},{20,52},{24,56},{28,60},{32,6... | collective-permute-start | bytes 1572872 | tf_op jit(solution)/shard_map/hop_direct/ppermute | solution.py:32
  121.4 18.3 %collective-permute-start.20 = (bf16[512,512]{1,0:T(8,128)(2,1)S(1)}, bf16[512,512]{1,0:T(8,128)(2,1)S(1)}, u32[]{:S(2)}, u32[]{:S(2)}) collective-permute-start(bf16[512,512]{1,0:T(8,128)(2,1)S(1)} %collective-permute-done.10.refs_0_), channel_id=1, source_target_pairs={{0,4},{4,0},{8,12},{12,8},{16,20},{20,16},{24,28},{28,24},{32,36},... | collective-permute-start | bytes 1572872 | tf_op jit(solution)/shard_map/cross_2/ppermute | solution.py:41
  121.4 18.3 %collective-permute-start.11 = (bf16[512,512]{1,0:T(8,128)(2,1)S(1)}, bf16[512,512]{1,0:T(8,128)(2,1)S(1)}, u32[]{:S(2)}, u32[]{:S(2)}) collective-permute-start(bf16[512,512]{1,0:T(8,128)(2,1)S(1)} %collective-permute-done.10.refs_0_), channel_id=1, source_target_pairs={{0,8},{4,12},{8,16},{12,20},{16,24},{20,28},{24,32},{28,36},{32,40... | collective-permute-start | bytes 1572872 | tf_op jit(solution)/shard_map/hop_3/ppermute | solution.py:32
  127.5 16.4 %collective-permute-start.19 = (bf16[512,512]{1,0:T(8,128)(2,1)S(1)}, bf16[512,512]{1,0:T(8,128)(2,1)S(1)}, u32[]{:S(2)}, u32[]{:S(2)}) collective-permute-start(bf16[512,512]{1,0:T(8,128)(2,1)S(1)} %collective-permute-done.16.refs_0_), channel_id=1, source_target_pairs={{0,4},{4,0},{8,12},{12,8},{16,20},{20,16},{24,28},{28,24},{32,36},... | collective-permute-start | bytes 1572872 | tf_op jit(solution)/shard_map/cross_4/ppermute | solution.py:41
  139.7 8.5 %collective-permute-start.15 = (bf16[512,512]{1,0:T(8,128)(2,1)S(1)}, bf16[512,512]{1,0:T(8,128)(2,1)S(1)}, u32[]{:S(2)}, u32[]{:S(2)}) collective-permute-start(bf16[512,512]{1,0:T(8,128)(2,1)S(1)} %collective-permute-done.11.refs_0_), channel_id=1, source_target_pairs={{0,4},{4,0},{8,12},{12,8},{16,20},{20,16},{24,28},{28,24},{32,36},... | collective-permute-start | bytes 1572872 | tf_op jit(solution)/shard_map/cross_3/ppermute | solution.py:41

commit v7 on v5

--- a/solution.py
+++ b/solution.py
@@ -270,7 +270,7 @@
         input_output_aliases=aliases,
         compiler_params=pltpu.CompilerParams(vmem_limit_bytes=8 << 20),
         cost_estimate=pl.CostEstimate(
-            flops=2000000 * keys,
+            flops=3500000 * keys,
             transcendentals=0,
             bytes_accessed=width * keys,
         ),

time: 125 us -> 116 us (0.928)
  waiting for transfers between devices: 33 us -> 26.2 us
    ppermute x12, waiting for transfers between devices: 27.2 us -> 19 us  [shifted(): return lax.ppermute(block, axis, route)]
    ppermute x8, starting transfers between devices: 17.5 us -> 14.7 us  [turned(): lax.ppermute(block, axis, [(i, (i + distance) % count) for i in range(cou...]
    ppermute x12, starting transfers between devices: 35 us -> 37.2 us  [shifted(): return lax.ppermute(block, axis, route)]
    ppermute x8, waiting for transfers between devices: 5.83 us -> 7.23 us  [turned(): lax.ppermute(block, axis, [(i, (i + distance) % count) for i in range(cou...]
  transfers between devices with their start and end apart: 29 -> 29, of which waited for: 12 -> 12; matrix products, arithmetic and copies ran while one was open for 5% -> 5% of each run, Pallas kernels for 20% -> 21%
where the time goes in v7:
time: 116 us
  starting transfers between devices  53.4 us (46%)
  Pallas kernels  29.4 us (25%)
  waiting for transfers between devices  26.2 us (23%)
  other arithmetic  4.73 us (4%)
  local copies, waits for them, and re-layouts  1.17 us (1%)
    ppermute x12, starting transfers between devices, shifted(): return lax.ppermute(block, axis, route)  37.2 us
    ppermute x12, waiting for transfers between devices, shifted(): return lax.ppermute(block, axis, route)  19 us
    pallas_call x7, Pallas kernels, attend(): pl.pallas_call(functools.partial(attend_kernel, places, first, last, guar...  17.9 us
    ppermute x8, starting transfers between devices, turned(): lax.ppermute(block, axis, [(i, (i + distance) % count) for i in range(cou...  14.7 us
    ppermute x8, waiting for transfers between devices, turned(): lax.ppermute(block, axis, [(i, (i + distance) % count) for i in range(cou...  7.23 us
    pallas_call x1, Pallas kernels, project_early(): pl.pallas_call(early_kernel, name='project_early', out_shape=tuple((jax.S...  5.78 us
  transfers between devices with their start and end apart: 29, of which 12 were waited for; matrix products, arithmetic and copies ran while one was open for 5% of the time, Pallas kernels for 21%

profile of v7, /device:TPU:6, one launch (start us, length us, event | category | flops | bytes accessed | tf_op | source)
XLA Modules:
  0.0 116.0 jit_solution(3066477446197631504)
XLA Ops:
  0.6 1.7 %collective-permute-start.4 = (bf16[512,1152]{1,0:T(8,128)(2,1)}, bf16[512,1152]{1,0:T(8,128)(2,1)S(1)}, u32[]{:S(2)}, u32[]{:S(2)}) collective-permute-start(bf16[512,1152]{1,0:T(8,128)(2,1)} %own.1), channel_id=1, source_target_pairs={{0,1},{1,2},{2,3},{3,0},{4,5},{5,6},{6,7},{7,4},{8,9},{9,10},{10,1... | collective-permute-start | bytes 3538952 | tf_op jit(solution)/shard_map/ppermute | solution.py:37
  2.3 1.7 %collective-permute-start.5 = (bf16[512,1152]{1,0:T(8,128)(2,1)}, bf16[512,1152]{1,0:T(8,128)(2,1)S(1)}, u32[]{:S(2)}, u32[]{:S(2)}) collective-permute-start(bf16[512,1152]{1,0:T(8,128)(2,1)} %own.1), channel_id=1, source_target_pairs={{0,3},{1,0},{2,1},{3,2},{4,7},{5,4},{6,5},{7,6},{8,11},{9,8},{10,9... | collective-permute-start | bytes 3538952 | tf_op jit(solution)/shard_map/ppermute | solution.py:37
  4.1 0.7 broadcast_add_fusion
  4.8 1.9 %collective-permute-start = (s32[1,512]{1,0:T(1,128)S(1)}, s32[1,512]{1,0:T(1,128)S(1)}, u32[]{:S(2)}, u32[]{:S(2)}) collective-permute-start(s32[1,512]{1,0:T(1,128)S(1)} %bitcast.27), channel_id=1, source_target_pairs={{0,4},{4,8},{8,12},{12,16},{16,20},{20,24},{24,28},{28,32},{32,36}... | collective-permute-start | bytes 6152 | tf_op jit(solution)/shard_map/ppermute | solution.py:32
  6.7 3.8 %collective-permute-start.1 = (s32[1,512]{1,0:T(1,128)S(1)}, s32[1,512]{1,0:T(1,128)S(1)}, u32[]{:S(2)}, u32[]{:S(2)}) collective-permute-start(s32[1,512]{1,0:T(1,128)S(1)} %bitcast.28), channel_id=1, source_target_pairs={{0,8},{4,12},{8,16},{12,20},{16,24},{20,28},{24,32},{28,36},{32,40... | collective-permute-start | bytes 6152 | tf_op jit(solution)/shard_map/ppermute | solution.py:32
  10.6 1.6 %multiply_reduce_fusion = f32[512]{0:T(512)S(1)} fusion(bf16[512,1152]{1,0:T(8,128)(2,1)} %own.1), kind=kLoop, calls=%fused_computation.1 | loop fusion | flops 1768960 | bytes 1181696 | tf_op jit(solution)/shard_map/far_square/reduce_sum | solution.py:350
  12.1 2.1 %collective-permute-start.8 = (f32[1,512]{1,0:T(1,128)S(1)}, f32[1,512]{1,0:T(1,128)S(1)}, u32[]{:S(2)}, u32[]{:S(2)}) collective-permute-start(f32[1,512]{1,0:T(1,128)S(1)} %bitcast.32), channel_id=1, source_target_pairs={{0,2},{1,3},{2,0},{3,1},{4,6},{5,7},{6,4},{7,5},{8,10},{9,11},{10,... | collective-permute-start | bytes 6152 | tf_op jit(solution)/shard_map/far_square/ppermute | solution.py:37
  14.5 1.8 %collective-permute-done.1 = s32[1,512]{1,0:T(1,128)S(1)} collective-permute-done((s32[1,512]{1,0:T(1,128)S(1)}, s32[1,512]{1,0:T(1,128)S(1)}, u32[]{:S(2)}, u32[]{:S(2)}) %collective-permute-start.1) | collective-permute-done | bytes 2080 | tf_op jit(solution)/shard_map/ppermute | solution.py:32
  16.3 3.1 %collective-permute-start.2 = (s32[3,512]{1,0:T(4,128)S(1)}, s32[3,512]{1,0:T(4,128)S(1)}, u32[]{:S(2)}, u32[]{:S(2)}) collective-permute-start(s32[3,512]{1,0:T(4,128)S(1)} %pad_add_fusion), channel_id=1, source_target_pairs={{0,12},{4,16},{8,20},{12,24},{16,28},{20,32},{24,36},{28,40},{32,4... | collective-permute-start | bytes 18440 | tf_op jit(solution)/shard_map/ppermute | solution.py:32
  19.5 5.9 %collective-permute-start.3 = (s32[3,512]{1,0:T(4,128)S(1)}, s32[3,512]{1,0:T(4,128)S(1)}, u32[]{:S(2)}, u32[]{:S(2)}) collective-permute-start(s32[3,512]{1,0:T(4,128)S(1)} %pad_add_fusion), channel_id=1, source_target_pairs={{0,24},{4,28},{8,32},{12,36},{16,40},{20,44},{24,48},{28,52},{32,5... | collective-permute-start | bytes 18440 | tf_op jit(solution)/shard_map/ppermute | solution.py:32
  25.4 0.7 reshape.55.gain.refs_3_
  26.2 2.7 %collective-permute-done.3 = s32[3,512]{1,0:T(4,128)S(1)} collective-permute-done((s32[3,512]{1,0:T(4,128)S(1)}, s32[3,512]{1,0:T(4,128)S(1)}, u32[]{:S(2)}, u32[]{:S(2)}) %collective-permute-start.3) | collective-permute-done | bytes 6176 | tf_op jit(solution)/shard_map/ppermute | solution.py:32
  29.0 0.9 collective-permute-done.4.left
  30.0 1.7 %collective-permute-start.6 = (bf16[256,1152]{1,0:T(8,128)(2,1)S(1)}, bf16[256,1152]{1,0:T(8,128)(2,1)S(1)}, u32[]{:S(2)}, u32[]{:S(2)}) collective-permute-start(bf16[256,1152]{1,0:T(8,128)(2,1)S(1)} %get-tuple-element.35), channel_id=1, source_target_pairs={{0,1},{1,2},{2,3},{3,0},{4,5},{5,6},{6,7},{7,4},{8,9},{9,10},{10,1... | collective-permute-start | bytes 1769480 | tf_op jit(solution)/shard_map/ppermute | solution.py:37
  31.7 1.0 convert_reduce_fusion
  32.7 1.7 %collective-permute-start.7 = (bf16[256,1152]{1,0:T(8,128)(2,1)S(1)}, bf16[256,1152]{1,0:T(8,128)(2,1)S(1)}, u32[]{:S(2)}, u32[]{:S(2)}) collective-permute-start(bf16[256,1152]{1,0:T(8,128)(2,1)S(1)} %get-tuple-element.37), channel_id=1, source_target_pairs={{0,3},{1,0},{2,1},{3,2},{4,7},{5,4},{6,5},{7,6},{8,11},{9,8},{10,9... | collective-permute-start | bytes 1769480 | tf_op jit(solution)/shard_map/ppermute | solution.py:37
  34.4 1.0 fusion
  35.6 5.8 %project_early.1 = (f32[512,128]{1,0:T(8,128)S(1)}, f32[512,512]{1,0:T(8,128)S(1)}, f32[512,256]{1,0:T(8,128)S(1)}, f32[512,256]{1,0:T(8,128)S(1)}) custom-call(s32[4]{0:T(128)S(1)} %and_select_fusion.shards, bf16[512,1152]{1,0:T(8,128)(2,1)S(1)} %copy-done.2, bf16[512,1152]{1,0:T(8,128)(2,1)S(1)} %collective-permute-done.4.left, ...), custom_call_target="tpu_custom_call" | custom-call | flops 3623878656 | bytes 3538944 | tf_op jit(solution)/shard_map/project_early/pallas_call | solution.py:82
  41.4 4.1 %collective-permute-done.6.refs_0_ = bf16[256,1152]{1,0:T(8,128)(2,1)S(1)} collective-permute-done((bf16[256,1152]{1,0:T(8,128)(2,1)S(1)}, bf16[256,1152]{1,0:T(8,128)(2,1)S(1)}, u32[]{:S(2)}, u32[]{:S(2)}) %collective-permute-start.6) | collective-permute-done | bytes 589856 | tf_op jit(solution)/shard_map/ppermute | solution.py:37
  45.6 0.8 collective-permute-done.7.refs_1_
  46.3 1.8 %project_kv.1 = (bf16[512,1152]{1,0:T(8,128)(2,1)S(1)}, bf16[512,512]{1,0:T(8,128)(2,1)S(1)}, bf16[256,512]{1,0:T(8,128)(2,1)S(1)}, bf16[256,512]{1,0:T(8,128)(2,1)S(1)}, bf16[4,128,512]{2,1,0:T(8,128)(2,1)S(1)}) custom-call(s32[4]{0:T(128)S(1)} %and_select_fusion.shards, s32[4]{0:T(128)S(1)} %bitcast.26, ...), custom_call_target="tpu_custom_call" | custom-call | flops 603979776 | bytes 1179648 | tf_op jit(solution)/shard_map/project_kv/pallas_call | solution.py:134
  48.1 4.0 %collective-permute-start.14 = (bf16[256,512]{1,0:T(8,128)(2,1)S(1)}, bf16[256,512]{1,0:T(8,128)(2,1)S(1)}, u32[]{:S(2)}, u32[]{:S(2)}) collective-permute-start(bf16[256,512]{1,0:T(8,128)(2,1)S(1)} %get-tuple-element.45), channel_id=1, source_target_pairs={{0,8},{4,12},{8,16},{12,20},{16,24},{20,28},{24,32},{28,36},{32,40... | collective-permute-start | bytes 786440 | tf_op jit(solution)/shard_map/hop_b1/ppermute | solution.py:32
  52.1 1.6 %project_q.1.q_ref = bf16[512,512]{1,0:T(8,128)(2,1)S(1)} custom-call(s32[4]{0:T(128)S(1)} %and_select_fusion.shards, bf16[512,1152]{1,0:T(8,128)(2,1)S(1)} %get-tuple-element.41.normed, bf16[4608,512]{1,0:T(8,128)(2,1)S(1)} %bitcast.25, f32[512,512]{1,0:T(8,128)S(1)} %get-tuple-element.42.part, f32[512,128]{1,0:T(8,128)S(1)} %get-tuple-element.73.refs_8_.cos, ...), custom_call_target="tpu_custom_call" | custom-call | flops 512000000 | bytes 262144 | tf_op jit(solution)/shard_map/project_q/pallas_call | solution.py:160
  53.8 3.8 %collective-permute-start.9 = (bf16[256,512]{1,0:T(8,128)(2,1)S(1)}, bf16[256,512]{1,0:T(8,128)(2,1)S(1)}, u32[]{:S(2)}, u32[]{:S(2)}) collective-permute-start(bf16[256,512]{1,0:T(8,128)(2,1)S(1)} %get-tuple-element.43), channel_id=1, source_target_pairs={{0,8},{4,12},{8,16},{12,20},{16,24},{20,28},{24,32},{28,36},{32,40... | collective-permute-start | bytes 786440 | tf_op jit(solution)/shard_map/hop_a1/ppermute | solution.py:32
  57.7 2.8 %collective-permute-done.14.refs_2_ = bf16[256,512]{1,0:T(8,128)(2,1)S(1)} collective-permute-done((bf16[256,512]{1,0:T(8,128)(2,1)S(1)}, bf16[256,512]{1,0:T(8,128)(2,1)S(1)}, u32[]{:S(2)}, u32[]{:S(2)}) %collective-permute-start.14) | collective-permute-done | bytes 262176 | tf_op jit(solution)/shard_map/hop_b1/ppermute | solution.py:32
  60.5 1.9 %collective-permute-start.15 = (bf16[256,512]{1,0:T(8,128)(2,1)S(1)}, bf16[256,512]{1,0:T(8,128)(2,1)S(1)}, u32[]{:S(2)}, u32[]{:S(2)}) collective-permute-start(bf16[256,512]{1,0:T(8,128)(2,1)S(1)} %collective-permute-done.14.refs_2_), channel_id=1, source_target_pairs={{0,8},{4,12},{8,16},{12,20},{16,24},{20,28},{24,32},{28,36},{32,40... | collective-permute-start | bytes 786440 | tf_op jit(solution)/shard_map/hop_b2/ppermute | solution.py:32
  62.5 1.8 %attend.6 = (f32[512,512]{1,0:T(8,128)S(1)}, f32[512,512]{1,0:T(8,128)S(1)}) custom-call(s32[21]{0:T(128)S(1)} %pad_add_fusion.1.meta, s32[512,128]{1,0:T(8,128)S(1)} %add.91.low_ref, bf16[512,512]{1,0:T(8,128)(2,1)S(1)} %project_q.1.q_ref, bf16[512,512]{1,0:T(8,128)(2,1)S(1)} %get-tuple-element.48.refs_0_), custom_call_target="tpu_custom_call" | custom-call | flops 1792000000 | bytes 262144 | tf_op jit(solution)/shard_map/attend/pallas_call | solution.py:263
  64.3 2.9 %collective-permute-done.9.refs_0_ = bf16[256,512]{1,0:T(8,128)(2,1)S(1)} collective-permute-done((bf16[256,512]{1,0:T(8,128)(2,1)S(1)}, bf16[256,512]{1,0:T(8,128)(2,1)S(1)}, u32[]{:S(2)}, u32[]{:S(2)}) %collective-permute-start.9) | collective-permute-done | bytes 262176 | tf_op jit(solution)/shard_map/hop_a1/ppermute | solution.py:32
  67.2 1.9 %collective-permute-start.10 = (bf16[256,512]{1,0:T(8,128)(2,1)S(1)}, bf16[256,512]{1,0:T(8,128)(2,1)S(1)}, u32[]{:S(2)}, u32[]{:S(2)}) collective-permute-start(bf16[256,512]{1,0:T(8,128)(2,1)S(1)} %collective-permute-done.9.refs_0_), channel_id=1, source_target_pairs={{0,8},{4,12},{8,16},{12,20},{16,24},{20,28},{24,32},{28,36},{32,40... | collective-permute-start | bytes 786440 | tf_op jit(solution)/shard_map/hop_a2/ppermute | solution.py:32
  69.7 2.8 %collective-permute-done.15.refs_2_ = bf16[256,512]{1,0:T(8,128)(2,1)S(1)} collective-permute-done((bf16[256,512]{1,0:T(8,128)(2,1)S(1)}, bf16[256,512]{1,0:T(8,128)(2,1)S(1)}, u32[]{:S(2)}, u32[]{:S(2)}) %collective-permute-start.15) | collective-permute-done | bytes 262176 | tf_op jit(solution)/shard_map/hop_b2/ppermute | solution.py:32
  72.6 1.4 %collective-permute-start.25 = (bf16[128,512]{1,0:T(8,128)(2,1)S(1)}, bf16[128,512]{1,0:T(8,128)(2,1)S(1)}, u32[]{:S(2)}, u32[]{:S(2)}) collective-permute-start(bf16[128,512]{1,0:T(8,128)(2,1)S(1)} %get-tuple-element.68), channel_id=1, source_target_pairs={{0,1},{1,2},{2,3},{3,0},{4,5},{5,6},{6,7},{7,4},{8,9},{9,10},{10,1... | collective-permute-start | bytes 393224 | tf_op jit(solution)/shard_map/ppermute | solution.py:37
  74.0 3.6 %collective-permute-start.26 = (bf16[128,512]{1,0:T(8,128)(2,1)S(1)}, bf16[128,512]{1,0:T(8,128)(2,1)S(1)}, u32[]{:S(2)}, u32[]{:S(2)}) collective-permute-start(bf16[128,512]{1,0:T(8,128)(2,1)S(1)} %get-tuple-element.67), channel_id=1, source_target_pairs={{0,2},{1,3},{2,0},{3,1},{4,6},{5,7},{6,4},{7,5},{8,10},{9,11},{10,... | collective-permute-start | bytes 393224 | tf_op jit(solution)/shard_map/ppermute | solution.py:37
  77.6 0.5 attend.7
  78.2 0.9 collective-permute-start.27
  79.1 2.0 %collective-permute-start.16 = (bf16[256,512]{1,0:T(8,128)(2,1)S(1)}, bf16[256,512]{1,0:T(8,128)(2,1)S(1)}, u32[]{:S(2)}, u32[]{:S(2)}) collective-permute-start(bf16[256,512]{1,0:T(8,128)(2,1)S(1)} %collective-permute-done.15.refs_2_), channel_id=1, source_target_pairs={{0,8},{4,12},{8,16},{12,20},{16,24},{20,28},{24,32},{28,36},{32,40... | collective-permute-start | bytes 786440 | tf_op jit(solution)/shard_map/hop_b3/ppermute | solution.py:32
  81.6 1.4 %collective-permute-done.26.refs_2_ = bf16[128,512]{1,0:T(8,128)(2,1)S(1)} collective-permute-done((bf16[128,512]{1,0:T(8,128)(2,1)S(1)}, bf16[128,512]{1,0:T(8,128)(2,1)S(1)}, u32[]{:S(2)}, u32[]{:S(2)}) %collective-permute-start.26) | collective-permute-done | bytes 131104 | tf_op jit(solution)/shard_map/ppermute | solution.py:37
  83.0 2.6 %collective-permute-start.11 = (bf16[256,512]{1,0:T(8,128)(2,1)S(1)}, bf16[256,512]{1,0:T(8,128)(2,1)S(1)}, u32[]{:S(2)}, u32[]{:S(2)}) collective-permute-start(bf16[256,512]{1,0:T(8,128)(2,1)S(1)} %collective-permute-done.10.refs_0_), channel_id=1, source_target_pairs={{0,8},{4,12},{8,16},{12,20},{16,24},{20,28},{24,32},{28,36},{32,40... | collective-permute-start | bytes 786440 | tf_op jit(solution)/shard_map/hop_a3/ppermute | solution.py:32
  85.6 3.4 %attend.8 = (f32[512,512]{1,0:T(8,128)S(1)}, f32[512,512]{1,0:T(8,128)S(1)}) custom-call(s32[21]{0:T(128)S(1)} %pad_add_fusion.1.meta, s32[512,128]{1,0:T(8,128)S(1)} %add.91.low_ref, bf16[512,512]{1,0:T(8,128)(2,1)S(1)} %project_q.1.q_ref, bf16[256,512]{1,0:T(8,128)(2,1)S(1)} %collective-permute-done.9.refs_0_, ...), custom_call_target="tpu_custom_call", output_to_operand_aliasing={{0}: (7, {}), {1}: (8, {})} | custom-call | flops 3584000000 | bytes 524288 | tf_op jit(solution)/shard_map/attend/pallas_call | solution.py:263
  89.0 2.2 %build_cache.1 = bf16[1,128,2,1024]{3,2,1,0:T(2,128)(2,1)} custom-call(s32[4]{0:T(128)S(1)} %and_select_fusion.shards, bf16[128,512]{1,0:T(8,128)(2,1)S(1)} %get-tuple-element.69.refs_0_, bf16[128,512]{1,0:T(8,128)(2,1)S(1)} %collective-permute-done.25.refs_1_, bf16[128,512]{1,0:T(8,128)(2,1)S(1)} %collective-permute-done.26.refs_2_, ...), custom_call_target="tpu_custom_call" | custom-call | flops 1000000000 | bytes 1000 | tf_op jit(solution)/shard_map/build_cache/pallas_call | solution.py:296
  91.2 0.9 collective-permute-done.16.refs_2_
  92.2 3.4 %collective-permute-start.17 = (bf16[256,512]{1,0:T(8,128)(2,1)S(1)}, bf16[256,512]{1,0:T(8,128)(2,1)S(1)}, u32[]{:S(2)}, u32[]{:S(2)}) collective-permute-start(bf16[256,512]{1,0:T(8,128)(2,1)S(1)} %collective-permute-done.16.refs_2_), channel_id=1, source_target_pairs={{0,8},{4,12},{8,16},{12,20},{16,24},{20,28},{24,32},{28,36},{32,40... | collective-permute-start | bytes 786440 | tf_op jit(solution)/shard_map/hop_b4/ppermute | solution.py:32
  95.6 1.8 %collective-permute-done.11.refs_0_ = bf16[256,512]{1,0:T(8,128)(2,1)S(1)} collective-permute-done((bf16[256,512]{1,0:T(8,128)(2,1)S(1)}, bf16[256,512]{1,0:T(8,128)(2,1)S(1)}, u32[]{:S(2)}, u32[]{:S(2)}) %collective-permute-start.11) | collective-permute-done | bytes 262176 | tf_op jit(solution)/shard_map/hop_a3/ppermute | solution.py:32
  97.4 2.7 %collective-permute-start.12 = (bf16[256,512]{1,0:T(8,128)(2,1)S(1)}, bf16[256,512]{1,0:T(8,128)(2,1)S(1)}, u32[]{:S(2)}, u32[]{:S(2)}) collective-permute-start(bf16[256,512]{1,0:T(8,128)(2,1)S(1)} %collective-permute-done.11.refs_0_), channel_id=1, source_target_pairs={{0,8},{4,12},{8,16},{12,20},{16,24},{20,28},{24,32},{28,36},{32,40... | collective-permute-start | bytes 786440 | tf_op jit(solution)/shard_map/hop_a4/ppermute | solution.py:32
  100.1 3.4 %attend.9 = (f32[512,512]{1,0:T(8,128)S(1)}, f32[512,512]{1,0:T(8,128)S(1)}) custom-call(s32[21]{0:T(128)S(1)} %pad_add_fusion.1.meta, s32[512,128]{1,0:T(8,128)S(1)} %add.91.low_ref, bf16[512,512]{1,0:T(8,128)(2,1)S(1)} %project_q.1.q_ref, bf16[256,512]{1,0:T(8,128)(2,1)S(1)} %collective-permute-done.10.refs_0_, ...), custom_call_target="tpu_custom_call", output_to_operand_aliasing={{0}: (7, {}), {1}: (8, {})} | custom-call | flops 3584000000 | bytes 524288 | tf_op jit(solution)/shard_map/attend/pallas_call | solution.py:263
  103.5 3.4 %attend.10 = (f32[512,512]{1,0:T(8,128)S(1)}, f32[512,512]{1,0:T(8,128)S(1)}) custom-call(s32[21]{0:T(128)S(1)} %pad_add_fusion.1.meta, s32[512,128]{1,0:T(8,128)S(1)} %add.91.low_ref, bf16[512,512]{1,0:T(8,128)(2,1)S(1)} %project_q.1.q_ref, bf16[256,512]{1,0:T(8,128)(2,1)S(1)} %collective-permute-done.11.refs_0_, ...), custom_call_target="tpu_custom_call", output_to_operand_aliasing={{0}: (7, {}), {1}: (8, {})} | custom-call | flops 3584000000 | bytes 524288 | tf_op jit(solution)/shard_map/attend/pallas_call | solution.py:263
  107.2 3.3 %collective-permute-done.12.refs_0_ = bf16[256,512]{1,0:T(8,128)(2,1)S(1)} collective-permute-done((bf16[256,512]{1,0:T(8,128)(2,1)S(1)}, bf16[256,512]{1,0:T(8,128)(2,1)S(1)}, u32[]{:S(2)}, u32[]{:S(2)}) %collective-permute-start.12) | collective-permute-done | bytes 262176 | tf_op jit(solution)/shard_map/hop_a4/ppermute | solution.py:32
  110.5 2.1 %attend.11 = (f32[512,512]{1,0:T(8,128)S(1)}, f32[512,512]{1,0:T(8,128)S(1)}) custom-call(s32[21]{0:T(128)S(1)} %pad_add_fusion.1.meta, s32[512,128]{1,0:T(8,128)S(1)} %add.91.low_ref, bf16[512,512]{1,0:T(8,128)(2,1)S(1)} %project_q.1.q_ref, bf16[256,512]{1,0:T(8,128)(2,1)S(1)} %collective-permute-done.12.refs_0_, ...), custom_call_target="tpu_custom_call", output_to_operand_aliasing={{0}: (5, {}), {1}: (6, {})} | custom-call | flops 1792000000 | bytes 262144 | tf_op jit(solution)/shard_map/attend/pallas_call | solution.py:263
  112.6 3.3 %attend_last.1 = bf16[512,512]{1,0:T(8,128)(2,1)} custom-call(s32[21]{0:T(128)S(1)} %pad_add_fusion.1.meta, s32[512,128]{1,0:T(8,128)S(1)} %add.91.low_ref, bf16[512,512]{1,0:T(8,128)(2,1)S(1)} %project_q.1.q_ref, bf16[256,512]{1,0:T(8,128)(2,1)S(1)} %collective-permute-done.13.refs_0_, bf16[256,512]{1,0:T(8,128)(2,1)S(1)} %collective-permute-done.28.refs_1_, ...), custom_call_target="tpu_custom_call" | custom-call | flops 1792000000 | bytes 262144 | tf_op jit(solution)/shard_map/attend_last/pallas_call | solution.py:263
  (56 shorter events, 2.5 us)
Async XLA Ops:
  0.6 29.3 %collective-permute-start.4 = (bf16[512,1152]{1,0:T(8,128)(2,1)}, bf16[512,1152]{1,0:T(8,128)(2,1)S(1)}, u32[]{:S(2)}, u32[]{:S(2)}) collective-permute-start(bf16[512,1152]{1,0:T(8,128)(2,1)} %own.1), channel_id=1, source_target_pairs={{0,1},{1,2},{2,3},{3,0},{4,5},{5,6},{6,7},{7,4},{8,9},{9,10},{10,1... | collective-permute-start | bytes 3538952 | tf_op jit(solution)/shard_map/ppermute | solution.py:37
  2.3 27.7 %collective-permute-start.5 = (bf16[512,1152]{1,0:T(8,128)(2,1)}, bf16[512,1152]{1,0:T(8,128)(2,1)S(1)}, u32[]{:S(2)}, u32[]{:S(2)}) collective-permute-start(bf16[512,1152]{1,0:T(8,128)(2,1)} %own.1), channel_id=1, source_target_pairs={{0,3},{1,0},{2,1},{3,2},{4,7},{5,4},{6,5},{7,6},{8,11},{9,8},{10,9... | collective-permute-start | bytes 3538952 | tf_op jit(solution)/shard_map/ppermute | solution.py:37
  4.8 9.7 %collective-permute-start = (s32[1,512]{1,0:T(1,128)S(1)}, s32[1,512]{1,0:T(1,128)S(1)}, u32[]{:S(2)}, u32[]{:S(2)}) collective-permute-start(s32[1,512]{1,0:T(1,128)S(1)} %bitcast.27), channel_id=1, source_target_pairs={{0,4},{4,8},{8,12},{12,16},{16,20},{20,24},{24,28},{28,32},{32,36}... | collective-permute-start | bytes 6152 | tf_op jit(solution)/shard_map/ppermute | solution.py:32
  6.7 9.6 %collective-permute-start.1 = (s32[1,512]{1,0:T(1,128)S(1)}, s32[1,512]{1,0:T(1,128)S(1)}, u32[]{:S(2)}, u32[]{:S(2)}) collective-permute-start(s32[1,512]{1,0:T(1,128)S(1)} %bitcast.28), channel_id=1, source_target_pairs={{0,8},{4,12},{8,16},{12,20},{16,24},{20,28},{24,32},{28,36},{32,40... | collective-permute-start | bytes 6152 | tf_op jit(solution)/shard_map/ppermute | solution.py:32
  12.1 23.3 %collective-permute-start.8 = (f32[1,512]{1,0:T(1,128)S(1)}, f32[1,512]{1,0:T(1,128)S(1)}, u32[]{:S(2)}, u32[]{:S(2)}) collective-permute-start(f32[1,512]{1,0:T(1,128)S(1)} %bitcast.32), channel_id=1, source_target_pairs={{0,2},{1,3},{2,0},{3,1},{4,6},{5,7},{6,4},{7,5},{8,10},{9,11},{10,... | collective-permute-start | bytes 6152 | tf_op jit(solution)/shard_map/far_square/ppermute | solution.py:37
  16.3 9.9 %collective-permute-start.2 = (s32[3,512]{1,0:T(4,128)S(1)}, s32[3,512]{1,0:T(4,128)S(1)}, u32[]{:S(2)}, u32[]{:S(2)}) collective-permute-start(s32[3,512]{1,0:T(4,128)S(1)} %pad_add_fusion), channel_id=1, source_target_pairs={{0,12},{4,16},{8,20},{12,24},{16,28},{20,32},{24,36},{28,40},{32,4... | collective-permute-start | bytes 18440 | tf_op jit(solution)/shard_map/ppermute | solution.py:32
  19.5 9.5 %collective-permute-start.3 = (s32[3,512]{1,0:T(4,128)S(1)}, s32[3,512]{1,0:T(4,128)S(1)}, u32[]{:S(2)}, u32[]{:S(2)}) collective-permute-start(s32[3,512]{1,0:T(4,128)S(1)} %pad_add_fusion), channel_id=1, source_target_pairs={{0,24},{4,28},{8,32},{12,36},{16,40},{20,44},{24,48},{28,52},{32,5... | collective-permute-start | bytes 18440 | tf_op jit(solution)/shard_map/ppermute | solution.py:32
  28.9 6.6 %slice-start = ((s8[4718592]{0:T(1024)(128)(4,1)}), s8[4194304]{0:T(1024)(128)(4,1)S(1)}, s32[]{:S(2)}) async-start(s8[4718592]{0:T(1024)(128)(4,1)} %bitcast.24), calls=%async_computation | async-start | bytes 8388608
  29.0 5.5 %copy-start.4 = (f32[128]{0:T(128)S(1)}, f32[128]{0:T(128)}, u32[]{:S(2)}) copy-start(f32[128]{0:T(128)} %constant.76) | copy-start | bytes 1540
  29.0 6.6 %slice-start.1 = ((s8[4718592]{0:T(1024)(128)(4,1)}), s8[524288]{0:T(1024)(128)(4,1)S(1)}, s32[]{:S(2)}) async-start(s8[4718592]{0:T(1024)(128)(4,1)} %bitcast.24), calls=%async_computation.1 | async-start | bytes 1048576
  29.0 6.6 %copy-start = (bf16[4608,256]{1,0:T(8,128)(2,1)S(1)}, bf16[4608,256]{1,0:T(8,128)(2,1)}, u32[]{:S(2)}) copy-start(bf16[4608,256]{1,0:T(8,128)(2,1)} %refs_4_.1) | copy-start | bytes 7077892
  29.0 6.6 %copy-start.1 = (bf16[4608,256]{1,0:T(8,128)(2,1)S(1)}, bf16[4608,256]{1,0:T(8,128)(2,1)}, u32[]{:S(2)}) copy-start(bf16[4608,256]{1,0:T(8,128)(2,1)} %refs_5_.1) | copy-start | bytes 7077892
  29.0 6.6 %copy-start.2 = (bf16[512,1152]{1,0:T(8,128)(2,1)S(1)}, bf16[512,1152]{1,0:T(8,128)(2,1)}, u32[]{:S(2)}) copy-start(bf16[512,1152]{1,0:T(8,128)(2,1)} %own.1) | copy-start | bytes 3538948
  30.0 15.5 %collective-permute-start.6 = (bf16[256,1152]{1,0:T(8,128)(2,1)S(1)}, bf16[256,1152]{1,0:T(8,128)(2,1)S(1)}, u32[]{:S(2)}, u32[]{:S(2)}) collective-permute-start(bf16[256,1152]{1,0:T(8,128)(2,1)S(1)} %get-tuple-element.35), channel_id=1, source_target_pairs={{0,1},{1,2},{2,3},{3,0},{4,5},{5,6},{6,7},{7,4},{8,9},{9,10},{10,1... | collective-permute-start | bytes 1769480 | tf_op jit(solution)/shard_map/ppermute | solution.py:37
  32.7 13.7 %collective-permute-start.7 = (bf16[256,1152]{1,0:T(8,128)(2,1)S(1)}, bf16[256,1152]{1,0:T(8,128)(2,1)S(1)}, u32[]{:S(2)}, u32[]{:S(2)}) collective-permute-start(bf16[256,1152]{1,0:T(8,128)(2,1)S(1)} %get-tuple-element.37), channel_id=1, source_target_pairs={{0,3},{1,0},{2,1},{3,2},{4,7},{5,4},{6,5},{7,6},{8,11},{9,8},{10,9... | collective-permute-start | bytes 1769480 | tf_op jit(solution)/shard_map/ppermute | solution.py:37
  35.6 10.7 %copy-start.3 = (s32[1,4]{1,0:T(1,128)S(1)}, s32[1,4]{1,0:T(1,128)}, u32[]{:S(2)}) copy-start(s32[1,4]{1,0:T(1,128)} %param.14) | copy-start | bytes 52
  48.1 12.4 %collective-permute-start.14 = (bf16[256,512]{1,0:T(8,128)(2,1)S(1)}, bf16[256,512]{1,0:T(8,128)(2,1)S(1)}, u32[]{:S(2)}, u32[]{:S(2)}) collective-permute-start(bf16[256,512]{1,0:T(8,128)(2,1)S(1)} %get-tuple-element.45), channel_id=1, source_target_pairs={{0,8},{4,12},{8,16},{12,20},{16,24},{20,28},{24,32},{28,36},{32,40... | collective-permute-start | bytes 786440 | tf_op jit(solution)/shard_map/hop_b1/ppermute | solution.py:32
  53.7 20.2 %collective-permute-start.24 = (bf16[512,512]{1,0:T(8,128)(2,1)S(1)}, bf16[512,512]{1,0:T(8,128)(2,1)S(1)}, u32[]{:S(2)}, u32[]{:S(2)}) collective-permute-start(bf16[512,512]{1,0:T(8,128)(2,1)S(1)} %get-tuple-element.48.refs_0_), channel_id=1, source_target_pairs={{0,4},{4,0},{8,12},{12,8},{16,20},{20,16},{24,28},{28,24},{32,36},... | collective-permute-start | bytes 1572872 | tf_op jit(solution)/shard_map/cross_own/ppermute | solution.py:41
  53.8 13.4 %collective-permute-start.9 = (bf16[256,512]{1,0:T(8,128)(2,1)S(1)}, bf16[256,512]{1,0:T(8,128)(2,1)S(1)}, u32[]{:S(2)}, u32[]{:S(2)}) collective-permute-start(bf16[256,512]{1,0:T(8,128)(2,1)S(1)} %get-tuple-element.43), channel_id=1, source_target_pairs={{0,8},{4,12},{8,16},{12,20},{16,24},{20,28},{24,32},{28,36},{32,40... | collective-permute-start | bytes 786440 | tf_op jit(solution)/shard_map/hop_a1/ppermute | solution.py:32
  60.5 12.1 %collective-permute-start.15 = (bf16[256,512]{1,0:T(8,128)(2,1)S(1)}, bf16[256,512]{1,0:T(8,128)(2,1)S(1)}, u32[]{:S(2)}, u32[]{:S(2)}) collective-permute-start(bf16[256,512]{1,0:T(8,128)(2,1)S(1)} %collective-permute-done.14.refs_2_), channel_id=1, source_target_pairs={{0,8},{4,12},{8,16},{12,20},{16,24},{20,28},{24,32},{28,36},{32,40... | collective-permute-start | bytes 786440 | tf_op jit(solution)/shard_map/hop_b2/ppermute | solution.py:32
  67.2 11.9 %collective-permute-start.10 = (bf16[256,512]{1,0:T(8,128)(2,1)S(1)}, bf16[256,512]{1,0:T(8,128)(2,1)S(1)}, u32[]{:S(2)}, u32[]{:S(2)}) collective-permute-start(bf16[256,512]{1,0:T(8,128)(2,1)S(1)} %collective-permute-done.9.refs_0_), channel_id=1, source_target_pairs={{0,8},{4,12},{8,16},{12,20},{16,24},{20,28},{24,32},{28,36},{32,40... | collective-permute-start | bytes 786440 | tf_op jit(solution)/shard_map/hop_a2/ppermute | solution.py:32
  69.1 9.1 %collective-permute-start.22 = (bf16[256,512]{1,0:T(8,128)(2,1)S(1)}, bf16[256,512]{1,0:T(8,128)(2,1)S(1)}, u32[]{:S(2)}, u32[]{:S(2)}) collective-permute-start(bf16[256,512]{1,0:T(8,128)(2,1)S(1)} %collective-permute-done.9.refs_0_), channel_id=1, source_target_pairs={{0,4},{4,0},{8,12},{12,8},{16,20},{20,16},{24,28},{28,24},{32,36},... | collective-permute-start | bytes 786440 | tf_op jit(solution)/shard_map/cross_a1/ppermute | solution.py:41
  69.2 9.8 %collective-permute-start.23 = (bf16[256,512]{1,0:T(8,128)(2,1)S(1)}, bf16[256,512]{1,0:T(8,128)(2,1)S(1)}, u32[]{:S(2)}, u32[]{:S(2)}) collective-permute-start(bf16[256,512]{1,0:T(8,128)(2,1)S(1)} %collective-permute-done.14.refs_2_), channel_id=1, source_target_pairs={{0,4},{4,0},{8,12},{12,8},{16,20},{20,16},{24,28},{28,24},{32,36},... | collective-permute-start | bytes 786440 | tf_op jit(solution)/shard_map/cross_b1/ppermute | solution.py:41
  72.6 8.5 %collective-permute-start.25 = (bf16[128,512]{1,0:T(8,128)(2,1)S(1)}, bf16[128,512]{1,0:T(8,128)(2,1)S(1)}, u32[]{:S(2)}, u32[]{:S(2)}) collective-permute-start(bf16[128,512]{1,0:T(8,128)(2,1)S(1)} %get-tuple-element.68), channel_id=1, source_target_pairs={{0,1},{1,2},{2,3},{3,0},{4,5},{5,6},{6,7},{7,4},{8,9},{9,10},{10,1... | collective-permute-start | bytes 393224 | tf_op jit(solution)/shard_map/ppermute | solution.py:37
  74.0 9.0 %collective-permute-start.26 = (bf16[128,512]{1,0:T(8,128)(2,1)S(1)}, bf16[128,512]{1,0:T(8,128)(2,1)S(1)}, u32[]{:S(2)}, u32[]{:S(2)}) collective-permute-start(bf16[128,512]{1,0:T(8,128)(2,1)S(1)} %get-tuple-element.67), channel_id=1, source_target_pairs={{0,2},{1,3},{2,0},{3,1},{4,6},{5,7},{6,4},{7,5},{8,10},{9,11},{10,... | collective-permute-start | bytes 393224 | tf_op jit(solution)/shard_map/ppermute | solution.py:37
  78.2 10.8 %collective-permute-start.27 = (bf16[128,512]{1,0:T(8,128)(2,1)S(1)}, bf16[128,512]{1,0:T(8,128)(2,1)S(1)}, u32[]{:S(2)}, u32[]{:S(2)}) collective-permute-start(bf16[128,512]{1,0:T(8,128)(2,1)S(1)} %get-tuple-element.66), channel_id=1, source_target_pairs={{0,3},{1,0},{2,1},{3,2},{4,7},{5,4},{6,5},{7,6},{8,11},{9,8},{10,9... | collective-permute-start | bytes 393224 | tf_op jit(solution)/shard_map/ppermute | solution.py:37
  79.1 18.3 %collective-permute-start.21 = (bf16[256,512]{1,0:T(8,128)(2,1)S(1)}, bf16[256,512]{1,0:T(8,128)(2,1)S(1)}, u32[]{:S(2)}, u32[]{:S(2)}) collective-permute-start(bf16[256,512]{1,0:T(8,128)(2,1)S(1)} %collective-permute-done.15.refs_2_), channel_id=1, source_target_pairs={{0,4},{4,0},{8,12},{12,8},{16,20},{20,16},{24,28},{28,24},{32,36},... | collective-permute-start | bytes 786440 | tf_op jit(solution)/shard_map/cross_b2/ppermute | solution.py:41
  79.1 13.1 %collective-permute-start.16 = (bf16[256,512]{1,0:T(8,128)(2,1)S(1)}, bf16[256,512]{1,0:T(8,128)(2,1)S(1)}, u32[]{:S(2)}, u32[]{:S(2)}) collective-permute-start(bf16[256,512]{1,0:T(8,128)(2,1)S(1)} %collective-permute-done.15.refs_2_), channel_id=1, source_target_pairs={{0,8},{4,12},{8,16},{12,20},{16,24},{20,28},{24,32},{28,36},{32,40... | collective-permute-start | bytes 786440 | tf_op jit(solution)/shard_map/hop_b3/ppermute | solution.py:32
  81.1 19.0 %collective-permute-start.20 = (bf16[256,512]{1,0:T(8,128)(2,1)S(1)}, bf16[256,512]{1,0:T(8,128)(2,1)S(1)}, u32[]{:S(2)}, u32[]{:S(2)}) collective-permute-start(bf16[256,512]{1,0:T(8,128)(2,1)S(1)} %collective-permute-done.10.refs_0_), channel_id=1, source_target_pairs={{0,4},{4,0},{8,12},{12,8},{16,20},{20,16},{24,28},{28,24},{32,36},... | collective-permute-start | bytes 786440 | tf_op jit(solution)/shard_map/cross_a2/ppermute | solution.py:41
  83.0 14.4 %collective-permute-start.11 = (bf16[256,512]{1,0:T(8,128)(2,1)S(1)}, bf16[256,512]{1,0:T(8,128)(2,1)S(1)}, u32[]{:S(2)}, u32[]{:S(2)}) collective-permute-start(bf16[256,512]{1,0:T(8,128)(2,1)S(1)} %collective-permute-done.10.refs_0_), channel_id=1, source_target_pairs={{0,8},{4,12},{8,16},{12,20},{16,24},{20,28},{24,32},{28,36},{32,40... | collective-permute-start | bytes 786440 | tf_op jit(solution)/shard_map/hop_a3/ppermute | solution.py:32
  92.2 11.4 %collective-permute-start.19 = (bf16[256,512]{1,0:T(8,128)(2,1)S(1)}, bf16[256,512]{1,0:T(8,128)(2,1)S(1)}, u32[]{:S(2)}, u32[]{:S(2)}) collective-permute-start(bf16[256,512]{1,0:T(8,128)(2,1)S(1)} %collective-permute-done.16.refs_2_), channel_id=1, source_target_pairs={{0,4},{4,0},{8,12},{12,8},{16,20},{20,16},{24,28},{28,24},{32,36},... | collective-permute-start | bytes 786440 | tf_op jit(solution)/shard_map/cross_b3/ppermute | solution.py:41
  92.2 14.8 %collective-permute-start.17 = (bf16[256,512]{1,0:T(8,128)(2,1)S(1)}, bf16[256,512]{1,0:T(8,128)(2,1)S(1)}, u32[]{:S(2)}, u32[]{:S(2)}) collective-permute-start(bf16[256,512]{1,0:T(8,128)(2,1)S(1)} %collective-permute-done.16.refs_2_), channel_id=1, source_target_pairs={{0,8},{4,12},{8,16},{12,20},{16,24},{20,28},{24,32},{28,36},{32,40... | collective-permute-start | bytes 786440 | tf_op jit(solution)/shard_map/hop_b4/ppermute | solution.py:32
  97.4 6.1 %collective-permute-start.18 = (bf16[256,512]{1,0:T(8,128)(2,1)S(1)}, bf16[256,512]{1,0:T(8,128)(2,1)S(1)}, u32[]{:S(2)}, u32[]{:S(2)}) collective-permute-start(bf16[256,512]{1,0:T(8,128)(2,1)S(1)} %collective-permute-done.11.refs_0_), channel_id=1, source_target_pairs={{0,4},{4,0},{8,12},{12,8},{16,20},{20,16},{24,28},{28,24},{32,36},... | collective-permute-start | bytes 786440 | tf_op jit(solution)/shard_map/cross_a3/ppermute | solution.py:41
  97.4 13.1 %collective-permute-start.12 = (bf16[256,512]{1,0:T(8,128)(2,1)S(1)}, bf16[256,512]{1,0:T(8,128)(2,1)S(1)}, u32[]{:S(2)}, u32[]{:S(2)}) collective-permute-start(bf16[256,512]{1,0:T(8,128)(2,1)S(1)} %collective-permute-done.11.refs_0_), channel_id=1, source_target_pairs={{0,8},{4,12},{8,16},{12,20},{16,24},{20,28},{24,32},{28,36},{32,40... | collective-permute-start | bytes 786440 | tf_op jit(solution)/shard_map/hop_a4/ppermute | solution.py:32
  106.9 5.7 %collective-permute-start.28 = (bf16[256,512]{1,0:T(8,128)(2,1)S(1)}, bf16[256,512]{1,0:T(8,128)(2,1)S(1)}, u32[]{:S(2)}, u32[]{:S(2)}) collective-permute-start(bf16[256,512]{1,0:T(8,128)(2,1)S(1)} %collective-permute-done.17.refs_1_), channel_id=1, source_target_pairs={{0,4},{4,0},{8,12},{12,8},{16,20},{20,16},{24,28},{28,24},{32,36},... | collective-permute-start | bytes 786440 | tf_op jit(solution)/shard_map/cross_b4/ppermute | solution.py:41
  110.5 2.1 %collective-permute-start.13 = (bf16[256,512]{1,0:T(8,128)(2,1)S(1)}, bf16[256,512]{1,0:T(8,128)(2,1)S(1)}, u32[]{:S(2)}, u32[]{:S(2)}) collective-permute-start(bf16[256,512]{1,0:T(8,128)(2,1)S(1)} %collective-permute-done.12.refs_0_), channel_id=1, source_target_pairs={{0,4},{4,0},{8,12},{12,8},{16,20},{20,16},{24,28},{28,24},{32,36},... | collective-permute-start | bytes 786440 | tf_op jit(solution)/shard_map/cross_a4/ppermute | solution.py:41
